TPU v7x, 32 devices: a whole 2x2x4 slice. The times are simulated.
32 devices in a mesh: groups: 2 (over x), ctx: 16 (over z, y, core).
Axes of the slice: x: 2, y: 2, z: 4, core: 2. Of those that a mesh axis runs over, the one named last changes fastest.
Arguments:
- queries: bfloat16 [4096, 2048], P(('groups', 'ctx')), parts along dimension 0, may hold values from -8 to 8
- keys: bfloat16 [4096, 2048], P(('groups', 'ctx')), parts along dimension 0, may hold values from -8 to 8
- values: bfloat16 [4096, 2048], P(('groups', 'ctx')), parts along dimension 0, may hold values from -8 to 8
- doc_start: int32 [32], P('groups'), parts along dimension 0, may hold values from 0 to 15, as said below
- out_weight: bfloat16 [2048, 4096], P(None, 'ctx'), may hold values from -0.125 to 0.125
Outputs:
- layer_out: bfloat16 [4096, 4096], P(('groups', 'ctx')), parts along dimension 0
There are 2 independent parts, one for each index of `groups`. A program takes and returns all parts, laid end to end along the dimension named above; an argument that names none is the same for every part. Nothing has to cross between parts.
Inputs may be any that keep to these rules, and one draw needn't show every extreme that they name: doc_start[b] <= b, entries never fall, doc_start[doc_start[b]] = doc_start[b]; one document covers at least blocks 16 // 4 to 12.
All inputs are finite; a program needn't handle non-finite values.
Results may differ from a plain program's by a relative error of at most 0.0053.
Values may be sent and summed in bfloat16 or wider, within the bound.
No kernel may reach another device: no remote copies, remote signals or barrier semaphores. Data moves between devices by JAX's collectives and lax.ppermute only.
A program may use at most 128 MiB of HBM per device.

v0:
```python
import jax
import jax.numpy as jnp
from jax import lax
from jax.sharding import PartitionSpec as P

HD = 128
BLOCK = 128


def partner(value, axis, apart):
    mask = 2**apart
    pairs = [(source, source ^ mask) for source in range(lax.axis_size(axis))]
    return lax.ppermute(value, axis, pairs)


def pair_mean(array):
    halves = array.reshape(array.shape[0] // 2, 2, array.shape[1]).astype(jnp.float32)
    return ((halves[:, 0] + halves[:, 1]) * 0.5).astype(jnp.bfloat16)


def doc_lookup(blocks, table):
    labels = jnp.arange(table.shape[0], dtype=jnp.int32)
    return jnp.sum(jnp.where(blocks[..., None] == labels, table, 0), axis=-1)


def covered(first_token, factor):
    return (first_token // BLOCK, (first_token + factor - 1) // BLOCK)


def trade(pair, bit):
    return partner((pair[0], pair[1]), "ctx", bit)


def per_device(queries, keys, values, doc_start, out_weight):
    length, width = queries.shape
    heads = width // HD
    blocks = length // BLOCK
    local_depth = blocks.bit_length() - 1
    devices = lax.axis_size("ctx")
    position = lax.axis_index("ctx")
    bit_count = devices.bit_length() - 1
    scale = HD ** (-0.5)
    offsets = jnp.arange(BLOCK, dtype=jnp.int32)
    block_ids = position * blocks + jnp.arange(blocks, dtype=jnp.int32)
    own_docs = doc_lookup(block_ids, doc_start)
    level_keys = [keys]
    level_values = [values]
    near_keys = keys.reshape(blocks, BLOCK, width)
    near_values = values.reshape(blocks, BLOCK, width)
    near_first = jnp.broadcast_to(block_ids[:, None], (blocks, BLOCK))
    near_last = jnp.broadcast_to(block_ids[:, None], (blocks, BLOCK))
    local_allowed = (doc_lookup(near_first, doc_start) == own_docs[:, None]) & (
        doc_lookup(near_last, doc_start) == own_docs[:, None]
    )
    query_blocks = queries.reshape(blocks, BLOCK, heads, HD)
    local_scores = (
        jnp.einsum(
            "bqhd,bkhd->bhqk",
            query_blocks,
            near_keys.reshape(blocks, -1, heads, HD),
            preferred_element_type=jnp.float32,
        )
        * scale
    )
    local_scores = jnp.where(local_allowed[:, None, None, :], local_scores, -jnp.inf)
    far_keys = []
    far_values = []
    far_first = []
    far_last = []

    def record(other_keys, other_values, bit):
        factor = 2 ** (local_depth + bit)
        sibling = jnp.bitwise_xor(position // 2**bit, 1)
        first_token = sibling * 2**bit * length + offsets * factor
        lower, upper = covered(first_token, factor)
        far_keys.append(other_keys)
        far_values.append(other_values)
        far_first.append(lower)
        far_last.append(upper)

    rep_keys = level_keys[local_depth]
    rep_values = level_values[local_depth]
    for bit in range(bit_count):
        other_keys, other_values = trade((rep_keys, rep_values), bit)
        record(other_keys, other_values, bit)
        if bit + 1 < bit_count:
            upper_half = position // 2**bit % 2 == 1
            low_keys = jnp.where(upper_half, other_keys, rep_keys)
            high_keys = jnp.where(upper_half, rep_keys, other_keys)
            low_values = jnp.where(upper_half, other_values, rep_values)
            high_values = jnp.where(upper_half, rep_values, other_values)
            rep_keys = jnp.concatenate([pair_mean(low_keys), pair_mean(high_keys)], 0)
            rep_values = jnp.concatenate([pair_mean(low_values), pair_mean(high_values)], 0)
    far_key_set = jnp.concatenate(far_keys, 0).reshape(-1, heads, HD)
    far_value_set = jnp.concatenate(far_values, 0).reshape(-1, heads, HD)
    far_lower = doc_lookup(jnp.concatenate(far_first, 0), doc_start)
    far_upper = doc_lookup(jnp.concatenate(far_last, 0), doc_start)
    far_allowed = (far_lower[None, :] == own_docs[:, None]) & (
        far_upper[None, :] == own_docs[:, None]
    )
    far_scores = (
        jnp.einsum("bqhd,khd->bhqk", query_blocks, far_key_set, preferred_element_type=jnp.float32)
        * scale
    )
    far_scores = jnp.where(far_allowed[:, None, None, :], far_scores, -jnp.inf)
    row_max = jnp.maximum(
        jnp.max(local_scores, axis=-1, keepdims=True), jnp.max(far_scores, axis=-1, keepdims=True)
    )
    local_raised = jnp.exp(local_scores - row_max)
    far_raised = jnp.exp(far_scores - row_max)
    total = jnp.sum(local_raised, axis=-1, keepdims=True) + jnp.sum(
        far_raised, axis=-1, keepdims=True
    )
    local_weights = (local_raised / total).astype(jnp.bfloat16)
    far_weights = (far_raised / total).astype(jnp.bfloat16)
    attended = jnp.einsum(
        "bhqk,bkhd->bqhd",
        local_weights,
        near_values.reshape(blocks, -1, heads, HD),
        preferred_element_type=jnp.float32,
    )
    attended = attended + jnp.einsum(
        "bhqk,khd->bqhd", far_weights, far_value_set, preferred_element_type=jnp.float32
    )
    attended = attended.reshape(length, width).astype(jnp.bfloat16)
    return jnp.dot(
        attended,
        lax.all_gather(out_weight, "ctx", axis=1, tiled=True),
        preferred_element_type=jnp.float32,
    ).astype(jnp.bfloat16)


def solution(mesh):
    placed = (
        P(("groups", "ctx"), None),
        P(("groups", "ctx"), None),
        P(("groups", "ctx"), None),
        P("groups"),
        P(None, "ctx"),
    )
    return jax.shard_map(
        per_device,
        mesh=mesh,
        in_specs=placed,
        out_specs=P(("groups", "ctx"), None),
        check_vma=False,
    )
```

profile of v0, /device:TPU:0, one launch (start us, length us, event | category | flops | bytes accessed | tf_op | source)
XLA Modules:
  0.0 208.6 jit_solution(16205559302625932448)
XLA Ops:
  6.5 0.7 all-gather.2.cloned.1.call-update
  7.3 0.5 collective-permute-start
  7.9 1.3 select_reduce_fusion.3
  9.3 0.7 select_reduce_fusion.2
  10.1 0.6 compare_and_fusion.1
  10.7 2.5 %fusion.55 = (f32[16,128]{1,0:T(8,128)S(1)}, f32[16,128,128]{1,2,0:T(8,128)}) fusion(pred[128]{0:T(512)(128)(4,1)S(1)} %compare_and_fusion.1, bf16[128,2048]{1,0:T(8,128)(2,1)} %param.6, bf16[128,2048]{1,0:T(8,128)(2,1)S(1)} %copy-done), kind=kOutput, calls=%fused_computation.144 | convolution fusion | flops 67893248 | bytes 2105472 | tf_op jit(solution)/shard_map/bqhd,bkhd->bhqk/dot_general | solution.py:57
  13.2 3.2 %select_convert_fusion.5 = (f32[128,2048]{1,0:T(8,128)}, f32[128,2048]{1,0:T(8,128)}, f32[128,2048]{1,0:T(8,128)S(1)}, f32[128,2048]{1,0:T(8,128)S(1)}) fusion(bf16[128,2048]{1,0:T(8,128)(2,1)} %collective-permute-done.4, bf16[128,2048]{1,0:T(8,128)(2,1)} %param.7, pred[]{:T(512)S(6)} %eq.117, bf16[128,2048]{1,0:T(8,128)(2,1)} %param.6, ...), kind=kLoop, calls=%fused_computation.61 | loop fusion | flops 2097152 | bytes 6291457 | tf_op jit(solution)/shard_map/convert_element_type | solution.py:17
  16.4 2.8 %reshape.259 = f32[64,2,2048]{2,1,0:T(2,128)} reshape(f32[128,2048]{1,0:T(8,128)} %get-tuple-element.12) | data formatting | bytes 2097152 | tf_op jit(solution)/shard_map/convert_element_type | solution.py:17
  19.2 2.8 %fusion.42 = bf16[64,1,2048]{2,1,0:T(2,128)(2,1)S(1)} fusion(f32[64,2,2048]{2,1,0:T(2,128)} %reshape.259), kind=kLoop, calls=%fused_computation.77 | loop fusion | flops 393216 | bytes 1310720 | tf_op jit(solution)/shard_map/convert_element_type | solution.py:18
  22.1 0.2 copy.383
  22.2 2.9 %reshape.258 = f32[64,2,2048]{2,1,0:T(2,128)} reshape(f32[128,2048]{1,0:T(8,128)} %get-tuple-element.11) | data formatting | bytes 2097152 | tf_op jit(solution)/shard_map/convert_element_type | solution.py:17
  25.1 2.6 %fusion.41 = bf16[64,1,2048]{2,1,0:T(2,128)(2,1)S(1)} fusion(f32[64,2,2048]{2,1,0:T(2,128)} %reshape.258), kind=kLoop, calls=%fused_computation.76 | loop fusion | flops 393216 | bytes 1310720 | tf_op jit(solution)/shard_map/convert_element_type | solution.py:18
  27.9 0.9 pad_maximum_fusion.5
  28.8 2.8 %collective-permute-start.5 = (bf16[128,2048]{1,0:T(8,128)(2,1)}, bf16[128,2048]{1,0:T(8,128)(2,1)}, u32[]{:S(2)}, u32[]{:S(2)}) collective-permute-start(bf16[128,2048]{1,0:T(8,128)(2,1)} %pad_maximum_fusion.5), channel_id=1, source_target_pairs={{0,2},{1,3},{2,0},{3,1},{4,6},{5,7},{6,4},{7,5},{8,10},{9,11},{10,... | collective-permute-start | bytes 1572872 | tf_op jit(solution)/shard_map/ppermute | solution.py:13
  31.6 1.6 reshape.253
  33.2 2.6 %fusion.36 = bf16[64,1,2048]{2,1,0:T(2,128)(2,1)S(1)} fusion(f32[64,2,2048]{2,1,0:T(2,128)} %reshape.253), kind=kLoop, calls=%fused_computation.71 | loop fusion | flops 393216 | bytes 1310720 | tf_op jit(solution)/shard_map/convert_element_type | solution.py:18
  36.0 0.6 reshape.252
  36.6 0.7 fusion.35
  37.5 0.8 pad_maximum_fusion.2
  38.3 7.7 %collective-permute-done.5 = bf16[128,2048]{1,0:T(8,128)(2,1)} collective-permute-done((bf16[128,2048]{1,0:T(8,128)(2,1)}, bf16[128,2048]{1,0:T(8,128)(2,1)}, u32[]{:S(2)}, u32[]{:S(2)}) %collective-permute-start.5) | collective-permute-done | bytes 524320 | tf_op jit(solution)/shard_map/ppermute | solution.py:13
  46.1 1.4 select_convert_fusion.3
  47.4 1.6 reshape.261
  49.0 2.6 %fusion.44 = bf16[64,1,2048]{2,1,0:T(2,128)(2,1)S(1)} fusion(f32[64,2,2048]{2,1,0:T(2,128)} %reshape.261), kind=kLoop, calls=%fused_computation.79 | loop fusion | flops 393216 | bytes 1310720 | tf_op jit(solution)/shard_map/convert_element_type | solution.py:18
  51.7 0.6 reshape.260
  52.4 0.9 fusion.43
  53.5 0.9 pad_maximum_fusion.6
  54.4 1.6 collective-permute-start.6
  56.0 1.1 collective-permute-done.1
  57.1 1.3 select_convert_fusion.9
  58.4 1.6 reshape.255
  60.0 2.6 %fusion.38 = bf16[64,1,2048]{2,1,0:T(2,128)(2,1)S(1)} fusion(f32[64,2,2048]{2,1,0:T(2,128)} %reshape.255), kind=kLoop, calls=%fused_computation.73 | loop fusion | flops 393216 | bytes 1310720 | tf_op jit(solution)/shard_map/convert_element_type | solution.py:18
  62.7 0.6 reshape.254
  63.3 0.7 fusion.37
  64.3 0.8 pad_maximum_fusion.3
  65.1 1.5 collective-permute-start.2
  66.6 13.1 %collective-permute-done.6 = bf16[128,2048]{1,0:T(8,128)(2,1)} collective-permute-done((bf16[128,2048]{1,0:T(8,128)(2,1)}, bf16[128,2048]{1,0:T(8,128)(2,1)}, u32[]{:S(2)}, u32[]{:S(2)}) %collective-permute-start.6) | collective-permute-done | bytes 524320 | tf_op jit(solution)/shard_map/ppermute | solution.py:13
  79.7 1.3 select_convert_fusion.1
  81.1 1.6 reshape.263
  82.7 2.6 %fusion.46 = bf16[64,1,2048]{2,1,0:T(2,128)(2,1)S(1)} fusion(f32[64,2,2048]{2,1,0:T(2,128)} %reshape.263), kind=kLoop, calls=%fused_computation.81 | loop fusion | flops 393216 | bytes 1310720 | tf_op jit(solution)/shard_map/convert_element_type | solution.py:18
  85.4 0.6 reshape.262
  86.0 0.7 fusion.45
  86.9 0.9 pad_maximum_fusion.7
  87.8 32.2 %collective-permute-done.2 = bf16[128,2048]{1,0:T(8,128)(2,1)} collective-permute-done((bf16[128,2048]{1,0:T(8,128)(2,1)}, bf16[128,2048]{1,0:T(8,128)(2,1)}, u32[]{:S(2)}, u32[]{:S(2)}) %collective-permute-start.2) | collective-permute-done | bytes 524320 | tf_op jit(solution)/shard_map/ppermute | solution.py:13
  120.0 1.3 select_convert_fusion.7
  121.3 1.6 reshape.257
  122.9 2.6 %fusion.40 = bf16[64,1,2048]{2,1,0:T(2,128)(2,1)S(1)} fusion(f32[64,2,2048]{2,1,0:T(2,128)} %reshape.257), kind=kLoop, calls=%fused_computation.75 | loop fusion | flops 393216 | bytes 1310720 | tf_op jit(solution)/shard_map/convert_element_type | solution.py:18
  125.7 0.6 reshape.256
  126.3 0.7 fusion.39
  127.2 0.8 pad_maximum_fusion.4
  128.1 1.2 copy.334
  129.3 0.6 compare_and_fusion
  130.0 1.8 pad_maximum_fusion.1
  131.8 2.5 %copy.329 = bf16[512,2048]{0,1:T(8,128)(2,1)} copy(bf16[512,2048]{1,0:T(8,128)(2,1)S(1)} %pad_maximum_fusion.1) | data formatting | bytes 4194304 | tf_op jit(solution)/shard_map/concatenate | solution.py:95
  134.3 42.1 %collective-permute-done.3 = bf16[128,2048]{1,0:T(8,128)(2,1)} collective-permute-done((bf16[128,2048]{1,0:T(8,128)(2,1)}, bf16[128,2048]{1,0:T(8,128)(2,1)}, u32[]{:S(2)}, u32[]{:S(2)}) %collective-permute-start.3) | collective-permute-done | bytes 524320 | tf_op jit(solution)/shard_map/ppermute | solution.py:13
  176.4 1.8 pad_maximum_fusion
  178.2 2.5 %copy.324 = bf16[512,2048]{0,1:T(8,128)(2,1)} copy(bf16[512,2048]{1,0:T(8,128)(2,1)S(1)} %pad_maximum_fusion) | data formatting | bytes 4194304 | tf_op jit(solution)/shard_map/concatenate | solution.py:94
  180.7 2.9 %bitcast_reduce_fusion = (f32[16,128]{1,0:T(8,128)S(1)}, f32[16,512,128]{2,1,0:T(8,128)S(1)}) fusion(pred[512]{0:T(512)(128)(4,1)S(1)} %compare_and_fusion, bf16[512,16,128]{0,2,1:T(8,128)(2,1)} %bitcast.130, bf16[128,2048]{1,0:T(8,128)(2,1)S(1)} %copy-done), kind=kOutput, calls=%fused_computation.2 | convolution fusion | flops 271579136 | bytes 6824448 | tf_op jit(solution)/shard_map/bqhd,khd->bhqk/dot_general | solution.py:102
  183.6 0.2 fusion.15
  183.8 0.9 fusion.1
  184.7 0.3 convolution_bitcast_fusion
  185.0 0.4 copy-done.4
  185.4 1.7 fusion.12
  187.1 5.6 %all-gather.2.cloned.1.call-done = bf16[2048,4096]{1,0:T(8,128)(2,1)} async-done(((bf16[2048,256]{1,0:T(8,128)(2,1)}), bf16[2048,4096]{1,0:T(8,128)(2,1)}) %all-gather.2.cloned.1.call-update) | async-done | bytes 16777232 | tf_op jit(solution)/shard_map/all_gather | solution.py:128
  192.7 9.1 %convolution_convert_fusion = bf16[128,4096]{1,0:T(8,128)(2,1)} fusion(bf16[128,2048]{0,1:T(8,128)(2,1)S(1)} %bitcast.152, bf16[2048,4096]{1,0:T(8,128)(2,1)} %all-gather.2.cloned.1.call-done), kind=kOutput, calls=%fused_computation | convolution fusion | flops 2148007936 | bytes 18350080 | tf_op jit(solution)/shard_map/dot_general | solution.py:126
  (47 shorter events, 2.0 us)
Async XLA Ops:
  6.5 4.2 %copy-start = (bf16[128,2048]{1,0:T(8,128)(2,1)S(1)}, bf16[128,2048]{1,0:T(8,128)(2,1)}, u32[]{:S(2)}) copy-start(bf16[128,2048]{1,0:T(8,128)(2,1)} %param.5) | copy-start | bytes 1572868
  6.5 186.2 %all-gather.2.cloned.1.call-start = ((), (), s32[]{:S(2)}) async-start(), calls=%async_computation | async-start | bytes 17825792 | tf_op jit(solution)/shard_map/all_gather | solution.py:128
  7.3 6.0 %collective-permute-start = (bf16[128,2048]{1,0:T(8,128)(2,1)}, bf16[128,2048]{1,0:T(8,128)(2,1)S(1)}, u32[]{:S(2)}, u32[]{:S(2)}) collective-permute-start(bf16[128,2048]{1,0:T(8,128)(2,1)} %param.6), channel_id=1, source_target_pairs={{0,1},{1,0},{2,3},{3,2},{4,5},{5,4},{6,7},{7,6},{8,9},{9,8},{10,11... | collective-permute-start | bytes 1572872 | tf_op jit(solution)/shard_map/ppermute | solution.py:13
  7.8 5.5 %collective-permute-start.4 = (bf16[128,2048]{1,0:T(8,128)(2,1)}, bf16[128,2048]{1,0:T(8,128)(2,1)}, u32[]{:S(2)}, u32[]{:S(2)}) collective-permute-start(bf16[128,2048]{1,0:T(8,128)(2,1)} %param.7), channel_id=1, source_target_pairs={{0,1},{1,0},{2,3},{3,2},{4,5},{5,4},{6,7},{7,6},{8,9},{9,8},{10,11... | collective-permute-start | bytes 1572872 | tf_op jit(solution)/shard_map/ppermute | solution.py:13
  13.2 6.0 %copy-start.5 = (bf16[128,2048]{1,0:T(8,128)(2,1)}, bf16[128,2048]{1,0:T(8,128)(2,1)S(1)}, u32[]{:S(2)}) copy-start(bf16[128,2048]{1,0:T(8,128)(2,1)S(1)} %collective-permute-done) | copy-start | bytes 1572868
  27.9 5.3 %copy-start.2 = (bf16[64,1,2048]{2,0,1:T(8,128)(2,1)}, bf16[64,1,2048]{2,0,1:T(8,128)(2,1)S(1)}, u32[]{:S(2)}) copy-start(bf16[64,1,2048]{2,0,1:T(8,128)(2,1)S(1)} %copy.384) | copy-start | bytes 786436
  28.8 17.2 %collective-permute-start.5 = (bf16[128,2048]{1,0:T(8,128)(2,1)}, bf16[128,2048]{1,0:T(8,128)(2,1)}, u32[]{:S(2)}, u32[]{:S(2)}) collective-permute-start(bf16[128,2048]{1,0:T(8,128)(2,1)} %pad_maximum_fusion.5), channel_id=1, source_target_pairs={{0,2},{1,3},{2,0},{3,1},{4,6},{5,7},{6,4},{7,5},{8,10},{9,11},{10,... | collective-permute-start | bytes 1572872 | tf_op jit(solution)/shard_map/ppermute | solution.py:13
  38.3 18.8 %collective-permute-start.1 = (bf16[128,2048]{1,0:T(8,128)(2,1)}, bf16[128,2048]{1,0:T(8,128)(2,1)}, u32[]{:S(2)}, u32[]{:S(2)}) collective-permute-start(bf16[128,2048]{1,0:T(8,128)(2,1)} %pad_maximum_fusion.2), channel_id=1, source_target_pairs={{0,2},{1,3},{2,0},{3,1},{4,6},{5,7},{6,4},{7,5},{8,10},{9,11},{10,... | collective-permute-start | bytes 1572872 | tf_op jit(solution)/shard_map/ppermute | solution.py:13
  53.5 2.5 %copy-start.1 = (bf16[64,1,2048]{2,0,1:T(8,128)(2,1)}, bf16[64,1,2048]{2,0,1:T(8,128)(2,1)S(1)}, u32[]{:S(2)}) copy-start(bf16[64,1,2048]{2,0,1:T(8,128)(2,1)S(1)} %copy.382) | copy-start | bytes 786436
  54.4 25.3 %collective-permute-start.6 = (bf16[128,2048]{1,0:T(8,128)(2,1)}, bf16[128,2048]{1,0:T(8,128)(2,1)}, u32[]{:S(2)}, u32[]{:S(2)}) collective-permute-start(bf16[128,2048]{1,0:T(8,128)(2,1)} %pad_maximum_fusion.6), channel_id=1, source_target_pairs={{0,4},{1,5},{2,6},{3,7},{4,0},{5,1},{6,2},{7,3},{8,12},{9,13},{10,... | collective-permute-start | bytes 1572872 | tf_op jit(solution)/shard_map/ppermute | solution.py:13
  65.1 54.9 %collective-permute-start.2 = (bf16[128,2048]{1,0:T(8,128)(2,1)}, bf16[128,2048]{1,0:T(8,128)(2,1)}, u32[]{:S(2)}, u32[]{:S(2)}) collective-permute-start(bf16[128,2048]{1,0:T(8,128)(2,1)} %pad_maximum_fusion.3), channel_id=1, source_target_pairs={{0,4},{1,5},{2,6},{3,7},{4,0},{5,1},{6,2},{7,3},{8,12},{9,13},{10,... | collective-permute-start | bytes 1572872 | tf_op jit(solution)/shard_map/ppermute | solution.py:13
  87.8 42.2 %collective-permute-start.7 = (bf16[128,2048]{1,0:T(8,128)(2,1)}, bf16[128,2048]{1,0:T(8,128)(2,1)}, u32[]{:S(2)}, u32[]{:S(2)}) collective-permute-start(bf16[128,2048]{1,0:T(8,128)(2,1)} %pad_maximum_fusion.7), channel_id=1, source_target_pairs={{0,8},{1,9},{2,10},{3,11},{4,12},{5,13},{6,14},{7,15},{8,0},{9,1},... | collective-permute-start | bytes 1572872 | tf_op jit(solution)/shard_map/ppermute | solution.py:13
  122.9 5.2 %copy-start.9 = (s32[16]{0:T(128)S(1)}, s32[16]{0:T(128)}, u32[]{:S(2)}) copy-start(s32[16]{0:T(128)} %param.8) | copy-start | bytes 196
  122.9 5.2 %copy-start.3 = (bf16[128,2048]{1,0:T(8,128)(2,1)S(1)}, bf16[128,2048]{1,0:T(8,128)(2,1)}, u32[]{:S(2)}) copy-start(bf16[128,2048]{1,0:T(8,128)(2,1)} %param.7) | copy-start | bytes 1572868
  128.0 48.4 %collective-permute-start.3 = (bf16[128,2048]{1,0:T(8,128)(2,1)}, bf16[128,2048]{1,0:T(8,128)(2,1)}, u32[]{:S(2)}, u32[]{:S(2)}) collective-permute-start(bf16[128,2048]{1,0:T(8,128)(2,1)} %pad_maximum_fusion.4), channel_id=1, source_target_pairs={{0,8},{1,9},{2,10},{3,11},{4,12},{5,13},{6,14},{7,15},{8,0},{9,1},... | collective-permute-start | bytes 1572872 | tf_op jit(solution)/shard_map/ppermute | solution.py:13
  130.0 46.4 %copy-start.6 = (bf16[128,2048]{1,0:T(8,128)(2,1)S(1)}, bf16[128,2048]{1,0:T(8,128)(2,1)}, u32[]{:S(2)}) copy-start(bf16[128,2048]{1,0:T(8,128)(2,1)} %copy-done.5) | copy-start | bytes 1572868
  180.7 2.9 %copy-start.7 = (f32[16,128,128]{1,2,0:T(8,128)S(1)}, f32[16,128,128]{1,2,0:T(8,128)}, u32[]{:S(2)}) copy-start(f32[16,128,128]{1,2,0:T(8,128)} %get-tuple-element.22) | copy-start | bytes 3145732
  183.6 1.1 copy-start.8
  183.8 1.6 copy-start.4
Sparse Core Ops, SparseCore 0:
  9.5 183.1 all-gather.1
where the time goes:
time: 210 us; the launch traced here: 209 us
  waiting for transfers between devices  103 us (49%)
  other arithmetic  44 us (21%)
  local copies, waits for them, and re-layouts  25.3 us (12%)
  matrix products  16.5 us (8%)
  between operations  13.8 us (7%)
  starting transfers between devices  6.47 us (3%)
    ppermute x8, waiting for transfers between devices, partner(): return lax.ppermute(value, axis, pairs)  96.3 us
    convert_element_type x12, other arithmetic, pair_mean(): return ((halves[:, 0] + halves[:, 1]) * 0.5).astype(jnp.bfloat16)  22.3 us
    convert_element_type x12, local copies, waits for them, and re-layouts, pair_mean(): array.reshape(array.shape[0] // 2, 2, array.shape[1]).astype(jnp.float32)  16.8 us
    dot_general x1, matrix products, per_device(): jnp.dot(attended, lax.all_gather(out_weight, 'ctx', axis=1, tiled=True),...  9.1 us
    convert_element_type x5, other arithmetic, pair_mean(): array.reshape(array.shape[0] // 2, 2, array.shape[1]).astype(jnp.float32)  8.44 us
    ppermute x8, starting transfers between devices, partner(): return lax.ppermute(value, axis, pairs)  6.47 us
    all_gather x1, waiting for transfers between devices, per_device(): lax.all_gather(out_weight, 'ctx', axis=1, tiled=True)  5.59 us
  transfers between devices with their start and end apart: 9, of which 6 were waited for; matrix products, arithmetic and copies ran while one was open for 37% of the time, Pallas kernels for 0%

commit v1 on v0

--- a/solution.py
+++ b/solution.py
@@ -1,10 +1,248 @@
+import functools
+
 import jax
 import jax.numpy as jnp
+import numpy as np
 from jax import lax
+from jax.experimental import pallas as pl
+from jax.experimental.pallas import tpu as pltpu
 from jax.sharding import PartitionSpec as P
 
 HD = 128
 BLOCK = 128
+
+CORE, Y, LOW, HIGH = 1, 2, 4, 8
+TEAM = (0, CORE, LOW, CORE | LOW)
+VMEM_LIMIT = 48 * 2**20
+
+
+def swap(value, mask):
+    pairs = [(source, source ^ mask) for source in range(lax.axis_size("ctx"))]
+    return lax.ppermute(value, "ctx", pairs)
+
+
+def swap_groups(value):
+    return lax.ppermute(value, "groups", [(0, 1), (1, 0)])
+
+
+def vmem(count):
+    return [pl.BlockSpec(memory_space=pltpu.VMEM)] * count
+
+
+def call(kernel, outs, in_specs, out_specs=None, **more):
+    return pl.pallas_call(
+        kernel,
+        out_shape=[jax.ShapeDtypeStruct(shape, jnp.bfloat16) for shape in outs],
+        in_specs=in_specs,
+        out_specs=vmem(len(outs)) if out_specs is None else out_specs,
+        compiler_params=pltpu.CompilerParams(vmem_limit_bytes=VMEM_LIMIT),
+        **more,
+    )
+
+
+def halve(rows):
+    count = rows.shape[0]
+    row = lax.broadcasted_iota(jnp.int32, (count // 2, count), 0)
+    column = lax.broadcasted_iota(jnp.int32, (count // 2, count), 1)
+    pick = jnp.where(column // 2 == row, 0.5, 0.0).astype(jnp.bfloat16)
+    return jnp.dot(pick, rows, preferred_element_type=jnp.float32).astype(jnp.bfloat16)
+
+
+def columns_of(place, j, width):
+    return pl.ds(pl.multiple_of(jnp.bitwise_xor(place, j) * width, width), width)
+
+
+def pack_kernel(place_ref, q_ref, k_ref, v_ref, a0, a1, a2, a3, y_ref, z_ref):
+    width = a0.shape[1]
+    for j, out in enumerate((a0, a1, a2, a3)):
+        columns = columns_of(place_ref[0], j, width)
+        for n, source in enumerate((q_ref, k_ref, v_ref)):
+            out[n * BLOCK : (n + 1) * BLOCK, :] = source[:, columns]
+    for n, source in enumerate((k_ref, v_ref)):
+        second = halve(source[...])
+        y_ref[n * 64 : (n + 1) * 64, :] = second
+        z_ref[n * 16 : (n + 1) * 16, :] = halve(halve(second))
+
+
+def repack_kernel(place_ref, y_ref, z_ref, zy_ref, b0, b1, b2, b3):
+    width = b0.shape[1]
+    for j, out in enumerate((b0, b1, b2, b3)):
+        columns = columns_of(place_ref[0], j, width)
+        out[0:128, :] = y_ref[:, columns]
+        out[128:160, :] = z_ref[:, columns]
+        out[160:192, :] = zy_ref[:, columns]
+
+
+def attention_kernel(bias_ref, a0, a1, a2, a3, b0, b1, b2, b3, out_ref, key_ref, value_ref):
+    own = (a0, a1, a2, a3)
+    far = (b0, b1, b2, b3)
+    heads = out_ref.shape[1] // HD
+    for n, rows_ref in enumerate((key_ref, value_ref)):
+        at = 128 + 128 * n
+        for j in range(4):
+            half, part = divmod(j, 2)
+            here, there = rows_ref.at[half], rows_ref.at[1 - half]
+            near = own[j][at : at + 128, :]
+            second = far[j][64 * n : 64 * n + 64, :]
+            here[128 * part : 128 * part + 128, :] = near
+            here[256 + 64 * part : 320 + 64 * part, :] = second
+            there[384 + 32 * part : 416 + 32 * part, :] = halve(halve(near))
+            there[448 + 32 * part : 480 + 32 * part, :] = halve(second)
+            for to in (here, there):
+                to[512 + 16 * j : 528 + 16 * j, :] = far[j][128 + 16 * n : 144 + 16 * n, :]
+                to[576 + 16 * j : 592 + 16 * j, :] = far[j][160 + 16 * n : 176 + 16 * n, :]
+    for half in range(2):
+        bias = jnp.concatenate(
+            [jnp.broadcast_to(bias_ref[2 * half + n : 2 * half + n + 1, :], (BLOCK, 640)) for n in range(2)], 0
+        )
+        for head in range(heads):
+            columns = slice(head * HD, (head + 1) * HD)
+            query = jnp.concatenate([own[2 * half][0:128, columns], own[2 * half + 1][0:128, columns]], 0)
+            score = lax.dot_general(
+                query, key_ref[half, :, columns], (((1,), (1,)), ((), ())), preferred_element_type=jnp.float32
+            )
+            score = score * HD ** (-0.5) + bias
+            raised = jnp.exp(score - jnp.max(score, axis=-1, keepdims=True))
+            weight = raised * (1.0 / jnp.sum(raised, axis=-1, keepdims=True))
+            mixed = jnp.dot(
+                weight.astype(jnp.bfloat16), value_ref[half, :, columns], preferred_element_type=jnp.float32
+            )
+            out_ref[256 * half : 256 * half + 256, columns] = mixed.astype(jnp.bfloat16)
+
+
+def project_kernel(place_ref, o0, o1, o2, o3, own_w, *refs):
+    halves, outs, weight_ref, sems = refs[:6], refs[6:10], refs[10], refs[11]
+    place, group = place_ref[0], place_ref[1]
+    rows = own_w.shape[0]
+    half = rows // 2
+    wide = own_w.shape[1]
+    ours = pl.ds(pl.multiple_of(group * half, half), half)
+    theirs = pl.ds(pl.multiple_of((1 - group) * half, half), half)
+    copies = [[pltpu.make_async_copy(own_w, weight_ref.at[0], sems.at[0])]]
+    for q in range(3):
+        copies.append(
+            [
+                pltpu.make_async_copy(halves[2 * q], weight_ref.at[q + 1, ours, :], sems.at[2 * q + 1]),
+                pltpu.make_async_copy(halves[2 * q + 1], weight_ref.at[q + 1, theirs, :], sems.at[2 * q + 2]),
+            ]
+        )
+    for pair in copies:
+        for copy in pair:
+            copy.start()
+    mixed = (o0, o1, o2, o3)
+    depth = o0.shape[1]
+    for q in range(4):
+        for copy in copies[q]:
+            copy.wait()
+        total = [None] * 4
+        for j in range(4):
+            part = weight_ref[q, pl.ds(pl.multiple_of(jnp.bitwise_xor(place, j) * depth, depth), depth), :]
+            product = jnp.dot(mixed[j][...], part, preferred_element_type=jnp.float32)
+            for r in range(4):
+                piece = product[(r ^ j) * BLOCK : (r ^ j) * BLOCK + BLOCK, :]
+                total[r] = piece if j == 0 else total[r] + piece
+        for r in range(4):
+            outs[r][:, q * wide : (q + 1) * wide] = total[r].astype(jnp.bfloat16)
+
+
+def place_kernel(place_ref, r0, r1, r2, r3, out_ref, sems):
+    wide = r0.shape[1] // 4
+    copies = []
+    for j, source in enumerate((r0, r1, r2, r3)):
+        for q in range(4):
+            mask = TEAM[j] | (Y if q & 1 else 0) | (HIGH if q & 2 else 0)
+            at = pl.multiple_of(jnp.bitwise_xor(place_ref[2], mask) * wide, wide)
+            copies.append(
+                pltpu.make_async_copy(
+                    source.at[:, q * wide : (q + 1) * wide], out_ref.at[:, pl.ds(at, wide)], sems.at[4 * j + q]
+                )
+            )
+    for copy in copies:
+        copy.start()
+    for copy in copies:
+        copy.wait()
+
+
+def key_masks():
+    masks = np.zeros((2, 640), np.int32)
+    for half in range(2):
+        for part in range(2):
+            near, across = TEAM[2 * half + part], TEAM[2 * (1 - half) + part]
+            masks[half, 128 * part : 128 * part + 128] = near
+            masks[half, 256 + 64 * part : 320 + 64 * part] = near ^ Y
+            masks[half, 384 + 32 * part : 416 + 32 * part] = across
+            masks[half, 448 + 32 * part : 480 + 32 * part] = across ^ Y
+        for j in range(4):
+            masks[half, 512 + 16 * j : 528 + 16 * j] = TEAM[j] ^ HIGH
+            masks[half, 576 + 16 * j : 592 + 16 * j] = TEAM[j] ^ HIGH ^ Y
+    return masks
+
+
+def per_device_fast(queries, keys, values, doc_start, out_weight):
+    length, width = queries.shape
+    share = width // 4
+    depth, wide = out_weight.shape
+    group = lax.axis_index("groups")
+    position = lax.axis_index("ctx")
+    place = (position & 1) | ((position >> 1) & 2)
+    places = jnp.stack([place, group, position]).astype(jnp.int32)
+    scalars = pl.BlockSpec(memory_space=pltpu.SMEM)
+    anywhere = pl.BlockSpec(memory_space=pl.ANY)
+
+    masks = key_masks()
+    key_docs = doc_lookup(jnp.bitwise_xor(position, masks), doc_start)
+    query_docs = doc_lookup(jnp.bitwise_xor(position, np.array(TEAM, np.int32)), doc_start)
+    allowed = jnp.repeat(key_docs, 2, axis=0) == query_docs[:, None]
+    bias = jnp.where(allowed, 0.0, -jnp.inf).astype(jnp.float32)
+
+    *team, to_y, to_z = call(
+        pack_kernel,
+        [(3 * length, share)] * 4 + [(length, width), (length // 4, width)],
+        [scalars] + vmem(3),
+        name="pack",
+    )(places, queries, keys, values)
+    from_y = swap(to_y, Y)
+    from_z = swap(to_z, HIGH)
+    from_zy = swap(to_z, HIGH | Y)
+    own = [team[0]] + [swap(team[j], TEAM[j]) for j in (1, 2, 3)]
+
+    half = lax.dynamic_slice_in_dim(out_weight, group * (depth // 2), depth // 2, 0)
+    half_y = swap(half, Y)
+    half_z = swap(half, HIGH)
+    half_d = swap(half_z, Y)
+    other_y, other_z, other_d = swap_groups(half_y), swap_groups(half_z), swap_groups(half_d)
+
+    extra = call(repack_kernel, [(192, share)] * 4, [scalars] + vmem(3), name="repack")(
+        places, from_y, from_z, from_zy
+    )
+    far = [extra[0]] + [swap(extra[j], TEAM[j]) for j in (1, 2, 3)]
+    (attended,) = call(
+        attention_kernel,
+        [(4 * length, share)],
+        vmem(9),
+        scratch_shapes=[pltpu.VMEM((2, 640, share), jnp.bfloat16)] * 2,
+        name="attend",
+    )(bias, *own, *far)
+    from_core = swap(attended, CORE)
+    from_low = swap(attended, LOW)
+    from_both = swap(from_low, CORE)
+    parts = call(
+        project_kernel,
+        [(length, 4 * wide)] * 4,
+        [scalars] + vmem(4) + [anywhere] * 7,
+        scratch_shapes=[pltpu.VMEM((4, depth, wide), jnp.bfloat16), pltpu.SemaphoreType.DMA((7,))],
+        name="project",
+    )(places, attended, from_core, from_low, from_both, out_weight, half_y, other_y, half_z, other_z, half_d, other_d)
+    received = [parts[0]] + [swap(parts[j], TEAM[j]) for j in (1, 2, 3)]
+    (out,) = call(
+        place_kernel,
+        [(length, 16 * wide)],
+        [scalars] + [anywhere] * 4,
+        [anywhere],
+        scratch_shapes=[pltpu.SemaphoreType.DMA((16,))],
+        name="place",
+    )(places, *received)
+    return out
 
 
 def partner(value, axis, apart):
@@ -131,6 +369,7 @@
 
 
 def solution(mesh):
+    fast = mesh.shape["groups"] == 2 and mesh.shape["ctx"] == 16
     placed = (
         P(("groups", "ctx"), None),
         P(("groups", "ctx"), None),
@@ -139,7 +378,7 @@
         P(None, "ctx"),
     )
     return jax.shard_map(
-        per_device,
+        per_device_fast if fast else per_device,
         mesh=mesh,
         in_specs=placed,
         out_specs=P(("groups", "ctx"), None),

time: 210 us -> 123 us (0.59)
  other arithmetic: 44 us -> 0.43 us
  waiting for transfers between devices: 103 us -> 80.3 us
  local copies, waits for them, and re-layouts: 25.3 us -> 5.83 us
  Pallas kernels: 0 us -> 16.9 us
  matrix products: 16.5 us -> 0 us
  between operations: 13.8 us -> 0.11 us
  starting transfers between devices: 6.47 us -> 17 us
    convert_element_type x17 -> x0, other arithmetic: 30.7 us -> none  [the longest x12 22.3 us: pair_mean(): return ((halves[:, 0] + halves[:, 1]) * 0.5).astype(jnp.bfloat16)]
    pallas_call x0 -> x5, Pallas kernels: none -> 16.9 us  [the longest x1 6.75 us: per_device_fast(): call(project_kernel, [(length, 4 * wide)] * 4, [scalars] + vmem(4) + [any...]
    convert_element_type x12 -> x0, local copies, waits for them, and re-layouts: 16.8 us -> none  [pair_mean(): array.reshape(array.shape[0] // 2, 2, array.shape[1]).astype(jnp.float32)]
    dot_general x5 -> x0, matrix products: 16.5 us -> none  [the longest x1 9.1 us: per_device(): jnp.dot(attended, lax.all_gather(out_weight, 'ctx', axis=1, tiled=True),...]
    ppermute x8 -> x21, waiting for transfers between devices: 96.3 us -> 80.3 us  [the longest x18 57.7 us: swap(): return lax.ppermute(value, 'ctx', pairs)]
    ppermute x8 -> x21, starting transfers between devices: 6.47 us -> 17 us  [the longest x18 13.2 us: swap(): return lax.ppermute(value, 'ctx', pairs)]
    concatenate x9 -> x0, other arithmetic: 8.72 us -> none  [the longest x3 2.65 us: per_device(): jnp.concatenate([pair_mean(low_values), pair_mean(high_values)], 0)]
    all_gather x1 -> x0, waiting for transfers between devices: 5.59 us -> none  [per_device(): lax.all_gather(out_weight, 'ctx', axis=1, tiled=True)]
  transfers between devices with their start and end apart: 9 -> 21, of which waited for: 6 -> 14; matrix products, arithmetic and copies ran while one was open for 37% -> 2% of each run, Pallas kernels for 0% -> 5%
where the time goes in v1:
time: 123 us; the launch traced here: 121 us
  waiting for transfers between devices  80.3 us (65%)
  starting transfers between devices  17 us (14%)
  Pallas kernels  16.9 us (14%)
  local copies, waits for them, and re-layouts  5.83 us (5%)
    ppermute x18, waiting for transfers between devices, swap(): return lax.ppermute(value, 'ctx', pairs)  57.7 us
    ppermute x3, waiting for transfers between devices, swap_groups(): return lax.ppermute(value, 'groups', [(0, 1), (1, 0)])  22.5 us
    ppermute x18, starting transfers between devices, swap(): return lax.ppermute(value, 'ctx', pairs)  13.2 us
    pallas_call x1, Pallas kernels, per_device_fast(): call(project_kernel, [(length, 4 * wide)] * 4, [scalars] + vmem(4) + [any...  6.75 us
    pallas_call x1, Pallas kernels, per_device_fast(): call(attention_kernel, [(4 * length, share)], vmem(9), scratch_shapes=[pl...  5.71 us
    unnamed x14, local copies, waits for them, and re-layouts  3.93 us
    ppermute x3, starting transfers between devices, swap_groups(): return lax.ppermute(value, 'groups', [(0, 1), (1, 0)])  3.83 us
  transfers between devices with their start and end apart: 21, of which 14 were waited for; matrix products, arithmetic and copies ran while one was open for 2% of the time, Pallas kernels for 5%

profile of v1, /device:TPU:0, one launch (start us, length us, event | category | flops | bytes accessed | tf_op | source)
XLA Modules:
  0.0 120.6 jit_solution(594278786346239207)
XLA Ops:
  0.0 0.1 pad_add_fusion.place_ref
  0.1 0.0 copy-start
  0.1 1.0 copy-done
  1.1 0.0 copy-start.1
  1.1 1.0 copy-done.1
  2.2 0.0 copy-start.2
  2.2 1.0 copy-done.2
  3.2 2.3 %pack.1 = (bf16[384,512]{1,0:T(8,128)(2,1)S(1)}, bf16[384,512]{1,0:T(8,128)(2,1)}, bf16[384,512]{1,0:T(8,128)(2,1)}, bf16[384,512]{1,0:T(8,128)(2,1)}, bf16[128,...) custom-call(s32[3]{0:T(128)S(1)} %pad_add_fusion.place_ref, bf16[128,2048]{1,0:T(8,128)(2,1)S(1)} %copy-done, ...), custom_call_target="tpu_custom_call" | custom-call | tf_op jit(solution)/shard_map/pack/pallas_call | solution.py:198
  5.5 0.0 copy-start.4
  5.5 4.0 %collective-permute-start.4 = (bf16[32,2048]{1,0:T(8,128)(2,1)S(1)}, bf16[32,2048]{1,0:T(8,128)(2,1)S(1)}, u32[]{:S(2)}, u32[]{:S(2)}) collective-permute-start(bf16[32,2048]{1,0:T(8,128)(2,1)S(1)} %get-tuple-element.24), channel_id=1, source_target_pairs={{0,8},{1,9},{2,10},{3,11},{4,12},{5,13},{6,14},{7,15},{8,0},{9,1},... | collective-permute-start | bytes 393224 | tf_op jit(solution)/shard_map/ppermute | solution.py:21
  9.5 1.3 %collective-permute-start.5 = (bf16[32,2048]{1,0:T(8,128)(2,1)S(1)}, bf16[32,2048]{1,0:T(8,128)(2,1)S(1)}, u32[]{:S(2)}, u32[]{:S(2)}) collective-permute-start(bf16[32,2048]{1,0:T(8,128)(2,1)S(1)} %get-tuple-element.24), channel_id=1, source_target_pairs={{0,10},{1,11},{2,8},{3,9},{4,14},{5,15},{6,12},{7,13},{8,2},{9,3},... | collective-permute-start | bytes 393224 | tf_op jit(solution)/shard_map/ppermute | solution.py:21
  10.8 0.2 collective-permute-start.3
  11.0 0.0 collective-permute-start
  11.0 1.8 %collective-permute-start.1 = (bf16[384,512]{1,0:T(8,128)(2,1)}, bf16[384,512]{1,0:T(8,128)(2,1)S(1)}, u32[]{:S(2)}, u32[]{:S(2)}) collective-permute-start(bf16[384,512]{1,0:T(8,128)(2,1)} %get-tuple-element.21), channel_id=1, source_target_pairs={{0,4},{1,5},{2,6},{3,7},{4,0},{5,1},{6,2},{7,3},{8,12},{9,13},{10,... | collective-permute-start | bytes 1179656 | tf_op jit(solution)/shard_map/ppermute | solution.py:21
  12.9 0.0 copy-done.4
  12.9 1.9 %constant_dynamic-slice_fusion = bf16[1024,256]{1,0:T(8,128)(2,1)} fusion(bf16[2048,256]{1,0:T(8,128)(2,1)} %own_w.1, s32[]{:T(128)S(6)} %select_n.18), kind=kLoop, calls=%fused_computation.8 | loop fusion | bytes 1048580 | tf_op jit(solution)/shard_map/dynamic_slice | solution.py:209
  14.8 4.7 %collective-permute-done.4.z_ref = bf16[32,2048]{1,0:T(8,128)(2,1)S(1)} collective-permute-done((bf16[32,2048]{1,0:T(8,128)(2,1)S(1)}, bf16[32,2048]{1,0:T(8,128)(2,1)S(1)}, u32[]{:S(2)}, u32[]{:S(2)}) %collective-permute-start.4) | collective-permute-done | bytes 131104 | tf_op jit(solution)/shard_map/ppermute | solution.py:21
  19.5 0.0 collective-permute-start.14
  19.5 0.0 copy-done.6
  19.5 0.0 copy-start.5
  19.5 3.2 %collective-permute-done.5.zy_ref = bf16[32,2048]{1,0:T(8,128)(2,1)S(1)} collective-permute-done((bf16[32,2048]{1,0:T(8,128)(2,1)S(1)}, bf16[32,2048]{1,0:T(8,128)(2,1)S(1)}, u32[]{:S(2)}, u32[]{:S(2)}) %collective-permute-start.5) | collective-permute-done | bytes 131104 | tf_op jit(solution)/shard_map/ppermute | solution.py:21
  22.7 0.0 collective-permute-start.2
  22.7 0.0 copy-done.5
  22.7 0.1 select_reduce_fusion
  22.8 0.2 select_reduce_fusion.1
  23.0 3.7 %collective-permute-done.3.y_ref = bf16[128,2048]{1,0:T(8,128)(2,1)S(1)} collective-permute-done((bf16[128,2048]{1,0:T(8,128)(2,1)S(1)}, bf16[128,2048]{1,0:T(8,128)(2,1)S(1)}, u32[]{:S(2)}, u32[]{:S(2)}) %collective-permute-start.3) | collective-permute-done | bytes 524320 | tf_op jit(solution)/shard_map/ppermute | solution.py:21
  26.7 0.6 repack.1
  27.3 0.1 collective-permute-start.6
  27.4 0.0 collective-permute-done.a1
  27.4 1.6 %collective-permute-start.7 = (bf16[192,512]{1,0:T(8,128)(2,1)S(1)}, bf16[192,512]{1,0:T(8,128)(2,1)S(1)}, u32[]{:S(2)}, u32[]{:S(2)}) collective-permute-start(bf16[192,512]{1,0:T(8,128)(2,1)S(1)} %get-tuple-element.27), channel_id=1, source_target_pairs={{0,4},{1,5},{2,6},{3,7},{4,0},{5,1},{6,2},{7,3},{8,12},{9,13},{10,... | collective-permute-start | bytes 589832 | tf_op jit(solution)/shard_map/ppermute | solution.py:21
  29.0 2.7 %collective-permute-done.1.a2 = bf16[384,512]{1,0:T(8,128)(2,1)S(1)} collective-permute-done((bf16[384,512]{1,0:T(8,128)(2,1)}, bf16[384,512]{1,0:T(8,128)(2,1)S(1)}, u32[]{:S(2)}, u32[]{:S(2)}) %collective-permute-start.1) | collective-permute-done | bytes 393248 | tf_op jit(solution)/shard_map/ppermute | solution.py:21
  31.7 0.0 collective-permute-start.8
  31.7 0.1 compare_select_fusion.bias_ref
  31.8 14.6 %collective-permute-done.2.a3 = bf16[384,512]{1,0:T(8,128)(2,1)S(1)} collective-permute-done((bf16[384,512]{1,0:T(8,128)(2,1)}, bf16[384,512]{1,0:T(8,128)(2,1)S(1)}, u32[]{:S(2)}, u32[]{:S(2)}) %collective-permute-start.2) | collective-permute-done | bytes 393248 | tf_op jit(solution)/shard_map/ppermute | solution.py:21
  46.4 1.9 %collective-permute-start.12 = (bf16[1024,256]{1,0:T(8,128)(2,1)}, bf16[1024,256]{1,0:T(8,128)(2,1)S(1)}, u32[]{:S(2)}, u32[]{:S(2)}) collective-permute-start(bf16[1024,256]{1,0:T(8,128)(2,1)} %constant_dynamic-slice_fusion), channel_id=1, source_target_pairs={{0,2},{1,3},{2,0},{3,1},{4,6},{5,7},{6,4},{7,5},{8,10},{9,11},{10,... | collective-permute-start | bytes 1572872 | tf_op jit(solution)/shard_map/ppermute | solution.py:21
  48.3 0.0 collective-permute-done.14.refs_2_
  48.4 0.1 collective-permute-start.16
  48.4 0.0 collective-permute-done.6.b1
  48.4 2.8 %collective-permute-done.7.b2 = bf16[192,512]{1,0:T(8,128)(2,1)S(1)} collective-permute-done((bf16[192,512]{1,0:T(8,128)(2,1)S(1)}, bf16[192,512]{1,0:T(8,128)(2,1)S(1)}, u32[]{:S(2)}, u32[]{:S(2)}) %collective-permute-start.7) | collective-permute-done | bytes 196640 | tf_op jit(solution)/shard_map/ppermute | solution.py:21
  51.2 3.6 %collective-permute-done.8.b3 = bf16[192,512]{1,0:T(8,128)(2,1)S(1)} collective-permute-done((bf16[192,512]{1,0:T(8,128)(2,1)S(1)}, bf16[192,512]{1,0:T(8,128)(2,1)S(1)}, u32[]{:S(2)}, u32[]{:S(2)}) %collective-permute-start.8) | collective-permute-done | bytes 196640 | tf_op jit(solution)/shard_map/ppermute | solution.py:21
  54.8 5.7 %attend.1.o0 = bf16[512,512]{1,0:T(8,128)(2,1)S(1)} custom-call(f32[4,640]{1,0:T(4,128)S(1)} %compare_select_fusion.bias_ref, bf16[384,512]{1,0:T(8,128)(2,1)S(1)} %get-tuple-element.19.a0, bf16[384,512]{1,0:T(8,128)(2,1)S(1)} %collective-permute-done.a1, bf16[384,512]{1,0:T(8,128)(2,1)S(1)} %collective-permute-done.1.a2, ...), custom_call_target="tpu_custom_call" | custom-call | tf_op jit(solution)/shard_map/attend/pallas_call | solution.py:219
  60.5 0.1 collective-permute-start.10
  60.6 1.6 %collective-permute-start.15 = (bf16[1024,256]{1,0:T(8,128)(2,1)S(1)}, bf16[1024,256]{1,0:T(8,128)(2,1)S(1)}, u32[]{:S(2)}, u32[]{:S(2)}) collective-permute-start(bf16[1024,256]{1,0:T(8,128)(2,1)S(1)} %collective-permute-done.14.refs_2_), channel_id=1, source_target_pairs={{0,16},{16,0},{1,17},{17,1},{2,18},{18,2},{3,19},{19,3},{4,20},{20... | collective-permute-start | bytes 1572872 | tf_op jit(solution)/shard_map/ppermute | solution.py:25
  62.3 0.0 collective-permute-done.12.refs_0_
  62.3 0.7 collective-permute-start.13
  63.0 0.0 collective-permute-start.9
  63.0 9.5 %collective-permute-done.16.refs_4_ = bf16[1024,256]{1,0:T(8,128)(2,1)S(1)} collective-permute-done((bf16[1024,256]{1,0:T(8,128)(2,1)S(1)}, bf16[1024,256]{1,0:T(8,128)(2,1)S(1)}, u32[]{:S(2)}, u32[]{:S(2)}) %collective-permute-start.16) | collective-permute-done | bytes 524320 | tf_op jit(solution)/shard_map/ppermute | solution.py:21
  72.5 1.5 %collective-permute-start.17 = (bf16[1024,256]{1,0:T(8,128)(2,1)S(1)}, bf16[1024,256]{1,0:T(8,128)(2,1)S(1)}, u32[]{:S(2)}, u32[]{:S(2)}) collective-permute-start(bf16[1024,256]{1,0:T(8,128)(2,1)S(1)} %collective-permute-done.16.refs_4_), channel_id=1, source_target_pairs={{0,16},{16,0},{1,17},{17,1},{2,18},{18,2},{3,19},{19,3},{4,20},{20... | collective-permute-start | bytes 1572872 | tf_op jit(solution)/shard_map/ppermute | solution.py:25
  74.0 0.9 collective-permute-done.10.o2
  74.9 0.0 collective-permute-start.11
  74.9 0.5 collective-permute-done.15.refs_3_
  75.4 11.2 %collective-permute-done.13.refs_1_ = bf16[1024,256]{1,0:T(8,128)(2,1)S(1)} collective-permute-done((bf16[1024,256]{1,0:T(8,128)(2,1)S(1)}, bf16[1024,256]{1,0:T(8,128)(2,1)S(1)}, u32[]{:S(2)}, u32[]{:S(2)}) %collective-permute-start.13) | collective-permute-done | bytes 524320 | tf_op jit(solution)/shard_map/ppermute | solution.py:25
  86.7 0.0 collective-permute-done.9.o1
  86.7 10.8 %collective-permute-done.17.refs_5_ = bf16[1024,256]{1,0:T(8,128)(2,1)S(1)} collective-permute-done((bf16[1024,256]{1,0:T(8,128)(2,1)S(1)}, bf16[1024,256]{1,0:T(8,128)(2,1)S(1)}, u32[]{:S(2)}, u32[]{:S(2)}) %collective-permute-start.17) | collective-permute-done | bytes 524320 | tf_op jit(solution)/shard_map/ppermute | solution.py:25
  97.4 0.0 collective-permute-done.11.o3
  97.4 0.8 copy-done.3
  98.2 6.8 %project.1 = (bf16[128,1024]{1,0:T(8,128)(2,1)S(1)}, bf16[128,1024]{1,0:T(8,128)(2,1)S(1)}, bf16[128,1024]{1,0:T(8,128)(2,1)S(1)}, bf16[128,1024]{1,0:T(8,128)(2,1)S(1)}) custom-call(s32[3]{0:T(128)S(1)} %pad_add_fusion.place_ref, bf16[512,512]{1,0:T(8,128)(2,1)S(1)} %attend.1.o0, bf16[512,512]{1,0:T(8,128)(2,1)S(1)} %collective-permute-done.9.o1, ...), custom_call_target="tpu_custom_call" | custom-call | tf_op jit(solution)/shard_map/project/pallas_call | solution.py:229
  105.0 0.1 collective-permute-start.18
  105.1 1.7 %collective-permute-start.19 = (bf16[128,1024]{1,0:T(8,128)(2,1)S(1)}, bf16[128,1024]{1,0:T(8,128)(2,1)S(1)}, u32[]{:S(2)}, u32[]{:S(2)}) collective-permute-start(bf16[128,1024]{1,0:T(8,128)(2,1)S(1)} %get-tuple-element.31), channel_id=1, source_target_pairs={{0,4},{1,5},{2,6},{3,7},{4,0},{5,1},{6,2},{7,3},{8,12},{9,13},{10,... | collective-permute-start | bytes 786440 | tf_op jit(solution)/shard_map/ppermute | solution.py:21
  106.8 0.1 collective-permute-start.20
  106.9 0.0 collective-permute-done.18.r1
  106.9 7.3 %collective-permute-done.19.r2 = bf16[128,1024]{1,0:T(8,128)(2,1)S(1)} collective-permute-done((bf16[128,1024]{1,0:T(8,128)(2,1)S(1)}, bf16[128,1024]{1,0:T(8,128)(2,1)S(1)}, u32[]{:S(2)}, u32[]{:S(2)}) %collective-permute-start.19) | collective-permute-done | bytes 262176 | tf_op jit(solution)/shard_map/ppermute | solution.py:21
  114.2 4.7 %collective-permute-done.20.r3 = bf16[128,1024]{1,0:T(8,128)(2,1)S(1)} collective-permute-done((bf16[128,1024]{1,0:T(8,128)(2,1)S(1)}, bf16[128,1024]{1,0:T(8,128)(2,1)S(1)}, u32[]{:S(2)}, u32[]{:S(2)}) %collective-permute-start.20) | collective-permute-done | bytes 262176 | tf_op jit(solution)/shard_map/ppermute | solution.py:21
  118.9 1.6 %place.1 = bf16[128,4096]{1,0:T(8,128)(2,1)} custom-call(s32[3]{0:T(128)S(1)} %pad_add_fusion.place_ref, bf16[128,1024]{1,0:T(8,128)(2,1)S(1)} %get-tuple-element.29.r0, bf16[128,1024]{1,0:T(8,128)(2,1)S(1)} %collective-permute-done.18.r1, bf16[128,1024]{1,0:T(8,128)(2,1)S(1)} %collective-permute-done.19.r2, bf16[128,1024]{1,0:T(8,128)(2,1)S(1)} %collective-permute-done.20.r3), custom_call_target="tpu_custom_call" | custom-call | tf_op jit(solution)/shard_map/place/pallas_call | solution.py:237
  (6 shorter events, 0.0 us)
Async XLA Ops:
  0.1 1.0 copy-start
  1.1 1.0 copy-start.1
  2.2 1.0 copy-start.2
  5.5 7.4 %copy-start.4 = (s32[2,640]{1,0:T(2,128)S(1)}, s32[2,640]{1,0:T(2,128)}, u32[]{:S(2)}) copy-start(s32[2,640]{1,0:T(2,128)} %constant.27.clone) | copy-start | bytes 15364
  5.5 14.0 %collective-permute-start.4 = (bf16[32,2048]{1,0:T(8,128)(2,1)S(1)}, bf16[32,2048]{1,0:T(8,128)(2,1)S(1)}, u32[]{:S(2)}, u32[]{:S(2)}) collective-permute-start(bf16[32,2048]{1,0:T(8,128)(2,1)S(1)} %get-tuple-element.24), channel_id=1, source_target_pairs={{0,8},{1,9},{2,10},{3,11},{4,12},{5,13},{6,14},{7,15},{8,0},{9,1},... | collective-permute-start | bytes 393224 | tf_op jit(solution)/shard_map/ppermute | solution.py:21
  9.5 13.2 %collective-permute-start.5 = (bf16[32,2048]{1,0:T(8,128)(2,1)S(1)}, bf16[32,2048]{1,0:T(8,128)(2,1)S(1)}, u32[]{:S(2)}, u32[]{:S(2)}) collective-permute-start(bf16[32,2048]{1,0:T(8,128)(2,1)S(1)} %get-tuple-element.24), channel_id=1, source_target_pairs={{0,10},{1,11},{2,8},{3,9},{4,14},{5,15},{6,12},{7,13},{8,2},{9,3},... | collective-permute-start | bytes 393224 | tf_op jit(solution)/shard_map/ppermute | solution.py:21
  10.8 15.9 %collective-permute-start.3 = (bf16[128,2048]{1,0:T(8,128)(2,1)S(1)}, bf16[128,2048]{1,0:T(8,128)(2,1)S(1)}, u32[]{:S(2)}, u32[]{:S(2)}) collective-permute-start(bf16[128,2048]{1,0:T(8,128)(2,1)S(1)} %get-tuple-element.23), channel_id=1, source_target_pairs={{0,2},{1,3},{2,0},{3,1},{4,6},{5,7},{6,4},{7,5},{8,10},{9,11},{10,... | collective-permute-start | bytes 1572872 | tf_op jit(solution)/shard_map/ppermute | solution.py:21
  11.0 16.4 %collective-permute-start = (bf16[384,512]{1,0:T(8,128)(2,1)}, bf16[384,512]{1,0:T(8,128)(2,1)S(1)}, u32[]{:S(2)}, u32[]{:S(2)}) collective-permute-start(bf16[384,512]{1,0:T(8,128)(2,1)} %get-tuple-element.20), channel_id=1, source_target_pairs={{0,1},{1,0},{2,3},{3,2},{4,5},{5,4},{6,7},{7,6},{8,9},{9,8},{10,11... | collective-permute-start | bytes 1179656 | tf_op jit(solution)/shard_map/ppermute | solution.py:21
  11.0 20.7 %collective-permute-start.1 = (bf16[384,512]{1,0:T(8,128)(2,1)}, bf16[384,512]{1,0:T(8,128)(2,1)S(1)}, u32[]{:S(2)}, u32[]{:S(2)}) collective-permute-start(bf16[384,512]{1,0:T(8,128)(2,1)} %get-tuple-element.21), channel_id=1, source_target_pairs={{0,4},{1,5},{2,6},{3,7},{4,0},{5,1},{6,2},{7,3},{8,12},{9,13},{10,... | collective-permute-start | bytes 1179656 | tf_op jit(solution)/shard_map/ppermute | solution.py:21
  12.9 6.6 %copy-start.6 = (s32[4]{0:T(128)S(1)}, s32[4]{0:T(128)}, u32[]{:S(2)}) copy-start(s32[4]{0:T(128)} %constant.28.clone) | copy-start | bytes 52
  19.5 28.8 %collective-permute-start.14 = (bf16[1024,256]{1,0:T(8,128)(2,1)}, bf16[1024,256]{1,0:T(8,128)(2,1)S(1)}, u32[]{:S(2)}, u32[]{:S(2)}) collective-permute-start(bf16[1024,256]{1,0:T(8,128)(2,1)} %constant_dynamic-slice_fusion), channel_id=1, source_target_pairs={{0,8},{1,9},{2,10},{3,11},{4,12},{5,13},{6,14},{7,15},{8,0},{9,1},... | collective-permute-start | bytes 1572872 | tf_op jit(solution)/shard_map/ppermute | solution.py:21
  19.5 3.2 %copy-start.5 = (s32[16]{0:T(128)S(1)}, s32[16]{0:T(128)}, u32[]{:S(2)}) copy-start(s32[16]{0:T(128)} %param.10) | copy-start | bytes 196
  22.7 23.7 %collective-permute-start.2 = (bf16[384,512]{1,0:T(8,128)(2,1)}, bf16[384,512]{1,0:T(8,128)(2,1)S(1)}, u32[]{:S(2)}, u32[]{:S(2)}) collective-permute-start(bf16[384,512]{1,0:T(8,128)(2,1)} %get-tuple-element.22), channel_id=1, source_target_pairs={{0,5},{1,4},{2,7},{3,6},{4,1},{5,0},{6,3},{7,2},{8,13},{9,12},{10,... | collective-permute-start | bytes 1179656 | tf_op jit(solution)/shard_map/ppermute | solution.py:21
  27.3 21.1 %collective-permute-start.6 = (bf16[192,512]{1,0:T(8,128)(2,1)S(1)}, bf16[192,512]{1,0:T(8,128)(2,1)S(1)}, u32[]{:S(2)}, u32[]{:S(2)}) collective-permute-start(bf16[192,512]{1,0:T(8,128)(2,1)S(1)} %get-tuple-element.26), channel_id=1, source_target_pairs={{0,1},{1,0},{2,3},{3,2},{4,5},{5,4},{6,7},{7,6},{8,9},{9,8},{10,11... | collective-permute-start | bytes 589832 | tf_op jit(solution)/shard_map/ppermute | solution.py:21
  27.4 23.8 %collective-permute-start.7 = (bf16[192,512]{1,0:T(8,128)(2,1)S(1)}, bf16[192,512]{1,0:T(8,128)(2,1)S(1)}, u32[]{:S(2)}, u32[]{:S(2)}) collective-permute-start(bf16[192,512]{1,0:T(8,128)(2,1)S(1)} %get-tuple-element.27), channel_id=1, source_target_pairs={{0,4},{1,5},{2,6},{3,7},{4,0},{5,1},{6,2},{7,3},{8,12},{9,13},{10,... | collective-permute-start | bytes 589832 | tf_op jit(solution)/shard_map/ppermute | solution.py:21
  31.7 23.1 %collective-permute-start.8 = (bf16[192,512]{1,0:T(8,128)(2,1)S(1)}, bf16[192,512]{1,0:T(8,128)(2,1)S(1)}, u32[]{:S(2)}, u32[]{:S(2)}) collective-permute-start(bf16[192,512]{1,0:T(8,128)(2,1)S(1)} %get-tuple-element.28), channel_id=1, source_target_pairs={{0,5},{1,4},{2,7},{3,6},{4,1},{5,0},{6,3},{7,2},{8,13},{9,12},{10,... | collective-permute-start | bytes 589832 | tf_op jit(solution)/shard_map/ppermute | solution.py:21
  46.4 15.9 %collective-permute-start.12 = (bf16[1024,256]{1,0:T(8,128)(2,1)}, bf16[1024,256]{1,0:T(8,128)(2,1)S(1)}, u32[]{:S(2)}, u32[]{:S(2)}) collective-permute-start(bf16[1024,256]{1,0:T(8,128)(2,1)} %constant_dynamic-slice_fusion), channel_id=1, source_target_pairs={{0,2},{1,3},{2,0},{3,1},{4,6},{5,7},{6,4},{7,5},{8,10},{9,11},{10,... | collective-permute-start | bytes 1572872 | tf_op jit(solution)/shard_map/ppermute | solution.py:21
  48.4 24.1 %collective-permute-start.16 = (bf16[1024,256]{1,0:T(8,128)(2,1)S(1)}, bf16[1024,256]{1,0:T(8,128)(2,1)S(1)}, u32[]{:S(2)}, u32[]{:S(2)}) collective-permute-start(bf16[1024,256]{1,0:T(8,128)(2,1)S(1)} %collective-permute-done.14.refs_2_), channel_id=1, source_target_pairs={{0,2},{1,3},{2,0},{3,1},{4,6},{5,7},{6,4},{7,5},{8,10},{9,11},{10,... | collective-permute-start | bytes 1572872 | tf_op jit(solution)/shard_map/ppermute | solution.py:21
  60.5 14.3 %collective-permute-start.10 = (bf16[512,512]{1,0:T(8,128)(2,1)S(1)}, bf16[512,512]{1,0:T(8,128)(2,1)S(1)}, u32[]{:S(2)}, u32[]{:S(2)}) collective-permute-start(bf16[512,512]{1,0:T(8,128)(2,1)S(1)} %attend.1.o0), channel_id=1, source_target_pairs={{0,4},{1,5},{2,6},{3,7},{4,0},{5,1},{6,2},{7,3},{8,12},{9,13},{10,... | collective-permute-start | bytes 1572872 | tf_op jit(solution)/shard_map/ppermute | solution.py:21
  60.6 14.8 %collective-permute-start.15 = (bf16[1024,256]{1,0:T(8,128)(2,1)S(1)}, bf16[1024,256]{1,0:T(8,128)(2,1)S(1)}, u32[]{:S(2)}, u32[]{:S(2)}) collective-permute-start(bf16[1024,256]{1,0:T(8,128)(2,1)S(1)} %collective-permute-done.14.refs_2_), channel_id=1, source_target_pairs={{0,16},{16,0},{1,17},{17,1},{2,18},{18,2},{3,19},{19,3},{4,20},{20... | collective-permute-start | bytes 1572872 | tf_op jit(solution)/shard_map/ppermute | solution.py:25
  62.3 24.4 %collective-permute-start.13 = (bf16[1024,256]{1,0:T(8,128)(2,1)S(1)}, bf16[1024,256]{1,0:T(8,128)(2,1)S(1)}, u32[]{:S(2)}, u32[]{:S(2)}) collective-permute-start(bf16[1024,256]{1,0:T(8,128)(2,1)S(1)} %collective-permute-done.12.refs_0_), channel_id=1, source_target_pairs={{0,16},{16,0},{1,17},{17,1},{2,18},{18,2},{3,19},{19,3},{4,20},{20... | collective-permute-start | bytes 1572872 | tf_op jit(solution)/shard_map/ppermute | solution.py:25
  63.0 23.7 %collective-permute-start.9 = (bf16[512,512]{1,0:T(8,128)(2,1)S(1)}, bf16[512,512]{1,0:T(8,128)(2,1)S(1)}, u32[]{:S(2)}, u32[]{:S(2)}) collective-permute-start(bf16[512,512]{1,0:T(8,128)(2,1)S(1)} %attend.1.o0), channel_id=1, source_target_pairs={{0,1},{1,0},{2,3},{3,2},{4,5},{5,4},{6,7},{7,6},{8,9},{9,8},{10,11... | collective-permute-start | bytes 1572872 | tf_op jit(solution)/shard_map/ppermute | solution.py:21
  72.5 24.9 %collective-permute-start.17 = (bf16[1024,256]{1,0:T(8,128)(2,1)S(1)}, bf16[1024,256]{1,0:T(8,128)(2,1)S(1)}, u32[]{:S(2)}, u32[]{:S(2)}) collective-permute-start(bf16[1024,256]{1,0:T(8,128)(2,1)S(1)} %collective-permute-done.16.refs_4_), channel_id=1, source_target_pairs={{0,16},{16,0},{1,17},{17,1},{2,18},{18,2},{3,19},{19,3},{4,20},{20... | collective-permute-start | bytes 1572872 | tf_op jit(solution)/shard_map/ppermute | solution.py:25
  74.9 22.6 %collective-permute-start.11 = (bf16[512,512]{1,0:T(8,128)(2,1)S(1)}, bf16[512,512]{1,0:T(8,128)(2,1)S(1)}, u32[]{:S(2)}, u32[]{:S(2)}) collective-permute-start(bf16[512,512]{1,0:T(8,128)(2,1)S(1)} %collective-permute-done.10.o2), channel_id=1, source_target_pairs={{0,1},{1,0},{2,3},{3,2},{4,5},{5,4},{6,7},{7,6},{8,9},{9,8},{10,11... | collective-permute-start | bytes 1572872 | tf_op jit(solution)/shard_map/ppermute | solution.py:21
  97.4 0.8 copy-start.3
  105.0 1.9 %collective-permute-start.18 = (bf16[128,1024]{1,0:T(8,128)(2,1)S(1)}, bf16[128,1024]{1,0:T(8,128)(2,1)S(1)}, u32[]{:S(2)}, u32[]{:S(2)}) collective-permute-start(bf16[128,1024]{1,0:T(8,128)(2,1)S(1)} %get-tuple-element.30), channel_id=1, source_target_pairs={{0,1},{1,0},{2,3},{3,2},{4,5},{5,4},{6,7},{7,6},{8,9},{9,8},{10,11... | collective-permute-start | bytes 786440 | tf_op jit(solution)/shard_map/ppermute | solution.py:21
  105.1 9.2 %collective-permute-start.19 = (bf16[128,1024]{1,0:T(8,128)(2,1)S(1)}, bf16[128,1024]{1,0:T(8,128)(2,1)S(1)}, u32[]{:S(2)}, u32[]{:S(2)}) collective-permute-start(bf16[128,1024]{1,0:T(8,128)(2,1)S(1)} %get-tuple-element.31), channel_id=1, source_target_pairs={{0,4},{1,5},{2,6},{3,7},{4,0},{5,1},{6,2},{7,3},{8,12},{9,13},{10,... | collective-permute-start | bytes 786440 | tf_op jit(solution)/shard_map/ppermute | solution.py:21
  106.8 12.2 %collective-permute-start.20 = (bf16[128,1024]{1,0:T(8,128)(2,1)S(1)}, bf16[128,1024]{1,0:T(8,128)(2,1)S(1)}, u32[]{:S(2)}, u32[]{:S(2)}) collective-permute-start(bf16[128,1024]{1,0:T(8,128)(2,1)S(1)} %get-tuple-element.32), channel_id=1, source_target_pairs={{0,5},{1,4},{2,7},{3,6},{4,1},{5,0},{6,3},{7,2},{8,13},{9,12},{10,... | collective-permute-start | bytes 786440 | tf_op jit(solution)/shard_map/ppermute | solution.py:21

commit v2 on v0

--- a/solution.py
+++ b/solution.py
@@ -1,10 +1,286 @@
+import functools
+
 import jax
 import jax.numpy as jnp
+import numpy as np
 from jax import lax
+from jax.experimental import pallas as pl
+from jax.experimental.pallas import tpu as pltpu
 from jax.sharding import PartitionSpec as P
 
 HD = 128
 BLOCK = 128
+
+LOW, HIGH = 4, 8
+VMEM_LIMIT = 48 * 2**20
+
+
+def swap(value, mask):
+    pairs = [(source, source ^ mask) for source in range(lax.axis_size("ctx"))]
+    return lax.ppermute(value, "ctx", pairs)
+
+
+def swap_groups(value):
+    return lax.ppermute(value, "groups", [(0, 1), (1, 0)])
+
+
+def after(value, other):
+    return lax.optimization_barrier((value, other))[0]
+
+
+def vmem(count):
+    return [pl.BlockSpec(memory_space=pltpu.VMEM)] * count
+
+
+def anywhere(count):
+    return [pl.BlockSpec(memory_space=pltpu.HBM)] * count
+
+
+def call(kernel, outs, in_specs, out_specs=None, **more):
+    return pl.pallas_call(
+        kernel,
+        out_shape=[jax.ShapeDtypeStruct(shape, jnp.bfloat16) for shape in outs],
+        in_specs=[pl.BlockSpec(memory_space=pltpu.SMEM)] + in_specs,
+        out_specs=vmem(len(outs)) if out_specs is None else out_specs,
+        compiler_params=pltpu.CompilerParams(vmem_limit_bytes=VMEM_LIMIT),
+        **more,
+    )
+
+
+def halve(rows):
+    count = rows.shape[0]
+    row = lax.broadcasted_iota(jnp.int32, (count // 2, count), 0)
+    column = lax.broadcasted_iota(jnp.int32, (count // 2, count), 1)
+    pick = jnp.where(column // 2 == row, 0.5, 0.0).astype(jnp.bfloat16)
+    return jnp.dot(pick, rows, preferred_element_type=jnp.float32).astype(jnp.bfloat16)
+
+
+def columns_of(place, j, width):
+    return pl.ds(pl.multiple_of(jnp.bitwise_xor(place, j) * width, width), width)
+
+
+def run_copies(copies):
+    for copy in copies:
+        copy.start()
+    for copy in copies:
+        copy.wait()
+
+
+def pack_kernel(place_ref, q_ref, k_ref, v_ref, weight_ref, ours_ref, theirs_ref, a0, a1, a2, a3, third_ref, fourth_ref, rows_ref, sems):
+    width = a0.shape[1]
+    half = ours_ref.shape[0]
+    ours = pl.ds(pl.multiple_of(place_ref[1] * half, half), half)
+    theirs = pl.ds(pl.multiple_of((1 - place_ref[1]) * half, half), half)
+    loads = [pltpu.make_async_copy(source, rows_ref.at[n], sems.at[n]) for n, source in enumerate((k_ref, v_ref))]
+    copies = [
+        pltpu.make_async_copy(weight_ref.at[ours, :], ours_ref, sems.at[14]),
+        pltpu.make_async_copy(weight_ref.at[theirs, :], theirs_ref, sems.at[15]),
+    ]
+    for j, out in ((2, a2), (3, a3), (1, a1), (0, a0)):
+        columns = columns_of(place_ref[0], j, width)
+        for n, source in enumerate((q_ref, k_ref, v_ref)):
+            to = out.at[n * BLOCK : (n + 1) * BLOCK, :]
+            copies.append(pltpu.make_async_copy(source.at[:, columns], to, sems.at[2 + 3 * j + n]))
+    for copy in loads + copies:
+        copy.start()
+    for n in range(2):
+        loads[n].wait()
+        third = halve(halve(rows_ref[n]))
+        third_ref[n * 32 : (n + 1) * 32, :] = third
+        fourth_ref[n * 16 : (n + 1) * 16, :] = halve(third)
+    for copy in copies:
+        copy.wait()
+
+
+def repack_kernel(place_ref, l_ref, h_ref, lh_ref, b0, b1, b2, b3):
+    width = b0.shape[1]
+    for j, out in enumerate((b0, b1, b2, b3)):
+        columns = columns_of(place_ref[0], j, width)
+        out[0:64, :] = l_ref[:, columns]
+        out[64:96, :] = h_ref[:, columns]
+        out[96:128, :] = lh_ref[:, columns]
+
+
+def attention_kernel(half, place_ref, bias_ref, a0, a1, a2, a3, b0, b1, b2, b3, before_ref, out_ref, key_ref, value_ref):
+    del place_ref, before_ref
+    own = (a0, a1, a2, a3)
+    far = (b0, b1, b2, b3)
+    heads = out_ref.shape[1] // HD
+    for n, rows_ref in enumerate((key_ref, value_ref)):
+        at = 128 + 128 * n
+        for part in range(2):
+            rows_ref[128 * part : 128 * part + 128, :] = own[2 * half + part][at : at + 128, :]
+            rows_ref[256 + 64 * part : 320 + 64 * part, :] = halve(own[2 - 2 * half + part][at : at + 128, :])
+        for j in range(4):
+            rows_ref[384 + 32 * j : 416 + 32 * j, :] = far[j][32 * n : 32 * n + 32, :]
+            rows_ref[512 + 16 * j : 528 + 16 * j, :] = far[j][64 + 16 * n : 80 + 16 * n, :]
+            rows_ref[576 + 16 * j : 592 + 16 * j, :] = far[j][96 + 16 * n : 112 + 16 * n, :]
+    for head in range(heads):
+        columns = slice(head * HD, (head + 1) * HD)
+        for part in range(2):
+            query = own[2 * half + part][0:128, columns]
+            score = lax.dot_general(
+                query, key_ref[:, columns], (((1,), (1,)), ((), ())), preferred_element_type=jnp.float32
+            )
+            score = score * HD ** (-0.5) + bias_ref[2 * half + part : 2 * half + part + 1, :]
+            raised = jnp.exp(score - jnp.max(score, axis=-1, keepdims=True))
+            weight = raised * (1.0 / jnp.sum(raised, axis=-1, keepdims=True))
+            mixed = jnp.dot(
+                weight.astype(jnp.bfloat16), value_ref[:, columns], preferred_element_type=jnp.float32
+            )
+            out_ref[128 * part : 128 * part + 128, columns] = mixed.astype(jnp.bfloat16)
+
+
+def project_kernel(count, place_ref, *refs):
+    mixed, refs = refs[:8], refs[8:]
+    blocks, outs, weight_ref, rows_ref, sems = refs[:-7], refs[-7:-3], refs[-3], refs[-2], refs[-1]
+    place, group = place_ref[0], place_ref[1]
+    depth, wide = weight_ref.shape[1:]
+    half = depth // 2
+    ours = pl.ds(pl.multiple_of(group * half, half), half)
+    theirs = pl.ds(pl.multiple_of((1 - group) * half, half), half)
+    copies = []
+    blocks = list(blocks)
+    for q in range(count):
+        if blocks[0].shape[0] == depth:
+            copies.append([pltpu.make_async_copy(blocks.pop(0), weight_ref.at[q], sems.at[2 * q])])
+        else:
+            copies.append(
+                [
+                    pltpu.make_async_copy(blocks.pop(0), weight_ref.at[q, ours, :], sems.at[2 * q]),
+                    pltpu.make_async_copy(blocks.pop(0), weight_ref.at[q, theirs, :], sems.at[2 * q + 1]),
+                ]
+            )
+    for pair in copies:
+        for copy in pair:
+            copy.start()
+    share = mixed[0].shape[1]
+    for j in range(4):
+        columns = columns_of(place, j, share)
+        for r in range(4):
+            piece = mixed[2 * j + ((r ^ j) >> 1)]
+            at = ((r ^ j) & 1) * BLOCK
+            rows_ref[r * BLOCK : (r + 1) * BLOCK, columns] = piece[at : at + BLOCK, :]
+    for q in range(count):
+        for copy in copies[q]:
+            copy.wait()
+        total = jnp.dot(rows_ref[...], weight_ref[q], preferred_element_type=jnp.float32).astype(jnp.bfloat16)
+        for r in range(4):
+            outs[r][:, q * wide : (q + 1) * wide] = total[r * BLOCK : (r + 1) * BLOCK, :]
+
+
+def place_kernel(place_ref, *refs):
+    sources, out_ref, sems = refs[:-2], refs[-2], refs[-1]
+    wide = out_ref.shape[1] // 16
+    copies = []
+    for n, source in enumerate(sources):
+        masks = ((0, HIGH), (LOW, LOW | HIGH))[n // 4]
+        for q, mask in enumerate(masks):
+            at = pl.multiple_of(jnp.bitwise_xor(place_ref[2], mask | n % 4) * wide, wide)
+            copies.append(
+                pltpu.make_async_copy(
+                    source.at[:, q * wide : (q + 1) * wide], out_ref.at[:, pl.ds(at, wide)], sems.at[len(copies)]
+                )
+            )
+    run_copies(copies)
+
+
+def key_masks():
+    masks = np.zeros((2, 640), np.int32)
+    for half in range(2):
+        for part in range(2):
+            masks[half, 128 * part : 128 * part + 128] = 2 * half + part
+            masks[half, 256 + 64 * part : 320 + 64 * part] = 2 - 2 * half + part
+        for j in range(4):
+            masks[half, 384 + 32 * j : 416 + 32 * j] = j | LOW
+            masks[half, 512 + 16 * j : 528 + 16 * j] = j | HIGH
+            masks[half, 576 + 16 * j : 592 + 16 * j] = j | LOW | HIGH
+    return masks
+
+
+def per_device_fast(queries, keys, values, doc_start, out_weight):
+    length, width = queries.shape
+    share = width // 4
+    depth, wide = out_weight.shape
+    group = lax.axis_index("groups")
+    position = lax.axis_index("ctx")
+    places = jnp.stack([position & 3, group, position]).astype(jnp.int32)
+
+    key_docs = doc_lookup(jnp.bitwise_xor(position, key_masks()), doc_start)
+    query_docs = doc_lookup(jnp.bitwise_xor(position, np.arange(4, dtype=np.int32)), doc_start)
+    allowed = jnp.repeat(key_docs, 2, axis=0) == query_docs[:, None]
+    bias = jnp.where(allowed, 0.0, -jnp.inf).astype(jnp.float32)
+
+    queries, keys, values, out_weight = (
+        pltpu.with_memory_space_constraint(array, pltpu.HBM) for array in (queries, keys, values, out_weight)
+    )
+    ours, theirs, *team, third, fourth = call(
+        pack_kernel,
+        [(depth // 2, wide)] * 2 + [(3 * length, share)] * 4 + [(length // 2, width), (length // 4, width)],
+        anywhere(4),
+        scratch_shapes=[pltpu.VMEM((2, length, width), jnp.bfloat16), pltpu.SemaphoreType.DMA((16,))],
+        name="pack",
+    )(places, queries, keys, values, out_weight)
+    half_h = swap(ours, HIGH)
+    own = [team[0], None, swap(team[2], 2), swap(team[3], 3)]
+    from_l = swap(third, LOW)
+    from_h = swap(fourth, HIGH)
+    from_lh = swap(from_h, LOW)
+    ours_l = swap(after(ours, from_l), LOW)
+    own[1] = swap(after(team[1], from_lh), 1)
+    extra = call(repack_kernel, [(length, share)] * 4, vmem(3), name="repack")(places, from_l, from_h, from_lh)
+    far = [
+        extra[0],
+        swap(after(extra[1], own[3]), 1),
+        swap(after(extra[2], own[2]), 2),
+        swap(after(extra[3], own[3]), 3),
+    ]
+
+    pieces = [[None] * 2 for _ in range(4)]
+    before = places
+    for n in range(2):
+        (attended,) = call(
+            functools.partial(attention_kernel, n),
+            [(2 * length, share)],
+            vmem(9) + [pl.BlockSpec(memory_space=pl.ANY)],
+            scratch_shapes=[pltpu.VMEM((640, share), jnp.bfloat16)] * 2,
+            name="attend%d" % n,
+        )(places, bias, *own, *far, before)
+        before = attended
+        pieces[0][n] = attended
+        pieces[2][n] = swap(attended, 2)
+        pieces[1][n] = swap(attended, 1)
+        pieces[3][n] = swap(pieces[2][n], 1)
+    half_h = after(half_h, pieces[0][0])
+    half_d = swap(after(half_h, ours_l), LOW)
+    other_h = swap_groups(half_h)
+    theirs_l = swap(after(theirs, half_d), LOW)
+    other_d = swap_groups(half_d)
+    mixed = [piece for pair in pieces for piece in pair]
+
+    received = []
+    for n, blocks in enumerate(((out_weight, half_h, other_h), (ours_l, theirs_l, half_d, other_d))):
+        parts = call(
+            functools.partial(project_kernel, 2),
+            [(length, 2 * wide)] * 4,
+            vmem(8) + anywhere(len(blocks)),
+            scratch_shapes=[
+                pltpu.VMEM((2, depth, wide), jnp.bfloat16),
+                pltpu.VMEM((4 * length, width), jnp.bfloat16),
+                pltpu.SemaphoreType.DMA((4,)),
+            ],
+            name="project%d" % n,
+        )(places, *mixed, *blocks)
+        received += [parts[0]] + [swap(parts[j], j) for j in (1, 2, 3)]
+    (out,) = call(
+        place_kernel,
+        [(length, 16 * wide)],
+        anywhere(8),
+        anywhere(1),
+        scratch_shapes=[pltpu.SemaphoreType.DMA((16,))],
+        name="place",
+    )(places, *received)
+    return out
 
 
 def partner(value, axis, apart):
@@ -131,6 +407,7 @@
 
 
 def solution(mesh):
+    fast = mesh.shape["groups"] == 2 and mesh.shape["ctx"] == 16
     placed = (
         P(("groups", "ctx"), None),
         P(("groups", "ctx"), None),
@@ -139,7 +416,7 @@
         P(None, "ctx"),
     )
     return jax.shard_map(
-        per_device,
+        per_device_fast if fast else per_device,
         mesh=mesh,
         in_specs=placed,
         out_specs=P(("groups", "ctx"), None),

time: 210 us -> 97.2 us (0.46)
  waiting for transfers between devices: 103 us -> 48.1 us
  other arithmetic: 44 us -> 1.6 us
  local copies, waits for them, and re-layouts: 25.3 us -> 1.98 us
  Pallas kernels: 0 us -> 22.2 us
  matrix products: 16.5 us -> 0 us
  starting transfers between devices: 6.47 us -> 22.9 us
  between operations: 13.8 us -> 0.12 us
    ppermute x8 -> x27, waiting for transfers between devices: 96.3 us -> 48.1 us  [the longest x25 41.1 us: swap(): return lax.ppermute(value, 'ctx', pairs)]
    convert_element_type x17 -> x0, other arithmetic: 30.7 us -> none  [the longest x12 22.3 us: pair_mean(): return ((halves[:, 0] + halves[:, 1]) * 0.5).astype(jnp.bfloat16)]
    pallas_call x0 -> x7, Pallas kernels: none -> 22.2 us  [the longest x2 8.03 us: per_device_fast(): call(functools.partial(attention_kernel, n), [(2 * length, share)], vmem(...]
    convert_element_type x12 -> x0, local copies, waits for them, and re-layouts: 16.8 us -> none  [pair_mean(): array.reshape(array.shape[0] // 2, 2, array.shape[1]).astype(jnp.float32)]
    dot_general x5 -> x0, matrix products: 16.5 us -> none  [the longest x1 9.1 us: per_device(): jnp.dot(attended, lax.all_gather(out_weight, 'ctx', axis=1, tiled=True),...]
    ppermute x8 -> x27, starting transfers between devices: 6.47 us -> 22.9 us  [the longest x25 19.9 us: swap(): return lax.ppermute(value, 'ctx', pairs)]
    concatenate x9 -> x0, other arithmetic: 8.72 us -> none  [the longest x3 2.65 us: per_device(): jnp.concatenate([pair_mean(low_values), pair_mean(high_values)], 0)]
    all_gather x1 -> x0, waiting for transfers between devices: 5.59 us -> none  [per_device(): lax.all_gather(out_weight, 'ctx', axis=1, tiled=True)]
  transfers between devices with their start and end apart: 9 -> 27, of which waited for: 6 -> 12; matrix products, arithmetic and copies ran while one was open for 37% -> 3% of each run, Pallas kernels for 0% -> 17%
where the time goes in v2:
time: 97.2 us; the launch traced here: 96.9 us
  waiting for transfers between devices  48.1 us (49%)
  starting transfers between devices  22.9 us (24%)
  Pallas kernels  22.2 us (23%)
  local copies, waits for them, and re-layouts  1.98 us (2%)
  other arithmetic  1.6 us (2%)
    ppermute x25, waiting for transfers between devices, swap(): return lax.ppermute(value, 'ctx', pairs)  41.1 us
    ppermute x25, starting transfers between devices, swap(): return lax.ppermute(value, 'ctx', pairs)  19.9 us
    pallas_call x2, Pallas kernels, per_device_fast(): call(functools.partial(attention_kernel, n), [(2 * length, share)], vmem(...  8.03 us
    pallas_call x2, Pallas kernels, per_device_fast(): call(functools.partial(project_kernel, 2), [(length, 2 * wide)] * 4, vmem...  7.61 us
    ppermute x2, waiting for transfers between devices, swap_groups(): return lax.ppermute(value, 'groups', [(0, 1), (1, 0)])  7 us
    pallas_call x1, Pallas kernels, per_device_fast(): call(pack_kernel, [(depth // 2, wide)] * 2 + [(3 * length, share)] * 4 +...  3.75 us
    ppermute x2, starting transfers between devices, swap_groups(): return lax.ppermute(value, 'groups', [(0, 1), (1, 0)])  2.99 us
  transfers between devices with their start and end apart: 27, of which 12 were waited for; matrix products, arithmetic and copies ran while one was open for 3% of the time, Pallas kernels for 17%

profile of v2, /device:TPU:0, one launch (start us, length us, event | category | flops | bytes accessed | tf_op | source)
XLA Modules:
  0.0 96.9 jit_solution(3566371678656731783)
XLA Ops:
  0.0 0.1 pad_add_fusion.place_ref.before_ref
  0.1 3.7 %pack.1 = (bf16[1024,256]{1,0:T(8,128)(2,1)}, bf16[1024,256]{1,0:T(8,128)(2,1)S(1)}, bf16[384,512]{1,0:T(8,128)(2,1)S(1)}, bf16[384,512]{1,0:T(8,128)(2,1)}, bf1...) custom-call(s32[3]{0:T(128)S(1)} %pad_add_fusion.place_ref.before_re, ...), custom_call_target="tpu_custom_call" | custom-call | tf_op jit(solution)/shard_map/pack/pallas_call | solution.py:217
  3.8 0.0 copy-start.1
  3.8 4.1 %collective-permute-start = (bf16[32,2048]{1,0:T(8,128)(2,1)S(1)}, bf16[32,2048]{1,0:T(8,128)(2,1)S(1)}, u32[]{:S(2)}, u32[]{:S(2)}) collective-permute-start(bf16[32,2048]{1,0:T(8,128)(2,1)S(1)} %get-tuple-element.35), channel_id=1, source_target_pairs={{0,8},{1,9},{2,10},{3,11},{4,12},{5,13},{6,14},{7,15},{8,0},{9,1},... | collective-permute-start | bytes 393224 | tf_op jit(solution)/shard_map/ppermute | solution.py:20
  7.9 1.5 %collective-permute-start.3 = (bf16[384,512]{1,0:T(8,128)(2,1)S(1)}, bf16[384,512]{1,0:T(8,128)(2,1)S(1)}, u32[]{:S(2)}, u32[]{:S(2)}) collective-permute-start(bf16[384,512]{1,0:T(8,128)(2,1)S(1)} %get-tuple-element.37), channel_id=1, source_target_pairs={{0,2},{1,3},{2,0},{3,1},{4,6},{5,7},{6,4},{7,5},{8,10},{9,11},{10,... | collective-permute-start | bytes 1179656 | tf_op jit(solution)/shard_map/ppermute | solution.py:20
  9.5 1.6 %collective-permute-start.5 = (bf16[64,2048]{1,0:T(8,128)(2,1)S(1)}, bf16[64,2048]{1,0:T(8,128)(2,1)S(1)}, u32[]{:S(2)}, u32[]{:S(2)}) collective-permute-start(bf16[64,2048]{1,0:T(8,128)(2,1)S(1)} %get-tuple-element.39), channel_id=1, source_target_pairs={{0,4},{1,5},{2,6},{3,7},{4,0},{5,1},{6,2},{7,3},{8,12},{9,13},{10,... | collective-permute-start | bytes 786440 | tf_op jit(solution)/shard_map/ppermute | solution.py:20
  11.0 0.0 collective-permute-start.4
  11.0 0.3 collective-permute-start.15
  11.4 3.0 %collective-permute-done.h_ref = bf16[32,2048]{1,0:T(8,128)(2,1)S(1)} collective-permute-done((bf16[32,2048]{1,0:T(8,128)(2,1)S(1)}, bf16[32,2048]{1,0:T(8,128)(2,1)S(1)}, u32[]{:S(2)}, u32[]{:S(2)}) %collective-permute-start) | collective-permute-done | bytes 131104 | tf_op jit(solution)/shard_map/ppermute | solution.py:20
  14.4 0.8 collective-permute-start.1
  15.1 7.4 %collective-permute-done.5.l_ref = bf16[64,2048]{1,0:T(8,128)(2,1)S(1)} collective-permute-done((bf16[64,2048]{1,0:T(8,128)(2,1)S(1)}, bf16[64,2048]{1,0:T(8,128)(2,1)S(1)}, u32[]{:S(2)}, u32[]{:S(2)}) %collective-permute-start.5) | collective-permute-done | bytes 262176 | tf_op jit(solution)/shard_map/ppermute | solution.py:20
  22.5 0.0 collective-permute-start.20
  22.5 0.1 select_reduce_fusion
  22.6 9.3 %collective-permute-done.1.lh_ref = bf16[32,2048]{1,0:T(8,128)(2,1)S(1)} collective-permute-done((bf16[32,2048]{1,0:T(8,128)(2,1)S(1)}, bf16[32,2048]{1,0:T(8,128)(2,1)S(1)}, u32[]{:S(2)}, u32[]{:S(2)}) %collective-permute-start.1) | collective-permute-done | bytes 131104 | tf_op jit(solution)/shard_map/ppermute | solution.py:20
  31.9 0.0 collective-permute-start.2
  31.9 1.2 %repack.1 = (bf16[128,512]{1,0:T(8,128)(2,1)S(1)}, bf16[128,512]{1,0:T(8,128)(2,1)S(1)}, bf16[128,512]{1,0:T(8,128)(2,1)}, bf16[128,512]{1,0:T(8,128)(2,1)S(1)}) custom-call(s32[3]{0:T(128)S(1)} %pad_add_fusion.place_ref.before_ref, bf16[64,2048]{1,0:T(8,128)(2,1)S(1)} %collective-permute-done.5.l_ref, bf16[32,2048]{1,0:T(8,128)(2,1)S(1)} %collective-permute-done.h_ref, ...), custom_call_target="tpu_custom_call" | custom-call | tf_op jit(solution)/shard_map/repack/pallas_call | solution.py:231
  33.1 0.7 copy-done
  33.8 0.0 collective-permute-done.3.a2
  33.8 1.2 %collective-permute-start.7 = (bf16[128,512]{1,0:T(8,128)(2,1)}, bf16[128,512]{1,0:T(8,128)(2,1)S(1)}, u32[]{:S(2)}, u32[]{:S(2)}) collective-permute-start(bf16[128,512]{1,0:T(8,128)(2,1)} %get-tuple-element.44), channel_id=1, source_target_pairs={{0,2},{1,3},{2,0},{3,1},{4,6},{5,7},{6,4},{7,5},{8,10},{9,11},{10,... | collective-permute-start | bytes 393224 | tf_op jit(solution)/shard_map/ppermute | solution.py:20
  35.0 0.5 iota_xor_fusion
  35.5 0.6 broadcast_in_dim.34
  36.1 0.7 reshape.6
  36.8 0.8 select_reduce_fusion.1
  37.6 0.0 collective-permute-done.4.a3
  37.6 0.3 collective-permute-start.6
  37.9 2.0 %collective-permute-done.7.b2 = bf16[128,512]{1,0:T(8,128)(2,1)S(1)} collective-permute-done((bf16[128,512]{1,0:T(8,128)(2,1)}, bf16[128,512]{1,0:T(8,128)(2,1)S(1)}, u32[]{:S(2)}, u32[]{:S(2)}) %collective-permute-start.7) | collective-permute-done | bytes 131104 | tf_op jit(solution)/shard_map/ppermute | solution.py:20
  39.9 0.5 collective-permute-start.8
  40.4 0.1 compare_select_fusion.bias_ref
  40.5 0.0 collective-permute-done.6.b1
  40.5 5.1 %collective-permute-done.8.b3 = bf16[128,512]{1,0:T(8,128)(2,1)S(1)} collective-permute-done((bf16[128,512]{1,0:T(8,128)(2,1)S(1)}, bf16[128,512]{1,0:T(8,128)(2,1)S(1)}, u32[]{:S(2)}, u32[]{:S(2)}) %collective-permute-start.8) | collective-permute-done | bytes 131104 | tf_op jit(solution)/shard_map/ppermute | solution.py:20
  45.6 4.0 %attend0.1.before_ref.refs_0_ = bf16[256,512]{1,0:T(8,128)(2,1)S(1)} custom-call(s32[3]{0:T(128)S(1)} %pad_add_fusion.place_ref.before_ref, f32[4,640]{1,0:T(4,128)S(1)} %compare_select_fusion.bias_ref, bf16[384,512]{1,0:T(8,128)(2,1)S(1)} %get-tuple-element.33.a0, bf16[384,512]{1,0:T(8,128)(2,1)S(1)} %collective-permute-done.2.a1, ...), custom_call_target="tpu_custom_call" | custom-call | tf_op jit(solution)/shard_map/attend0/pallas_call | solution.py:242
  49.6 0.0 collective-permute-done.15.refs_9_
  49.7 2.5 %collective-permute-start.21 = (bf16[1024,256]{1,0:T(8,128)(2,1)S(1)}, bf16[1024,256]{1,0:T(8,128)(2,1)S(1)}, u32[]{:S(2)}, u32[]{:S(2)}) collective-permute-start(bf16[1024,256]{1,0:T(8,128)(2,1)S(1)} %collective-permute-done.15.refs_9_), channel_id=1, source_target_pairs={{0,4},{1,5},{2,6},{3,7},{4,0},{5,1},{6,2},{7,3},{8,12},{9,13},{10,... | collective-permute-start | bytes 1572872 | tf_op jit(solution)/shard_map/ppermute | solution.py:20
  52.2 4.0 %attend1.1.refs_1_ = bf16[256,512]{1,0:T(8,128)(2,1)S(1)} custom-call(s32[3]{0:T(128)S(1)} %pad_add_fusion.place_ref.before_ref, f32[4,640]{1,0:T(4,128)S(1)} %compare_select_fusion.bias_ref, bf16[384,512]{1,0:T(8,128)(2,1)S(1)} %get-tuple-element.33.a0, bf16[384,512]{1,0:T(8,128)(2,1)S(1)} %collective-permute-done.2.a1, ...), custom_call_target="tpu_custom_call" | custom-call | tf_op jit(solution)/shard_map/attend1/pallas_call | solution.py:242
  56.2 1.3 %collective-permute-start.12 = (bf16[256,512]{1,0:T(8,128)(2,1)S(1)}, bf16[256,512]{1,0:T(8,128)(2,1)S(1)}, u32[]{:S(2)}, u32[]{:S(2)}) collective-permute-start(bf16[256,512]{1,0:T(8,128)(2,1)S(1)} %attend1.1.refs_1_), channel_id=1, source_target_pairs={{0,2},{1,3},{2,0},{3,1},{4,6},{5,7},{6,4},{7,5},{8,10},{9,11},{10,... | collective-permute-start | bytes 786440 | tf_op jit(solution)/shard_map/ppermute | solution.py:20
  57.5 0.8 collective-permute-start.11
  58.3 1.5 %collective-permute-start.16 = (bf16[1024,256]{1,0:T(8,128)(2,1)S(1)}, bf16[1024,256]{1,0:T(8,128)(2,1)S(1)}, u32[]{:S(2)}, u32[]{:S(2)}) collective-permute-start(bf16[1024,256]{1,0:T(8,128)(2,1)S(1)} %collective-permute-done.15.refs_9_), channel_id=1, source_target_pairs={{0,16},{16,0},{1,17},{17,1},{2,18},{18,2},{3,19},{19,3},{4,20},{20... | collective-permute-start | bytes 1572872 | tf_op jit(solution)/shard_map/ppermute | solution.py:24
  59.8 4.5 %collective-permute-done.21.refs_10_ = bf16[1024,256]{1,0:T(8,128)(2,1)S(1)} collective-permute-done((bf16[1024,256]{1,0:T(8,128)(2,1)S(1)}, bf16[1024,256]{1,0:T(8,128)(2,1)S(1)}, u32[]{:S(2)}, u32[]{:S(2)}) %collective-permute-start.21) | collective-permute-done | bytes 524320 | tf_op jit(solution)/shard_map/ppermute | solution.py:20
  64.3 0.0 collective-permute-start.9
  64.3 1.2 %collective-permute-done.12.refs_5_ = bf16[256,512]{1,0:T(8,128)(2,1)S(1)} collective-permute-done((bf16[256,512]{1,0:T(8,128)(2,1)S(1)}, bf16[256,512]{1,0:T(8,128)(2,1)S(1)}, u32[]{:S(2)}, u32[]{:S(2)}) %collective-permute-start.12) | collective-permute-done | bytes 262176 | tf_op jit(solution)/shard_map/ppermute | solution.py:20
  65.5 0.6 collective-permute-start.22
  66.1 0.0 collective-permute-done.10.refs_3_
  66.1 1.5 %collective-permute-start.23 = (bf16[1024,256]{1,0:T(8,128)(2,1)S(1)}, bf16[1024,256]{1,0:T(8,128)(2,1)S(1)}, u32[]{:S(2)}, u32[]{:S(2)}) collective-permute-start(bf16[1024,256]{1,0:T(8,128)(2,1)S(1)} %collective-permute-done.21.refs_10_), channel_id=1, source_target_pairs={{0,16},{16,0},{1,17},{17,1},{2,18},{18,2},{3,19},{19,3},{4,20},{20... | collective-permute-start | bytes 1572872 | tf_op jit(solution)/shard_map/ppermute | solution.py:24
  67.6 2.3 %collective-permute-done.11.refs_4_ = bf16[256,512]{1,0:T(8,128)(2,1)S(1)} collective-permute-done((bf16[256,512]{1,0:T(8,128)(2,1)S(1)}, bf16[256,512]{1,0:T(8,128)(2,1)S(1)}, u32[]{:S(2)}, u32[]{:S(2)}) %collective-permute-start.11) | collective-permute-done | bytes 262176 | tf_op jit(solution)/shard_map/ppermute | solution.py:20
  69.9 0.0 collective-permute-start.14
  69.9 0.0 collective-permute-done.9.refs_2_
  69.9 0.5 collective-permute-start.13
  70.4 2.7 %collective-permute-done.16.refs_10_ = bf16[1024,256]{1,0:T(8,128)(2,1)S(1)} collective-permute-done((bf16[1024,256]{1,0:T(8,128)(2,1)S(1)}, bf16[1024,256]{1,0:T(8,128)(2,1)S(1)}, u32[]{:S(2)}, u32[]{:S(2)}) %collective-permute-start.16) | collective-permute-done | bytes 524320 | tf_op jit(solution)/shard_map/ppermute | solution.py:24
  73.1 4.3 %project0.1 = (bf16[128,512]{1,0:T(8,128)(2,1)S(1)}, bf16[128,512]{1,0:T(8,128)(2,1)S(1)}, bf16[128,512]{1,0:T(8,128)(2,1)S(1)}, bf16[128,512]{1,0:T(8,128)(2,1)S(1)}) custom-call(s32[3]{0:T(128)S(1)} %pad_add_fusion.place_ref.before_ref, bf16[256,512]{1,0:T(8,128)(2,1)S(1)} %attend0.1.before_ref.refs_0_, bf16[256,512]{1,0:T(8,128)(2,1)S(1)} %attend1.1.refs_1_, ...), custom_call_target="tpu_custom_call" | custom-call | tf_op jit(solution)/shard_map/project0/pallas_call | solution.py:263
  77.3 0.1 collective-permute-start.17
  77.4 1.3 %collective-permute-start.18 = (bf16[128,512]{1,0:T(8,128)(2,1)S(1)}, bf16[128,512]{1,0:T(8,128)(2,1)S(1)}, u32[]{:S(2)}, u32[]{:S(2)}) collective-permute-start(bf16[128,512]{1,0:T(8,128)(2,1)S(1)} %get-tuple-element.51), channel_id=1, source_target_pairs={{0,2},{1,3},{2,0},{3,1},{4,6},{5,7},{6,4},{7,5},{8,10},{9,11},{10,... | collective-permute-start | bytes 393224 | tf_op jit(solution)/shard_map/ppermute | solution.py:20
  78.7 0.6 collective-permute-start.19
  79.3 4.3 %collective-permute-done.23.refs_11_ = bf16[1024,256]{1,0:T(8,128)(2,1)S(1)} collective-permute-done((bf16[1024,256]{1,0:T(8,128)(2,1)S(1)}, bf16[1024,256]{1,0:T(8,128)(2,1)S(1)}, u32[]{:S(2)}, u32[]{:S(2)}) %collective-permute-start.23) | collective-permute-done | bytes 524320 | tf_op jit(solution)/shard_map/ppermute | solution.py:24
  83.6 3.3 %project1.1 = (bf16[128,512]{1,0:T(8,128)(2,1)S(1)}, bf16[128,512]{1,0:T(8,128)(2,1)S(1)}, bf16[128,512]{1,0:T(8,128)(2,1)S(1)}, bf16[128,512]{1,0:T(8,128)(2,1)S(1)}) custom-call(s32[3]{0:T(128)S(1)} %pad_add_fusion.place_ref.before_ref, bf16[256,512]{1,0:T(8,128)(2,1)S(1)} %attend0.1.before_ref.refs_0_, bf16[256,512]{1,0:T(8,128)(2,1)S(1)} %attend1.1.refs_1_, ...), custom_call_target="tpu_custom_call" | custom-call | tf_op jit(solution)/shard_map/project1/pallas_call | solution.py:263
  87.0 0.1 collective-permute-start.24
  87.0 1.3 %collective-permute-start.25 = (bf16[128,512]{1,0:T(8,128)(2,1)S(1)}, bf16[128,512]{1,0:T(8,128)(2,1)S(1)}, u32[]{:S(2)}, u32[]{:S(2)}) collective-permute-start(bf16[128,512]{1,0:T(8,128)(2,1)S(1)} %get-tuple-element.59), channel_id=1, source_target_pairs={{0,2},{1,3},{2,0},{3,1},{4,6},{5,7},{6,4},{7,5},{8,10},{9,11},{10,... | collective-permute-start | bytes 393224 | tf_op jit(solution)/shard_map/ppermute | solution.py:20
  88.3 0.0 collective-permute-done.17.refs_1_
  88.3 0.6 collective-permute-start.26
  88.9 0.0 collective-permute-done.18.refs_2_
  88.9 0.0 collective-permute-done.19.refs_3_
  88.9 0.0 collective-permute-done.24.refs_5_
  88.9 4.5 %collective-permute-done.25.refs_6_ = bf16[128,512]{1,0:T(8,128)(2,1)S(1)} collective-permute-done((bf16[128,512]{1,0:T(8,128)(2,1)S(1)}, bf16[128,512]{1,0:T(8,128)(2,1)S(1)}, u32[]{:S(2)}, u32[]{:S(2)}) %collective-permute-start.25) | collective-permute-done | bytes 131104 | tf_op jit(solution)/shard_map/ppermute | solution.py:20
  93.4 1.9 %collective-permute-done.26.refs_7_ = bf16[128,512]{1,0:T(8,128)(2,1)S(1)} collective-permute-done((bf16[128,512]{1,0:T(8,128)(2,1)S(1)}, bf16[128,512]{1,0:T(8,128)(2,1)S(1)}, u32[]{:S(2)}, u32[]{:S(2)}) %collective-permute-start.26) | collective-permute-done | bytes 131104 | tf_op jit(solution)/shard_map/ppermute | solution.py:20
  95.3 1.6 %place.1 = bf16[128,4096]{1,0:T(8,128)(2,1)} custom-call(s32[3]{0:T(128)S(1)} %pad_add_fusion.place_ref.before_ref, bf16[128,512]{1,0:T(8,128)(2,1)S(1)} %get-tuple-element.49.refs_0_, bf16[128,512]{1,0:T(8,128)(2,1)S(1)} %collective-permute-done.17.refs_1_, bf16[128,512]{1,0:T(8,128)(2,1)S(1)} %collective-permute-done.18.refs_2_, ...), custom_call_target="tpu_custom_call" | custom-call | tf_op jit(solution)/shard_map/place/pallas_call | solution.py:275
  (11 shorter events, 0.0 us)
Async XLA Ops:
  3.8 11.3 %copy-start.1 = (s32[2,640]{1,0:T(2,128)S(1)}, s32[2,640]{1,0:T(2,128)}, u32[]{:S(2)}) copy-start(s32[2,640]{1,0:T(2,128)} %constant.21.clone) | copy-start | bytes 15364
  3.8 10.5 %collective-permute-start = (bf16[32,2048]{1,0:T(8,128)(2,1)S(1)}, bf16[32,2048]{1,0:T(8,128)(2,1)S(1)}, u32[]{:S(2)}, u32[]{:S(2)}) collective-permute-start(bf16[32,2048]{1,0:T(8,128)(2,1)S(1)} %get-tuple-element.35), channel_id=1, source_target_pairs={{0,8},{1,9},{2,10},{3,11},{4,12},{5,13},{6,14},{7,15},{8,0},{9,1},... | collective-permute-start | bytes 393224 | tf_op jit(solution)/shard_map/ppermute | solution.py:20
  7.9 25.8 %collective-permute-start.3 = (bf16[384,512]{1,0:T(8,128)(2,1)S(1)}, bf16[384,512]{1,0:T(8,128)(2,1)S(1)}, u32[]{:S(2)}, u32[]{:S(2)}) collective-permute-start(bf16[384,512]{1,0:T(8,128)(2,1)S(1)} %get-tuple-element.37), channel_id=1, source_target_pairs={{0,2},{1,3},{2,0},{3,1},{4,6},{5,7},{6,4},{7,5},{8,10},{9,11},{10,... | collective-permute-start | bytes 1179656 | tf_op jit(solution)/shard_map/ppermute | solution.py:20
  9.5 13.0 %collective-permute-start.5 = (bf16[64,2048]{1,0:T(8,128)(2,1)S(1)}, bf16[64,2048]{1,0:T(8,128)(2,1)S(1)}, u32[]{:S(2)}, u32[]{:S(2)}) collective-permute-start(bf16[64,2048]{1,0:T(8,128)(2,1)S(1)} %get-tuple-element.39), channel_id=1, source_target_pairs={{0,4},{1,5},{2,6},{3,7},{4,0},{5,1},{6,2},{7,3},{8,12},{9,13},{10,... | collective-permute-start | bytes 786440 | tf_op jit(solution)/shard_map/ppermute | solution.py:20
  11.0 26.6 %collective-permute-start.4 = (bf16[384,512]{1,0:T(8,128)(2,1)}, bf16[384,512]{1,0:T(8,128)(2,1)S(1)}, u32[]{:S(2)}, u32[]{:S(2)}) collective-permute-start(bf16[384,512]{1,0:T(8,128)(2,1)} %get-tuple-element.38), channel_id=1, source_target_pairs={{0,3},{1,2},{2,1},{3,0},{4,7},{5,6},{6,5},{7,4},{8,11},{9,10},{10,... | collective-permute-start | bytes 1179656 | tf_op jit(solution)/shard_map/ppermute | solution.py:20
  11.0 11.4 %copy-start.2 = (s32[16]{0:T(128)S(1)}, s32[16]{0:T(128)}, u32[]{:S(2)}) copy-start(s32[16]{0:T(128)} %param.10) | copy-start | bytes 196
  11.0 38.6 %collective-permute-start.15 = (bf16[1024,256]{1,0:T(8,128)(2,1)}, bf16[1024,256]{1,0:T(8,128)(2,1)S(1)}, u32[]{:S(2)}, u32[]{:S(2)}) collective-permute-start(bf16[1024,256]{1,0:T(8,128)(2,1)} %get-tuple-element.53), channel_id=1, source_target_pairs={{0,8},{1,9},{2,10},{3,11},{4,12},{5,13},{6,14},{7,15},{8,0},{9,1},... | collective-permute-start | bytes 1572872 | tf_op jit(solution)/shard_map/ppermute | solution.py:20
  14.4 17.5 %collective-permute-start.1 = (bf16[32,2048]{1,0:T(8,128)(2,1)S(1)}, bf16[32,2048]{1,0:T(8,128)(2,1)S(1)}, u32[]{:S(2)}, u32[]{:S(2)}) collective-permute-start(bf16[32,2048]{1,0:T(8,128)(2,1)S(1)} %collective-permute-done.h_ref), channel_id=1, source_target_pairs={{0,4},{1,5},{2,6},{3,7},{4,0},{5,1},{6,2},{7,3},{8,12},{9,13},{10,... | collective-permute-start | bytes 393224 | tf_op jit(solution)/shard_map/ppermute | solution.py:20
  22.5 27.2 %collective-permute-start.20 = (bf16[1024,256]{1,0:T(8,128)(2,1)}, bf16[1024,256]{1,0:T(8,128)(2,1)S(1)}, u32[]{:S(2)}, u32[]{:S(2)}) collective-permute-start(bf16[1024,256]{1,0:T(8,128)(2,1)} %get-tuple-element.53), channel_id=1, source_target_pairs={{0,4},{1,5},{2,6},{3,7},{4,0},{5,1},{6,2},{7,3},{8,12},{9,13},{10,... | collective-permute-start | bytes 1572872 | tf_op jit(solution)/shard_map/ppermute | solution.py:20
  31.9 13.7 %collective-permute-start.2 = (bf16[384,512]{1,0:T(8,128)(2,1)}, bf16[384,512]{1,0:T(8,128)(2,1)S(1)}, u32[]{:S(2)}, u32[]{:S(2)}) collective-permute-start(bf16[384,512]{1,0:T(8,128)(2,1)} %get-tuple-element.36), channel_id=1, source_target_pairs={{0,1},{1,0},{2,3},{3,2},{4,5},{5,4},{6,7},{7,6},{8,9},{9,8},{10,11... | collective-permute-start | bytes 1179656 | tf_op jit(solution)/shard_map/ppermute | solution.py:20
  33.1 0.7 copy-start
  33.8 6.1 %collective-permute-start.7 = (bf16[128,512]{1,0:T(8,128)(2,1)}, bf16[128,512]{1,0:T(8,128)(2,1)S(1)}, u32[]{:S(2)}, u32[]{:S(2)}) collective-permute-start(bf16[128,512]{1,0:T(8,128)(2,1)} %get-tuple-element.44), channel_id=1, source_target_pairs={{0,2},{1,3},{2,0},{3,1},{4,6},{5,7},{6,4},{7,5},{8,10},{9,11},{10,... | collective-permute-start | bytes 393224 | tf_op jit(solution)/shard_map/ppermute | solution.py:20
  37.6 2.9 %collective-permute-start.6 = (bf16[128,512]{1,0:T(8,128)(2,1)}, bf16[128,512]{1,0:T(8,128)(2,1)S(1)}, u32[]{:S(2)}, u32[]{:S(2)}) collective-permute-start(bf16[128,512]{1,0:T(8,128)(2,1)} %copy-done), channel_id=1, source_target_pairs={{0,1},{1,0},{2,3},{3,2},{4,5},{5,4},{6,7},{7,6},{8,9},{9,8},{10,11... | collective-permute-start | bytes 393224 | tf_op jit(solution)/shard_map/ppermute | solution.py:20
  39.9 5.7 %collective-permute-start.8 = (bf16[128,512]{1,0:T(8,128)(2,1)S(1)}, bf16[128,512]{1,0:T(8,128)(2,1)S(1)}, u32[]{:S(2)}, u32[]{:S(2)}) collective-permute-start(bf16[128,512]{1,0:T(8,128)(2,1)S(1)} %get-tuple-element.46), channel_id=1, source_target_pairs={{0,3},{1,2},{2,1},{3,0},{4,7},{5,6},{6,5},{7,4},{8,11},{9,10},{10,... | collective-permute-start | bytes 393224 | tf_op jit(solution)/shard_map/ppermute | solution.py:20
  49.7 14.7 %collective-permute-start.21 = (bf16[1024,256]{1,0:T(8,128)(2,1)S(1)}, bf16[1024,256]{1,0:T(8,128)(2,1)S(1)}, u32[]{:S(2)}, u32[]{:S(2)}) collective-permute-start(bf16[1024,256]{1,0:T(8,128)(2,1)S(1)} %collective-permute-done.15.refs_9_), channel_id=1, source_target_pairs={{0,4},{1,5},{2,6},{3,7},{4,0},{5,1},{6,2},{7,3},{8,12},{9,13},{10,... | collective-permute-start | bytes 1572872 | tf_op jit(solution)/shard_map/ppermute | solution.py:20
  56.2 9.3 %collective-permute-start.12 = (bf16[256,512]{1,0:T(8,128)(2,1)S(1)}, bf16[256,512]{1,0:T(8,128)(2,1)S(1)}, u32[]{:S(2)}, u32[]{:S(2)}) collective-permute-start(bf16[256,512]{1,0:T(8,128)(2,1)S(1)} %attend1.1.refs_1_), channel_id=1, source_target_pairs={{0,2},{1,3},{2,0},{3,1},{4,6},{5,7},{6,4},{7,5},{8,10},{9,11},{10,... | collective-permute-start | bytes 786440 | tf_op jit(solution)/shard_map/ppermute | solution.py:20
  57.5 8.6 %collective-permute-start.10 = (bf16[256,512]{1,0:T(8,128)(2,1)S(1)}, bf16[256,512]{1,0:T(8,128)(2,1)S(1)}, u32[]{:S(2)}, u32[]{:S(2)}) collective-permute-start(bf16[256,512]{1,0:T(8,128)(2,1)S(1)} %attend1.1.refs_1_), channel_id=1, source_target_pairs={{0,1},{1,0},{2,3},{3,2},{4,5},{5,4},{6,7},{7,6},{8,9},{9,8},{10,11... | collective-permute-start | bytes 786440 | tf_op jit(solution)/shard_map/ppermute | solution.py:20
  57.5 12.4 %collective-permute-start.11 = (bf16[256,512]{1,0:T(8,128)(2,1)S(1)}, bf16[256,512]{1,0:T(8,128)(2,1)S(1)}, u32[]{:S(2)}, u32[]{:S(2)}) collective-permute-start(bf16[256,512]{1,0:T(8,128)(2,1)S(1)} %attend0.1.before_ref.refs_0_), channel_id=1, source_target_pairs={{0,2},{1,3},{2,0},{3,1},{4,6},{5,7},{6,4},{7,5},{8,10},{9,11},{10,... | collective-permute-start | bytes 786440 | tf_op jit(solution)/shard_map/ppermute | solution.py:20
  58.3 14.8 %collective-permute-start.16 = (bf16[1024,256]{1,0:T(8,128)(2,1)S(1)}, bf16[1024,256]{1,0:T(8,128)(2,1)S(1)}, u32[]{:S(2)}, u32[]{:S(2)}) collective-permute-start(bf16[1024,256]{1,0:T(8,128)(2,1)S(1)} %collective-permute-done.15.refs_9_), channel_id=1, source_target_pairs={{0,16},{16,0},{1,17},{17,1},{2,18},{18,2},{3,19},{19,3},{4,20},{20... | collective-permute-start | bytes 1572872 | tf_op jit(solution)/shard_map/ppermute | solution.py:24
  64.3 5.6 %collective-permute-start.9 = (bf16[256,512]{1,0:T(8,128)(2,1)S(1)}, bf16[256,512]{1,0:T(8,128)(2,1)S(1)}, u32[]{:S(2)}, u32[]{:S(2)}) collective-permute-start(bf16[256,512]{1,0:T(8,128)(2,1)S(1)} %attend0.1.before_ref.refs_0_), channel_id=1, source_target_pairs={{0,1},{1,0},{2,3},{3,2},{4,5},{5,4},{6,7},{7,6},{8,9},{9,8},{10,11... | collective-permute-start | bytes 786440 | tf_op jit(solution)/shard_map/ppermute | solution.py:20
  65.5 13.8 %collective-permute-start.22 = (bf16[1024,256]{1,0:T(8,128)(2,1)S(1)}, bf16[1024,256]{1,0:T(8,128)(2,1)S(1)}, u32[]{:S(2)}, u32[]{:S(2)}) collective-permute-start(bf16[1024,256]{1,0:T(8,128)(2,1)S(1)} %get-tuple-element.56), channel_id=1, source_target_pairs={{0,4},{1,5},{2,6},{3,7},{4,0},{5,1},{6,2},{7,3},{8,12},{9,13},{10,... | collective-permute-start | bytes 1572872 | tf_op jit(solution)/shard_map/ppermute | solution.py:20
  66.1 17.5 %collective-permute-start.23 = (bf16[1024,256]{1,0:T(8,128)(2,1)S(1)}, bf16[1024,256]{1,0:T(8,128)(2,1)S(1)}, u32[]{:S(2)}, u32[]{:S(2)}) collective-permute-start(bf16[1024,256]{1,0:T(8,128)(2,1)S(1)} %collective-permute-done.21.refs_10_), channel_id=1, source_target_pairs={{0,16},{16,0},{1,17},{17,1},{2,18},{18,2},{3,19},{19,3},{4,20},{20... | collective-permute-start | bytes 1572872 | tf_op jit(solution)/shard_map/ppermute | solution.py:24
  69.9 3.2 %collective-permute-start.14 = (bf16[256,512]{1,0:T(8,128)(2,1)S(1)}, bf16[256,512]{1,0:T(8,128)(2,1)S(1)}, u32[]{:S(2)}, u32[]{:S(2)}) collective-permute-start(bf16[256,512]{1,0:T(8,128)(2,1)S(1)} %collective-permute-done.12.refs_5_), channel_id=1, source_target_pairs={{0,1},{1,0},{2,3},{3,2},{4,5},{5,4},{6,7},{7,6},{8,9},{9,8},{10,11... | collective-permute-start | bytes 786440 | tf_op jit(solution)/shard_map/ppermute | solution.py:20
  69.9 3.2 %collective-permute-start.13 = (bf16[256,512]{1,0:T(8,128)(2,1)S(1)}, bf16[256,512]{1,0:T(8,128)(2,1)S(1)}, u32[]{:S(2)}, u32[]{:S(2)}) collective-permute-start(bf16[256,512]{1,0:T(8,128)(2,1)S(1)} %collective-permute-done.11.refs_4_), channel_id=1, source_target_pairs={{0,1},{1,0},{2,3},{3,2},{4,5},{5,4},{6,7},{7,6},{8,9},{9,8},{10,11... | collective-permute-start | bytes 786440 | tf_op jit(solution)/shard_map/ppermute | solution.py:20
  77.3 10.9 %collective-permute-start.17 = (bf16[128,512]{1,0:T(8,128)(2,1)S(1)}, bf16[128,512]{1,0:T(8,128)(2,1)S(1)}, u32[]{:S(2)}, u32[]{:S(2)}) collective-permute-start(bf16[128,512]{1,0:T(8,128)(2,1)S(1)} %get-tuple-element.50), channel_id=1, source_target_pairs={{0,1},{1,0},{2,3},{3,2},{4,5},{5,4},{6,7},{7,6},{8,9},{9,8},{10,11... | collective-permute-start | bytes 393224 | tf_op jit(solution)/shard_map/ppermute | solution.py:20
  77.4 11.5 %collective-permute-start.18 = (bf16[128,512]{1,0:T(8,128)(2,1)S(1)}, bf16[128,512]{1,0:T(8,128)(2,1)S(1)}, u32[]{:S(2)}, u32[]{:S(2)}) collective-permute-start(bf16[128,512]{1,0:T(8,128)(2,1)S(1)} %get-tuple-element.51), channel_id=1, source_target_pairs={{0,2},{1,3},{2,0},{3,1},{4,6},{5,7},{6,4},{7,5},{8,10},{9,11},{10,... | collective-permute-start | bytes 393224 | tf_op jit(solution)/shard_map/ppermute | solution.py:20
  78.7 10.2 %collective-permute-start.19 = (bf16[128,512]{1,0:T(8,128)(2,1)S(1)}, bf16[128,512]{1,0:T(8,128)(2,1)S(1)}, u32[]{:S(2)}, u32[]{:S(2)}) collective-permute-start(bf16[128,512]{1,0:T(8,128)(2,1)S(1)} %get-tuple-element.52), channel_id=1, source_target_pairs={{0,3},{1,2},{2,1},{3,0},{4,7},{5,6},{6,5},{7,4},{8,11},{9,10},{10,... | collective-permute-start | bytes 393224 | tf_op jit(solution)/shard_map/ppermute | solution.py:20
  87.0 2.0 %collective-permute-start.24 = (bf16[128,512]{1,0:T(8,128)(2,1)S(1)}, bf16[128,512]{1,0:T(8,128)(2,1)S(1)}, u32[]{:S(2)}, u32[]{:S(2)}) collective-permute-start(bf16[128,512]{1,0:T(8,128)(2,1)S(1)} %get-tuple-element.58), channel_id=1, source_target_pairs={{0,1},{1,0},{2,3},{3,2},{4,5},{5,4},{6,7},{7,6},{8,9},{9,8},{10,11... | collective-permute-start | bytes 393224 | tf_op jit(solution)/shard_map/ppermute | solution.py:20
  87.0 6.4 %collective-permute-start.25 = (bf16[128,512]{1,0:T(8,128)(2,1)S(1)}, bf16[128,512]{1,0:T(8,128)(2,1)S(1)}, u32[]{:S(2)}, u32[]{:S(2)}) collective-permute-start(bf16[128,512]{1,0:T(8,128)(2,1)S(1)} %get-tuple-element.59), channel_id=1, source_target_pairs={{0,2},{1,3},{2,0},{3,1},{4,6},{5,7},{6,4},{7,5},{8,10},{9,11},{10,... | collective-permute-start | bytes 393224 | tf_op jit(solution)/shard_map/ppermute | solution.py:20
  88.3 7.0 %collective-permute-start.26 = (bf16[128,512]{1,0:T(8,128)(2,1)S(1)}, bf16[128,512]{1,0:T(8,128)(2,1)S(1)}, u32[]{:S(2)}, u32[]{:S(2)}) collective-permute-start(bf16[128,512]{1,0:T(8,128)(2,1)S(1)} %get-tuple-element.60), channel_id=1, source_target_pairs={{0,3},{1,2},{2,1},{3,0},{4,7},{5,6},{6,5},{7,4},{8,11},{9,10},{10,... | collective-permute-start | bytes 393224 | tf_op jit(solution)/shard_map/ppermute | solution.py:20

commit v3 on v0

--- a/solution.py
+++ b/solution.py
@@ -1,10 +1,278 @@
+import functools
+
 import jax
 import jax.numpy as jnp
 from jax import lax
+from jax.experimental import pallas as pl
+from jax.experimental.pallas import tpu as pltpu
 from jax.sharding import PartitionSpec as P
 
 HD = 128
 BLOCK = 128
+
+LOW, HIGH = 4, 8
+LOG2_E = 1.4426950408889634
+VMEM_LIMIT = 48 * 2**20
+
+
+def swap(value, mask):
+    pairs = [(source, source ^ mask) for source in range(lax.axis_size("ctx"))]
+    return lax.ppermute(value, "ctx", pairs)
+
+
+def swap_groups(value):
+    return lax.ppermute(value, "groups", [(0, 1), (1, 0)])
+
+
+def after(value, other):
+    return lax.optimization_barrier((value, other))[0]
+
+
+def vmem(count):
+    return [pl.BlockSpec(memory_space=pltpu.VMEM)] * count
+
+
+def anywhere(count):
+    return [pl.BlockSpec(memory_space=pltpu.HBM)] * count
+
+
+def loose(count):
+    return [pl.BlockSpec(memory_space=pl.ANY)] * count
+
+
+def call(kernel, outs, in_specs, out_specs=None, work=None, **more):
+    return pl.pallas_call(
+        kernel,
+        out_shape=[jax.ShapeDtypeStruct(shape, jnp.bfloat16) for shape in outs],
+        in_specs=[pl.BlockSpec(memory_space=pltpu.SMEM)] + in_specs,
+        out_specs=vmem(len(outs)) if out_specs is None else out_specs,
+        compiler_params=pltpu.CompilerParams(vmem_limit_bytes=VMEM_LIMIT),
+        cost_estimate=None if work is None else pl.CostEstimate(flops=work, bytes_accessed=work // 50, transcendentals=0),
+        **more,
+    )
+
+
+def halve(rows):
+    count = rows.shape[0]
+    row = lax.broadcasted_iota(jnp.int32, (count // 2, count), 0)
+    column = lax.broadcasted_iota(jnp.int32, (count // 2, count), 1)
+    pick = jnp.where(column // 2 == row, 0.5, 0.0).astype(jnp.bfloat16)
+    return jnp.dot(pick, rows, preferred_element_type=jnp.float32).astype(jnp.bfloat16)
+
+
+def columns_of(place, j, width):
+    return pl.ds(pl.multiple_of(jnp.bitwise_xor(place, j) * width, width), width)
+
+
+def run_copies(copies):
+    for copy in copies:
+        copy.start()
+    for copy in copies:
+        copy.wait()
+
+
+def pack_kernel(places_of, place_ref, q_ref, k_ref, v_ref, other_ref, *refs):
+    outs, sems = refs[:-1], refs[-1]
+    copies = []
+    if len(outs) > len(places_of):
+        half = outs[0].shape[0]
+        for n in range(2):
+            rows = pl.ds(pl.multiple_of(place_ref[1] * half + n * (half // 2), half // 2), half // 2)
+            to = outs[0].at[n * (half // 2) : (n + 1) * (half // 2), :]
+            copies.append(pltpu.make_async_copy(other_ref.at[rows, :], to, sems.at[n]))
+        outs = outs[1:]
+    for j, out in zip(places_of, outs):
+        columns = columns_of(place_ref[0], j, out.shape[1])
+        for n, source in enumerate((q_ref, k_ref, v_ref)):
+            to = out.at[n * BLOCK : (n + 1) * BLOCK, :]
+            copies.append(pltpu.make_async_copy(source.at[:, columns], to, sems.at[len(copies)]))
+    run_copies(copies)
+
+
+def coarse_kernel(place_ref, a0, a1, a2, a3, third_ref, fourth_ref):
+    del place_ref
+    row = lax.broadcasted_iota(jnp.int32, (96, 256), 0)
+    column = lax.broadcasted_iota(jnp.int32, (96, 256), 1)
+    pick = jnp.where(
+        row < 64,
+        jnp.where(column // 4 == row, 0.25, 0.0),
+        jnp.where(column // 8 == row - 64, 0.125, 0.0),
+    ).astype(jnp.bfloat16)
+    for j, source in enumerate((a0, a1, a2, a3)):
+        means = jnp.dot(pick, source[BLOCK : 3 * BLOCK, :], preferred_element_type=jnp.float32).astype(jnp.bfloat16)
+        for n in range(2):
+            third_ref[n * 128 + 32 * j : n * 128 + 32 * j + 32, :] = means[32 * n : 32 * n + 32, :]
+            fourth_ref[n * 64 + 16 * j : n * 64 + 16 * j + 16, :] = means[64 + 16 * n : 80 + 16 * n, :]
+
+
+def attention_kernel(half, place_ref, doc_ref, *refs):
+    a0, a1, a2, a3, l_ref, h_ref, lh_ref = refs[:7]
+    out_ref, key_ref, value_ref = refs[-3:]
+    own = (a0, a1, a2, a3)
+    heads = out_ref.shape[1] // HD
+    for n, rows_ref in enumerate((key_ref, value_ref)):
+        at = 128 + 128 * n
+        for part in range(2):
+            rows_ref[128 * part : 128 * part + 128, :] = own[2 * half + part][at : at + 128, :]
+            rows_ref[256 + 64 * part : 320 + 64 * part, :] = halve(own[2 - 2 * half + part][at : at + 128, :])
+        rows_ref[384:512, :] = l_ref[128 * n : 128 * n + 128, :]
+        rows_ref[512:576, :] = h_ref[64 * n : 64 * n + 64, :]
+        rows_ref[576:640, :] = lh_ref[64 * n : 64 * n + 64, :]
+    row = lax.broadcasted_iota(jnp.int32, (1, 640), 1)
+    document = jnp.zeros((1, 640), jnp.int32)
+    for first, mask in key_places(half):
+        document = jnp.where(row >= first, doc_ref[jnp.bitwise_xor(place_ref[2], mask)], document)
+    bias = [
+        jnp.where(document == doc_ref[jnp.bitwise_xor(place_ref[2], 2 * half + part)], 0.0, -jnp.inf)
+        for part in range(2)
+    ]
+    for head in range(heads):
+        columns = slice(head * HD, (head + 1) * HD)
+        for part in range(2):
+            query = own[2 * half + part][0:128, columns]
+            score = lax.dot_general(
+                query, key_ref[:, columns], (((1,), (1,)), ((), ())), preferred_element_type=jnp.float32
+            )
+            score = score + bias[part]
+            raised = jnp.exp2((score - jnp.max(score, axis=-1, keepdims=True)) * (HD ** (-0.5) * LOG2_E))
+            mixed = jnp.dot(
+                raised.astype(jnp.bfloat16), value_ref[:, columns], preferred_element_type=jnp.float32
+            )
+            mixed = mixed * (1.0 / jnp.sum(raised, axis=-1, keepdims=True))
+            out_ref[128 * part : 128 * part + 128, columns] = mixed.astype(jnp.bfloat16)
+
+
+def gather_kernel(place_ref, *refs):
+    mixed, rows_ref = refs[:8], refs[8]
+    share = mixed[0].shape[1]
+    for j in range(4):
+        columns = columns_of(place_ref[0], j, share)
+        for r in range(4):
+            piece = mixed[2 * j + ((r ^ j) >> 1)]
+            at = ((r ^ j) & 1) * BLOCK
+            rows_ref[r * BLOCK : (r + 1) * BLOCK, columns] = piece[at : at + BLOCK, :]
+
+
+def project_kernel(place_ref, rows_ref, *refs):
+    blocks, outs = list(refs[:-4]), refs[-4:]
+    depth = rows_ref.shape[1]
+    half = depth // 2
+    group = place_ref[1]
+    q = 0
+    while blocks:
+        block = blocks.pop(0)
+        if block.shape[0] == depth:
+            total = jnp.dot(rows_ref[...], block[...], preferred_element_type=jnp.float32)
+        else:
+            ours = rows_ref[:, pl.ds(pl.multiple_of(group * half, half), half)]
+            theirs = rows_ref[:, pl.ds(pl.multiple_of((1 - group) * half, half), half)]
+            total = jnp.dot(ours, block[...], preferred_element_type=jnp.float32)
+            total += jnp.dot(theirs, blocks.pop(0)[...], preferred_element_type=jnp.float32)
+        wide = block.shape[1]
+        for r in range(4):
+            outs[r][:, q * wide : (q + 1) * wide] = total[r * BLOCK : (r + 1) * BLOCK, :].astype(jnp.bfloat16)
+        q += 1
+
+
+def place_kernel(place_ref, *refs):
+    sources, out_ref, sems = refs[:-2], refs[-2], refs[-1]
+    wide = out_ref.shape[1] // 16
+    copies = []
+    for n, source in enumerate(sources):
+        masks = ((0, HIGH), (LOW, LOW | HIGH))[n // 4]
+        for q, mask in enumerate(masks):
+            at = pl.multiple_of(jnp.bitwise_xor(place_ref[2], mask | n % 4) * wide, wide)
+            copies.append(
+                pltpu.make_async_copy(
+                    source.at[:, q * wide : (q + 1) * wide], out_ref.at[:, pl.ds(at, wide)], sems.at[len(copies)]
+                )
+            )
+    run_copies(copies)
+
+
+def key_places(half):
+    places = [(128 * part, 2 * half + part) for part in range(2)]
+    places += [(256 + 64 * part, 2 - 2 * half + part) for part in range(2)]
+    places += [(384 + 32 * j, j | LOW) for j in range(4)]
+    places += [(512 + 16 * j, j | HIGH) for j in range(4)]
+    places += [(576 + 16 * j, j | LOW | HIGH) for j in range(4)]
+    return places
+
+
+def per_device_fast(queries, keys, values, doc_start, out_weight):
+    length, width = queries.shape
+    share = width // 4
+    depth, wide = out_weight.shape
+    group = lax.axis_index("groups")
+    position = lax.axis_index("ctx")
+    places = jnp.stack([position & 3, group, position]).astype(jnp.int32)
+
+    queries, keys, values, out_weight = (
+        pltpu.with_memory_space_constraint(array, pltpu.HBM) for array in (queries, keys, values, out_weight)
+    )
+    ours, *across = call(
+        functools.partial(pack_kernel, (2, 3)),
+        [(depth // 2, wide)] + [(3 * length, share)] * 2,
+        anywhere(4),
+        scratch_shapes=[pltpu.SemaphoreType.DMA((8,))],
+        name="pack0",
+    )(places, queries, keys, values, out_weight)
+    near = call(
+        functools.partial(pack_kernel, (1, 0)),
+        [(3 * length, share)] * 2,
+        anywhere(3) + loose(1),
+        scratch_shapes=[pltpu.SemaphoreType.DMA((6,))],
+        work=2 * 10**9,
+        name="pack1",
+    )(places, queries, keys, values, across[0])
+    own = [near[1], swap(near[0], 1), swap(across[0], 2), swap(across[1], 3)]
+    half_h = swap(ours, HIGH)
+    ours_l = swap(ours, LOW)
+    third, fourth = call(
+        coarse_kernel, [(2 * length, share), (length, share)], vmem(4), name="coarse"
+    )(places, *own)
+    third, fourth = after((third, fourth), (half_h, ours_l))
+    far = [swap(third, LOW), swap(fourth, HIGH), swap(fourth, LOW | HIGH)]
+    other_h = swap_groups(after(half_h, third))
+    half_d = swap(after(half_h, far[0]), LOW)
+    other_l = swap_groups(after(ours_l, other_h))
+    other_d = swap_groups(after(half_d, other_l))
+
+    pieces = [[None] * 2 for _ in range(4)]
+    before = near[1]
+    for n in range(2):
+        (attended,) = call(
+            functools.partial(attention_kernel, n),
+            [(2 * length, share)],
+            [pl.BlockSpec(memory_space=pltpu.SMEM)] + vmem(7) + loose(1),
+            scratch_shapes=[pltpu.VMEM((640, share), jnp.bfloat16)] * 2,
+            work=2 * 10**9,
+            name="attend%d" % n,
+        )(places, doc_start, *own, *far, before)
+        before = attended
+        pieces[0][n] = attended
+        pieces[2][n] = swap(attended if n == 0 else after(attended, pieces[2][0]), 2)
+    for n in range(2):
+        pieces[1][n] = swap(after(pieces[0][n], (pieces[2][0], half_d)), 1)
+        pieces[3][n] = swap(after(pieces[2][n], half_d), 1)
+    mixed = [piece for pair in pieces for piece in pair]
+
+    (rows,) = call(gather_kernel, [(4 * length, width)], vmem(8), name="gather")(places, *mixed)
+    received = []
+    for n, blocks in enumerate(((out_weight, half_h, other_h), (ours_l, other_l, half_d, other_d))):
+        parts = call(project_kernel, [(length, 2 * wide)] * 4, vmem(1 + len(blocks)), name="project%d" % n)(
+            places, rows, *blocks
+        )
+        received += [parts[0]] + [swap(parts[j], j) for j in (1, 2, 3)]
+    (out,) = call(
+        place_kernel,
+        [(length, 16 * wide)],
+        anywhere(8),
+        anywhere(1),
+        scratch_shapes=[pltpu.SemaphoreType.DMA((16,))],
+        name="place",
+    )(places, *received)
+    return out
 
 
 def partner(value, axis, apart):
@@ -131,6 +399,7 @@
 
 
 def solution(mesh):
+    fast = mesh.shape["groups"] == 2 and mesh.shape["ctx"] == 16
     placed = (
         P(("groups", "ctx"), None),
         P(("groups", "ctx"), None),
@@ -139,7 +408,7 @@
         P(None, "ctx"),
     )
     return jax.shard_map(
-        per_device,
+        per_device_fast if fast else per_device,
         mesh=mesh,
         in_specs=placed,
         out_specs=P(("groups", "ctx"), None),

time: 210 us -> 85.5 us (0.41)
  waiting for transfers between devices: 103 us -> 45.2 us
  other arithmetic: 44 us -> 0.08 us
  local copies, waits for them, and re-layouts: 25.3 us -> 0.01 us
  Pallas kernels: 0 us -> 17.6 us
  matrix products: 16.5 us -> 0 us
  starting transfers between devices: 6.47 us -> 21.9 us
  between operations: 13.8 us -> 0.1 us
    ppermute x8 -> x24, waiting for transfers between devices: 96.3 us -> 45.2 us  [the longest x21 45 us: swap(): return lax.ppermute(value, 'ctx', pairs)]
    convert_element_type x17 -> x0, other arithmetic: 30.7 us -> none  [the longest x12 22.3 us: pair_mean(): return ((halves[:, 0] + halves[:, 1]) * 0.5).astype(jnp.bfloat16)]
    pallas_call x0 -> x9, Pallas kernels: none -> 17.6 us  [the longest x2 6.46 us: per_device_fast(): call(functools.partial(attention_kernel, n), [(2 * length, share)], [pl.B...]
    convert_element_type x12 -> x0, local copies, waits for them, and re-layouts: 16.8 us -> none  [pair_mean(): array.reshape(array.shape[0] // 2, 2, array.shape[1]).astype(jnp.float32)]
    dot_general x5 -> x0, matrix products: 16.5 us -> none  [the longest x1 9.1 us: per_device(): jnp.dot(attended, lax.all_gather(out_weight, 'ctx', axis=1, tiled=True),...]
    ppermute x8 -> x24, starting transfers between devices: 6.47 us -> 21.9 us  [the longest x21 18.9 us: swap(): return lax.ppermute(value, 'ctx', pairs)]
    concatenate x9 -> x0, other arithmetic: 8.72 us -> none  [the longest x3 2.65 us: per_device(): jnp.concatenate([pair_mean(low_values), pair_mean(high_values)], 0)]
    all_gather x1 -> x0, waiting for transfers between devices: 5.59 us -> none  [per_device(): lax.all_gather(out_weight, 'ctx', axis=1, tiled=True)]
  transfers between devices with their start and end apart: 9 -> 24, of which waited for: 6 -> 15; matrix products, arithmetic and copies ran while one was open for 37% -> 0% of each run, Pallas kernels for 0% -> 17%
where the time goes in v3:
time: 85.5 us; the launch traced here: 84.9 us
  waiting for transfers between devices  45.2 us (53%)
  starting transfers between devices  21.9 us (26%)
  Pallas kernels  17.6 us (21%)
    ppermute x21, waiting for transfers between devices, swap(): return lax.ppermute(value, 'ctx', pairs)  45 us
    ppermute x21, starting transfers between devices, swap(): return lax.ppermute(value, 'ctx', pairs)  18.9 us
    pallas_call x2, Pallas kernels, per_device_fast(): call(functools.partial(attention_kernel, n), [(2 * length, share)], [pl.B...  6.46 us
    pallas_call x2, Pallas kernels, per_device_fast(): call(project_kernel, [(length, 2 * wide)] * 4, vmem(1 + len(blocks)), nam...  4.28 us
    ppermute x3, starting transfers between devices, swap_groups(): return lax.ppermute(value, 'groups', [(0, 1), (1, 0)])  3.06 us
    pallas_call x1, Pallas kernels, per_device_fast(): call(functools.partial(pack_kernel, (2, 3)), [(depth // 2, wide)] + [(3 *...  1.88 us
    pallas_call x1, Pallas kernels, per_device_fast(): call(functools.partial(pack_kernel, (1, 0)), [(3 * length, share)] * 2, a...  1.8 us
  transfers between devices with their start and end apart: 24, of which 15 were waited for; matrix products, arithmetic and copies ran while one was open for 0% of the time, Pallas kernels for 17%

profile of v3, /device:TPU:0, one launch (start us, length us, event | category | flops | bytes accessed | tf_op | source)
XLA Modules:
  0.0 84.9 jit_solution(15057863207376409874)
XLA Ops:
  0.0 0.1 pad_add_fusion.place_ref
  0.1 1.9 %pack0.1 = (bf16[1024,256]{1,0:T(8,128)(2,1)S(1)}, bf16[384,512]{1,0:T(8,128)(2,1)S(1)}, bf16[384,512]{1,0:T(8,128)(2,1)S(1)}) custom-call(s32[3]{0:T(128)S(1)} %pad_add_fusion.place_ref, bf16[128,2048]{1,0:T(8,128)(2,1)} %q_ref.3, bf16[128,2048]{1,0:T(8,128)(2,1)} %k_ref.3, bf16[128,2048]{1,0:T(8,128)(2,1)} %v_ref.3, bf16[2048,256]{1,0:T(8,128)(2,1)} %refs_0_.1), custom_call_target="tpu_custom_call" | custom-call | tf_op jit(solution)/shard_map/pack0/pallas_call | solution.py:213
  2.0 3.1 %collective-permute-start.4 = (bf16[1024,256]{1,0:T(8,128)(2,1)S(1)}, bf16[1024,256]{1,0:T(8,128)(2,1)S(1)}, u32[]{:S(2)}, u32[]{:S(2)}) collective-permute-start(bf16[1024,256]{1,0:T(8,128)(2,1)S(1)} %get-tuple-element.37), channel_id=1, source_target_pairs={{0,4},{1,5},{2,6},{3,7},{4,0},{5,1},{6,2},{7,3},{8,12},{9,13},{10,... | collective-permute-start | bytes 1572872 | tf_op jit(solution)/shard_map/ppermute | solution.py:20
  5.1 2.6 %collective-permute-start.3 = (bf16[1024,256]{1,0:T(8,128)(2,1)S(1)}, bf16[1024,256]{1,0:T(8,128)(2,1)S(1)}, u32[]{:S(2)}, u32[]{:S(2)}) collective-permute-start(bf16[1024,256]{1,0:T(8,128)(2,1)S(1)} %get-tuple-element.37), channel_id=1, source_target_pairs={{0,8},{1,9},{2,10},{3,11},{4,12},{5,13},{6,14},{7,15},{8,0},{9,1},... | collective-permute-start | bytes 1572872 | tf_op jit(solution)/shard_map/ppermute | solution.py:20
  7.6 0.4 collective-permute-start.2
  8.0 0.0 copy-start
  8.0 1.2 %collective-permute-start.1 = (bf16[384,512]{1,0:T(8,128)(2,1)S(1)}, bf16[384,512]{1,0:T(8,128)(2,1)S(1)}, u32[]{:S(2)}, u32[]{:S(2)}) collective-permute-start(bf16[384,512]{1,0:T(8,128)(2,1)S(1)} %get-tuple-element.31.other_ref), channel_id=1, source_target_pairs={{0,2},{1,3},{2,0},{3,1},{4,6},{5,7},{6,4},{7,5},{8,10},{9,11},{10,... | collective-permute-start | bytes 1179656 | tf_op jit(solution)/shard_map/ppermute | solution.py:20
  9.2 1.8 %pack1.1 = (bf16[384,512]{1,0:T(8,128)(2,1)S(1)}, bf16[384,512]{1,0:T(8,128)(2,1)S(1)}) custom-call(s32[3]{0:T(128)S(1)} %pad_add_fusion.place_ref, bf16[128,2048]{1,0:T(8,128)(2,1)} %q_ref.3, bf16[128,2048]{1,0:T(8,128)(2,1)} %k_ref.3, bf16[128,2048]{1,0:T(8,128)(2,1)} %v_ref.3, bf16[384,512]{1,0:T(8,128)(2,1)S(1)} %get-tuple-element.31.other_ref), custom_call_target="tpu_custom_call" | custom-call | flops 2000000000 | bytes 40000000 | tf_op jit(solution)/shard_map/pack1/pallas_call | solution.py:220
  11.0 0.4 collective-permute-start
  11.4 7.6 %collective-permute-done.2.a3.refs_3_ = bf16[384,512]{1,0:T(8,128)(2,1)S(1)} collective-permute-done((bf16[384,512]{1,0:T(8,128)(2,1)S(1)}, bf16[384,512]{1,0:T(8,128)(2,1)S(1)}, u32[]{:S(2)}, u32[]{:S(2)}) %collective-permute-start.2) | collective-permute-done | bytes 393248 | tf_op jit(solution)/shard_map/ppermute | solution.py:20
  19.0 8.5 %collective-permute-done.1.a2.refs_2_ = bf16[384,512]{1,0:T(8,128)(2,1)S(1)} collective-permute-done((bf16[384,512]{1,0:T(8,128)(2,1)S(1)}, bf16[384,512]{1,0:T(8,128)(2,1)S(1)}, u32[]{:S(2)}, u32[]{:S(2)}) %collective-permute-start.1) | collective-permute-done | bytes 393248 | tf_op jit(solution)/shard_map/ppermute | solution.py:20
  27.5 0.0 collective-permute-done.a1.refs_1_
  27.5 0.8 coarse.1
  28.3 0.0 collective-permute-done.4.refs_0_
  28.3 2.3 %collective-permute-done.3.refs_1_ = bf16[1024,256]{1,0:T(8,128)(2,1)S(1)} collective-permute-done((bf16[1024,256]{1,0:T(8,128)(2,1)S(1)}, bf16[1024,256]{1,0:T(8,128)(2,1)S(1)}, u32[]{:S(2)}, u32[]{:S(2)}) %collective-permute-start.3) | collective-permute-done | bytes 524320 | tf_op jit(solution)/shard_map/ppermute | solution.py:20
  30.6 1.5 %collective-permute-start.15 = (bf16[1024,256]{1,0:T(8,128)(2,1)S(1)}, bf16[1024,256]{1,0:T(8,128)(2,1)S(1)}, u32[]{:S(2)}, u32[]{:S(2)}) collective-permute-start(bf16[1024,256]{1,0:T(8,128)(2,1)S(1)} %collective-permute-done.3.refs_1_), channel_id=1, source_target_pairs={{0,16},{16,0},{1,17},{17,1},{2,18},{18,2},{3,19},{19,3},{4,20},{20... | collective-permute-start | bytes 1572872 | tf_op jit(solution)/shard_map/ppermute | solution.py:24
  32.1 0.4 collective-permute-start.5
  32.6 2.1 %collective-permute-start.7 = (bf16[128,512]{1,0:T(8,128)(2,1)S(1)}, bf16[128,512]{1,0:T(8,128)(2,1)S(1)}, u32[]{:S(2)}, u32[]{:S(2)}) collective-permute-start(bf16[128,512]{1,0:T(8,128)(2,1)S(1)} %get-tuple-element.39), channel_id=1, source_target_pairs={{0,12},{1,13},{2,14},{3,15},{4,8},{5,9},{6,10},{7,11},{8,4},{9,5},... | collective-permute-start | bytes 393224 | tf_op jit(solution)/shard_map/ppermute | solution.py:20
  34.6 1.0 %collective-permute-start.6 = (bf16[128,512]{1,0:T(8,128)(2,1)S(1)}, bf16[128,512]{1,0:T(8,128)(2,1)S(1)}, u32[]{:S(2)}, u32[]{:S(2)}) collective-permute-start(bf16[128,512]{1,0:T(8,128)(2,1)S(1)} %get-tuple-element.39), channel_id=1, source_target_pairs={{0,8},{1,9},{2,10},{3,11},{4,12},{5,13},{6,14},{7,15},{8,0},{9,1},... | collective-permute-start | bytes 393224 | tf_op jit(solution)/shard_map/ppermute | solution.py:20
  35.6 10.9 %collective-permute-done.5.refs_4_ = bf16[256,512]{1,0:T(8,128)(2,1)S(1)} collective-permute-done((bf16[256,512]{1,0:T(8,128)(2,1)S(1)}, bf16[256,512]{1,0:T(8,128)(2,1)S(1)}, u32[]{:S(2)}, u32[]{:S(2)}) %collective-permute-start.5) | collective-permute-done | bytes 262176 | tf_op jit(solution)/shard_map/ppermute | solution.py:20
  46.5 0.0 collective-permute-start.9
  46.5 0.0 collective-permute-done.15.refs_2_
  46.5 0.5 collective-permute-start.19
  47.1 0.0 collective-permute-done.7.refs_6_
  47.1 0.0 collective-permute-done.6.refs_5_
  47.1 0.0 copy-done
  47.1 3.2 %attend0.1.refs_7_.refs_0_ = bf16[256,512]{1,0:T(8,128)(2,1)S(1)} custom-call(s32[3]{0:T(128)S(1)} %pad_add_fusion.place_ref, s32[16]{0:T(128)S(1)} %copy-done, bf16[384,512]{1,0:T(8,128)(2,1)S(1)} %get-tuple-element.32.a0.refs_0_.refs_7_, bf16[384,512]{1,0:T(8,128)(2,1)S(1)} %collective-permute-done.a1.refs_1_, ...), custom_call_target="tpu_custom_call" | custom-call | flops 2000000000 | bytes 40000000 | tf_op jit(solution)/shard_map/attend0/pallas_call | solution.py:244
  50.3 1.6 %collective-permute-start.8 = (bf16[256,512]{1,0:T(8,128)(2,1)S(1)}, bf16[256,512]{1,0:T(8,128)(2,1)S(1)}, u32[]{:S(2)}, u32[]{:S(2)}) collective-permute-start(bf16[256,512]{1,0:T(8,128)(2,1)S(1)} %attend0.1.refs_7_.refs_0_), channel_id=1, source_target_pairs={{0,2},{1,3},{2,0},{3,1},{4,6},{5,7},{6,4},{7,5},{8,10},{9,11},{10,... | collective-permute-start | bytes 786440 | tf_op jit(solution)/shard_map/ppermute | solution.py:20
  51.9 3.2 %attend1.1.refs_1_ = bf16[256,512]{1,0:T(8,128)(2,1)S(1)} custom-call(s32[3]{0:T(128)S(1)} %pad_add_fusion.place_ref, s32[16]{0:T(128)S(1)} %copy-done, bf16[384,512]{1,0:T(8,128)(2,1)S(1)} %get-tuple-element.32.a0.refs_0_.refs_7_, bf16[384,512]{1,0:T(8,128)(2,1)S(1)} %collective-permute-done.a1.refs_1_, ...), custom_call_target="tpu_custom_call" | custom-call | flops 2000000000 | bytes 40000000 | tf_op jit(solution)/shard_map/attend1/pallas_call | solution.py:244
  55.1 2.1 %collective-permute-done.8.refs_4_ = bf16[256,512]{1,0:T(8,128)(2,1)S(1)} collective-permute-done((bf16[256,512]{1,0:T(8,128)(2,1)S(1)}, bf16[256,512]{1,0:T(8,128)(2,1)S(1)}, u32[]{:S(2)}, u32[]{:S(2)}) %collective-permute-start.8) | collective-permute-done | bytes 262176 | tf_op jit(solution)/shard_map/ppermute | solution.py:20
  57.2 1.3 %collective-permute-start.12 = (bf16[256,512]{1,0:T(8,128)(2,1)S(1)}, bf16[256,512]{1,0:T(8,128)(2,1)S(1)}, u32[]{:S(2)}, u32[]{:S(2)}) collective-permute-start(bf16[256,512]{1,0:T(8,128)(2,1)S(1)} %attend1.1.refs_1_), channel_id=1, source_target_pairs={{0,2},{1,3},{2,0},{3,1},{4,6},{5,7},{6,4},{7,5},{8,10},{9,11},{10,... | collective-permute-start | bytes 786440 | tf_op jit(solution)/shard_map/ppermute | solution.py:20
  58.5 0.0 collective-permute-done.9.refs_2_
  58.5 0.2 collective-permute-done.19.refs_1_
  58.7 1.0 %collective-permute-start.20 = (bf16[1024,256]{1,0:T(8,128)(2,1)S(1)}, bf16[1024,256]{1,0:T(8,128)(2,1)S(1)}, u32[]{:S(2)}, u32[]{:S(2)}) collective-permute-start(bf16[1024,256]{1,0:T(8,128)(2,1)S(1)} %collective-permute-done.9.refs_2_), channel_id=1, source_target_pairs={{0,16},{16,0},{1,17},{17,1},{2,18},{18,2},{3,19},{19,3},{4,20},{20... | collective-permute-start | bytes 1572872 | tf_op jit(solution)/shard_map/ppermute | solution.py:24
  59.8 3.8 %collective-permute-done.12.refs_5_ = bf16[256,512]{1,0:T(8,128)(2,1)S(1)} collective-permute-done((bf16[256,512]{1,0:T(8,128)(2,1)S(1)}, bf16[256,512]{1,0:T(8,128)(2,1)S(1)}, u32[]{:S(2)}, u32[]{:S(2)}) %collective-permute-start.12) | collective-permute-done | bytes 262176 | tf_op jit(solution)/shard_map/ppermute | solution.py:20
  63.5 0.0 collective-permute-start.10
  63.6 0.5 collective-permute-start.11
  64.1 0.0 collective-permute-start.13
  64.1 0.5 collective-permute-start.14
  64.6 0.5 collective-permute-done.10.refs_2_
  65.1 0.4 collective-permute-done.11.refs_3_
  65.5 0.4 collective-permute-done.13.refs_6_
  65.8 0.4 collective-permute-done.14.refs_7_
  66.2 0.7 gather.1.rows_ref
  66.9 2.5 %project0.1 = (bf16[128,512]{1,0:T(8,128)(2,1)S(1)}, bf16[128,512]{1,0:T(8,128)(2,1)S(1)}, bf16[128,512]{1,0:T(8,128)(2,1)S(1)}, bf16[128,512]{1,0:T(8,128)(2,1)S(1)}) custom-call(s32[3]{0:T(128)S(1)} %pad_add_fusion.place_ref, bf16[512,2048]{1,0:T(8,128)(2,1)S(1)} %gather.1.rows_ref, bf16[2048,256]{1,0:T(8,128)(2,1)} %refs_0_.1, ...), custom_call_target="tpu_custom_call" | custom-call | tf_op jit(solution)/shard_map/project0/pallas_call | solution.py:263
  69.4 0.2 collective-permute-start.16
  69.6 1.3 %collective-permute-start.17 = (bf16[128,512]{1,0:T(8,128)(2,1)S(1)}, bf16[128,512]{1,0:T(8,128)(2,1)S(1)}, u32[]{:S(2)}, u32[]{:S(2)}) collective-permute-start(bf16[128,512]{1,0:T(8,128)(2,1)S(1)} %get-tuple-element.49), channel_id=1, source_target_pairs={{0,2},{1,3},{2,0},{3,1},{4,6},{5,7},{6,4},{7,5},{8,10},{9,11},{10,... | collective-permute-start | bytes 393224 | tf_op jit(solution)/shard_map/ppermute | solution.py:20
  71.0 0.4 collective-permute-start.18
  71.3 0.0 collective-permute-done.20.refs_3_
  71.3 1.8 %project1.1 = (bf16[128,512]{1,0:T(8,128)(2,1)S(1)}, bf16[128,512]{1,0:T(8,128)(2,1)S(1)}, bf16[128,512]{1,0:T(8,128)(2,1)S(1)}, bf16[128,512]{1,0:T(8,128)(2,1)S(1)}) custom-call(s32[3]{0:T(128)S(1)} %pad_add_fusion.place_ref, bf16[512,2048]{1,0:T(8,128)(2,1)S(1)} %gather.1.rows_ref, bf16[1024,256]{1,0:T(8,128)(2,1)S(1)} %collective-permute-done.4.refs_0_, ...), custom_call_target="tpu_custom_call" | custom-call | tf_op jit(solution)/shard_map/project1/pallas_call | solution.py:263
  73.1 0.5 collective-permute-start.21
  73.6 1.3 %collective-permute-start.22 = (bf16[128,512]{1,0:T(8,128)(2,1)S(1)}, bf16[128,512]{1,0:T(8,128)(2,1)S(1)}, u32[]{:S(2)}, u32[]{:S(2)}) collective-permute-start(bf16[128,512]{1,0:T(8,128)(2,1)S(1)} %get-tuple-element.55), channel_id=1, source_target_pairs={{0,2},{1,3},{2,0},{3,1},{4,6},{5,7},{6,4},{7,5},{8,10},{9,11},{10,... | collective-permute-start | bytes 393224 | tf_op jit(solution)/shard_map/ppermute | solution.py:20
  75.0 0.0 collective-permute-done.16.refs_1_
  75.0 0.1 collective-permute-start.23
  75.1 0.9 %collective-permute-done.17.refs_2_ = bf16[128,512]{1,0:T(8,128)(2,1)S(1)} collective-permute-done((bf16[128,512]{1,0:T(8,128)(2,1)S(1)}, bf16[128,512]{1,0:T(8,128)(2,1)S(1)}, u32[]{:S(2)}, u32[]{:S(2)}) %collective-permute-start.17) | collective-permute-done | bytes 131104 | tf_op jit(solution)/shard_map/ppermute | solution.py:20
  75.9 1.7 %collective-permute-done.18.refs_3_ = bf16[128,512]{1,0:T(8,128)(2,1)S(1)} collective-permute-done((bf16[128,512]{1,0:T(8,128)(2,1)S(1)}, bf16[128,512]{1,0:T(8,128)(2,1)S(1)}, u32[]{:S(2)}, u32[]{:S(2)}) %collective-permute-start.18) | collective-permute-done | bytes 131104 | tf_op jit(solution)/shard_map/ppermute | solution.py:20
  77.6 0.0 collective-permute-done.21.refs_5_
  77.6 3.9 %collective-permute-done.22.refs_6_ = bf16[128,512]{1,0:T(8,128)(2,1)S(1)} collective-permute-done((bf16[128,512]{1,0:T(8,128)(2,1)S(1)}, bf16[128,512]{1,0:T(8,128)(2,1)S(1)}, u32[]{:S(2)}, u32[]{:S(2)}) %collective-permute-start.22) | collective-permute-done | bytes 131104 | tf_op jit(solution)/shard_map/ppermute | solution.py:20
  81.6 1.7 %collective-permute-done.23.refs_7_ = bf16[128,512]{1,0:T(8,128)(2,1)S(1)} collective-permute-done((bf16[128,512]{1,0:T(8,128)(2,1)S(1)}, bf16[128,512]{1,0:T(8,128)(2,1)S(1)}, u32[]{:S(2)}, u32[]{:S(2)}) %collective-permute-start.23) | collective-permute-done | bytes 131104 | tf_op jit(solution)/shard_map/ppermute | solution.py:20
  83.3 1.6 %place.1 = bf16[128,4096]{1,0:T(8,128)(2,1)} custom-call(s32[3]{0:T(128)S(1)} %pad_add_fusion.place_ref, bf16[128,512]{1,0:T(8,128)(2,1)S(1)} %get-tuple-element.47.refs_0_, bf16[128,512]{1,0:T(8,128)(2,1)S(1)} %collective-permute-done.16.refs_1_, bf16[128,512]{1,0:T(8,128)(2,1)S(1)} %collective-permute-done.17.refs_2_, ...), custom_call_target="tpu_custom_call" | custom-call | tf_op jit(solution)/shard_map/place/pallas_call | solution.py:267
Async XLA Ops:
  2.0 26.4 %collective-permute-start.4 = (bf16[1024,256]{1,0:T(8,128)(2,1)S(1)}, bf16[1024,256]{1,0:T(8,128)(2,1)S(1)}, u32[]{:S(2)}, u32[]{:S(2)}) collective-permute-start(bf16[1024,256]{1,0:T(8,128)(2,1)S(1)} %get-tuple-element.37), channel_id=1, source_target_pairs={{0,4},{1,5},{2,6},{3,7},{4,0},{5,1},{6,2},{7,3},{8,12},{9,13},{10,... | collective-permute-start | bytes 1572872 | tf_op jit(solution)/shard_map/ppermute | solution.py:20
  5.1 25.6 %collective-permute-start.3 = (bf16[1024,256]{1,0:T(8,128)(2,1)S(1)}, bf16[1024,256]{1,0:T(8,128)(2,1)S(1)}, u32[]{:S(2)}, u32[]{:S(2)}) collective-permute-start(bf16[1024,256]{1,0:T(8,128)(2,1)S(1)} %get-tuple-element.37), channel_id=1, source_target_pairs={{0,8},{1,9},{2,10},{3,11},{4,12},{5,13},{6,14},{7,15},{8,0},{9,1},... | collective-permute-start | bytes 1572872 | tf_op jit(solution)/shard_map/ppermute | solution.py:20
  7.6 11.3 %collective-permute-start.2 = (bf16[384,512]{1,0:T(8,128)(2,1)S(1)}, bf16[384,512]{1,0:T(8,128)(2,1)S(1)}, u32[]{:S(2)}, u32[]{:S(2)}) collective-permute-start(bf16[384,512]{1,0:T(8,128)(2,1)S(1)} %get-tuple-element.34), channel_id=1, source_target_pairs={{0,3},{1,2},{2,1},{3,0},{4,7},{5,6},{6,5},{7,4},{8,11},{9,10},{10,... | collective-permute-start | bytes 1179656 | tf_op jit(solution)/shard_map/ppermute | solution.py:20
  8.0 39.0 %copy-start = (s32[16]{0:T(128)S(1)}, s32[16]{0:T(128)}, u32[]{:S(2)}) copy-start(s32[16]{0:T(128)} %doc_ref.3) | copy-start | bytes 196
  8.0 19.4 %collective-permute-start.1 = (bf16[384,512]{1,0:T(8,128)(2,1)S(1)}, bf16[384,512]{1,0:T(8,128)(2,1)S(1)}, u32[]{:S(2)}, u32[]{:S(2)}) collective-permute-start(bf16[384,512]{1,0:T(8,128)(2,1)S(1)} %get-tuple-element.31.other_ref), channel_id=1, source_target_pairs={{0,2},{1,3},{2,0},{3,1},{4,6},{5,7},{6,4},{7,5},{8,10},{9,11},{10,... | collective-permute-start | bytes 1179656 | tf_op jit(solution)/shard_map/ppermute | solution.py:20
  11.0 16.5 %collective-permute-start = (bf16[384,512]{1,0:T(8,128)(2,1)S(1)}, bf16[384,512]{1,0:T(8,128)(2,1)S(1)}, u32[]{:S(2)}, u32[]{:S(2)}) collective-permute-start(bf16[384,512]{1,0:T(8,128)(2,1)S(1)} %get-tuple-element.33), channel_id=1, source_target_pairs={{0,1},{1,0},{2,3},{3,2},{4,5},{5,4},{6,7},{7,6},{8,9},{9,8},{10,11... | collective-permute-start | bytes 1179656 | tf_op jit(solution)/shard_map/ppermute | solution.py:20
  30.6 15.9 %collective-permute-start.15 = (bf16[1024,256]{1,0:T(8,128)(2,1)S(1)}, bf16[1024,256]{1,0:T(8,128)(2,1)S(1)}, u32[]{:S(2)}, u32[]{:S(2)}) collective-permute-start(bf16[1024,256]{1,0:T(8,128)(2,1)S(1)} %collective-permute-done.3.refs_1_), channel_id=1, source_target_pairs={{0,16},{16,0},{1,17},{17,1},{2,18},{18,2},{3,19},{19,3},{4,20},{20... | collective-permute-start | bytes 1572872 | tf_op jit(solution)/shard_map/ppermute | solution.py:24
  32.1 14.4 %collective-permute-start.5 = (bf16[256,512]{1,0:T(8,128)(2,1)S(1)}, bf16[256,512]{1,0:T(8,128)(2,1)S(1)}, u32[]{:S(2)}, u32[]{:S(2)}) collective-permute-start(bf16[256,512]{1,0:T(8,128)(2,1)S(1)} %get-tuple-element.38), channel_id=1, source_target_pairs={{0,4},{1,5},{2,6},{3,7},{4,0},{5,1},{6,2},{7,3},{8,12},{9,13},{10,... | collective-permute-start | bytes 786440 | tf_op jit(solution)/shard_map/ppermute | solution.py:20
  32.6 14.5 %collective-permute-start.7 = (bf16[128,512]{1,0:T(8,128)(2,1)S(1)}, bf16[128,512]{1,0:T(8,128)(2,1)S(1)}, u32[]{:S(2)}, u32[]{:S(2)}) collective-permute-start(bf16[128,512]{1,0:T(8,128)(2,1)S(1)} %get-tuple-element.39), channel_id=1, source_target_pairs={{0,12},{1,13},{2,14},{3,15},{4,8},{5,9},{6,10},{7,11},{8,4},{9,5},... | collective-permute-start | bytes 393224 | tf_op jit(solution)/shard_map/ppermute | solution.py:20
  34.6 12.4 %collective-permute-start.6 = (bf16[128,512]{1,0:T(8,128)(2,1)S(1)}, bf16[128,512]{1,0:T(8,128)(2,1)S(1)}, u32[]{:S(2)}, u32[]{:S(2)}) collective-permute-start(bf16[128,512]{1,0:T(8,128)(2,1)S(1)} %get-tuple-element.39), channel_id=1, source_target_pairs={{0,8},{1,9},{2,10},{3,11},{4,12},{5,13},{6,14},{7,15},{8,0},{9,1},... | collective-permute-start | bytes 393224 | tf_op jit(solution)/shard_map/ppermute | solution.py:20
  46.5 12.0 %collective-permute-start.9 = (bf16[1024,256]{1,0:T(8,128)(2,1)S(1)}, bf16[1024,256]{1,0:T(8,128)(2,1)S(1)}, u32[]{:S(2)}, u32[]{:S(2)}) collective-permute-start(bf16[1024,256]{1,0:T(8,128)(2,1)S(1)} %collective-permute-done.3.refs_1_), channel_id=1, source_target_pairs={{0,4},{1,5},{2,6},{3,7},{4,0},{5,1},{6,2},{7,3},{8,12},{9,13},{10,... | collective-permute-start | bytes 1572872 | tf_op jit(solution)/shard_map/ppermute | solution.py:20
  46.5 12.2 %collective-permute-start.19 = (bf16[1024,256]{1,0:T(8,128)(2,1)S(1)}, bf16[1024,256]{1,0:T(8,128)(2,1)S(1)}, u32[]{:S(2)}, u32[]{:S(2)}) collective-permute-start(bf16[1024,256]{1,0:T(8,128)(2,1)S(1)} %collective-permute-done.4.refs_0_), channel_id=1, source_target_pairs={{0,16},{16,0},{1,17},{17,1},{2,18},{18,2},{3,19},{19,3},{4,20},{20... | collective-permute-start | bytes 1572872 | tf_op jit(solution)/shard_map/ppermute | solution.py:24
  50.3 6.9 %collective-permute-start.8 = (bf16[256,512]{1,0:T(8,128)(2,1)S(1)}, bf16[256,512]{1,0:T(8,128)(2,1)S(1)}, u32[]{:S(2)}, u32[]{:S(2)}) collective-permute-start(bf16[256,512]{1,0:T(8,128)(2,1)S(1)} %attend0.1.refs_7_.refs_0_), channel_id=1, source_target_pairs={{0,2},{1,3},{2,0},{3,1},{4,6},{5,7},{6,4},{7,5},{8,10},{9,11},{10,... | collective-permute-start | bytes 786440 | tf_op jit(solution)/shard_map/ppermute | solution.py:20
  57.2 6.4 %collective-permute-start.12 = (bf16[256,512]{1,0:T(8,128)(2,1)S(1)}, bf16[256,512]{1,0:T(8,128)(2,1)S(1)}, u32[]{:S(2)}, u32[]{:S(2)}) collective-permute-start(bf16[256,512]{1,0:T(8,128)(2,1)S(1)} %attend1.1.refs_1_), channel_id=1, source_target_pairs={{0,2},{1,3},{2,0},{3,1},{4,6},{5,7},{6,4},{7,5},{8,10},{9,11},{10,... | collective-permute-start | bytes 786440 | tf_op jit(solution)/shard_map/ppermute | solution.py:20
  58.7 12.6 %collective-permute-start.20 = (bf16[1024,256]{1,0:T(8,128)(2,1)S(1)}, bf16[1024,256]{1,0:T(8,128)(2,1)S(1)}, u32[]{:S(2)}, u32[]{:S(2)}) collective-permute-start(bf16[1024,256]{1,0:T(8,128)(2,1)S(1)} %collective-permute-done.9.refs_2_), channel_id=1, source_target_pairs={{0,16},{16,0},{1,17},{17,1},{2,18},{18,2},{3,19},{19,3},{4,20},{20... | collective-permute-start | bytes 1572872 | tf_op jit(solution)/shard_map/ppermute | solution.py:24
  63.5 1.5 %collective-permute-start.10 = (bf16[256,512]{1,0:T(8,128)(2,1)S(1)}, bf16[256,512]{1,0:T(8,128)(2,1)S(1)}, u32[]{:S(2)}, u32[]{:S(2)}) collective-permute-start(bf16[256,512]{1,0:T(8,128)(2,1)S(1)} %attend0.1.refs_7_.refs_0_), channel_id=1, source_target_pairs={{0,1},{1,0},{2,3},{3,2},{4,5},{5,4},{6,7},{7,6},{8,9},{9,8},{10,11... | collective-permute-start | bytes 786440 | tf_op jit(solution)/shard_map/ppermute | solution.py:20
  63.6 1.9 %collective-permute-start.11 = (bf16[256,512]{1,0:T(8,128)(2,1)S(1)}, bf16[256,512]{1,0:T(8,128)(2,1)S(1)}, u32[]{:S(2)}, u32[]{:S(2)}) collective-permute-start(bf16[256,512]{1,0:T(8,128)(2,1)S(1)} %attend1.1.refs_1_), channel_id=1, source_target_pairs={{0,1},{1,0},{2,3},{3,2},{4,5},{5,4},{6,7},{7,6},{8,9},{9,8},{10,11... | collective-permute-start | bytes 786440 | tf_op jit(solution)/shard_map/ppermute | solution.py:20
  64.1 1.8 %collective-permute-start.13 = (bf16[256,512]{1,0:T(8,128)(2,1)S(1)}, bf16[256,512]{1,0:T(8,128)(2,1)S(1)}, u32[]{:S(2)}, u32[]{:S(2)}) collective-permute-start(bf16[256,512]{1,0:T(8,128)(2,1)S(1)} %collective-permute-done.8.refs_4_), channel_id=1, source_target_pairs={{0,1},{1,0},{2,3},{3,2},{4,5},{5,4},{6,7},{7,6},{8,9},{9,8},{10,11... | collective-permute-start | bytes 786440 | tf_op jit(solution)/shard_map/ppermute | solution.py:20
  64.1 2.1 %collective-permute-start.14 = (bf16[256,512]{1,0:T(8,128)(2,1)S(1)}, bf16[256,512]{1,0:T(8,128)(2,1)S(1)}, u32[]{:S(2)}, u32[]{:S(2)}) collective-permute-start(bf16[256,512]{1,0:T(8,128)(2,1)S(1)} %collective-permute-done.12.refs_5_), channel_id=1, source_target_pairs={{0,1},{1,0},{2,3},{3,2},{4,5},{5,4},{6,7},{7,6},{8,9},{9,8},{10,11... | collective-permute-start | bytes 786440 | tf_op jit(solution)/shard_map/ppermute | solution.py:20
  69.4 5.5 %collective-permute-start.16 = (bf16[128,512]{1,0:T(8,128)(2,1)S(1)}, bf16[128,512]{1,0:T(8,128)(2,1)S(1)}, u32[]{:S(2)}, u32[]{:S(2)}) collective-permute-start(bf16[128,512]{1,0:T(8,128)(2,1)S(1)} %get-tuple-element.48), channel_id=1, source_target_pairs={{0,1},{1,0},{2,3},{3,2},{4,5},{5,4},{6,7},{7,6},{8,9},{9,8},{10,11... | collective-permute-start | bytes 393224 | tf_op jit(solution)/shard_map/ppermute | solution.py:20
  69.6 6.3 %collective-permute-start.17 = (bf16[128,512]{1,0:T(8,128)(2,1)S(1)}, bf16[128,512]{1,0:T(8,128)(2,1)S(1)}, u32[]{:S(2)}, u32[]{:S(2)}) collective-permute-start(bf16[128,512]{1,0:T(8,128)(2,1)S(1)} %get-tuple-element.49), channel_id=1, source_target_pairs={{0,2},{1,3},{2,0},{3,1},{4,6},{5,7},{6,4},{7,5},{8,10},{9,11},{10,... | collective-permute-start | bytes 393224 | tf_op jit(solution)/shard_map/ppermute | solution.py:20
  71.0 6.7 %collective-permute-start.18 = (bf16[128,512]{1,0:T(8,128)(2,1)S(1)}, bf16[128,512]{1,0:T(8,128)(2,1)S(1)}, u32[]{:S(2)}, u32[]{:S(2)}) collective-permute-start(bf16[128,512]{1,0:T(8,128)(2,1)S(1)} %get-tuple-element.50), channel_id=1, source_target_pairs={{0,3},{1,2},{2,1},{3,0},{4,7},{5,6},{6,5},{7,4},{8,11},{9,10},{10,... | collective-permute-start | bytes 393224 | tf_op jit(solution)/shard_map/ppermute | solution.py:20
  73.1 4.5 %collective-permute-start.21 = (bf16[128,512]{1,0:T(8,128)(2,1)S(1)}, bf16[128,512]{1,0:T(8,128)(2,1)S(1)}, u32[]{:S(2)}, u32[]{:S(2)}) collective-permute-start(bf16[128,512]{1,0:T(8,128)(2,1)S(1)} %get-tuple-element.54), channel_id=1, source_target_pairs={{0,1},{1,0},{2,3},{3,2},{4,5},{5,4},{6,7},{7,6},{8,9},{9,8},{10,11... | collective-permute-start | bytes 393224 | tf_op jit(solution)/shard_map/ppermute | solution.py:20
  73.6 7.9 %collective-permute-start.22 = (bf16[128,512]{1,0:T(8,128)(2,1)S(1)}, bf16[128,512]{1,0:T(8,128)(2,1)S(1)}, u32[]{:S(2)}, u32[]{:S(2)}) collective-permute-start(bf16[128,512]{1,0:T(8,128)(2,1)S(1)} %get-tuple-element.55), channel_id=1, source_target_pairs={{0,2},{1,3},{2,0},{3,1},{4,6},{5,7},{6,4},{7,5},{8,10},{9,11},{10,... | collective-permute-start | bytes 393224 | tf_op jit(solution)/shard_map/ppermute | solution.py:20
  75.0 8.3 %collective-permute-start.23 = (bf16[128,512]{1,0:T(8,128)(2,1)S(1)}, bf16[128,512]{1,0:T(8,128)(2,1)S(1)}, u32[]{:S(2)}, u32[]{:S(2)}) collective-permute-start(bf16[128,512]{1,0:T(8,128)(2,1)S(1)} %get-tuple-element.56), channel_id=1, source_target_pairs={{0,3},{1,2},{2,1},{3,0},{4,7},{5,6},{6,5},{7,4},{8,11},{9,10},{10,... | collective-permute-start | bytes 393224 | tf_op jit(solution)/shard_map/ppermute | solution.py:20

commit v4 on v3

--- a/solution.py
+++ b/solution.py
@@ -71,26 +71,23 @@
         copy.wait()
 
 
-def pack_kernel(places_of, place_ref, q_ref, k_ref, v_ref, other_ref, *refs):
-    outs, sems = refs[:-1], refs[-1]
-    copies = []
-    if len(outs) > len(places_of):
-        half = outs[0].shape[0]
-        for n in range(2):
-            rows = pl.ds(pl.multiple_of(place_ref[1] * half + n * (half // 2), half // 2), half // 2)
-            to = outs[0].at[n * (half // 2) : (n + 1) * (half // 2), :]
-            copies.append(pltpu.make_async_copy(other_ref.at[rows, :], to, sems.at[n]))
-        outs = outs[1:]
-    for j, out in zip(places_of, outs):
-        columns = columns_of(place_ref[0], j, out.shape[1])
-        for n, source in enumerate((q_ref, k_ref, v_ref)):
-            to = out.at[n * BLOCK : (n + 1) * BLOCK, :]
-            copies.append(pltpu.make_async_copy(source.at[:, columns], to, sems.at[len(copies)]))
-    run_copies(copies)
-
-
-def coarse_kernel(place_ref, a0, a1, a2, a3, third_ref, fourth_ref):
-    del place_ref
+def copies_for(place, j, sources, out, sems):
+    columns = columns_of(place, j, out.shape[1])
+    return [
+        pltpu.make_async_copy(source.at[:, columns], out.at[n * BLOCK : (n + 1) * BLOCK, :], sems.at[3 * j + n])
+        for n, source in enumerate(sources)
+    ]
+
+
+def pack_kernel(place_ref, q_ref, k_ref, v_ref, third_ref, fourth_ref, a2, a3, rows_ref, sems):
+    loads = [
+        pltpu.make_async_copy(source, rows_ref.at[n * BLOCK : (n + 1) * BLOCK, :], sems.at[n])
+        for n, source in enumerate((k_ref, v_ref))
+    ]
+    copies = copies_for(place_ref[0], 2, (q_ref, k_ref, v_ref), a2, sems)
+    copies += copies_for(place_ref[0], 3, (q_ref, k_ref, v_ref), a3, sems)
+    for copy in loads + copies:
+        copy.start()
     row = lax.broadcasted_iota(jnp.int32, (96, 256), 0)
     column = lax.broadcasted_iota(jnp.int32, (96, 256), 1)
     pick = jnp.where(
@@ -98,15 +95,37 @@
         jnp.where(column // 4 == row, 0.25, 0.0),
         jnp.where(column // 8 == row - 64, 0.125, 0.0),
     ).astype(jnp.bfloat16)
-    for j, source in enumerate((a0, a1, a2, a3)):
-        means = jnp.dot(pick, source[BLOCK : 3 * BLOCK, :], preferred_element_type=jnp.float32).astype(jnp.bfloat16)
-        for n in range(2):
-            third_ref[n * 128 + 32 * j : n * 128 + 32 * j + 32, :] = means[32 * n : 32 * n + 32, :]
-            fourth_ref[n * 64 + 16 * j : n * 64 + 16 * j + 16, :] = means[64 + 16 * n : 80 + 16 * n, :]
+    for load in loads:
+        load.wait()
+    means = jnp.dot(pick, rows_ref[...], preferred_element_type=jnp.float32).astype(jnp.bfloat16)
+    third_ref[...] = means[0:64, :]
+    fourth_ref[...] = means[64:96, :]
+    for copy in copies:
+        copy.wait()
+
+
+def pack_rest_kernel(place_ref, q_ref, k_ref, v_ref, weight_ref, before_ref, a0, a1, ours_ref, theirs_ref, sems):
+    del before_ref
+    copies = copies_for(place_ref[0], 1, (q_ref, k_ref, v_ref), a1, sems)
+    copies += copies_for(place_ref[0], 0, (q_ref, k_ref, v_ref), a0, sems)
+    half = ours_ref.shape[0]
+    for n, out in enumerate((ours_ref, theirs_ref)):
+        rows = pl.ds(pl.multiple_of(jnp.bitwise_xor(place_ref[1], n) * half, half), half)
+        copies.append(pltpu.make_async_copy(weight_ref.at[rows, :], out, sems.at[6 + n]))
+    run_copies(copies)
+
+
+def repack_kernel(place_ref, l_ref, h_ref, lh_ref, b0, b1, b2, b3):
+    for j, out in enumerate((b0, b1, b2, b3)):
+        columns = columns_of(place_ref[0], j, out.shape[1])
+        out[0:64, :] = l_ref[:, columns]
+        out[64:96, :] = h_ref[:, columns]
+        out[96:128, :] = lh_ref[:, columns]
 
 
 def attention_kernel(half, place_ref, doc_ref, *refs):
-    a0, a1, a2, a3, l_ref, h_ref, lh_ref = refs[:7]
+    a0, a1, a2, a3 = refs[:4]
+    far = refs[4:8]
     out_ref, key_ref, value_ref = refs[-3:]
     own = (a0, a1, a2, a3)
     heads = out_ref.shape[1] // HD
@@ -115,9 +134,10 @@
         for part in range(2):
             rows_ref[128 * part : 128 * part + 128, :] = own[2 * half + part][at : at + 128, :]
             rows_ref[256 + 64 * part : 320 + 64 * part, :] = halve(own[2 - 2 * half + part][at : at + 128, :])
-        rows_ref[384:512, :] = l_ref[128 * n : 128 * n + 128, :]
-        rows_ref[512:576, :] = h_ref[64 * n : 64 * n + 64, :]
-        rows_ref[576:640, :] = lh_ref[64 * n : 64 * n + 64, :]
+        for j in range(4):
+            rows_ref[384 + 32 * j : 416 + 32 * j, :] = far[j][32 * n : 32 * n + 32, :]
+            rows_ref[512 + 16 * j : 528 + 16 * j, :] = far[j][64 + 16 * n : 80 + 16 * n, :]
+            rows_ref[576 + 16 * j : 592 + 16 * j, :] = far[j][96 + 16 * n : 112 + 16 * n, :]
     row = lax.broadcasted_iota(jnp.int32, (1, 640), 1)
     document = jnp.zeros((1, 640), jnp.int32)
     for first, mask in key_places(half):
@@ -210,56 +230,60 @@
     queries, keys, values, out_weight = (
         pltpu.with_memory_space_constraint(array, pltpu.HBM) for array in (queries, keys, values, out_weight)
     )
-    ours, *across = call(
-        functools.partial(pack_kernel, (2, 3)),
-        [(depth // 2, wide)] + [(3 * length, share)] * 2,
-        anywhere(4),
+    third, fourth, *across = call(
+        pack_kernel,
+        [(length // 2, width), (length // 4, width)] + [(3 * length, share)] * 2,
+        anywhere(3),
+        scratch_shapes=[pltpu.VMEM((2 * length, width), jnp.bfloat16), pltpu.SemaphoreType.DMA((12,))],
+        name="pack",
+    )(places, queries, keys, values)
+    *near, ours, theirs = call(
+        pack_rest_kernel,
+        [(3 * length, share)] * 2 + [(depth // 2, wide)] * 2,
+        anywhere(4) + loose(1),
         scratch_shapes=[pltpu.SemaphoreType.DMA((8,))],
-        name="pack0",
-    )(places, queries, keys, values, out_weight)
-    near = call(
-        functools.partial(pack_kernel, (1, 0)),
-        [(3 * length, share)] * 2,
-        anywhere(3) + loose(1),
-        scratch_shapes=[pltpu.SemaphoreType.DMA((6,))],
         work=2 * 10**9,
-        name="pack1",
-    )(places, queries, keys, values, across[0])
-    own = [near[1], swap(near[0], 1), swap(across[0], 2), swap(across[1], 3)]
-    half_h = swap(ours, HIGH)
-    ours_l = swap(ours, LOW)
-    third, fourth = call(
-        coarse_kernel, [(2 * length, share), (length, share)], vmem(4), name="coarse"
-    )(places, *own)
-    third, fourth = after((third, fourth), (half_h, ours_l))
-    far = [swap(third, LOW), swap(fourth, HIGH), swap(fourth, LOW | HIGH)]
-    other_h = swap_groups(after(half_h, third))
-    half_d = swap(after(half_h, far[0]), LOW)
-    other_l = swap_groups(after(ours_l, other_h))
-    other_d = swap_groups(after(half_d, other_l))
+        name="rest",
+    )(places, queries, keys, values, out_weight, fourth)
+    from_l, from_h, from_lh = swap(third, LOW), swap(fourth, HIGH), swap(fourth, LOW | HIGH)
+    own = [near[0], swap(after(near[1], from_lh), 1), swap(across[0], 2), swap(across[1], 3)]
+    half_h = swap(after(ours, from_h), HIGH)
+    ours_l = swap(after(ours, (from_l, from_lh)), LOW)
+    extra = call(repack_kernel, [(length, share)] * 4, vmem(3), name="repack")(places, from_l, from_h, from_lh)
+    far = [
+        extra[0],
+        swap(after(extra[1], own[3]), 1),
+        swap(after(extra[2], own[2]), 2),
+        swap(after(extra[3], own[3]), 3),
+    ]
 
     pieces = [[None] * 2 for _ in range(4)]
-    before = near[1]
+    before = near[0]
     for n in range(2):
         (attended,) = call(
             functools.partial(attention_kernel, n),
             [(2 * length, share)],
-            [pl.BlockSpec(memory_space=pltpu.SMEM)] + vmem(7) + loose(1),
+            [pl.BlockSpec(memory_space=pltpu.SMEM)] + vmem(8) + loose(1),
             scratch_shapes=[pltpu.VMEM((640, share), jnp.bfloat16)] * 2,
-            work=2 * 10**9,
+            work=10**6,
             name="attend%d" % n,
         )(places, doc_start, *own, *far, before)
         before = attended
         pieces[0][n] = attended
         pieces[2][n] = swap(attended if n == 0 else after(attended, pieces[2][0]), 2)
+    half_h = after(half_h, pieces[0][0])
+    other_h = swap_groups(half_h)
+    half_d = swap(after(half_h, ours_l), LOW)
+    other_d = swap_groups(after(half_d, other_h))
+    theirs_l = swap(after(theirs, half_d), LOW)
     for n in range(2):
-        pieces[1][n] = swap(after(pieces[0][n], (pieces[2][0], half_d)), 1)
-        pieces[3][n] = swap(after(pieces[2][n], half_d), 1)
+        pieces[1][n] = swap(after(pieces[0][n], pieces[2][0]), 1)
+        pieces[3][n] = swap(pieces[2][n], 1)
     mixed = [piece for pair in pieces for piece in pair]
 
     (rows,) = call(gather_kernel, [(4 * length, width)], vmem(8), name="gather")(places, *mixed)
     received = []
-    for n, blocks in enumerate(((out_weight, half_h, other_h), (ours_l, other_l, half_d, other_d))):
+    for n, blocks in enumerate(((out_weight, half_h, other_h), (ours_l, theirs_l, half_d, other_d))):
         parts = call(project_kernel, [(length, 2 * wide)] * 4, vmem(1 + len(blocks)), name="project%d" % n)(
             places, rows, *blocks
         )

time: 85.5 us -> 83.8 us (0.980)
  waiting for transfers between devices: 45.2 us -> 29.9 us
  starting transfers between devices: 21.9 us -> 35.5 us
    ppermute x21 -> x25, waiting for transfers between devices: 45 us -> 26.4 us  [swap(): return lax.ppermute(value, 'ctx', pairs)]
    ppermute x21 -> x25, starting transfers between devices: 18.9 us -> 32.5 us  [swap(): return lax.ppermute(value, 'ctx', pairs)]
    ppermute x3 -> x2, waiting for transfers between devices: 0.24 us -> 3.51 us  [swap_groups(): return lax.ppermute(value, 'groups', [(0, 1), (1, 0)])]
    ppermute x3 -> x2, starting transfers between devices: 3.06 us -> 3.07 us  [swap_groups(): return lax.ppermute(value, 'groups', [(0, 1), (1, 0)])]
  transfers between devices with their start and end apart: 24 -> 27, of which waited for: 15 -> 14; matrix products, arithmetic and copies ran while one was open for 0% -> 0% of each run, Pallas kernels for 17% -> 17%
where the time goes in v4:
time: 83.8 us; the launch traced here: 83.6 us
  starting transfers between devices  35.5 us (42%)
  waiting for transfers between devices  29.9 us (36%)
  Pallas kernels  18 us (21%)
    ppermute x25, starting transfers between devices, swap(): return lax.ppermute(value, 'ctx', pairs)  32.5 us
    ppermute x25, waiting for transfers between devices, swap(): return lax.ppermute(value, 'ctx', pairs)  26.4 us
    pallas_call x2, Pallas kernels, per_device_fast(): call(functools.partial(attention_kernel, n), [(2 * length, share)], [pl.B...  6.45 us
    pallas_call x2, Pallas kernels, per_device_fast(): call(project_kernel, [(length, 2 * wide)] * 4, vmem(1 + len(blocks)), nam...  4.29 us
    ppermute x2, waiting for transfers between devices, swap_groups(): return lax.ppermute(value, 'groups', [(0, 1), (1, 0)])  3.51 us
    ppermute x2, starting transfers between devices, swap_groups(): return lax.ppermute(value, 'groups', [(0, 1), (1, 0)])  3.07 us
    pallas_call x1, Pallas kernels, per_device_fast(): call(pack_kernel, [(length // 2, width), (length // 4, width)] + [(3 * le...  2.17 us
    pallas_call x1, Pallas kernels, per_device_fast(): call(pack_rest_kernel, [(3 * length, share)] * 2 + [(depth // 2, wide)] *...  2.16 us
  transfers between devices with their start and end apart: 27, of which 14 were waited for; matrix products, arithmetic and copies ran while one was open for 0% of the time, Pallas kernels for 17%

profile of v4, /device:TPU:0, one launch (start us, length us, event | category | flops | bytes accessed | tf_op | source)
XLA Modules:
  0.0 83.6 jit_solution(1589467101985648107)
XLA Ops:
  0.0 0.1 pad_add_fusion.place_ref
  0.1 2.2 %pack.1 = (bf16[64,2048]{1,0:T(8,128)(2,1)S(1)}, bf16[32,2048]{1,0:T(8,128)(2,1)S(1)}, bf16[384,512]{1,0:T(8,128)(2,1)S(1)}, bf16[384,512]{1,0:T(8,128)(2,1)S(1)}) custom-call(s32[3]{0:T(128)S(1)} %pad_add_fusion.place_ref, bf16[128,2048]{1,0:T(8,128)(2,1)} %q_ref.3, bf16[128,2048]{1,0:T(8,128)(2,1)} %k_ref.3, bf16[128,2048]{1,0:T(8,128)(2,1)} %v_ref.3), custom_call_target="tpu_custom_call" | custom-call | tf_op jit(solution)/shard_map/pack/pallas_call | solution.py:233
  2.3 3.1 %collective-permute-start.4 = (bf16[64,2048]{1,0:T(8,128)(2,1)S(1)}, bf16[64,2048]{1,0:T(8,128)(2,1)S(1)}, u32[]{:S(2)}, u32[]{:S(2)}) collective-permute-start(bf16[64,2048]{1,0:T(8,128)(2,1)S(1)} %get-tuple-element.43), channel_id=1, source_target_pairs={{0,4},{1,5},{2,6},{3,7},{4,0},{5,1},{6,2},{7,3},{8,12},{9,13},{10,... | collective-permute-start | bytes 786440 | tf_op jit(solution)/shard_map/ppermute | solution.py:20
  5.3 2.6 %collective-permute-start.5 = (bf16[32,2048]{1,0:T(8,128)(2,1)S(1)}, bf16[32,2048]{1,0:T(8,128)(2,1)S(1)}, u32[]{:S(2)}, u32[]{:S(2)}) collective-permute-start(bf16[32,2048]{1,0:T(8,128)(2,1)S(1)} %get-tuple-element.37.before_ref), channel_id=1, source_target_pairs={{0,8},{1,9},{2,10},{3,11},{4,12},{5,13},{6,14},{7,15},{8,0},{9,1},... | collective-permute-start | bytes 393224 | tf_op jit(solution)/shard_map/ppermute | solution.py:20
  7.9 0.0 collective-permute-start
  7.9 1.7 %collective-permute-start.2 = (bf16[384,512]{1,0:T(8,128)(2,1)S(1)}, bf16[384,512]{1,0:T(8,128)(2,1)S(1)}, u32[]{:S(2)}, u32[]{:S(2)}) collective-permute-start(bf16[384,512]{1,0:T(8,128)(2,1)S(1)} %get-tuple-element.41), channel_id=1, source_target_pairs={{0,2},{1,3},{2,0},{3,1},{4,6},{5,7},{6,4},{7,5},{8,10},{9,11},{10,... | collective-permute-start | bytes 1179656 | tf_op jit(solution)/shard_map/ppermute | solution.py:20
  9.7 0.0 collective-permute-start.3
  9.7 2.2 %rest.1 = (bf16[384,512]{1,0:T(8,128)(2,1)S(1)}, bf16[384,512]{1,0:T(8,128)(2,1)S(1)}, bf16[1024,256]{1,0:T(8,128)(2,1)S(1)}, bf16[1024,256]{1,0:T(8,128)(2,1)S(1)}) custom-call(s32[3]{0:T(128)S(1)} %pad_add_fusion.place_ref, bf16[128,2048]{1,0:T(8,128)(2,1)} %q_ref.3, bf16[128,2048]{1,0:T(8,128)(2,1)} %k_ref.3, bf16[128,2048]{1,0:T(8,128)(2,1)} %v_ref.3, ...), custom_call_target="tpu_custom_call" | custom-call | flops 2000000000 | bytes 40000000 | tf_op jit(solution)/shard_map/rest/pallas_call | solution.py:240
  11.8 3.1 %collective-permute-done.5.h_ref = bf16[32,2048]{1,0:T(8,128)(2,1)S(1)} collective-permute-done((bf16[32,2048]{1,0:T(8,128)(2,1)S(1)}, bf16[32,2048]{1,0:T(8,128)(2,1)S(1)}, u32[]{:S(2)}, u32[]{:S(2)}) %collective-permute-start.5) | collective-permute-done | bytes 131104 | tf_op jit(solution)/shard_map/ppermute | solution.py:20
  14.9 3.4 %collective-permute-start.15 = (bf16[1024,256]{1,0:T(8,128)(2,1)S(1)}, bf16[1024,256]{1,0:T(8,128)(2,1)S(1)}, u32[]{:S(2)}, u32[]{:S(2)}) collective-permute-start(bf16[1024,256]{1,0:T(8,128)(2,1)S(1)} %get-tuple-element.60), channel_id=1, source_target_pairs={{0,8},{1,9},{2,10},{3,11},{4,12},{5,13},{6,14},{7,15},{8,0},{9,1},... | collective-permute-start | bytes 1572872 | tf_op jit(solution)/shard_map/ppermute | solution.py:20
  18.3 1.5 %collective-permute-done.lh_ref = bf16[32,2048]{1,0:T(8,128)(2,1)S(1)} collective-permute-done((bf16[32,2048]{1,0:T(8,128)(2,1)S(1)}, bf16[32,2048]{1,0:T(8,128)(2,1)S(1)}, u32[]{:S(2)}, u32[]{:S(2)}) %collective-permute-start) | collective-permute-done | bytes 131104 | tf_op jit(solution)/shard_map/ppermute | solution.py:20
  19.9 0.0 collective-permute-done.4.l_ref
  19.9 10.9 %collective-permute-start.20 = (bf16[1024,256]{1,0:T(8,128)(2,1)S(1)}, bf16[1024,256]{1,0:T(8,128)(2,1)S(1)}, u32[]{:S(2)}, u32[]{:S(2)}) collective-permute-start(bf16[1024,256]{1,0:T(8,128)(2,1)S(1)} %get-tuple-element.60), channel_id=1, source_target_pairs={{0,4},{1,5},{2,6},{3,7},{4,0},{5,1},{6,2},{7,3},{8,12},{9,13},{10,... | collective-permute-start | bytes 1572872 | tf_op jit(solution)/shard_map/ppermute | solution.py:20
  30.8 0.0 collective-permute-start.1
  30.8 0.6 repack.1
  31.4 0.0 collective-permute-done.3.refs_3_
  31.4 1.7 %collective-permute-start.8 = (bf16[128,512]{1,0:T(8,128)(2,1)S(1)}, bf16[128,512]{1,0:T(8,128)(2,1)S(1)}, u32[]{:S(2)}, u32[]{:S(2)}) collective-permute-start(bf16[128,512]{1,0:T(8,128)(2,1)S(1)} %get-tuple-element.50), channel_id=1, source_target_pairs={{0,3},{1,2},{2,1},{3,0},{4,7},{5,6},{6,5},{7,4},{8,11},{9,10},{10,... | collective-permute-start | bytes 393224 | tf_op jit(solution)/shard_map/ppermute | solution.py:20
  33.1 0.0 collective-permute-done.2.refs_2_
  33.1 0.5 collective-permute-start.7
  33.6 3.3 %collective-permute-done.8.refs_7_ = bf16[128,512]{1,0:T(8,128)(2,1)S(1)} collective-permute-done((bf16[128,512]{1,0:T(8,128)(2,1)S(1)}, bf16[128,512]{1,0:T(8,128)(2,1)S(1)}, u32[]{:S(2)}, u32[]{:S(2)}) %collective-permute-start.8) | collective-permute-done | bytes 131104 | tf_op jit(solution)/shard_map/ppermute | solution.py:20
  36.9 1.1 %collective-permute-start.6 = (bf16[128,512]{1,0:T(8,128)(2,1)S(1)}, bf16[128,512]{1,0:T(8,128)(2,1)S(1)}, u32[]{:S(2)}, u32[]{:S(2)}) collective-permute-start(bf16[128,512]{1,0:T(8,128)(2,1)S(1)} %get-tuple-element.46), channel_id=1, source_target_pairs={{0,1},{1,0},{2,3},{3,2},{4,5},{5,4},{6,7},{7,6},{8,9},{9,8},{10,11... | collective-permute-start | bytes 393224 | tf_op jit(solution)/shard_map/ppermute | solution.py:20
  38.0 2.1 %collective-permute-done.7.refs_6_ = bf16[128,512]{1,0:T(8,128)(2,1)S(1)} collective-permute-done((bf16[128,512]{1,0:T(8,128)(2,1)S(1)}, bf16[128,512]{1,0:T(8,128)(2,1)S(1)}, u32[]{:S(2)}, u32[]{:S(2)}) %collective-permute-start.7) | collective-permute-done | bytes 131104 | tf_op jit(solution)/shard_map/ppermute | solution.py:20
  40.1 0.0 collective-permute-done.6.refs_5_
  40.1 0.0 collective-permute-done.1.refs_1_
  40.1 3.2 %attend0.1.refs_8_.refs_0_ = bf16[256,512]{1,0:T(8,128)(2,1)S(1)} custom-call(s32[3]{0:T(128)S(1)} %pad_add_fusion.place_ref, s32[16]{0:T(128)S(1)} %copy-done, bf16[384,512]{1,0:T(8,128)(2,1)S(1)} %get-tuple-element.38.refs_0_.refs_8_, bf16[384,512]{1,0:T(8,128)(2,1)S(1)} %collective-permute-done.1.refs_1_, ...), custom_call_target="tpu_custom_call" | custom-call | flops 1000000 | bytes 20000 | tf_op jit(solution)/shard_map/attend0/pallas_call | solution.py:263
  43.3 0.0 collective-permute-done.15.refs_1_
  43.3 1.6 %collective-permute-start.16 = (bf16[1024,256]{1,0:T(8,128)(2,1)S(1)}, bf16[1024,256]{1,0:T(8,128)(2,1)S(1)}, u32[]{:S(2)}, u32[]{:S(2)}) collective-permute-start(bf16[1024,256]{1,0:T(8,128)(2,1)S(1)} %collective-permute-done.15.refs_1_), channel_id=1, source_target_pairs={{0,16},{16,0},{1,17},{17,1},{2,18},{18,2},{3,19},{19,3},{4,20},{20... | collective-permute-start | bytes 1572872 | tf_op jit(solution)/shard_map/ppermute | solution.py:24
  44.9 2.6 %collective-permute-done.20.refs_0_ = bf16[1024,256]{1,0:T(8,128)(2,1)S(1)} collective-permute-done((bf16[1024,256]{1,0:T(8,128)(2,1)S(1)}, bf16[1024,256]{1,0:T(8,128)(2,1)S(1)}, u32[]{:S(2)}, u32[]{:S(2)}) %collective-permute-start.20) | collective-permute-done | bytes 524320 | tf_op jit(solution)/shard_map/ppermute | solution.py:20
  47.5 0.0 collective-permute-start.21
  47.5 1.5 %collective-permute-start.9 = (bf16[256,512]{1,0:T(8,128)(2,1)S(1)}, bf16[256,512]{1,0:T(8,128)(2,1)S(1)}, u32[]{:S(2)}, u32[]{:S(2)}) collective-permute-start(bf16[256,512]{1,0:T(8,128)(2,1)S(1)} %attend0.1.refs_8_.refs_0_), channel_id=1, source_target_pairs={{0,2},{1,3},{2,0},{3,1},{4,6},{5,7},{6,4},{7,5},{8,10},{9,11},{10,... | collective-permute-start | bytes 786440 | tf_op jit(solution)/shard_map/ppermute | solution.py:20
  49.0 3.2 %attend1.1.refs_1_ = bf16[256,512]{1,0:T(8,128)(2,1)S(1)} custom-call(s32[3]{0:T(128)S(1)} %pad_add_fusion.place_ref, s32[16]{0:T(128)S(1)} %copy-done, bf16[384,512]{1,0:T(8,128)(2,1)S(1)} %get-tuple-element.38.refs_0_.refs_8_, bf16[384,512]{1,0:T(8,128)(2,1)S(1)} %collective-permute-done.1.refs_1_, bf16[384,512]{1,0:T(8,128)(2,1)S(1)} %collective-permute-done.2.refs_2_, ...), custom_call_target="tpu_custom_call" | custom-call | flops 1000000 | bytes 20000 | tf_op jit(solution)/shard_map/attend1/pallas_call | solution.py:263
  52.2 1.6 %collective-permute-done.9.refs_4_ = bf16[256,512]{1,0:T(8,128)(2,1)S(1)} collective-permute-done((bf16[256,512]{1,0:T(8,128)(2,1)S(1)}, bf16[256,512]{1,0:T(8,128)(2,1)S(1)}, u32[]{:S(2)}, u32[]{:S(2)}) %collective-permute-start.9) | collective-permute-done | bytes 262176 | tf_op jit(solution)/shard_map/ppermute | solution.py:20
  53.8 0.0 collective-permute-start.10
  53.8 1.5 %collective-permute-start.12 = (bf16[256,512]{1,0:T(8,128)(2,1)S(1)}, bf16[256,512]{1,0:T(8,128)(2,1)S(1)}, u32[]{:S(2)}, u32[]{:S(2)}) collective-permute-start(bf16[256,512]{1,0:T(8,128)(2,1)S(1)} %attend1.1.refs_1_), channel_id=1, source_target_pairs={{0,2},{1,3},{2,0},{3,1},{4,6},{5,7},{6,4},{7,5},{8,10},{9,11},{10,... | collective-permute-start | bytes 786440 | tf_op jit(solution)/shard_map/ppermute | solution.py:20
  55.4 1.4 %collective-permute-done.16.refs_2_ = bf16[1024,256]{1,0:T(8,128)(2,1)S(1)} collective-permute-done((bf16[1024,256]{1,0:T(8,128)(2,1)S(1)}, bf16[1024,256]{1,0:T(8,128)(2,1)S(1)}, u32[]{:S(2)}, u32[]{:S(2)}) %collective-permute-start.16) | collective-permute-done | bytes 524320 | tf_op jit(solution)/shard_map/ppermute | solution.py:24
  56.7 1.6 %collective-permute-done.21.refs_2_ = bf16[1024,256]{1,0:T(8,128)(2,1)S(1)} collective-permute-done((bf16[1024,256]{1,0:T(8,128)(2,1)S(1)}, bf16[1024,256]{1,0:T(8,128)(2,1)S(1)}, u32[]{:S(2)}, u32[]{:S(2)}) %collective-permute-start.21) | collective-permute-done | bytes 524320 | tf_op jit(solution)/shard_map/ppermute | solution.py:20
  58.3 0.0 collective-permute-start.22
  58.3 1.5 %collective-permute-start.23 = (bf16[1024,256]{1,0:T(8,128)(2,1)S(1)}, bf16[1024,256]{1,0:T(8,128)(2,1)S(1)}, u32[]{:S(2)}, u32[]{:S(2)}) collective-permute-start(bf16[1024,256]{1,0:T(8,128)(2,1)S(1)} %collective-permute-done.21.refs_2_), channel_id=1, source_target_pairs={{0,16},{16,0},{1,17},{17,1},{2,18},{18,2},{3,19},{19,3},{4,20},{20... | collective-permute-start | bytes 1572872 | tf_op jit(solution)/shard_map/ppermute | solution.py:24
  59.8 0.0 collective-permute-start.11
  59.8 0.0 collective-permute-done.10.refs_2_
  59.8 0.5 collective-permute-start.13
  60.3 2.2 %collective-permute-done.12.refs_5_ = bf16[256,512]{1,0:T(8,128)(2,1)S(1)} collective-permute-done((bf16[256,512]{1,0:T(8,128)(2,1)S(1)}, bf16[256,512]{1,0:T(8,128)(2,1)S(1)}, u32[]{:S(2)}, u32[]{:S(2)}) %collective-permute-start.12) | collective-permute-done | bytes 262176 | tf_op jit(solution)/shard_map/ppermute | solution.py:20
  62.6 0.0 collective-permute-start.14
  62.6 0.0 collective-permute-done.11.refs_3_
  62.6 0.0 collective-permute-done.13.refs_6_
  62.6 1.5 %collective-permute-done.14.refs_7_ = bf16[256,512]{1,0:T(8,128)(2,1)S(1)} collective-permute-done((bf16[256,512]{1,0:T(8,128)(2,1)S(1)}, bf16[256,512]{1,0:T(8,128)(2,1)S(1)}, u32[]{:S(2)}, u32[]{:S(2)}) %collective-permute-start.14) | collective-permute-done | bytes 262176 | tf_op jit(solution)/shard_map/ppermute | solution.py:20
  64.1 0.7 gather.1.rows_ref
  64.8 2.5 %project0.1 = (bf16[128,512]{1,0:T(8,128)(2,1)S(1)}, bf16[128,512]{1,0:T(8,128)(2,1)S(1)}, bf16[128,512]{1,0:T(8,128)(2,1)S(1)}, bf16[128,512]{1,0:T(8,128)(2,1)S(1)}) custom-call(s32[3]{0:T(128)S(1)} %pad_add_fusion.place_ref, bf16[512,2048]{1,0:T(8,128)(2,1)S(1)} %gather.1.rows_ref, bf16[2048,256]{1,0:T(8,128)(2,1)} %refs_0_.1, ...), custom_call_target="tpu_custom_call" | custom-call | tf_op jit(solution)/shard_map/project0/pallas_call | solution.py:287
  67.3 0.2 collective-permute-start.17
  67.5 1.5 %collective-permute-start.18 = (bf16[128,512]{1,0:T(8,128)(2,1)S(1)}, bf16[128,512]{1,0:T(8,128)(2,1)S(1)}, u32[]{:S(2)}, u32[]{:S(2)}) collective-permute-start(bf16[128,512]{1,0:T(8,128)(2,1)S(1)} %get-tuple-element.58), channel_id=1, source_target_pairs={{0,2},{1,3},{2,0},{3,1},{4,6},{5,7},{6,4},{7,5},{8,10},{9,11},{10,... | collective-permute-start | bytes 393224 | tf_op jit(solution)/shard_map/ppermute | solution.py:20
  69.0 0.2 collective-permute-start.19
  69.2 0.5 collective-permute-done.22.refs_1_
  69.7 2.2 %collective-permute-done.23.refs_3_ = bf16[1024,256]{1,0:T(8,128)(2,1)S(1)} collective-permute-done((bf16[1024,256]{1,0:T(8,128)(2,1)S(1)}, bf16[1024,256]{1,0:T(8,128)(2,1)S(1)}, u32[]{:S(2)}, u32[]{:S(2)}) %collective-permute-start.23) | collective-permute-done | bytes 524320 | tf_op jit(solution)/shard_map/ppermute | solution.py:24
  71.9 1.8 %project1.1 = (bf16[128,512]{1,0:T(8,128)(2,1)S(1)}, bf16[128,512]{1,0:T(8,128)(2,1)S(1)}, bf16[128,512]{1,0:T(8,128)(2,1)S(1)}, bf16[128,512]{1,0:T(8,128)(2,1)S(1)}) custom-call(s32[3]{0:T(128)S(1)} %pad_add_fusion.place_ref, bf16[512,2048]{1,0:T(8,128)(2,1)S(1)} %gather.1.rows_ref, bf16[1024,256]{1,0:T(8,128)(2,1)S(1)} %collective-permute-done.20.refs_0_, ...), custom_call_target="tpu_custom_call" | custom-call | tf_op jit(solution)/shard_map/project1/pallas_call | solution.py:287
  73.7 0.1 collective-permute-start.24
  73.7 0.6 collective-permute-start.25
  74.3 0.0 collective-permute-done.17.refs_1_
  74.3 1.3 %collective-permute-start.26 = (bf16[128,512]{1,0:T(8,128)(2,1)S(1)}, bf16[128,512]{1,0:T(8,128)(2,1)S(1)}, u32[]{:S(2)}, u32[]{:S(2)}) collective-permute-start(bf16[128,512]{1,0:T(8,128)(2,1)S(1)} %get-tuple-element.68), channel_id=1, source_target_pairs={{0,3},{1,2},{2,1},{3,0},{4,7},{5,6},{6,5},{7,4},{8,11},{9,10},{10,... | collective-permute-start | bytes 393224 | tf_op jit(solution)/shard_map/ppermute | solution.py:20
  75.6 0.0 collective-permute-done.18.refs_2_
  75.6 0.0 collective-permute-done.19.refs_3_
  75.6 0.0 collective-permute-done.24.refs_5_
  75.6 4.5 %collective-permute-done.25.refs_6_ = bf16[128,512]{1,0:T(8,128)(2,1)S(1)} collective-permute-done((bf16[128,512]{1,0:T(8,128)(2,1)S(1)}, bf16[128,512]{1,0:T(8,128)(2,1)S(1)}, u32[]{:S(2)}, u32[]{:S(2)}) %collective-permute-start.25) | collective-permute-done | bytes 131104 | tf_op jit(solution)/shard_map/ppermute | solution.py:20
  80.1 1.9 %collective-permute-done.26.refs_7_ = bf16[128,512]{1,0:T(8,128)(2,1)S(1)} collective-permute-done((bf16[128,512]{1,0:T(8,128)(2,1)S(1)}, bf16[128,512]{1,0:T(8,128)(2,1)S(1)}, u32[]{:S(2)}, u32[]{:S(2)}) %collective-permute-start.26) | collective-permute-done | bytes 131104 | tf_op jit(solution)/shard_map/ppermute | solution.py:20
  82.0 1.6 %place.1 = bf16[128,4096]{1,0:T(8,128)(2,1)} custom-call(s32[3]{0:T(128)S(1)} %pad_add_fusion.place_ref, bf16[128,512]{1,0:T(8,128)(2,1)S(1)} %get-tuple-element.56.refs_0_, bf16[128,512]{1,0:T(8,128)(2,1)S(1)} %collective-permute-done.17.refs_1_, bf16[128,512]{1,0:T(8,128)(2,1)S(1)} %collective-permute-done.18.refs_2_, ...), custom_call_target="tpu_custom_call" | custom-call | tf_op jit(solution)/shard_map/place/pallas_call | solution.py:291
  (2 shorter events, 0.0 us)
Async XLA Ops:
  2.3 17.6 %collective-permute-start.4 = (bf16[64,2048]{1,0:T(8,128)(2,1)S(1)}, bf16[64,2048]{1,0:T(8,128)(2,1)S(1)}, u32[]{:S(2)}, u32[]{:S(2)}) collective-permute-start(bf16[64,2048]{1,0:T(8,128)(2,1)S(1)} %get-tuple-element.43), channel_id=1, source_target_pairs={{0,4},{1,5},{2,6},{3,7},{4,0},{5,1},{6,2},{7,3},{8,12},{9,13},{10,... | collective-permute-start | bytes 786440 | tf_op jit(solution)/shard_map/ppermute | solution.py:20
  5.3 9.6 %collective-permute-start.5 = (bf16[32,2048]{1,0:T(8,128)(2,1)S(1)}, bf16[32,2048]{1,0:T(8,128)(2,1)S(1)}, u32[]{:S(2)}, u32[]{:S(2)}) collective-permute-start(bf16[32,2048]{1,0:T(8,128)(2,1)S(1)} %get-tuple-element.37.before_ref), channel_id=1, source_target_pairs={{0,8},{1,9},{2,10},{3,11},{4,12},{5,13},{6,14},{7,15},{8,0},{9,1},... | collective-permute-start | bytes 393224 | tf_op jit(solution)/shard_map/ppermute | solution.py:20
  7.9 12.0 %collective-permute-start = (bf16[32,2048]{1,0:T(8,128)(2,1)S(1)}, bf16[32,2048]{1,0:T(8,128)(2,1)S(1)}, u32[]{:S(2)}, u32[]{:S(2)}) collective-permute-start(bf16[32,2048]{1,0:T(8,128)(2,1)S(1)} %get-tuple-element.37.before_ref), channel_id=1, source_target_pairs={{0,12},{1,13},{2,14},{3,15},{4,8},{5,9},{6,10},{7,11},{8,4},{9,5},... | collective-permute-start | bytes 393224 | tf_op jit(solution)/shard_map/ppermute | solution.py:20
  7.9 25.2 %collective-permute-start.2 = (bf16[384,512]{1,0:T(8,128)(2,1)S(1)}, bf16[384,512]{1,0:T(8,128)(2,1)S(1)}, u32[]{:S(2)}, u32[]{:S(2)}) collective-permute-start(bf16[384,512]{1,0:T(8,128)(2,1)S(1)} %get-tuple-element.41), channel_id=1, source_target_pairs={{0,2},{1,3},{2,0},{3,1},{4,6},{5,7},{6,4},{7,5},{8,10},{9,11},{10,... | collective-permute-start | bytes 1179656 | tf_op jit(solution)/shard_map/ppermute | solution.py:20
  9.7 30.4 %copy-start = (s32[16]{0:T(128)S(1)}, s32[16]{0:T(128)}, u32[]{:S(2)}) copy-start(s32[16]{0:T(128)} %doc_ref.3) | copy-start | bytes 196
  9.7 21.7 %collective-permute-start.3 = (bf16[384,512]{1,0:T(8,128)(2,1)S(1)}, bf16[384,512]{1,0:T(8,128)(2,1)S(1)}, u32[]{:S(2)}, u32[]{:S(2)}) collective-permute-start(bf16[384,512]{1,0:T(8,128)(2,1)S(1)} %get-tuple-element.42), channel_id=1, source_target_pairs={{0,3},{1,2},{2,1},{3,0},{4,7},{5,6},{6,5},{7,4},{8,11},{9,10},{10,... | collective-permute-start | bytes 1179656 | tf_op jit(solution)/shard_map/ppermute | solution.py:20
  14.9 28.4 %collective-permute-start.15 = (bf16[1024,256]{1,0:T(8,128)(2,1)S(1)}, bf16[1024,256]{1,0:T(8,128)(2,1)S(1)}, u32[]{:S(2)}, u32[]{:S(2)}) collective-permute-start(bf16[1024,256]{1,0:T(8,128)(2,1)S(1)} %get-tuple-element.60), channel_id=1, source_target_pairs={{0,8},{1,9},{2,10},{3,11},{4,12},{5,13},{6,14},{7,15},{8,0},{9,1},... | collective-permute-start | bytes 1572872 | tf_op jit(solution)/shard_map/ppermute | solution.py:20
  19.9 27.6 %collective-permute-start.20 = (bf16[1024,256]{1,0:T(8,128)(2,1)S(1)}, bf16[1024,256]{1,0:T(8,128)(2,1)S(1)}, u32[]{:S(2)}, u32[]{:S(2)}) collective-permute-start(bf16[1024,256]{1,0:T(8,128)(2,1)S(1)} %get-tuple-element.60), channel_id=1, source_target_pairs={{0,4},{1,5},{2,6},{3,7},{4,0},{5,1},{6,2},{7,3},{8,12},{9,13},{10,... | collective-permute-start | bytes 1572872 | tf_op jit(solution)/shard_map/ppermute | solution.py:20
  30.8 9.3 %collective-permute-start.1 = (bf16[384,512]{1,0:T(8,128)(2,1)S(1)}, bf16[384,512]{1,0:T(8,128)(2,1)S(1)}, u32[]{:S(2)}, u32[]{:S(2)}) collective-permute-start(bf16[384,512]{1,0:T(8,128)(2,1)S(1)} %get-tuple-element.40), channel_id=1, source_target_pairs={{0,1},{1,0},{2,3},{3,2},{4,5},{5,4},{6,7},{7,6},{8,9},{9,8},{10,11... | collective-permute-start | bytes 1179656 | tf_op jit(solution)/shard_map/ppermute | solution.py:20
  31.4 5.5 %collective-permute-start.8 = (bf16[128,512]{1,0:T(8,128)(2,1)S(1)}, bf16[128,512]{1,0:T(8,128)(2,1)S(1)}, u32[]{:S(2)}, u32[]{:S(2)}) collective-permute-start(bf16[128,512]{1,0:T(8,128)(2,1)S(1)} %get-tuple-element.50), channel_id=1, source_target_pairs={{0,3},{1,2},{2,1},{3,0},{4,7},{5,6},{6,5},{7,4},{8,11},{9,10},{10,... | collective-permute-start | bytes 393224 | tf_op jit(solution)/shard_map/ppermute | solution.py:20
  33.1 7.0 %collective-permute-start.7 = (bf16[128,512]{1,0:T(8,128)(2,1)S(1)}, bf16[128,512]{1,0:T(8,128)(2,1)S(1)}, u32[]{:S(2)}, u32[]{:S(2)}) collective-permute-start(bf16[128,512]{1,0:T(8,128)(2,1)S(1)} %get-tuple-element.48), channel_id=1, source_target_pairs={{0,2},{1,3},{2,0},{3,1},{4,6},{5,7},{6,4},{7,5},{8,10},{9,11},{10,... | collective-permute-start | bytes 393224 | tf_op jit(solution)/shard_map/ppermute | solution.py:20
  36.9 3.1 %collective-permute-start.6 = (bf16[128,512]{1,0:T(8,128)(2,1)S(1)}, bf16[128,512]{1,0:T(8,128)(2,1)S(1)}, u32[]{:S(2)}, u32[]{:S(2)}) collective-permute-start(bf16[128,512]{1,0:T(8,128)(2,1)S(1)} %get-tuple-element.46), channel_id=1, source_target_pairs={{0,1},{1,0},{2,3},{3,2},{4,5},{5,4},{6,7},{7,6},{8,9},{9,8},{10,11... | collective-permute-start | bytes 393224 | tf_op jit(solution)/shard_map/ppermute | solution.py:20
  43.3 13.4 %collective-permute-start.16 = (bf16[1024,256]{1,0:T(8,128)(2,1)S(1)}, bf16[1024,256]{1,0:T(8,128)(2,1)S(1)}, u32[]{:S(2)}, u32[]{:S(2)}) collective-permute-start(bf16[1024,256]{1,0:T(8,128)(2,1)S(1)} %collective-permute-done.15.refs_1_), channel_id=1, source_target_pairs={{0,16},{16,0},{1,17},{17,1},{2,18},{18,2},{3,19},{19,3},{4,20},{20... | collective-permute-start | bytes 1572872 | tf_op jit(solution)/shard_map/ppermute | solution.py:24
  47.5 10.9 %collective-permute-start.21 = (bf16[1024,256]{1,0:T(8,128)(2,1)S(1)}, bf16[1024,256]{1,0:T(8,128)(2,1)S(1)}, u32[]{:S(2)}, u32[]{:S(2)}) collective-permute-start(bf16[1024,256]{1,0:T(8,128)(2,1)S(1)} %collective-permute-done.15.refs_1_), channel_id=1, source_target_pairs={{0,4},{1,5},{2,6},{3,7},{4,0},{5,1},{6,2},{7,3},{8,12},{9,13},{10,... | collective-permute-start | bytes 1572872 | tf_op jit(solution)/shard_map/ppermute | solution.py:20
  47.5 6.4 %collective-permute-start.9 = (bf16[256,512]{1,0:T(8,128)(2,1)S(1)}, bf16[256,512]{1,0:T(8,128)(2,1)S(1)}, u32[]{:S(2)}, u32[]{:S(2)}) collective-permute-start(bf16[256,512]{1,0:T(8,128)(2,1)S(1)} %attend0.1.refs_8_.refs_0_), channel_id=1, source_target_pairs={{0,2},{1,3},{2,0},{3,1},{4,6},{5,7},{6,4},{7,5},{8,10},{9,11},{10,... | collective-permute-start | bytes 786440 | tf_op jit(solution)/shard_map/ppermute | solution.py:20
  53.8 6.0 %collective-permute-start.10 = (bf16[256,512]{1,0:T(8,128)(2,1)S(1)}, bf16[256,512]{1,0:T(8,128)(2,1)S(1)}, u32[]{:S(2)}, u32[]{:S(2)}) collective-permute-start(bf16[256,512]{1,0:T(8,128)(2,1)S(1)} %attend0.1.refs_8_.refs_0_), channel_id=1, source_target_pairs={{0,1},{1,0},{2,3},{3,2},{4,5},{5,4},{6,7},{7,6},{8,9},{9,8},{10,11... | collective-permute-start | bytes 786440 | tf_op jit(solution)/shard_map/ppermute | solution.py:20
  53.8 8.7 %collective-permute-start.12 = (bf16[256,512]{1,0:T(8,128)(2,1)S(1)}, bf16[256,512]{1,0:T(8,128)(2,1)S(1)}, u32[]{:S(2)}, u32[]{:S(2)}) collective-permute-start(bf16[256,512]{1,0:T(8,128)(2,1)S(1)} %attend1.1.refs_1_), channel_id=1, source_target_pairs={{0,2},{1,3},{2,0},{3,1},{4,6},{5,7},{6,4},{7,5},{8,10},{9,11},{10,... | collective-permute-start | bytes 786440 | tf_op jit(solution)/shard_map/ppermute | solution.py:20
  58.3 11.4 %collective-permute-start.22 = (bf16[1024,256]{1,0:T(8,128)(2,1)S(1)}, bf16[1024,256]{1,0:T(8,128)(2,1)S(1)}, u32[]{:S(2)}, u32[]{:S(2)}) collective-permute-start(bf16[1024,256]{1,0:T(8,128)(2,1)S(1)} %get-tuple-element.63), channel_id=1, source_target_pairs={{0,4},{1,5},{2,6},{3,7},{4,0},{5,1},{6,2},{7,3},{8,12},{9,13},{10,... | collective-permute-start | bytes 1572872 | tf_op jit(solution)/shard_map/ppermute | solution.py:20
  58.3 13.5 %collective-permute-start.23 = (bf16[1024,256]{1,0:T(8,128)(2,1)S(1)}, bf16[1024,256]{1,0:T(8,128)(2,1)S(1)}, u32[]{:S(2)}, u32[]{:S(2)}) collective-permute-start(bf16[1024,256]{1,0:T(8,128)(2,1)S(1)} %collective-permute-done.21.refs_2_), channel_id=1, source_target_pairs={{0,16},{16,0},{1,17},{17,1},{2,18},{18,2},{3,19},{19,3},{4,20},{20... | collective-permute-start | bytes 1572872 | tf_op jit(solution)/shard_map/ppermute | solution.py:24
  59.8 2.7 %collective-permute-start.11 = (bf16[256,512]{1,0:T(8,128)(2,1)S(1)}, bf16[256,512]{1,0:T(8,128)(2,1)S(1)}, u32[]{:S(2)}, u32[]{:S(2)}) collective-permute-start(bf16[256,512]{1,0:T(8,128)(2,1)S(1)} %attend1.1.refs_1_), channel_id=1, source_target_pairs={{0,1},{1,0},{2,3},{3,2},{4,5},{5,4},{6,7},{7,6},{8,9},{9,8},{10,11... | collective-permute-start | bytes 786440 | tf_op jit(solution)/shard_map/ppermute | solution.py:20
  59.8 2.7 %collective-permute-start.13 = (bf16[256,512]{1,0:T(8,128)(2,1)S(1)}, bf16[256,512]{1,0:T(8,128)(2,1)S(1)}, u32[]{:S(2)}, u32[]{:S(2)}) collective-permute-start(bf16[256,512]{1,0:T(8,128)(2,1)S(1)} %collective-permute-done.9.refs_4_), channel_id=1, source_target_pairs={{0,1},{1,0},{2,3},{3,2},{4,5},{5,4},{6,7},{7,6},{8,9},{9,8},{10,11... | collective-permute-start | bytes 786440 | tf_op jit(solution)/shard_map/ppermute | solution.py:20
  62.6 1.5 %collective-permute-start.14 = (bf16[256,512]{1,0:T(8,128)(2,1)S(1)}, bf16[256,512]{1,0:T(8,128)(2,1)S(1)}, u32[]{:S(2)}, u32[]{:S(2)}) collective-permute-start(bf16[256,512]{1,0:T(8,128)(2,1)S(1)} %collective-permute-done.12.refs_5_), channel_id=1, source_target_pairs={{0,1},{1,0},{2,3},{3,2},{4,5},{5,4},{6,7},{7,6},{8,9},{9,8},{10,11... | collective-permute-start | bytes 786440 | tf_op jit(solution)/shard_map/ppermute | solution.py:20
  67.3 7.0 %collective-permute-start.17 = (bf16[128,512]{1,0:T(8,128)(2,1)S(1)}, bf16[128,512]{1,0:T(8,128)(2,1)S(1)}, u32[]{:S(2)}, u32[]{:S(2)}) collective-permute-start(bf16[128,512]{1,0:T(8,128)(2,1)S(1)} %get-tuple-element.57), channel_id=1, source_target_pairs={{0,1},{1,0},{2,3},{3,2},{4,5},{5,4},{6,7},{7,6},{8,9},{9,8},{10,11... | collective-permute-start | bytes 393224 | tf_op jit(solution)/shard_map/ppermute | solution.py:20
  67.5 8.1 %collective-permute-start.18 = (bf16[128,512]{1,0:T(8,128)(2,1)S(1)}, bf16[128,512]{1,0:T(8,128)(2,1)S(1)}, u32[]{:S(2)}, u32[]{:S(2)}) collective-permute-start(bf16[128,512]{1,0:T(8,128)(2,1)S(1)} %get-tuple-element.58), channel_id=1, source_target_pairs={{0,2},{1,3},{2,0},{3,1},{4,6},{5,7},{6,4},{7,5},{8,10},{9,11},{10,... | collective-permute-start | bytes 393224 | tf_op jit(solution)/shard_map/ppermute | solution.py:20
  69.0 6.6 %collective-permute-start.19 = (bf16[128,512]{1,0:T(8,128)(2,1)S(1)}, bf16[128,512]{1,0:T(8,128)(2,1)S(1)}, u32[]{:S(2)}, u32[]{:S(2)}) collective-permute-start(bf16[128,512]{1,0:T(8,128)(2,1)S(1)} %get-tuple-element.59), channel_id=1, source_target_pairs={{0,3},{1,2},{2,1},{3,0},{4,7},{5,6},{6,5},{7,4},{8,11},{9,10},{10,... | collective-permute-start | bytes 393224 | tf_op jit(solution)/shard_map/ppermute | solution.py:20
  73.7 2.0 %collective-permute-start.24 = (bf16[128,512]{1,0:T(8,128)(2,1)S(1)}, bf16[128,512]{1,0:T(8,128)(2,1)S(1)}, u32[]{:S(2)}, u32[]{:S(2)}) collective-permute-start(bf16[128,512]{1,0:T(8,128)(2,1)S(1)} %get-tuple-element.66), channel_id=1, source_target_pairs={{0,1},{1,0},{2,3},{3,2},{4,5},{5,4},{6,7},{7,6},{8,9},{9,8},{10,11... | collective-permute-start | bytes 393224 | tf_op jit(solution)/shard_map/ppermute | solution.py:20
  73.7 6.4 %collective-permute-start.25 = (bf16[128,512]{1,0:T(8,128)(2,1)S(1)}, bf16[128,512]{1,0:T(8,128)(2,1)S(1)}, u32[]{:S(2)}, u32[]{:S(2)}) collective-permute-start(bf16[128,512]{1,0:T(8,128)(2,1)S(1)} %get-tuple-element.67), channel_id=1, source_target_pairs={{0,2},{1,3},{2,0},{3,1},{4,6},{5,7},{6,4},{7,5},{8,10},{9,11},{10,... | collective-permute-start | bytes 393224 | tf_op jit(solution)/shard_map/ppermute | solution.py:20
  74.3 7.7 %collective-permute-start.26 = (bf16[128,512]{1,0:T(8,128)(2,1)S(1)}, bf16[128,512]{1,0:T(8,128)(2,1)S(1)}, u32[]{:S(2)}, u32[]{:S(2)}) collective-permute-start(bf16[128,512]{1,0:T(8,128)(2,1)S(1)} %get-tuple-element.68), channel_id=1, source_target_pairs={{0,3},{1,2},{2,1},{3,0},{4,7},{5,6},{6,5},{7,4},{8,11},{9,10},{10,... | collective-permute-start | bytes 393224 | tf_op jit(solution)/shard_map/ppermute | solution.py:20

commit v5 on v3

--- a/solution.py
+++ b/solution.py
@@ -251,10 +251,11 @@
         )(places, doc_start, *own, *far, before)
         before = attended
         pieces[0][n] = attended
-        pieces[2][n] = swap(attended if n == 0 else after(attended, pieces[2][0]), 2)
+        pieces[2][n] = swap(attended, 2)
     for n in range(2):
         pieces[1][n] = swap(after(pieces[0][n], (pieces[2][0], half_d)), 1)
-        pieces[3][n] = swap(after(pieces[2][n], half_d), 1)
+    pieces[3][0] = swap(after(pieces[2][0], half_d), 1)
+    pieces[3][1] = swap(after(pieces[2][1], pieces[3][0]), 1)
     mixed = [piece for pair in pieces for piece in pair]
 
     (rows,) = call(gather_kernel, [(4 * length, width)], vmem(8), name="gather")(places, *mixed)

time: 85.5 us -> 83.1 us (0.972)
  waiting for transfers between devices: 45.2 us -> 43.9 us
    ppermute x21, waiting for transfers between devices: 45 us -> 41 us  [swap(): return lax.ppermute(value, 'ctx', pairs)]
    ppermute x3, waiting for transfers between devices: 0.24 us -> 2.87 us  [swap_groups(): return lax.ppermute(value, 'groups', [(0, 1), (1, 0)])]
    ppermute x21, starting transfers between devices: 18.9 us -> 17.6 us  [swap(): return lax.ppermute(value, 'ctx', pairs)]
  transfers between devices with their start and end apart: 24 -> 24, of which waited for: 15 -> 10; matrix products, arithmetic and copies ran while one was open for 0% -> 0% of each run, Pallas kernels for 17% -> 17%
where the time goes in v5:
time: 83.1 us; the launch traced here: 82.9 us
  waiting for transfers between devices  43.9 us (53%)
  starting transfers between devices  21.2 us (26%)
  Pallas kernels  17.6 us (21%)
    ppermute x21, waiting for transfers between devices, swap(): return lax.ppermute(value, 'ctx', pairs)  41 us
    ppermute x21, starting transfers between devices, swap(): return lax.ppermute(value, 'ctx', pairs)  17.6 us
    pallas_call x2, Pallas kernels, per_device_fast(): call(functools.partial(attention_kernel, n), [(2 * length, share)], [pl.B...  6.46 us
    pallas_call x2, Pallas kernels, per_device_fast(): call(project_kernel, [(length, 2 * wide)] * 4, vmem(1 + len(blocks)), nam...  4.28 us
    ppermute x3, starting transfers between devices, swap_groups(): return lax.ppermute(value, 'groups', [(0, 1), (1, 0)])  3.59 us
    ppermute x3, waiting for transfers between devices, swap_groups(): return lax.ppermute(value, 'groups', [(0, 1), (1, 0)])  2.87 us
    pallas_call x1, Pallas kernels, per_device_fast(): call(functools.partial(pack_kernel, (2, 3)), [(depth // 2, wide)] + [(3 *...  1.88 us
    pallas_call x1, Pallas kernels, per_device_fast(): call(functools.partial(pack_kernel, (1, 0)), [(3 * length, share)] * 2, a...  1.8 us
  transfers between devices with their start and end apart: 24, of which 10 were waited for; matrix products, arithmetic and copies ran while one was open for 0% of the time, Pallas kernels for 17%

profile of v5, /device:TPU:0, one launch (start us, length us, event | category | flops | bytes accessed | tf_op | source)
XLA Modules:
  0.0 82.9 jit_solution(12891674923985935789)
XLA Ops:
  0.0 0.1 pad_add_fusion.place_ref
  0.1 1.9 %pack0.1 = (bf16[1024,256]{1,0:T(8,128)(2,1)S(1)}, bf16[384,512]{1,0:T(8,128)(2,1)S(1)}, bf16[384,512]{1,0:T(8,128)(2,1)S(1)}) custom-call(s32[3]{0:T(128)S(1)} %pad_add_fusion.place_ref, bf16[128,2048]{1,0:T(8,128)(2,1)} %q_ref.3, bf16[128,2048]{1,0:T(8,128)(2,1)} %k_ref.3, bf16[128,2048]{1,0:T(8,128)(2,1)} %v_ref.3, bf16[2048,256]{1,0:T(8,128)(2,1)} %refs_0_.1), custom_call_target="tpu_custom_call" | custom-call | tf_op jit(solution)/shard_map/pack0/pallas_call | solution.py:213
  2.0 3.1 %collective-permute-start.4 = (bf16[1024,256]{1,0:T(8,128)(2,1)S(1)}, bf16[1024,256]{1,0:T(8,128)(2,1)S(1)}, u32[]{:S(2)}, u32[]{:S(2)}) collective-permute-start(bf16[1024,256]{1,0:T(8,128)(2,1)S(1)} %get-tuple-element.36), channel_id=1, source_target_pairs={{0,4},{1,5},{2,6},{3,7},{4,0},{5,1},{6,2},{7,3},{8,12},{9,13},{10,... | collective-permute-start | bytes 1572872 | tf_op jit(solution)/shard_map/ppermute | solution.py:20
  5.1 2.6 %collective-permute-start.3 = (bf16[1024,256]{1,0:T(8,128)(2,1)S(1)}, bf16[1024,256]{1,0:T(8,128)(2,1)S(1)}, u32[]{:S(2)}, u32[]{:S(2)}) collective-permute-start(bf16[1024,256]{1,0:T(8,128)(2,1)S(1)} %get-tuple-element.36), channel_id=1, source_target_pairs={{0,8},{1,9},{2,10},{3,11},{4,12},{5,13},{6,14},{7,15},{8,0},{9,1},... | collective-permute-start | bytes 1572872 | tf_op jit(solution)/shard_map/ppermute | solution.py:20
  7.6 0.4 collective-permute-start.2
  8.0 0.0 copy-start
  8.0 1.2 %collective-permute-start.1 = (bf16[384,512]{1,0:T(8,128)(2,1)S(1)}, bf16[384,512]{1,0:T(8,128)(2,1)S(1)}, u32[]{:S(2)}, u32[]{:S(2)}) collective-permute-start(bf16[384,512]{1,0:T(8,128)(2,1)S(1)} %get-tuple-element.30.other_ref), channel_id=1, source_target_pairs={{0,2},{1,3},{2,0},{3,1},{4,6},{5,7},{6,4},{7,5},{8,10},{9,11},{10,... | collective-permute-start | bytes 1179656 | tf_op jit(solution)/shard_map/ppermute | solution.py:20
  9.2 1.8 %pack1.1 = (bf16[384,512]{1,0:T(8,128)(2,1)S(1)}, bf16[384,512]{1,0:T(8,128)(2,1)S(1)}) custom-call(s32[3]{0:T(128)S(1)} %pad_add_fusion.place_ref, bf16[128,2048]{1,0:T(8,128)(2,1)} %q_ref.3, bf16[128,2048]{1,0:T(8,128)(2,1)} %k_ref.3, bf16[128,2048]{1,0:T(8,128)(2,1)} %v_ref.3, bf16[384,512]{1,0:T(8,128)(2,1)S(1)} %get-tuple-element.30.other_ref), custom_call_target="tpu_custom_call" | custom-call | flops 2000000000 | bytes 40000000 | tf_op jit(solution)/shard_map/pack1/pallas_call | solution.py:220
  11.0 0.4 collective-permute-start
  11.4 7.6 %collective-permute-done.2.a3.refs_3_ = bf16[384,512]{1,0:T(8,128)(2,1)S(1)} collective-permute-done((bf16[384,512]{1,0:T(8,128)(2,1)S(1)}, bf16[384,512]{1,0:T(8,128)(2,1)S(1)}, u32[]{:S(2)}, u32[]{:S(2)}) %collective-permute-start.2) | collective-permute-done | bytes 393248 | tf_op jit(solution)/shard_map/ppermute | solution.py:20
  19.0 8.5 %collective-permute-done.1.a2.refs_2_ = bf16[384,512]{1,0:T(8,128)(2,1)S(1)} collective-permute-done((bf16[384,512]{1,0:T(8,128)(2,1)S(1)}, bf16[384,512]{1,0:T(8,128)(2,1)S(1)}, u32[]{:S(2)}, u32[]{:S(2)}) %collective-permute-start.1) | collective-permute-done | bytes 393248 | tf_op jit(solution)/shard_map/ppermute | solution.py:20
  27.5 0.0 collective-permute-done.a1.refs_1_
  27.5 0.8 %coarse.1 = (bf16[256,512]{1,0:T(8,128)(2,1)S(1)}, bf16[128,512]{1,0:T(8,128)(2,1)S(1)}) custom-call(s32[3]{0:T(128)S(1)} %pad_add_fusion.place_ref, bf16[384,512]{1,0:T(8,128)(2,1)S(1)} %get-tuple-element.31.a0.refs_0_.refs_7_, bf16[384,512]{1,0:T(8,128)(2,1)S(1)} %collective-permute-done.a1.refs_1_, ...), custom_call_target="tpu_custom_call" | custom-call | tf_op jit(solution)/shard_map/coarse/pallas_call | solution.py:231
  28.3 0.0 collective-permute-done.4.refs_0_
  28.3 2.3 %collective-permute-done.3.refs_1_ = bf16[1024,256]{1,0:T(8,128)(2,1)S(1)} collective-permute-done((bf16[1024,256]{1,0:T(8,128)(2,1)S(1)}, bf16[1024,256]{1,0:T(8,128)(2,1)S(1)}, u32[]{:S(2)}, u32[]{:S(2)}) %collective-permute-start.3) | collective-permute-done | bytes 524320 | tf_op jit(solution)/shard_map/ppermute | solution.py:20
  30.6 1.5 %collective-permute-start.15 = (bf16[1024,256]{1,0:T(8,128)(2,1)S(1)}, bf16[1024,256]{1,0:T(8,128)(2,1)S(1)}, u32[]{:S(2)}, u32[]{:S(2)}) collective-permute-start(bf16[1024,256]{1,0:T(8,128)(2,1)S(1)} %collective-permute-done.3.refs_1_), channel_id=1, source_target_pairs={{0,16},{16,0},{1,17},{17,1},{2,18},{18,2},{3,19},{19,3},{4,20},{20... | collective-permute-start | bytes 1572872 | tf_op jit(solution)/shard_map/ppermute | solution.py:24
  32.1 0.4 collective-permute-start.5
  32.6 2.1 %collective-permute-start.7 = (bf16[128,512]{1,0:T(8,128)(2,1)S(1)}, bf16[128,512]{1,0:T(8,128)(2,1)S(1)}, u32[]{:S(2)}, u32[]{:S(2)}) collective-permute-start(bf16[128,512]{1,0:T(8,128)(2,1)S(1)} %get-tuple-element.38), channel_id=1, source_target_pairs={{0,12},{1,13},{2,14},{3,15},{4,8},{5,9},{6,10},{7,11},{8,4},{9,5},... | collective-permute-start | bytes 393224 | tf_op jit(solution)/shard_map/ppermute | solution.py:20
  34.6 1.0 %collective-permute-start.6 = (bf16[128,512]{1,0:T(8,128)(2,1)S(1)}, bf16[128,512]{1,0:T(8,128)(2,1)S(1)}, u32[]{:S(2)}, u32[]{:S(2)}) collective-permute-start(bf16[128,512]{1,0:T(8,128)(2,1)S(1)} %get-tuple-element.38), channel_id=1, source_target_pairs={{0,8},{1,9},{2,10},{3,11},{4,12},{5,13},{6,14},{7,15},{8,0},{9,1},... | collective-permute-start | bytes 393224 | tf_op jit(solution)/shard_map/ppermute | solution.py:20
  35.6 10.9 %collective-permute-done.5.refs_4_ = bf16[256,512]{1,0:T(8,128)(2,1)S(1)} collective-permute-done((bf16[256,512]{1,0:T(8,128)(2,1)S(1)}, bf16[256,512]{1,0:T(8,128)(2,1)S(1)}, u32[]{:S(2)}, u32[]{:S(2)}) %collective-permute-start.5) | collective-permute-done | bytes 262176 | tf_op jit(solution)/shard_map/ppermute | solution.py:20
  46.5 0.0 collective-permute-start.9
  46.5 0.0 collective-permute-done.15.refs_2_
  46.5 0.5 collective-permute-start.19
  47.1 0.0 collective-permute-done.7.refs_6_
  47.1 0.0 collective-permute-done.6.refs_5_
  47.1 0.0 copy-done
  47.1 3.2 %attend0.1.refs_7_.refs_0_ = bf16[256,512]{1,0:T(8,128)(2,1)S(1)} custom-call(s32[3]{0:T(128)S(1)} %pad_add_fusion.place_ref, s32[16]{0:T(128)S(1)} %copy-done, bf16[384,512]{1,0:T(8,128)(2,1)S(1)} %get-tuple-element.31.a0.refs_0_.refs_7_, bf16[384,512]{1,0:T(8,128)(2,1)S(1)} %collective-permute-done.a1.refs_1_, ...), custom_call_target="tpu_custom_call" | custom-call | flops 2000000000 | bytes 40000000 | tf_op jit(solution)/shard_map/attend0/pallas_call | solution.py:244
  50.3 1.6 %collective-permute-start.8 = (bf16[256,512]{1,0:T(8,128)(2,1)S(1)}, bf16[256,512]{1,0:T(8,128)(2,1)S(1)}, u32[]{:S(2)}, u32[]{:S(2)}) collective-permute-start(bf16[256,512]{1,0:T(8,128)(2,1)S(1)} %attend0.1.refs_7_.refs_0_), channel_id=1, source_target_pairs={{0,2},{1,3},{2,0},{3,1},{4,6},{5,7},{6,4},{7,5},{8,10},{9,11},{10,... | collective-permute-start | bytes 786440 | tf_op jit(solution)/shard_map/ppermute | solution.py:20
  51.9 3.2 %attend1.1.refs_1_ = bf16[256,512]{1,0:T(8,128)(2,1)S(1)} custom-call(s32[3]{0:T(128)S(1)} %pad_add_fusion.place_ref, s32[16]{0:T(128)S(1)} %copy-done, bf16[384,512]{1,0:T(8,128)(2,1)S(1)} %get-tuple-element.31.a0.refs_0_.refs_7_, bf16[384,512]{1,0:T(8,128)(2,1)S(1)} %collective-permute-done.a1.refs_1_, ...), custom_call_target="tpu_custom_call" | custom-call | flops 2000000000 | bytes 40000000 | tf_op jit(solution)/shard_map/attend1/pallas_call | solution.py:244
  55.1 0.6 collective-permute-start.12
  55.7 1.0 %collective-permute-done.8.refs_4_ = bf16[256,512]{1,0:T(8,128)(2,1)S(1)} collective-permute-done((bf16[256,512]{1,0:T(8,128)(2,1)S(1)}, bf16[256,512]{1,0:T(8,128)(2,1)S(1)}, u32[]{:S(2)}, u32[]{:S(2)}) %collective-permute-start.8) | collective-permute-done | bytes 262176 | tf_op jit(solution)/shard_map/ppermute | solution.py:20
  56.8 0.0 collective-permute-done.9.refs_2_
  56.8 0.0 collective-permute-start.13
  56.8 0.0 collective-permute-done.19.refs_1_
  56.8 1.6 %collective-permute-start.20 = (bf16[1024,256]{1,0:T(8,128)(2,1)S(1)}, bf16[1024,256]{1,0:T(8,128)(2,1)S(1)}, u32[]{:S(2)}, u32[]{:S(2)}) collective-permute-start(bf16[1024,256]{1,0:T(8,128)(2,1)S(1)} %collective-permute-done.9.refs_2_), channel_id=1, source_target_pairs={{0,16},{16,0},{1,17},{17,1},{2,18},{18,2},{3,19},{19,3},{4,20},{20... | collective-permute-start | bytes 1572872 | tf_op jit(solution)/shard_map/ppermute | solution.py:24
  58.3 0.2 collective-permute-start.10
  58.5 0.3 collective-permute-start.11
  58.8 2.7 %collective-permute-done.12.refs_5_ = bf16[256,512]{1,0:T(8,128)(2,1)S(1)} collective-permute-done((bf16[256,512]{1,0:T(8,128)(2,1)S(1)}, bf16[256,512]{1,0:T(8,128)(2,1)S(1)}, u32[]{:S(2)}, u32[]{:S(2)}) %collective-permute-start.12) | collective-permute-done | bytes 262176 | tf_op jit(solution)/shard_map/ppermute | solution.py:20
  61.6 0.0 collective-permute-done.13.refs_6_
  61.6 0.0 collective-permute-start.14
  61.6 0.0 collective-permute-done.10.refs_2_
  61.6 0.0 collective-permute-done.11.refs_3_
  61.6 1.5 %collective-permute-done.14.refs_7_ = bf16[256,512]{1,0:T(8,128)(2,1)S(1)} collective-permute-done((bf16[256,512]{1,0:T(8,128)(2,1)S(1)}, bf16[256,512]{1,0:T(8,128)(2,1)S(1)}, u32[]{:S(2)}, u32[]{:S(2)}) %collective-permute-start.14) | collective-permute-done | bytes 262176 | tf_op jit(solution)/shard_map/ppermute | solution.py:20
  63.1 0.7 gather.1.rows_ref
  63.8 2.5 %project0.1 = (bf16[128,512]{1,0:T(8,128)(2,1)S(1)}, bf16[128,512]{1,0:T(8,128)(2,1)S(1)}, bf16[128,512]{1,0:T(8,128)(2,1)S(1)}, bf16[128,512]{1,0:T(8,128)(2,1)S(1)}) custom-call(s32[3]{0:T(128)S(1)} %pad_add_fusion.place_ref, bf16[512,2048]{1,0:T(8,128)(2,1)S(1)} %gather.1.rows_ref, bf16[2048,256]{1,0:T(8,128)(2,1)} %refs_0_.1, ...), custom_call_target="tpu_custom_call" | custom-call | tf_op jit(solution)/shard_map/project0/pallas_call | solution.py:264
  66.3 0.2 collective-permute-start.16
  66.5 0.5 collective-permute-start.17
  67.0 1.2 %collective-permute-start.18 = (bf16[128,512]{1,0:T(8,128)(2,1)S(1)}, bf16[128,512]{1,0:T(8,128)(2,1)S(1)}, u32[]{:S(2)}, u32[]{:S(2)}) collective-permute-start(bf16[128,512]{1,0:T(8,128)(2,1)S(1)} %get-tuple-element.48), channel_id=1, source_target_pairs={{0,3},{1,2},{2,1},{3,0},{4,7},{5,6},{6,5},{7,4},{8,11},{9,10},{10,... | collective-permute-start | bytes 393224 | tf_op jit(solution)/shard_map/ppermute | solution.py:20
  68.2 2.9 %collective-permute-done.20.refs_3_ = bf16[1024,256]{1,0:T(8,128)(2,1)S(1)} collective-permute-done((bf16[1024,256]{1,0:T(8,128)(2,1)S(1)}, bf16[1024,256]{1,0:T(8,128)(2,1)S(1)}, u32[]{:S(2)}, u32[]{:S(2)}) %collective-permute-start.20) | collective-permute-done | bytes 524320 | tf_op jit(solution)/shard_map/ppermute | solution.py:24
  71.1 1.8 %project1.1 = (bf16[128,512]{1,0:T(8,128)(2,1)S(1)}, bf16[128,512]{1,0:T(8,128)(2,1)S(1)}, bf16[128,512]{1,0:T(8,128)(2,1)S(1)}, bf16[128,512]{1,0:T(8,128)(2,1)S(1)}) custom-call(s32[3]{0:T(128)S(1)} %pad_add_fusion.place_ref, bf16[512,2048]{1,0:T(8,128)(2,1)S(1)} %gather.1.rows_ref, bf16[1024,256]{1,0:T(8,128)(2,1)S(1)} %collective-permute-done.4.refs_0_, ...), custom_call_target="tpu_custom_call" | custom-call | tf_op jit(solution)/shard_map/project1/pallas_call | solution.py:264
  72.9 0.1 collective-permute-start.21
  73.0 1.6 %collective-permute-start.22 = (bf16[128,512]{1,0:T(8,128)(2,1)S(1)}, bf16[128,512]{1,0:T(8,128)(2,1)S(1)}, u32[]{:S(2)}, u32[]{:S(2)}) collective-permute-start(bf16[128,512]{1,0:T(8,128)(2,1)S(1)} %get-tuple-element.53), channel_id=1, source_target_pairs={{0,2},{1,3},{2,0},{3,1},{4,6},{5,7},{6,4},{7,5},{8,10},{9,11},{10,... | collective-permute-start | bytes 393224 | tf_op jit(solution)/shard_map/ppermute | solution.py:20
  74.5 0.0 collective-permute-done.16.refs_1_
  74.6 0.3 collective-permute-start.23
  74.8 0.0 collective-permute-done.17.refs_2_
  74.8 0.0 collective-permute-done.18.refs_3_
  74.8 0.0 collective-permute-done.21.refs_5_
  74.9 4.5 %collective-permute-done.22.refs_6_ = bf16[128,512]{1,0:T(8,128)(2,1)S(1)} collective-permute-done((bf16[128,512]{1,0:T(8,128)(2,1)S(1)}, bf16[128,512]{1,0:T(8,128)(2,1)S(1)}, u32[]{:S(2)}, u32[]{:S(2)}) %collective-permute-start.22) | collective-permute-done | bytes 131104 | tf_op jit(solution)/shard_map/ppermute | solution.py:20
  79.3 1.9 %collective-permute-done.23.refs_7_ = bf16[128,512]{1,0:T(8,128)(2,1)S(1)} collective-permute-done((bf16[128,512]{1,0:T(8,128)(2,1)S(1)}, bf16[128,512]{1,0:T(8,128)(2,1)S(1)}, u32[]{:S(2)}, u32[]{:S(2)}) %collective-permute-start.23) | collective-permute-done | bytes 131104 | tf_op jit(solution)/shard_map/ppermute | solution.py:20
  81.2 1.6 %place.1 = bf16[128,4096]{1,0:T(8,128)(2,1)} custom-call(s32[3]{0:T(128)S(1)} %pad_add_fusion.place_ref, bf16[128,512]{1,0:T(8,128)(2,1)S(1)} %get-tuple-element.45.refs_0_, bf16[128,512]{1,0:T(8,128)(2,1)S(1)} %collective-permute-done.16.refs_1_, bf16[128,512]{1,0:T(8,128)(2,1)S(1)} %collective-permute-done.17.refs_2_, ...), custom_call_target="tpu_custom_call" | custom-call | tf_op jit(solution)/shard_map/place/pallas_call | solution.py:268
Async XLA Ops:
  2.0 26.4 %collective-permute-start.4 = (bf16[1024,256]{1,0:T(8,128)(2,1)S(1)}, bf16[1024,256]{1,0:T(8,128)(2,1)S(1)}, u32[]{:S(2)}, u32[]{:S(2)}) collective-permute-start(bf16[1024,256]{1,0:T(8,128)(2,1)S(1)} %get-tuple-element.36), channel_id=1, source_target_pairs={{0,4},{1,5},{2,6},{3,7},{4,0},{5,1},{6,2},{7,3},{8,12},{9,13},{10,... | collective-permute-start | bytes 1572872 | tf_op jit(solution)/shard_map/ppermute | solution.py:20
  5.1 25.6 %collective-permute-start.3 = (bf16[1024,256]{1,0:T(8,128)(2,1)S(1)}, bf16[1024,256]{1,0:T(8,128)(2,1)S(1)}, u32[]{:S(2)}, u32[]{:S(2)}) collective-permute-start(bf16[1024,256]{1,0:T(8,128)(2,1)S(1)} %get-tuple-element.36), channel_id=1, source_target_pairs={{0,8},{1,9},{2,10},{3,11},{4,12},{5,13},{6,14},{7,15},{8,0},{9,1},... | collective-permute-start | bytes 1572872 | tf_op jit(solution)/shard_map/ppermute | solution.py:20
  7.6 11.3 %collective-permute-start.2 = (bf16[384,512]{1,0:T(8,128)(2,1)S(1)}, bf16[384,512]{1,0:T(8,128)(2,1)S(1)}, u32[]{:S(2)}, u32[]{:S(2)}) collective-permute-start(bf16[384,512]{1,0:T(8,128)(2,1)S(1)} %get-tuple-element.33), channel_id=1, source_target_pairs={{0,3},{1,2},{2,1},{3,0},{4,7},{5,6},{6,5},{7,4},{8,11},{9,10},{10,... | collective-permute-start | bytes 1179656 | tf_op jit(solution)/shard_map/ppermute | solution.py:20
  8.0 39.0 %copy-start = (s32[16]{0:T(128)S(1)}, s32[16]{0:T(128)}, u32[]{:S(2)}) copy-start(s32[16]{0:T(128)} %doc_ref.3) | copy-start | bytes 196
  8.0 19.4 %collective-permute-start.1 = (bf16[384,512]{1,0:T(8,128)(2,1)S(1)}, bf16[384,512]{1,0:T(8,128)(2,1)S(1)}, u32[]{:S(2)}, u32[]{:S(2)}) collective-permute-start(bf16[384,512]{1,0:T(8,128)(2,1)S(1)} %get-tuple-element.30.other_ref), channel_id=1, source_target_pairs={{0,2},{1,3},{2,0},{3,1},{4,6},{5,7},{6,4},{7,5},{8,10},{9,11},{10,... | collective-permute-start | bytes 1179656 | tf_op jit(solution)/shard_map/ppermute | solution.py:20
  11.0 16.5 %collective-permute-start = (bf16[384,512]{1,0:T(8,128)(2,1)S(1)}, bf16[384,512]{1,0:T(8,128)(2,1)S(1)}, u32[]{:S(2)}, u32[]{:S(2)}) collective-permute-start(bf16[384,512]{1,0:T(8,128)(2,1)S(1)} %get-tuple-element.32), channel_id=1, source_target_pairs={{0,1},{1,0},{2,3},{3,2},{4,5},{5,4},{6,7},{7,6},{8,9},{9,8},{10,11... | collective-permute-start | bytes 1179656 | tf_op jit(solution)/shard_map/ppermute | solution.py:20
  30.6 15.9 %collective-permute-start.15 = (bf16[1024,256]{1,0:T(8,128)(2,1)S(1)}, bf16[1024,256]{1,0:T(8,128)(2,1)S(1)}, u32[]{:S(2)}, u32[]{:S(2)}) collective-permute-start(bf16[1024,256]{1,0:T(8,128)(2,1)S(1)} %collective-permute-done.3.refs_1_), channel_id=1, source_target_pairs={{0,16},{16,0},{1,17},{17,1},{2,18},{18,2},{3,19},{19,3},{4,20},{20... | collective-permute-start | bytes 1572872 | tf_op jit(solution)/shard_map/ppermute | solution.py:24
  32.1 14.4 %collective-permute-start.5 = (bf16[256,512]{1,0:T(8,128)(2,1)S(1)}, bf16[256,512]{1,0:T(8,128)(2,1)S(1)}, u32[]{:S(2)}, u32[]{:S(2)}) collective-permute-start(bf16[256,512]{1,0:T(8,128)(2,1)S(1)} %get-tuple-element.37), channel_id=1, source_target_pairs={{0,4},{1,5},{2,6},{3,7},{4,0},{5,1},{6,2},{7,3},{8,12},{9,13},{10,... | collective-permute-start | bytes 786440 | tf_op jit(solution)/shard_map/ppermute | solution.py:20
  32.6 14.5 %collective-permute-start.7 = (bf16[128,512]{1,0:T(8,128)(2,1)S(1)}, bf16[128,512]{1,0:T(8,128)(2,1)S(1)}, u32[]{:S(2)}, u32[]{:S(2)}) collective-permute-start(bf16[128,512]{1,0:T(8,128)(2,1)S(1)} %get-tuple-element.38), channel_id=1, source_target_pairs={{0,12},{1,13},{2,14},{3,15},{4,8},{5,9},{6,10},{7,11},{8,4},{9,5},... | collective-permute-start | bytes 393224 | tf_op jit(solution)/shard_map/ppermute | solution.py:20
  34.6 12.4 %collective-permute-start.6 = (bf16[128,512]{1,0:T(8,128)(2,1)S(1)}, bf16[128,512]{1,0:T(8,128)(2,1)S(1)}, u32[]{:S(2)}, u32[]{:S(2)}) collective-permute-start(bf16[128,512]{1,0:T(8,128)(2,1)S(1)} %get-tuple-element.38), channel_id=1, source_target_pairs={{0,8},{1,9},{2,10},{3,11},{4,12},{5,13},{6,14},{7,15},{8,0},{9,1},... | collective-permute-start | bytes 393224 | tf_op jit(solution)/shard_map/ppermute | solution.py:20
  46.5 10.2 %collective-permute-start.9 = (bf16[1024,256]{1,0:T(8,128)(2,1)S(1)}, bf16[1024,256]{1,0:T(8,128)(2,1)S(1)}, u32[]{:S(2)}, u32[]{:S(2)}) collective-permute-start(bf16[1024,256]{1,0:T(8,128)(2,1)S(1)} %collective-permute-done.3.refs_1_), channel_id=1, source_target_pairs={{0,4},{1,5},{2,6},{3,7},{4,0},{5,1},{6,2},{7,3},{8,12},{9,13},{10,... | collective-permute-start | bytes 1572872 | tf_op jit(solution)/shard_map/ppermute | solution.py:20
  46.5 10.2 %collective-permute-start.19 = (bf16[1024,256]{1,0:T(8,128)(2,1)S(1)}, bf16[1024,256]{1,0:T(8,128)(2,1)S(1)}, u32[]{:S(2)}, u32[]{:S(2)}) collective-permute-start(bf16[1024,256]{1,0:T(8,128)(2,1)S(1)} %collective-permute-done.4.refs_0_), channel_id=1, source_target_pairs={{0,16},{16,0},{1,17},{17,1},{2,18},{18,2},{3,19},{19,3},{4,20},{20... | collective-permute-start | bytes 1572872 | tf_op jit(solution)/shard_map/ppermute | solution.py:24
  50.3 6.4 %collective-permute-start.8 = (bf16[256,512]{1,0:T(8,128)(2,1)S(1)}, bf16[256,512]{1,0:T(8,128)(2,1)S(1)}, u32[]{:S(2)}, u32[]{:S(2)}) collective-permute-start(bf16[256,512]{1,0:T(8,128)(2,1)S(1)} %attend0.1.refs_7_.refs_0_), channel_id=1, source_target_pairs={{0,2},{1,3},{2,0},{3,1},{4,6},{5,7},{6,4},{7,5},{8,10},{9,11},{10,... | collective-permute-start | bytes 786440 | tf_op jit(solution)/shard_map/ppermute | solution.py:20
  55.1 6.4 %collective-permute-start.12 = (bf16[256,512]{1,0:T(8,128)(2,1)S(1)}, bf16[256,512]{1,0:T(8,128)(2,1)S(1)}, u32[]{:S(2)}, u32[]{:S(2)}) collective-permute-start(bf16[256,512]{1,0:T(8,128)(2,1)S(1)} %attend1.1.refs_1_), channel_id=1, source_target_pairs={{0,2},{1,3},{2,0},{3,1},{4,6},{5,7},{6,4},{7,5},{8,10},{9,11},{10,... | collective-permute-start | bytes 786440 | tf_op jit(solution)/shard_map/ppermute | solution.py:20
  56.8 4.8 %collective-permute-start.13 = (bf16[256,512]{1,0:T(8,128)(2,1)S(1)}, bf16[256,512]{1,0:T(8,128)(2,1)S(1)}, u32[]{:S(2)}, u32[]{:S(2)}) collective-permute-start(bf16[256,512]{1,0:T(8,128)(2,1)S(1)} %collective-permute-done.8.refs_4_), channel_id=1, source_target_pairs={{0,1},{1,0},{2,3},{3,2},{4,5},{5,4},{6,7},{7,6},{8,9},{9,8},{10,11... | collective-permute-start | bytes 786440 | tf_op jit(solution)/shard_map/ppermute | solution.py:20
  56.8 14.3 %collective-permute-start.20 = (bf16[1024,256]{1,0:T(8,128)(2,1)S(1)}, bf16[1024,256]{1,0:T(8,128)(2,1)S(1)}, u32[]{:S(2)}, u32[]{:S(2)}) collective-permute-start(bf16[1024,256]{1,0:T(8,128)(2,1)S(1)} %collective-permute-done.9.refs_2_), channel_id=1, source_target_pairs={{0,16},{16,0},{1,17},{17,1},{2,18},{18,2},{3,19},{19,3},{4,20},{20... | collective-permute-start | bytes 1572872 | tf_op jit(solution)/shard_map/ppermute | solution.py:24
  58.3 3.2 %collective-permute-start.10 = (bf16[256,512]{1,0:T(8,128)(2,1)S(1)}, bf16[256,512]{1,0:T(8,128)(2,1)S(1)}, u32[]{:S(2)}, u32[]{:S(2)}) collective-permute-start(bf16[256,512]{1,0:T(8,128)(2,1)S(1)} %attend0.1.refs_7_.refs_0_), channel_id=1, source_target_pairs={{0,1},{1,0},{2,3},{3,2},{4,5},{5,4},{6,7},{7,6},{8,9},{9,8},{10,11... | collective-permute-start | bytes 786440 | tf_op jit(solution)/shard_map/ppermute | solution.py:20
  58.5 3.1 %collective-permute-start.11 = (bf16[256,512]{1,0:T(8,128)(2,1)S(1)}, bf16[256,512]{1,0:T(8,128)(2,1)S(1)}, u32[]{:S(2)}, u32[]{:S(2)}) collective-permute-start(bf16[256,512]{1,0:T(8,128)(2,1)S(1)} %attend1.1.refs_1_), channel_id=1, source_target_pairs={{0,1},{1,0},{2,3},{3,2},{4,5},{5,4},{6,7},{7,6},{8,9},{9,8},{10,11... | collective-permute-start | bytes 786440 | tf_op jit(solution)/shard_map/ppermute | solution.py:20
  61.6 1.5 %collective-permute-start.14 = (bf16[256,512]{1,0:T(8,128)(2,1)S(1)}, bf16[256,512]{1,0:T(8,128)(2,1)S(1)}, u32[]{:S(2)}, u32[]{:S(2)}) collective-permute-start(bf16[256,512]{1,0:T(8,128)(2,1)S(1)} %collective-permute-done.12.refs_5_), channel_id=1, source_target_pairs={{0,1},{1,0},{2,3},{3,2},{4,5},{5,4},{6,7},{7,6},{8,9},{9,8},{10,11... | collective-permute-start | bytes 786440 | tf_op jit(solution)/shard_map/ppermute | solution.py:20
  66.3 8.2 %collective-permute-start.16 = (bf16[128,512]{1,0:T(8,128)(2,1)S(1)}, bf16[128,512]{1,0:T(8,128)(2,1)S(1)}, u32[]{:S(2)}, u32[]{:S(2)}) collective-permute-start(bf16[128,512]{1,0:T(8,128)(2,1)S(1)} %get-tuple-element.46), channel_id=1, source_target_pairs={{0,1},{1,0},{2,3},{3,2},{4,5},{5,4},{6,7},{7,6},{8,9},{9,8},{10,11... | collective-permute-start | bytes 393224 | tf_op jit(solution)/shard_map/ppermute | solution.py:20
  66.5 8.3 %collective-permute-start.17 = (bf16[128,512]{1,0:T(8,128)(2,1)S(1)}, bf16[128,512]{1,0:T(8,128)(2,1)S(1)}, u32[]{:S(2)}, u32[]{:S(2)}) collective-permute-start(bf16[128,512]{1,0:T(8,128)(2,1)S(1)} %get-tuple-element.47), channel_id=1, source_target_pairs={{0,2},{1,3},{2,0},{3,1},{4,6},{5,7},{6,4},{7,5},{8,10},{9,11},{10,... | collective-permute-start | bytes 393224 | tf_op jit(solution)/shard_map/ppermute | solution.py:20
  67.0 7.8 %collective-permute-start.18 = (bf16[128,512]{1,0:T(8,128)(2,1)S(1)}, bf16[128,512]{1,0:T(8,128)(2,1)S(1)}, u32[]{:S(2)}, u32[]{:S(2)}) collective-permute-start(bf16[128,512]{1,0:T(8,128)(2,1)S(1)} %get-tuple-element.48), channel_id=1, source_target_pairs={{0,3},{1,2},{2,1},{3,0},{4,7},{5,6},{6,5},{7,4},{8,11},{9,10},{10,... | collective-permute-start | bytes 393224 | tf_op jit(solution)/shard_map/ppermute | solution.py:20
  72.9 2.0 %collective-permute-start.21 = (bf16[128,512]{1,0:T(8,128)(2,1)S(1)}, bf16[128,512]{1,0:T(8,128)(2,1)S(1)}, u32[]{:S(2)}, u32[]{:S(2)}) collective-permute-start(bf16[128,512]{1,0:T(8,128)(2,1)S(1)} %get-tuple-element.52), channel_id=1, source_target_pairs={{0,1},{1,0},{2,3},{3,2},{4,5},{5,4},{6,7},{7,6},{8,9},{9,8},{10,11... | collective-permute-start | bytes 393224 | tf_op jit(solution)/shard_map/ppermute | solution.py:20
  73.0 6.4 %collective-permute-start.22 = (bf16[128,512]{1,0:T(8,128)(2,1)S(1)}, bf16[128,512]{1,0:T(8,128)(2,1)S(1)}, u32[]{:S(2)}, u32[]{:S(2)}) collective-permute-start(bf16[128,512]{1,0:T(8,128)(2,1)S(1)} %get-tuple-element.53), channel_id=1, source_target_pairs={{0,2},{1,3},{2,0},{3,1},{4,6},{5,7},{6,4},{7,5},{8,10},{9,11},{10,... | collective-permute-start | bytes 393224 | tf_op jit(solution)/shard_map/ppermute | solution.py:20
  74.6 6.7 %collective-permute-start.23 = (bf16[128,512]{1,0:T(8,128)(2,1)S(1)}, bf16[128,512]{1,0:T(8,128)(2,1)S(1)}, u32[]{:S(2)}, u32[]{:S(2)}) collective-permute-start(bf16[128,512]{1,0:T(8,128)(2,1)S(1)} %get-tuple-element.54), channel_id=1, source_target_pairs={{0,3},{1,2},{2,1},{3,0},{4,7},{5,6},{6,5},{7,4},{8,11},{9,10},{10,... | collective-permute-start | bytes 393224 | tf_op jit(solution)/shard_map/ppermute | solution.py:20

commit v6 on v5

--- a/solution.py
+++ b/solution.py
@@ -128,18 +128,20 @@
     ]
     for head in range(heads):
         columns = slice(head * HD, (head + 1) * HD)
+        query = jnp.concatenate([own[2 * half + part][0:128, columns] for part in range(2)], 0)
+        score = lax.dot_general(
+            query, key_ref[:, columns], (((1,), (1,)), ((), ())), preferred_element_type=jnp.float32
+        )
+        raised, inverse = [], []
         for part in range(2):
-            query = own[2 * half + part][0:128, columns]
-            score = lax.dot_general(
-                query, key_ref[:, columns], (((1,), (1,)), ((), ())), preferred_element_type=jnp.float32
-            )
-            score = score + bias[part]
-            raised = jnp.exp2((score - jnp.max(score, axis=-1, keepdims=True)) * (HD ** (-0.5) * LOG2_E))
-            mixed = jnp.dot(
-                raised.astype(jnp.bfloat16), value_ref[:, columns], preferred_element_type=jnp.float32
-            )
-            mixed = mixed * (1.0 / jnp.sum(raised, axis=-1, keepdims=True))
-            out_ref[128 * part : 128 * part + 128, columns] = mixed.astype(jnp.bfloat16)
+            biased = score[128 * part : 128 * part + 128, :] + bias[part]
+            power = jnp.exp2((biased - jnp.max(biased, axis=-1, keepdims=True)) * (HD ** (-0.5) * LOG2_E))
+            raised.append(power.astype(jnp.bfloat16))
+            inverse.append(1.0 / jnp.sum(power, axis=-1, keepdims=True))
+        mixed = jnp.dot(jnp.concatenate(raised, 0), value_ref[:, columns], preferred_element_type=jnp.float32)
+        for part in range(2):
+            run = slice(128 * part, 128 * part + 128)
+            out_ref[run, columns] = (mixed[run, :] * inverse[part]).astype(jnp.bfloat16)
 
 
 def gather_kernel(place_ref, *refs):
@@ -157,18 +159,21 @@
     blocks, outs = list(refs[:-4]), refs[-4:]
     depth = rows_ref.shape[1]
     half = depth // 2
-    group = place_ref[1]
     q = 0
     while blocks:
-        block = blocks.pop(0)
-        if block.shape[0] == depth:
-            total = jnp.dot(rows_ref[...], block[...], preferred_element_type=jnp.float32)
-        else:
-            ours = rows_ref[:, pl.ds(pl.multiple_of(group * half, half), half)]
-            theirs = rows_ref[:, pl.ds(pl.multiple_of((1 - group) * half, half), half)]
-            total = jnp.dot(ours, block[...], preferred_element_type=jnp.float32)
-            total += jnp.dot(theirs, blocks.pop(0)[...], preferred_element_type=jnp.float32)
-        wide = block.shape[1]
+        total, done = None, 0
+        wide = blocks[0].shape[1]
+        while done < depth:
+            block = blocks.pop(0)
+            run = block.shape[0]
+            if run == depth:
+                rows = rows_ref[...]
+            else:
+                first = jnp.bitwise_xor(place_ref[1], done // half) * half + done % half
+                rows = rows_ref[:, pl.ds(pl.multiple_of(first, HD), run)]
+            product = jnp.dot(rows, block[...], preferred_element_type=jnp.float32)
+            total = product if total is None else total + product
+            done += run
         for r in range(4):
             outs[r][:, q * wide : (q + 1) * wide] = total[r * BLOCK : (r + 1) * BLOCK, :].astype(jnp.bfloat16)
         q += 1
@@ -207,16 +212,24 @@
     position = lax.axis_index("ctx")
     places = jnp.stack([position & 3, group, position]).astype(jnp.int32)
 
+    own_block = out_weight
     queries, keys, values, out_weight = (
         pltpu.with_memory_space_constraint(array, pltpu.HBM) for array in (queries, keys, values, out_weight)
     )
-    ours, *across = call(
+    (ours,) = call(
+        functools.partial(pack_kernel, ()),
+        [(depth // 2, wide)],
+        anywhere(4),
+        scratch_shapes=[pltpu.SemaphoreType.DMA((2,))],
+        name="pack",
+    )(places, queries, keys, values, out_weight)
+    across = call(
         functools.partial(pack_kernel, (2, 3)),
-        [(depth // 2, wide)] + [(3 * length, share)] * 2,
-        anywhere(4),
-        scratch_shapes=[pltpu.SemaphoreType.DMA((8,))],
+        [(3 * length, share)] * 2,
+        anywhere(3) + loose(1),
+        scratch_shapes=[pltpu.SemaphoreType.DMA((6,))],
         name="pack0",
-    )(places, queries, keys, values, out_weight)
+    )(places, queries, keys, values, ours)
     near = call(
         functools.partial(pack_kernel, (1, 0)),
         [(3 * length, share)] * 2,
@@ -236,7 +249,8 @@
     other_h = swap_groups(after(half_h, third))
     half_d = swap(after(half_h, far[0]), LOW)
     other_l = swap_groups(after(ours_l, other_h))
-    other_d = swap_groups(after(half_d, other_l))
+    quarter = depth // 4
+    other_d = [swap_groups(after(half_d, other_l)[:quarter]), swap(after(other_h, half_d)[quarter:], LOW)]
 
     pieces = [[None] * 2 for _ in range(4)]
     before = near[1]
@@ -260,7 +274,7 @@
 
     (rows,) = call(gather_kernel, [(4 * length, width)], vmem(8), name="gather")(places, *mixed)
     received = []
-    for n, blocks in enumerate(((out_weight, half_h, other_h), (ours_l, other_l, half_d, other_d))):
+    for n, blocks in enumerate(((own_block, half_h, other_h), (ours_l, other_l, half_d, *other_d))):
         parts = call(project_kernel, [(length, 2 * wide)] * 4, vmem(1 + len(blocks)), name="project%d" % n)(
             places, rows, *blocks
         )

time: 83.1 us -> 81.2 us (0.977)
  Pallas kernels: 17.6 us -> 16.7 us
  starting transfers between devices: 21.2 us -> 20.3 us
    ppermute x3, waiting for transfers between devices: 2.87 us -> 0.38 us  [swap_groups(): return lax.ppermute(value, 'groups', [(0, 1), (1, 0)])]
    ppermute x21 -> x22, waiting for transfers between devices: 41 us -> 43.3 us  [swap(): return lax.ppermute(value, 'ctx', pairs)]
    ppermute x3, starting transfers between devices: 3.59 us -> 1.9 us  [swap_groups(): return lax.ppermute(value, 'groups', [(0, 1), (1, 0)])]
    pallas_call x2, Pallas kernels: 6.46 us -> 4.79 us  [per_device_fast(): call(functools.partial(attention_kernel, n), [(2 * length, share)], [pl.B...]
    pallas_call x1 -> x2, Pallas kernels: 1.88 us -> 3.39 us  [the longest x1 1.8 us: per_device_fast(): call(functools.partial(pack_kernel, (2, 3)), [(3 * length, share)] * 2, a...]
    ppermute x21 -> x22, starting transfers between devices: 17.6 us -> 18.4 us  [swap(): return lax.ppermute(value, 'ctx', pairs)]
  transfers between devices with their start and end apart: 24 -> 25, of which waited for: 10 -> 13; matrix products, arithmetic and copies ran while one was open for 0% -> 0% of each run, Pallas kernels for 17% -> 17%
where the time goes in v6:
time: 81.2 us; the launch traced here: 81 us
  waiting for transfers between devices  43.7 us (54%)
  starting transfers between devices  20.3 us (25%)
  Pallas kernels  16.7 us (21%)
    ppermute x22, waiting for transfers between devices, swap(): return lax.ppermute(value, 'ctx', pairs)  43.3 us
    ppermute x22, starting transfers between devices, swap(): return lax.ppermute(value, 'ctx', pairs)  18.4 us
    pallas_call x2, Pallas kernels, per_device_fast(): call(functools.partial(attention_kernel, n), [(2 * length, share)], [pl.B...  4.79 us
    pallas_call x2, Pallas kernels, per_device_fast(): call(project_kernel, [(length, 2 * wide)] * 4, vmem(1 + len(blocks)), nam...  3.59 us
    ppermute x3, starting transfers between devices, swap_groups(): return lax.ppermute(value, 'groups', [(0, 1), (1, 0)])  1.9 us
    pallas_call x1, Pallas kernels, per_device_fast(): call(functools.partial(pack_kernel, (1, 0)), [(3 * length, share)] * 2, a...  1.8 us
    pallas_call x1, Pallas kernels, per_device_fast(): call(functools.partial(pack_kernel, (2, 3)), [(3 * length, share)] * 2, a...  1.8 us
    pallas_call x1, Pallas kernels, per_device_fast(): call(place_kernel, [(length, 16 * wide)], anywhere(8), anywhere(1), scrat...  1.63 us
  transfers between devices with their start and end apart: 25, of which 13 were waited for; matrix products, arithmetic and copies ran while one was open for 0% of the time, Pallas kernels for 17%

profile of v6, /device:TPU:0, one launch (start us, length us, event | category | flops | bytes accessed | tf_op | source)
XLA Modules:
  0.0 81.0 jit_solution(17320611832746162907)
XLA Ops:
  0.0 0.1 pad_add_fusion.place_ref
  0.1 1.6 %pack.1.other_ref = bf16[1024,256]{1,0:T(8,128)(2,1)S(1)} custom-call(s32[3]{0:T(128)S(1)} %pad_add_fusion.place_ref, bf16[128,2048]{1,0:T(8,128)(2,1)} %q_ref.5, bf16[128,2048]{1,0:T(8,128)(2,1)} %k_ref.5, bf16[128,2048]{1,0:T(8,128)(2,1)} %v_ref.5, bf16[2048,256]{1,0:T(8,128)(2,1)} %refs_0_.1), custom_call_target="tpu_custom_call" | custom-call | tf_op jit(solution)/shard_map/pack/pallas_call | solution.py:219
  1.7 3.1 %collective-permute-start.4 = (bf16[1024,256]{1,0:T(8,128)(2,1)S(1)}, bf16[1024,256]{1,0:T(8,128)(2,1)S(1)}, u32[]{:S(2)}, u32[]{:S(2)}) collective-permute-start(bf16[1024,256]{1,0:T(8,128)(2,1)S(1)} %pack.1.other_ref), channel_id=1, source_target_pairs={{0,4},{1,5},{2,6},{3,7},{4,0},{5,1},{6,2},{7,3},{8,12},{9,13},{10,... | collective-permute-start | bytes 1572872 | tf_op jit(solution)/shard_map/ppermute | solution.py:20
  4.8 2.6 %collective-permute-start.3 = (bf16[1024,256]{1,0:T(8,128)(2,1)S(1)}, bf16[1024,256]{1,0:T(8,128)(2,1)S(1)}, u32[]{:S(2)}, u32[]{:S(2)}) collective-permute-start(bf16[1024,256]{1,0:T(8,128)(2,1)S(1)} %pack.1.other_ref), channel_id=1, source_target_pairs={{0,8},{1,9},{2,10},{3,11},{4,12},{5,13},{6,14},{7,15},{8,0},{9,1},... | collective-permute-start | bytes 1572872 | tf_op jit(solution)/shard_map/ppermute | solution.py:20
  7.4 1.8 %pack0.1 = (bf16[384,512]{1,0:T(8,128)(2,1)S(1)}, bf16[384,512]{1,0:T(8,128)(2,1)S(1)}) custom-call(s32[3]{0:T(128)S(1)} %pad_add_fusion.place_ref, bf16[128,2048]{1,0:T(8,128)(2,1)} %q_ref.5, bf16[128,2048]{1,0:T(8,128)(2,1)} %k_ref.5, bf16[128,2048]{1,0:T(8,128)(2,1)} %v_ref.5, bf16[1024,256]{1,0:T(8,128)(2,1)S(1)} %pack.1.other_ref), custom_call_target="tpu_custom_call" | custom-call | tf_op jit(solution)/shard_map/pack0/pallas_call | solution.py:226
  9.2 0.5 collective-permute-start.2
  9.6 1.2 %collective-permute-start.1 = (bf16[384,512]{1,0:T(8,128)(2,1)S(1)}, bf16[384,512]{1,0:T(8,128)(2,1)S(1)}, u32[]{:S(2)}, u32[]{:S(2)}) collective-permute-start(bf16[384,512]{1,0:T(8,128)(2,1)S(1)} %get-tuple-element.30.other_ref), channel_id=1, source_target_pairs={{0,2},{1,3},{2,0},{3,1},{4,6},{5,7},{6,4},{7,5},{8,10},{9,11},{10,... | collective-permute-start | bytes 1179656 | tf_op jit(solution)/shard_map/ppermute | solution.py:20
  10.8 1.8 %pack1.1 = (bf16[384,512]{1,0:T(8,128)(2,1)S(1)}, bf16[384,512]{1,0:T(8,128)(2,1)S(1)}) custom-call(s32[3]{0:T(128)S(1)} %pad_add_fusion.place_ref, bf16[128,2048]{1,0:T(8,128)(2,1)} %q_ref.5, bf16[128,2048]{1,0:T(8,128)(2,1)} %k_ref.5, bf16[128,2048]{1,0:T(8,128)(2,1)} %v_ref.5, bf16[384,512]{1,0:T(8,128)(2,1)S(1)} %get-tuple-element.30.other_ref), custom_call_target="tpu_custom_call" | custom-call | flops 2000000000 | bytes 40000000 | tf_op jit(solution)/shard_map/pack1/pallas_call | solution.py:233
  12.7 0.3 collective-permute-start
  13.0 7.6 %collective-permute-done.2.a3.refs_3_ = bf16[384,512]{1,0:T(8,128)(2,1)S(1)} collective-permute-done((bf16[384,512]{1,0:T(8,128)(2,1)S(1)}, bf16[384,512]{1,0:T(8,128)(2,1)S(1)}, u32[]{:S(2)}, u32[]{:S(2)}) %collective-permute-start.2) | collective-permute-done | bytes 393248 | tf_op jit(solution)/shard_map/ppermute | solution.py:20
  20.6 8.5 %collective-permute-done.1.a2.refs_2_ = bf16[384,512]{1,0:T(8,128)(2,1)S(1)} collective-permute-done((bf16[384,512]{1,0:T(8,128)(2,1)S(1)}, bf16[384,512]{1,0:T(8,128)(2,1)S(1)}, u32[]{:S(2)}, u32[]{:S(2)}) %collective-permute-start.1) | collective-permute-done | bytes 393248 | tf_op jit(solution)/shard_map/ppermute | solution.py:20
  29.1 0.0 collective-permute-done.a1.refs_1_
  29.1 0.8 %coarse.1 = (bf16[256,512]{1,0:T(8,128)(2,1)S(1)}, bf16[128,512]{1,0:T(8,128)(2,1)S(1)}) custom-call(s32[3]{0:T(128)S(1)} %pad_add_fusion.place_ref, bf16[384,512]{1,0:T(8,128)(2,1)S(1)} %get-tuple-element.31.a0.refs_0_.refs_7_, bf16[384,512]{1,0:T(8,128)(2,1)S(1)} %collective-permute-done.a1.refs_1_, ...), custom_call_target="tpu_custom_call" | custom-call | tf_op jit(solution)/shard_map/coarse/pallas_call | solution.py:244
  29.9 0.0 collective-permute-done.4.refs_0_
  29.9 0.4 collective-permute-done.3.refs_1_
  30.3 0.4 collective-permute-start.5
  30.8 1.5 %collective-permute-start.15 = (bf16[1024,256]{1,0:T(8,128)(2,1)S(1)}, bf16[1024,256]{1,0:T(8,128)(2,1)S(1)}, u32[]{:S(2)}, u32[]{:S(2)}) collective-permute-start(bf16[1024,256]{1,0:T(8,128)(2,1)S(1)} %collective-permute-done.3.refs_1_), channel_id=1, source_target_pairs={{0,16},{16,0},{1,17},{17,1},{2,18},{18,2},{3,19},{19,3},{4,20},{20... | collective-permute-start | bytes 1572872 | tf_op jit(solution)/shard_map/ppermute | solution.py:24
  32.3 2.0 %collective-permute-start.7 = (bf16[128,512]{1,0:T(8,128)(2,1)S(1)}, bf16[128,512]{1,0:T(8,128)(2,1)S(1)}, u32[]{:S(2)}, u32[]{:S(2)}) collective-permute-start(bf16[128,512]{1,0:T(8,128)(2,1)S(1)} %get-tuple-element.37), channel_id=1, source_target_pairs={{0,12},{1,13},{2,14},{3,15},{4,8},{5,9},{6,10},{7,11},{8,4},{9,5},... | collective-permute-start | bytes 393224 | tf_op jit(solution)/shard_map/ppermute | solution.py:20
  34.3 1.0 %collective-permute-start.6 = (bf16[128,512]{1,0:T(8,128)(2,1)S(1)}, bf16[128,512]{1,0:T(8,128)(2,1)S(1)}, u32[]{:S(2)}, u32[]{:S(2)}) collective-permute-start(bf16[128,512]{1,0:T(8,128)(2,1)S(1)} %get-tuple-element.37), channel_id=1, source_target_pairs={{0,8},{1,9},{2,10},{3,11},{4,12},{5,13},{6,14},{7,15},{8,0},{9,1},... | collective-permute-start | bytes 393224 | tf_op jit(solution)/shard_map/ppermute | solution.py:20
  35.3 5.6 %collective-permute-done.5.refs_4_ = bf16[256,512]{1,0:T(8,128)(2,1)S(1)} collective-permute-done((bf16[256,512]{1,0:T(8,128)(2,1)S(1)}, bf16[256,512]{1,0:T(8,128)(2,1)S(1)}, u32[]{:S(2)}, u32[]{:S(2)}) %collective-permute-start.5) | collective-permute-done | bytes 262176 | tf_op jit(solution)/shard_map/ppermute | solution.py:20
  40.9 0.0 collective-permute-start.9
  40.9 1.9 %collective-permute-done.7.refs_6_ = bf16[128,512]{1,0:T(8,128)(2,1)S(1)} collective-permute-done((bf16[128,512]{1,0:T(8,128)(2,1)S(1)}, bf16[128,512]{1,0:T(8,128)(2,1)S(1)}, u32[]{:S(2)}, u32[]{:S(2)}) %collective-permute-start.7) | collective-permute-done | bytes 131104 | tf_op jit(solution)/shard_map/ppermute | solution.py:20
  42.9 3.4 %collective-permute-done.6.refs_5_ = bf16[128,512]{1,0:T(8,128)(2,1)S(1)} collective-permute-done((bf16[128,512]{1,0:T(8,128)(2,1)S(1)}, bf16[128,512]{1,0:T(8,128)(2,1)S(1)}, u32[]{:S(2)}, u32[]{:S(2)}) %collective-permute-start.6) | collective-permute-done | bytes 131104 | tf_op jit(solution)/shard_map/ppermute | solution.py:20
  46.3 0.0 copy-done.1
  46.3 2.4 %attend0.1.refs_7_.refs_0_ = bf16[256,512]{1,0:T(8,128)(2,1)S(1)} custom-call(s32[3]{0:T(128)S(1)} %pad_add_fusion.place_ref, s32[16]{0:T(128)S(1)} %copy-done.1, bf16[384,512]{1,0:T(8,128)(2,1)S(1)} %get-tuple-element.31.a0.refs_0_.refs_7_, bf16[384,512]{1,0:T(8,128)(2,1)S(1)} %collective-permute-done.a1.refs_1_, ...), custom_call_target="tpu_custom_call" | custom-call | flops 2000000000 | bytes 40000000 | tf_op jit(solution)/shard_map/attend0/pallas_call | solution.py:258
  48.7 1.1 %collective-permute-start.8 = (bf16[256,512]{1,0:T(8,128)(2,1)S(1)}, bf16[256,512]{1,0:T(8,128)(2,1)S(1)}, u32[]{:S(2)}, u32[]{:S(2)}) collective-permute-start(bf16[256,512]{1,0:T(8,128)(2,1)S(1)} %attend0.1.refs_7_.refs_0_), channel_id=1, source_target_pairs={{0,2},{1,3},{2,0},{3,1},{4,6},{5,7},{6,4},{7,5},{8,10},{9,11},{10,... | collective-permute-start | bytes 786440 | tf_op jit(solution)/shard_map/ppermute | solution.py:20
  49.8 0.0 collective-permute-done.15.refs_2_
  49.8 0.0 collective-permute-start.19
  49.8 2.4 %attend1.1.refs_1_ = bf16[256,512]{1,0:T(8,128)(2,1)S(1)} custom-call(s32[3]{0:T(128)S(1)} %pad_add_fusion.place_ref, s32[16]{0:T(128)S(1)} %copy-done.1, bf16[384,512]{1,0:T(8,128)(2,1)S(1)} %get-tuple-element.31.a0.refs_0_.refs_7_, bf16[384,512]{1,0:T(8,128)(2,1)S(1)} %collective-permute-done.a1.refs_1_, ...), custom_call_target="tpu_custom_call" | custom-call | flops 2000000000 | bytes 40000000 | tf_op jit(solution)/shard_map/attend1/pallas_call | solution.py:258
  52.2 1.1 %collective-permute-start.12 = (bf16[256,512]{1,0:T(8,128)(2,1)S(1)}, bf16[256,512]{1,0:T(8,128)(2,1)S(1)}, u32[]{:S(2)}, u32[]{:S(2)}) collective-permute-start(bf16[256,512]{1,0:T(8,128)(2,1)S(1)} %attend1.1.refs_1_), channel_id=1, source_target_pairs={{0,2},{1,3},{2,0},{3,1},{4,6},{5,7},{6,4},{7,5},{8,10},{9,11},{10,... | collective-permute-start | bytes 786440 | tf_op jit(solution)/shard_map/ppermute | solution.py:20
  53.4 3.8 %collective-permute-done.8.refs_4_ = bf16[256,512]{1,0:T(8,128)(2,1)S(1)} collective-permute-done((bf16[256,512]{1,0:T(8,128)(2,1)S(1)}, bf16[256,512]{1,0:T(8,128)(2,1)S(1)}, u32[]{:S(2)}, u32[]{:S(2)}) %collective-permute-start.8) | collective-permute-done | bytes 262176 | tf_op jit(solution)/shard_map/ppermute | solution.py:20
  57.2 0.0 collective-permute-done.9.refs_2_
  57.2 0.0 collective-permute-start.13
  57.2 0.5 collective-permute-start.10
  57.7 0.0 collective-permute-start.11
  57.7 2.3 %collective-permute-done.12.refs_5_ = bf16[256,512]{1,0:T(8,128)(2,1)S(1)} collective-permute-done((bf16[256,512]{1,0:T(8,128)(2,1)S(1)}, bf16[256,512]{1,0:T(8,128)(2,1)S(1)}, u32[]{:S(2)}, u32[]{:S(2)}) %collective-permute-start.12) | collective-permute-done | bytes 262176 | tf_op jit(solution)/shard_map/ppermute | solution.py:20
  60.0 0.0 collective-permute-done.13.refs_6_
  60.0 0.0 collective-permute-start.14
  60.0 0.6 collective-permute-start.21
  60.7 0.0 collective-permute-done.19.refs_1_
  60.7 0.0 copy-start
  60.7 0.4 collective-permute-start.20
  61.1 0.0 collective-permute-done.10.refs_2_
  61.1 0.0 collective-permute-done.11.refs_3_
  61.1 0.4 collective-permute-done.14.refs_7_
  61.6 0.7 gather.1.rows_ref
  62.3 0.0 copy-done
  62.3 1.8 %project0.1 = (bf16[128,512]{1,0:T(8,128)(2,1)S(1)}, bf16[128,512]{1,0:T(8,128)(2,1)S(1)}, bf16[128,512]{1,0:T(8,128)(2,1)S(1)}, bf16[128,512]{1,0:T(8,128)(2,1)S(1)}) custom-call(s32[3]{0:T(128)S(1)} %pad_add_fusion.place_ref, bf16[512,2048]{1,0:T(8,128)(2,1)S(1)} %gather.1.rows_ref, bf16[2048,256]{1,0:T(8,128)(2,1)S(1)} %copy-done, ...), custom_call_target="tpu_custom_call" | custom-call | tf_op jit(solution)/shard_map/project0/pallas_call | solution.py:278
  64.1 0.2 collective-permute-start.16
  64.3 1.4 %collective-permute-start.17 = (bf16[128,512]{1,0:T(8,128)(2,1)S(1)}, bf16[128,512]{1,0:T(8,128)(2,1)S(1)}, u32[]{:S(2)}, u32[]{:S(2)}) collective-permute-start(bf16[128,512]{1,0:T(8,128)(2,1)S(1)} %get-tuple-element.46), channel_id=1, source_target_pairs={{0,2},{1,3},{2,0},{3,1},{4,6},{5,7},{6,4},{7,5},{8,10},{9,11},{10,... | collective-permute-start | bytes 393224 | tf_op jit(solution)/shard_map/ppermute | solution.py:20
  65.7 0.3 collective-permute-start.18
  66.0 2.8 %collective-permute-done.21.refs_4_ = bf16[512,256]{1,0:T(8,128)(2,1)S(1)} collective-permute-done((bf16[512,256]{1,0:T(8,128)(2,1)S(1)}, bf16[512,256]{1,0:T(8,128)(2,1)S(1)}, u32[]{:S(2)}, u32[]{:S(2)}) %collective-permute-start.21) | collective-permute-done | bytes 262176 | tf_op jit(solution)/shard_map/ppermute | solution.py:20
  68.8 0.4 collective-permute-done.20.refs_3_
  69.2 1.8 %project1.1 = (bf16[128,512]{1,0:T(8,128)(2,1)S(1)}, bf16[128,512]{1,0:T(8,128)(2,1)S(1)}, bf16[128,512]{1,0:T(8,128)(2,1)S(1)}, bf16[128,512]{1,0:T(8,128)(2,1)S(1)}) custom-call(s32[3]{0:T(128)S(1)} %pad_add_fusion.place_ref, bf16[512,2048]{1,0:T(8,128)(2,1)S(1)} %gather.1.rows_ref, bf16[1024,256]{1,0:T(8,128)(2,1)S(1)} %collective-permute-done.4.refs_0_, ...), custom_call_target="tpu_custom_call" | custom-call | tf_op jit(solution)/shard_map/project1/pallas_call | solution.py:278
  71.0 0.1 collective-permute-start.22
  71.1 1.2 %collective-permute-start.23 = (bf16[128,512]{1,0:T(8,128)(2,1)S(1)}, bf16[128,512]{1,0:T(8,128)(2,1)S(1)}, u32[]{:S(2)}, u32[]{:S(2)}) collective-permute-start(bf16[128,512]{1,0:T(8,128)(2,1)S(1)} %get-tuple-element.53), channel_id=1, source_target_pairs={{0,2},{1,3},{2,0},{3,1},{4,6},{5,7},{6,4},{7,5},{8,10},{9,11},{10,... | collective-permute-start | bytes 393224 | tf_op jit(solution)/shard_map/ppermute | solution.py:20
  72.3 0.0 collective-permute-done.16.refs_1_
  72.3 0.6 collective-permute-start.24
  73.0 0.0 collective-permute-done.17.refs_2_
  73.0 0.0 collective-permute-done.18.refs_3_
  73.0 0.0 collective-permute-done.22.refs_5_
  73.0 4.5 %collective-permute-done.23.refs_6_ = bf16[128,512]{1,0:T(8,128)(2,1)S(1)} collective-permute-done((bf16[128,512]{1,0:T(8,128)(2,1)S(1)}, bf16[128,512]{1,0:T(8,128)(2,1)S(1)}, u32[]{:S(2)}, u32[]{:S(2)}) %collective-permute-start.23) | collective-permute-done | bytes 131104 | tf_op jit(solution)/shard_map/ppermute | solution.py:20
  77.5 1.9 %collective-permute-done.24.refs_7_ = bf16[128,512]{1,0:T(8,128)(2,1)S(1)} collective-permute-done((bf16[128,512]{1,0:T(8,128)(2,1)S(1)}, bf16[128,512]{1,0:T(8,128)(2,1)S(1)}, u32[]{:S(2)}, u32[]{:S(2)}) %collective-permute-start.24) | collective-permute-done | bytes 131104 | tf_op jit(solution)/shard_map/ppermute | solution.py:20
  79.4 1.6 %place.1 = bf16[128,4096]{1,0:T(8,128)(2,1)} custom-call(s32[3]{0:T(128)S(1)} %pad_add_fusion.place_ref, bf16[128,512]{1,0:T(8,128)(2,1)S(1)} %get-tuple-element.44.refs_0_, bf16[128,512]{1,0:T(8,128)(2,1)S(1)} %collective-permute-done.16.refs_1_, bf16[128,512]{1,0:T(8,128)(2,1)S(1)} %collective-permute-done.17.refs_2_, ...), custom_call_target="tpu_custom_call" | custom-call | tf_op jit(solution)/shard_map/place/pallas_call | solution.py:282
  (3 shorter events, 0.0 us)
Async XLA Ops:
  1.7 28.2 %collective-permute-start.4 = (bf16[1024,256]{1,0:T(8,128)(2,1)S(1)}, bf16[1024,256]{1,0:T(8,128)(2,1)S(1)}, u32[]{:S(2)}, u32[]{:S(2)}) collective-permute-start(bf16[1024,256]{1,0:T(8,128)(2,1)S(1)} %pack.1.other_ref), channel_id=1, source_target_pairs={{0,4},{1,5},{2,6},{3,7},{4,0},{5,1},{6,2},{7,3},{8,12},{9,13},{10,... | collective-permute-start | bytes 1572872 | tf_op jit(solution)/shard_map/ppermute | solution.py:20
  4.8 25.6 %collective-permute-start.3 = (bf16[1024,256]{1,0:T(8,128)(2,1)S(1)}, bf16[1024,256]{1,0:T(8,128)(2,1)S(1)}, u32[]{:S(2)}, u32[]{:S(2)}) collective-permute-start(bf16[1024,256]{1,0:T(8,128)(2,1)S(1)} %pack.1.other_ref), channel_id=1, source_target_pairs={{0,8},{1,9},{2,10},{3,11},{4,12},{5,13},{6,14},{7,15},{8,0},{9,1},... | collective-permute-start | bytes 1572872 | tf_op jit(solution)/shard_map/ppermute | solution.py:20
  9.2 11.4 %collective-permute-start.2 = (bf16[384,512]{1,0:T(8,128)(2,1)S(1)}, bf16[384,512]{1,0:T(8,128)(2,1)S(1)}, u32[]{:S(2)}, u32[]{:S(2)}) collective-permute-start(bf16[384,512]{1,0:T(8,128)(2,1)S(1)} %get-tuple-element.33), channel_id=1, source_target_pairs={{0,3},{1,2},{2,1},{3,0},{4,7},{5,6},{6,5},{7,4},{8,11},{9,10},{10,... | collective-permute-start | bytes 1179656 | tf_op jit(solution)/shard_map/ppermute | solution.py:20
  9.6 36.7 %copy-start.1 = (s32[16]{0:T(128)S(1)}, s32[16]{0:T(128)}, u32[]{:S(2)}) copy-start(s32[16]{0:T(128)} %doc_ref.3) | copy-start | bytes 196
  9.6 19.4 %collective-permute-start.1 = (bf16[384,512]{1,0:T(8,128)(2,1)S(1)}, bf16[384,512]{1,0:T(8,128)(2,1)S(1)}, u32[]{:S(2)}, u32[]{:S(2)}) collective-permute-start(bf16[384,512]{1,0:T(8,128)(2,1)S(1)} %get-tuple-element.30.other_ref), channel_id=1, source_target_pairs={{0,2},{1,3},{2,0},{3,1},{4,6},{5,7},{6,4},{7,5},{8,10},{9,11},{10,... | collective-permute-start | bytes 1179656 | tf_op jit(solution)/shard_map/ppermute | solution.py:20
  12.7 16.4 %collective-permute-start = (bf16[384,512]{1,0:T(8,128)(2,1)S(1)}, bf16[384,512]{1,0:T(8,128)(2,1)S(1)}, u32[]{:S(2)}, u32[]{:S(2)}) collective-permute-start(bf16[384,512]{1,0:T(8,128)(2,1)S(1)} %get-tuple-element.32), channel_id=1, source_target_pairs={{0,1},{1,0},{2,3},{3,2},{4,5},{5,4},{6,7},{7,6},{8,9},{9,8},{10,11... | collective-permute-start | bytes 1179656 | tf_op jit(solution)/shard_map/ppermute | solution.py:20
  30.3 10.6 %collective-permute-start.5 = (bf16[256,512]{1,0:T(8,128)(2,1)S(1)}, bf16[256,512]{1,0:T(8,128)(2,1)S(1)}, u32[]{:S(2)}, u32[]{:S(2)}) collective-permute-start(bf16[256,512]{1,0:T(8,128)(2,1)S(1)} %get-tuple-element.36), channel_id=1, source_target_pairs={{0,4},{1,5},{2,6},{3,7},{4,0},{5,1},{6,2},{7,3},{8,12},{9,13},{10,... | collective-permute-start | bytes 786440 | tf_op jit(solution)/shard_map/ppermute | solution.py:20
  30.8 19.1 %collective-permute-start.15 = (bf16[1024,256]{1,0:T(8,128)(2,1)S(1)}, bf16[1024,256]{1,0:T(8,128)(2,1)S(1)}, u32[]{:S(2)}, u32[]{:S(2)}) collective-permute-start(bf16[1024,256]{1,0:T(8,128)(2,1)S(1)} %collective-permute-done.3.refs_1_), channel_id=1, source_target_pairs={{0,16},{16,0},{1,17},{17,1},{2,18},{18,2},{3,19},{19,3},{4,20},{20... | collective-permute-start | bytes 1572872 | tf_op jit(solution)/shard_map/ppermute | solution.py:24
  32.3 10.6 %collective-permute-start.7 = (bf16[128,512]{1,0:T(8,128)(2,1)S(1)}, bf16[128,512]{1,0:T(8,128)(2,1)S(1)}, u32[]{:S(2)}, u32[]{:S(2)}) collective-permute-start(bf16[128,512]{1,0:T(8,128)(2,1)S(1)} %get-tuple-element.37), channel_id=1, source_target_pairs={{0,12},{1,13},{2,14},{3,15},{4,8},{5,9},{6,10},{7,11},{8,4},{9,5},... | collective-permute-start | bytes 393224 | tf_op jit(solution)/shard_map/ppermute | solution.py:20
  34.3 12.0 %collective-permute-start.6 = (bf16[128,512]{1,0:T(8,128)(2,1)S(1)}, bf16[128,512]{1,0:T(8,128)(2,1)S(1)}, u32[]{:S(2)}, u32[]{:S(2)}) collective-permute-start(bf16[128,512]{1,0:T(8,128)(2,1)S(1)} %get-tuple-element.37), channel_id=1, source_target_pairs={{0,8},{1,9},{2,10},{3,11},{4,12},{5,13},{6,14},{7,15},{8,0},{9,1},... | collective-permute-start | bytes 393224 | tf_op jit(solution)/shard_map/ppermute | solution.py:20
  40.9 16.3 %collective-permute-start.9 = (bf16[1024,256]{1,0:T(8,128)(2,1)S(1)}, bf16[1024,256]{1,0:T(8,128)(2,1)S(1)}, u32[]{:S(2)}, u32[]{:S(2)}) collective-permute-start(bf16[1024,256]{1,0:T(8,128)(2,1)S(1)} %collective-permute-done.3.refs_1_), channel_id=1, source_target_pairs={{0,4},{1,5},{2,6},{3,7},{4,0},{5,1},{6,2},{7,3},{8,12},{9,13},{10,... | collective-permute-start | bytes 1572872 | tf_op jit(solution)/shard_map/ppermute | solution.py:20
  48.7 8.5 %collective-permute-start.8 = (bf16[256,512]{1,0:T(8,128)(2,1)S(1)}, bf16[256,512]{1,0:T(8,128)(2,1)S(1)}, u32[]{:S(2)}, u32[]{:S(2)}) collective-permute-start(bf16[256,512]{1,0:T(8,128)(2,1)S(1)} %attend0.1.refs_7_.refs_0_), channel_id=1, source_target_pairs={{0,2},{1,3},{2,0},{3,1},{4,6},{5,7},{6,4},{7,5},{8,10},{9,11},{10,... | collective-permute-start | bytes 786440 | tf_op jit(solution)/shard_map/ppermute | solution.py:20
  49.8 10.8 %collective-permute-start.19 = (bf16[1024,256]{1,0:T(8,128)(2,1)S(1)}, bf16[1024,256]{1,0:T(8,128)(2,1)S(1)}, u32[]{:S(2)}, u32[]{:S(2)}) collective-permute-start(bf16[1024,256]{1,0:T(8,128)(2,1)S(1)} %collective-permute-done.4.refs_0_), channel_id=1, source_target_pairs={{0,16},{16,0},{1,17},{17,1},{2,18},{18,2},{3,19},{19,3},{4,20},{20... | collective-permute-start | bytes 1572872 | tf_op jit(solution)/shard_map/ppermute | solution.py:24
  52.2 7.8 %collective-permute-start.12 = (bf16[256,512]{1,0:T(8,128)(2,1)S(1)}, bf16[256,512]{1,0:T(8,128)(2,1)S(1)}, u32[]{:S(2)}, u32[]{:S(2)}) collective-permute-start(bf16[256,512]{1,0:T(8,128)(2,1)S(1)} %attend1.1.refs_1_), channel_id=1, source_target_pairs={{0,2},{1,3},{2,0},{3,1},{4,6},{5,7},{6,4},{7,5},{8,10},{9,11},{10,... | collective-permute-start | bytes 786440 | tf_op jit(solution)/shard_map/ppermute | solution.py:20
  57.2 2.8 %collective-permute-start.13 = (bf16[256,512]{1,0:T(8,128)(2,1)S(1)}, bf16[256,512]{1,0:T(8,128)(2,1)S(1)}, u32[]{:S(2)}, u32[]{:S(2)}) collective-permute-start(bf16[256,512]{1,0:T(8,128)(2,1)S(1)} %collective-permute-done.8.refs_4_), channel_id=1, source_target_pairs={{0,1},{1,0},{2,3},{3,2},{4,5},{5,4},{6,7},{7,6},{8,9},{9,8},{10,11... | collective-permute-start | bytes 786440 | tf_op jit(solution)/shard_map/ppermute | solution.py:20
  57.2 3.9 %collective-permute-start.10 = (bf16[256,512]{1,0:T(8,128)(2,1)S(1)}, bf16[256,512]{1,0:T(8,128)(2,1)S(1)}, u32[]{:S(2)}, u32[]{:S(2)}) collective-permute-start(bf16[256,512]{1,0:T(8,128)(2,1)S(1)} %attend0.1.refs_7_.refs_0_), channel_id=1, source_target_pairs={{0,1},{1,0},{2,3},{3,2},{4,5},{5,4},{6,7},{7,6},{8,9},{9,8},{10,11... | collective-permute-start | bytes 786440 | tf_op jit(solution)/shard_map/ppermute | solution.py:20
  57.7 3.4 %collective-permute-start.11 = (bf16[256,512]{1,0:T(8,128)(2,1)S(1)}, bf16[256,512]{1,0:T(8,128)(2,1)S(1)}, u32[]{:S(2)}, u32[]{:S(2)}) collective-permute-start(bf16[256,512]{1,0:T(8,128)(2,1)S(1)} %attend1.1.refs_1_), channel_id=1, source_target_pairs={{0,1},{1,0},{2,3},{3,2},{4,5},{5,4},{6,7},{7,6},{8,9},{9,8},{10,11... | collective-permute-start | bytes 786440 | tf_op jit(solution)/shard_map/ppermute | solution.py:20
  60.0 1.5 %collective-permute-start.14 = (bf16[256,512]{1,0:T(8,128)(2,1)S(1)}, bf16[256,512]{1,0:T(8,128)(2,1)S(1)}, u32[]{:S(2)}, u32[]{:S(2)}) collective-permute-start(bf16[256,512]{1,0:T(8,128)(2,1)S(1)} %collective-permute-done.12.refs_5_), channel_id=1, source_target_pairs={{0,1},{1,0},{2,3},{3,2},{4,5},{5,4},{6,7},{7,6},{8,9},{9,8},{10,11... | collective-permute-start | bytes 786440 | tf_op jit(solution)/shard_map/ppermute | solution.py:20
  60.0 8.8 %collective-permute-start.21 = (bf16[512,256]{1,0:T(8,128)(2,1)S(1)}, bf16[512,256]{1,0:T(8,128)(2,1)S(1)}, u32[]{:S(2)}, u32[]{:S(2)}) collective-permute-start(bf16[512,256]{1,0:T(8,128)(2,1)S(1)} %slice.7), channel_id=1, source_target_pairs={{0,4},{1,5},{2,6},{3,7},{4,0},{5,1},{6,2},{7,3},{8,12},{9,13},{10,... | collective-permute-start | bytes 786440 | tf_op jit(solution)/shard_map/ppermute | solution.py:20
  60.7 1.6 %copy-start = (bf16[2048,256]{1,0:T(8,128)(2,1)S(1)}, bf16[2048,256]{1,0:T(8,128)(2,1)}, u32[]{:S(2)}) copy-start(bf16[2048,256]{1,0:T(8,128)(2,1)} %refs_0_.1) | copy-start | bytes 3145732
  60.7 8.5 %collective-permute-start.20 = (bf16[512,256]{1,0:T(8,128)(2,1)S(1)}, bf16[512,256]{1,0:T(8,128)(2,1)S(1)}, u32[]{:S(2)}, u32[]{:S(2)}) collective-permute-start(bf16[512,256]{1,0:T(8,128)(2,1)S(1)} %slice.6), channel_id=1, source_target_pairs={{0,16},{16,0},{1,17},{17,1},{2,18},{18,2},{3,19},{19,3},{4,20},{20... | collective-permute-start | bytes 786440 | tf_op jit(solution)/shard_map/ppermute | solution.py:24
  64.1 8.2 %collective-permute-start.16 = (bf16[128,512]{1,0:T(8,128)(2,1)S(1)}, bf16[128,512]{1,0:T(8,128)(2,1)S(1)}, u32[]{:S(2)}, u32[]{:S(2)}) collective-permute-start(bf16[128,512]{1,0:T(8,128)(2,1)S(1)} %get-tuple-element.45), channel_id=1, source_target_pairs={{0,1},{1,0},{2,3},{3,2},{4,5},{5,4},{6,7},{7,6},{8,9},{9,8},{10,11... | collective-permute-start | bytes 393224 | tf_op jit(solution)/shard_map/ppermute | solution.py:20
  64.3 8.7 %collective-permute-start.17 = (bf16[128,512]{1,0:T(8,128)(2,1)S(1)}, bf16[128,512]{1,0:T(8,128)(2,1)S(1)}, u32[]{:S(2)}, u32[]{:S(2)}) collective-permute-start(bf16[128,512]{1,0:T(8,128)(2,1)S(1)} %get-tuple-element.46), channel_id=1, source_target_pairs={{0,2},{1,3},{2,0},{3,1},{4,6},{5,7},{6,4},{7,5},{8,10},{9,11},{10,... | collective-permute-start | bytes 393224 | tf_op jit(solution)/shard_map/ppermute | solution.py:20
  65.7 7.3 %collective-permute-start.18 = (bf16[128,512]{1,0:T(8,128)(2,1)S(1)}, bf16[128,512]{1,0:T(8,128)(2,1)S(1)}, u32[]{:S(2)}, u32[]{:S(2)}) collective-permute-start(bf16[128,512]{1,0:T(8,128)(2,1)S(1)} %get-tuple-element.47), channel_id=1, source_target_pairs={{0,3},{1,2},{2,1},{3,0},{4,7},{5,6},{6,5},{7,4},{8,11},{9,10},{10,... | collective-permute-start | bytes 393224 | tf_op jit(solution)/shard_map/ppermute | solution.py:20
  71.0 2.0 %collective-permute-start.22 = (bf16[128,512]{1,0:T(8,128)(2,1)S(1)}, bf16[128,512]{1,0:T(8,128)(2,1)S(1)}, u32[]{:S(2)}, u32[]{:S(2)}) collective-permute-start(bf16[128,512]{1,0:T(8,128)(2,1)S(1)} %get-tuple-element.52), channel_id=1, source_target_pairs={{0,1},{1,0},{2,3},{3,2},{4,5},{5,4},{6,7},{7,6},{8,9},{9,8},{10,11... | collective-permute-start | bytes 393224 | tf_op jit(solution)/shard_map/ppermute | solution.py:20
  71.1 6.4 %collective-permute-start.23 = (bf16[128,512]{1,0:T(8,128)(2,1)S(1)}, bf16[128,512]{1,0:T(8,128)(2,1)S(1)}, u32[]{:S(2)}, u32[]{:S(2)}) collective-permute-start(bf16[128,512]{1,0:T(8,128)(2,1)S(1)} %get-tuple-element.53), channel_id=1, source_target_pairs={{0,2},{1,3},{2,0},{3,1},{4,6},{5,7},{6,4},{7,5},{8,10},{9,11},{10,... | collective-permute-start | bytes 393224 | tf_op jit(solution)/shard_map/ppermute | solution.py:20
  72.3 7.0 %collective-permute-start.24 = (bf16[128,512]{1,0:T(8,128)(2,1)S(1)}, bf16[128,512]{1,0:T(8,128)(2,1)S(1)}, u32[]{:S(2)}, u32[]{:S(2)}) collective-permute-start(bf16[128,512]{1,0:T(8,128)(2,1)S(1)} %get-tuple-element.54), channel_id=1, source_target_pairs={{0,3},{1,2},{2,1},{3,0},{4,7},{5,6},{6,5},{7,4},{8,11},{9,10},{10,... | collective-permute-start | bytes 393224 | tf_op jit(solution)/shard_map/ppermute | solution.py:20

commit v7 on v6

--- a/solution.py
+++ b/solution.py
@@ -179,19 +179,15 @@
         q += 1
 
 
-def place_kernel(place_ref, *refs):
-    sources, out_ref, sems = refs[:-2], refs[-2], refs[-1]
-    wide = out_ref.shape[1] // 16
+def place_kernel(group, place_ref, *refs):
+    sources, out_ref, sems = refs[:4], refs[-2], refs[-1]
+    wide = sources[0].shape[1] // 2
     copies = []
-    for n, source in enumerate(sources):
-        masks = ((0, HIGH), (LOW, LOW | HIGH))[n // 4]
-        for q, mask in enumerate(masks):
-            at = pl.multiple_of(jnp.bitwise_xor(place_ref[2], mask | n % 4) * wide, wide)
-            copies.append(
-                pltpu.make_async_copy(
-                    source.at[:, q * wide : (q + 1) * wide], out_ref.at[:, pl.ds(at, wide)], sems.at[len(copies)]
-                )
-            )
+    for j, source in enumerate(sources):
+        for q, mask in enumerate(((0, HIGH), (LOW, LOW | HIGH))[group]):
+            at = pl.multiple_of(jnp.bitwise_xor(place_ref[2], mask | j) * wide, wide)
+            to = out_ref.at[:, pl.ds(at, wide)]
+            copies.append(pltpu.make_async_copy(source.at[:, q * wide : (q + 1) * wide], to, sems.at[2 * j + q]))
     run_copies(copies)
 
 
@@ -245,9 +241,10 @@
         coarse_kernel, [(2 * length, share), (length, share)], vmem(4), name="coarse"
     )(places, *own)
     third, fourth = after((third, fourth), (half_h, ours_l))
-    far = [swap(third, LOW), swap(fourth, HIGH), swap(fourth, LOW | HIGH)]
+    from_h, from_lh = swap(fourth, HIGH), swap(fourth, LOW | HIGH)
+    far = [swap(third, LOW), from_h, from_lh]
     other_h = swap_groups(after(half_h, third))
-    half_d = swap(after(half_h, far[0]), LOW)
+    half_d = swap(after(half_h, far[1]), LOW)
     other_l = swap_groups(after(ours_l, other_h))
     quarter = depth // 4
     other_d = [swap_groups(after(half_d, other_l)[:quarter]), swap(after(other_h, half_d)[quarter:], LOW)]
@@ -279,14 +276,17 @@
             places, rows, *blocks
         )
         received += [parts[0]] + [swap(parts[j], j) for j in (1, 2, 3)]
-    (out,) = call(
-        place_kernel,
-        [(length, 16 * wide)],
-        anywhere(8),
-        anywhere(1),
-        scratch_shapes=[pltpu.SemaphoreType.DMA((16,))],
-        name="place",
-    )(places, *received)
+    for n in range(2):
+        earlier = [] if n == 0 else [out]
+        (out,) = call(
+            functools.partial(place_kernel, n),
+            [(length, 16 * wide)],
+            anywhere(4 + len(earlier)),
+            anywhere(1),
+            scratch_shapes=[pltpu.SemaphoreType.DMA((8,))],
+            input_output_aliases={5: 0} if earlier else {},
+            name="place%d" % n,
+        )(places, *received[4 * n : 4 * n + 4], *earlier)
     return out
 
 

time: 81.2 us -> 80.2 us (0.988)
  waiting for transfers between devices: 43.7 us -> 37.4 us
  starting transfers between devices: 20.3 us -> 24.5 us
  Pallas kernels: 16.7 us -> 17.9 us
    ppermute x22, waiting for transfers between devices: 43.3 us -> 37.2 us  [swap(): return lax.ppermute(value, 'ctx', pairs)]
    ppermute x22, starting transfers between devices: 18.4 us -> 20.9 us  [swap(): return lax.ppermute(value, 'ctx', pairs)]
    ppermute x3, starting transfers between devices: 1.9 us -> 3.57 us  [swap_groups(): return lax.ppermute(value, 'groups', [(0, 1), (1, 0)])]
    pallas_call x1 -> x2, Pallas kernels: 1.63 us -> 2.79 us  [per_device_fast(): call(functools.partial(place_kernel, n), [(length, 16 * wide)], anywhere(...]
  transfers between devices with their start and end apart: 25 -> 25, of which waited for: 13 -> 12; matrix products, arithmetic and copies ran while one was open for 0% -> 0% of each run, Pallas kernels for 17% -> 19%
where the time goes in v7:
time: 80.2 us; the launch traced here: 80 us
  waiting for transfers between devices  37.4 us (47%)
  starting transfers between devices  24.5 us (31%)
  Pallas kernels  17.9 us (22%)
    ppermute x22, waiting for transfers between devices, swap(): return lax.ppermute(value, 'ctx', pairs)  37.2 us
    ppermute x22, starting transfers between devices, swap(): return lax.ppermute(value, 'ctx', pairs)  20.9 us
    pallas_call x2, Pallas kernels, per_device_fast(): call(functools.partial(attention_kernel, n), [(2 * length, share)], [pl.B...  4.77 us
    pallas_call x2, Pallas kernels, per_device_fast(): call(project_kernel, [(length, 2 * wide)] * 4, vmem(1 + len(blocks)), nam...  3.59 us
    ppermute x3, starting transfers between devices, swap_groups(): return lax.ppermute(value, 'groups', [(0, 1), (1, 0)])  3.57 us
    pallas_call x2, Pallas kernels, per_device_fast(): call(functools.partial(place_kernel, n), [(length, 16 * wide)], anywhere(...  2.79 us
    pallas_call x1, Pallas kernels, per_device_fast(): call(functools.partial(pack_kernel, (1, 0)), [(3 * length, share)] * 2, a...  1.8 us
    pallas_call x1, Pallas kernels, per_device_fast(): call(functools.partial(pack_kernel, (2, 3)), [(3 * length, share)] * 2, a...  1.8 us
  transfers between devices with their start and end apart: 25, of which 12 were waited for; matrix products, arithmetic and copies ran while one was open for 0% of the time, Pallas kernels for 19%

profile of v7, /device:TPU:0, one launch (start us, length us, event | category | flops | bytes accessed | tf_op | source)
XLA Modules:
  0.0 80.0 jit_solution(6306363123871546303)
XLA Ops:
  0.0 0.1 pad_add_fusion.place_ref
  0.1 1.6 %pack.1.other_ref = bf16[1024,256]{1,0:T(8,128)(2,1)S(1)} custom-call(s32[3]{0:T(128)S(1)} %pad_add_fusion.place_ref, bf16[128,2048]{1,0:T(8,128)(2,1)} %q_ref.5, bf16[128,2048]{1,0:T(8,128)(2,1)} %k_ref.5, bf16[128,2048]{1,0:T(8,128)(2,1)} %v_ref.5, bf16[2048,256]{1,0:T(8,128)(2,1)} %refs_0_.1), custom_call_target="tpu_custom_call" | custom-call | tf_op jit(solution)/shard_map/pack/pallas_call | solution.py:215
  1.7 3.1 %collective-permute-start.4 = (bf16[1024,256]{1,0:T(8,128)(2,1)S(1)}, bf16[1024,256]{1,0:T(8,128)(2,1)S(1)}, u32[]{:S(2)}, u32[]{:S(2)}) collective-permute-start(bf16[1024,256]{1,0:T(8,128)(2,1)S(1)} %pack.1.other_ref), channel_id=1, source_target_pairs={{0,4},{1,5},{2,6},{3,7},{4,0},{5,1},{6,2},{7,3},{8,12},{9,13},{10,... | collective-permute-start | bytes 1572872 | tf_op jit(solution)/shard_map/ppermute | solution.py:20
  4.8 2.6 %collective-permute-start.3 = (bf16[1024,256]{1,0:T(8,128)(2,1)S(1)}, bf16[1024,256]{1,0:T(8,128)(2,1)S(1)}, u32[]{:S(2)}, u32[]{:S(2)}) collective-permute-start(bf16[1024,256]{1,0:T(8,128)(2,1)S(1)} %pack.1.other_ref), channel_id=1, source_target_pairs={{0,8},{1,9},{2,10},{3,11},{4,12},{5,13},{6,14},{7,15},{8,0},{9,1},... | collective-permute-start | bytes 1572872 | tf_op jit(solution)/shard_map/ppermute | solution.py:20
  7.4 1.8 %pack0.1 = (bf16[384,512]{1,0:T(8,128)(2,1)S(1)}, bf16[384,512]{1,0:T(8,128)(2,1)S(1)}) custom-call(s32[3]{0:T(128)S(1)} %pad_add_fusion.place_ref, bf16[128,2048]{1,0:T(8,128)(2,1)} %q_ref.5, bf16[128,2048]{1,0:T(8,128)(2,1)} %k_ref.5, bf16[128,2048]{1,0:T(8,128)(2,1)} %v_ref.5, bf16[1024,256]{1,0:T(8,128)(2,1)S(1)} %pack.1.other_ref), custom_call_target="tpu_custom_call" | custom-call | tf_op jit(solution)/shard_map/pack0/pallas_call | solution.py:222
  9.2 0.5 collective-permute-start.2
  9.6 1.2 %collective-permute-start.1 = (bf16[384,512]{1,0:T(8,128)(2,1)S(1)}, bf16[384,512]{1,0:T(8,128)(2,1)S(1)}, u32[]{:S(2)}, u32[]{:S(2)}) collective-permute-start(bf16[384,512]{1,0:T(8,128)(2,1)S(1)} %get-tuple-element.30.other_ref), channel_id=1, source_target_pairs={{0,2},{1,3},{2,0},{3,1},{4,6},{5,7},{6,4},{7,5},{8,10},{9,11},{10,... | collective-permute-start | bytes 1179656 | tf_op jit(solution)/shard_map/ppermute | solution.py:20
  10.8 1.8 %pack1.1 = (bf16[384,512]{1,0:T(8,128)(2,1)S(1)}, bf16[384,512]{1,0:T(8,128)(2,1)S(1)}) custom-call(s32[3]{0:T(128)S(1)} %pad_add_fusion.place_ref, bf16[128,2048]{1,0:T(8,128)(2,1)} %q_ref.5, bf16[128,2048]{1,0:T(8,128)(2,1)} %k_ref.5, bf16[128,2048]{1,0:T(8,128)(2,1)} %v_ref.5, bf16[384,512]{1,0:T(8,128)(2,1)S(1)} %get-tuple-element.30.other_ref), custom_call_target="tpu_custom_call" | custom-call | flops 2000000000 | bytes 40000000 | tf_op jit(solution)/shard_map/pack1/pallas_call | solution.py:229
  12.7 0.3 collective-permute-start
  13.0 7.6 %collective-permute-done.2.a3.refs_3_ = bf16[384,512]{1,0:T(8,128)(2,1)S(1)} collective-permute-done((bf16[384,512]{1,0:T(8,128)(2,1)S(1)}, bf16[384,512]{1,0:T(8,128)(2,1)S(1)}, u32[]{:S(2)}, u32[]{:S(2)}) %collective-permute-start.2) | collective-permute-done | bytes 393248 | tf_op jit(solution)/shard_map/ppermute | solution.py:20
  20.6 8.5 %collective-permute-done.1.a2.refs_2_ = bf16[384,512]{1,0:T(8,128)(2,1)S(1)} collective-permute-done((bf16[384,512]{1,0:T(8,128)(2,1)S(1)}, bf16[384,512]{1,0:T(8,128)(2,1)S(1)}, u32[]{:S(2)}, u32[]{:S(2)}) %collective-permute-start.1) | collective-permute-done | bytes 393248 | tf_op jit(solution)/shard_map/ppermute | solution.py:20
  29.1 0.0 collective-permute-done.a1.refs_1_
  29.1 0.8 %coarse.1 = (bf16[256,512]{1,0:T(8,128)(2,1)S(1)}, bf16[128,512]{1,0:T(8,128)(2,1)S(1)}) custom-call(s32[3]{0:T(128)S(1)} %pad_add_fusion.place_ref, bf16[384,512]{1,0:T(8,128)(2,1)S(1)} %get-tuple-element.31.a0.refs_0_.refs_7_, bf16[384,512]{1,0:T(8,128)(2,1)S(1)} %collective-permute-done.a1.refs_1_, ...), custom_call_target="tpu_custom_call" | custom-call | tf_op jit(solution)/shard_map/coarse/pallas_call | solution.py:240
  29.9 0.0 collective-permute-done.4.refs_0_
  29.9 0.4 collective-permute-done.3.refs_1_
  30.3 1.5 %collective-permute-start.15 = (bf16[1024,256]{1,0:T(8,128)(2,1)S(1)}, bf16[1024,256]{1,0:T(8,128)(2,1)S(1)}, u32[]{:S(2)}, u32[]{:S(2)}) collective-permute-start(bf16[1024,256]{1,0:T(8,128)(2,1)S(1)} %collective-permute-done.3.refs_1_), channel_id=1, source_target_pairs={{0,16},{16,0},{1,17},{17,1},{2,18},{18,2},{3,19},{19,3},{4,20},{20... | collective-permute-start | bytes 1572872 | tf_op jit(solution)/shard_map/ppermute | solution.py:24
  31.8 0.4 collective-permute-start.5
  32.3 2.6 %collective-permute-start.6 = (bf16[128,512]{1,0:T(8,128)(2,1)S(1)}, bf16[128,512]{1,0:T(8,128)(2,1)S(1)}, u32[]{:S(2)}, u32[]{:S(2)}) collective-permute-start(bf16[128,512]{1,0:T(8,128)(2,1)S(1)} %get-tuple-element.37), channel_id=1, source_target_pairs={{0,8},{1,9},{2,10},{3,11},{4,12},{5,13},{6,14},{7,15},{8,0},{9,1},... | collective-permute-start | bytes 393224 | tf_op jit(solution)/shard_map/ppermute | solution.py:20
  34.9 1.4 %collective-permute-start.7 = (bf16[128,512]{1,0:T(8,128)(2,1)S(1)}, bf16[128,512]{1,0:T(8,128)(2,1)S(1)}, u32[]{:S(2)}, u32[]{:S(2)}) collective-permute-start(bf16[128,512]{1,0:T(8,128)(2,1)S(1)} %get-tuple-element.37), channel_id=1, source_target_pairs={{0,12},{1,13},{2,14},{3,15},{4,8},{5,9},{6,10},{7,11},{8,4},{9,5},... | collective-permute-start | bytes 393224 | tf_op jit(solution)/shard_map/ppermute | solution.py:20
  36.2 5.7 %collective-permute-done.6.refs_5_ = bf16[128,512]{1,0:T(8,128)(2,1)S(1)} collective-permute-done((bf16[128,512]{1,0:T(8,128)(2,1)S(1)}, bf16[128,512]{1,0:T(8,128)(2,1)S(1)}, u32[]{:S(2)}, u32[]{:S(2)}) %collective-permute-start.6) | collective-permute-done | bytes 131104 | tf_op jit(solution)/shard_map/ppermute | solution.py:20
  41.9 2.2 %collective-permute-start.9 = (bf16[1024,256]{1,0:T(8,128)(2,1)S(1)}, bf16[1024,256]{1,0:T(8,128)(2,1)S(1)}, u32[]{:S(2)}, u32[]{:S(2)}) collective-permute-start(bf16[1024,256]{1,0:T(8,128)(2,1)S(1)} %collective-permute-done.3.refs_1_), channel_id=1, source_target_pairs={{0,4},{1,5},{2,6},{3,7},{4,0},{5,1},{6,2},{7,3},{8,12},{9,13},{10,... | collective-permute-start | bytes 1572872 | tf_op jit(solution)/shard_map/ppermute | solution.py:20
  44.1 1.7 %collective-permute-done.7.refs_6_ = bf16[128,512]{1,0:T(8,128)(2,1)S(1)} collective-permute-done((bf16[128,512]{1,0:T(8,128)(2,1)S(1)}, bf16[128,512]{1,0:T(8,128)(2,1)S(1)}, u32[]{:S(2)}, u32[]{:S(2)}) %collective-permute-start.7) | collective-permute-done | bytes 131104 | tf_op jit(solution)/shard_map/ppermute | solution.py:20
  45.9 0.4 collective-permute-done.5.refs_4_
  46.3 0.0 copy-done.1
  46.3 2.4 %attend0.1.refs_7_.refs_0_ = bf16[256,512]{1,0:T(8,128)(2,1)S(1)} custom-call(s32[3]{0:T(128)S(1)} %pad_add_fusion.place_ref, s32[16]{0:T(128)S(1)} %copy-done.1, bf16[384,512]{1,0:T(8,128)(2,1)S(1)} %get-tuple-element.31.a0.refs_0_.refs_7_, bf16[384,512]{1,0:T(8,128)(2,1)S(1)} %collective-permute-done.a1.refs_1_, ...), custom_call_target="tpu_custom_call" | custom-call | flops 2000000000 | bytes 40000000 | tf_op jit(solution)/shard_map/attend0/pallas_call | solution.py:255
  48.7 1.1 %collective-permute-start.8 = (bf16[256,512]{1,0:T(8,128)(2,1)S(1)}, bf16[256,512]{1,0:T(8,128)(2,1)S(1)}, u32[]{:S(2)}, u32[]{:S(2)}) collective-permute-start(bf16[256,512]{1,0:T(8,128)(2,1)S(1)} %attend0.1.refs_7_.refs_0_), channel_id=1, source_target_pairs={{0,2},{1,3},{2,0},{3,1},{4,6},{5,7},{6,4},{7,5},{8,10},{9,11},{10,... | collective-permute-start | bytes 786440 | tf_op jit(solution)/shard_map/ppermute | solution.py:20
  49.9 0.0 collective-permute-done.15.refs_2_
  49.9 0.5 collective-permute-start.16
  50.4 2.4 %attend1.1.refs_1_ = bf16[256,512]{1,0:T(8,128)(2,1)S(1)} custom-call(s32[3]{0:T(128)S(1)} %pad_add_fusion.place_ref, s32[16]{0:T(128)S(1)} %copy-done.1, bf16[384,512]{1,0:T(8,128)(2,1)S(1)} %get-tuple-element.31.a0.refs_0_.refs_7_, bf16[384,512]{1,0:T(8,128)(2,1)S(1)} %collective-permute-done.a1.refs_1_, ...), custom_call_target="tpu_custom_call" | custom-call | flops 2000000000 | bytes 40000000 | tf_op jit(solution)/shard_map/attend1/pallas_call | solution.py:255
  52.8 1.0 %collective-permute-start.12 = (bf16[256,512]{1,0:T(8,128)(2,1)S(1)}, bf16[256,512]{1,0:T(8,128)(2,1)S(1)}, u32[]{:S(2)}, u32[]{:S(2)}) collective-permute-start(bf16[256,512]{1,0:T(8,128)(2,1)S(1)} %attend1.1.refs_1_), channel_id=1, source_target_pairs={{0,2},{1,3},{2,0},{3,1},{4,6},{5,7},{6,4},{7,5},{8,10},{9,11},{10,... | collective-permute-start | bytes 786440 | tf_op jit(solution)/shard_map/ppermute | solution.py:20
  53.8 2.9 %collective-permute-done.8.refs_4_ = bf16[256,512]{1,0:T(8,128)(2,1)S(1)} collective-permute-done((bf16[256,512]{1,0:T(8,128)(2,1)S(1)}, bf16[256,512]{1,0:T(8,128)(2,1)S(1)}, u32[]{:S(2)}, u32[]{:S(2)}) %collective-permute-start.8) | collective-permute-done | bytes 262176 | tf_op jit(solution)/shard_map/ppermute | solution.py:20
  56.7 0.0 collective-permute-done.9.refs_2_
  56.7 0.0 collective-permute-start.13
  56.7 0.5 collective-permute-start.10
  57.2 0.0 collective-permute-start.11
  57.2 2.3 %collective-permute-done.12.refs_5_ = bf16[256,512]{1,0:T(8,128)(2,1)S(1)} collective-permute-done((bf16[256,512]{1,0:T(8,128)(2,1)S(1)}, bf16[256,512]{1,0:T(8,128)(2,1)S(1)}, u32[]{:S(2)}, u32[]{:S(2)}) %collective-permute-start.12) | collective-permute-done | bytes 262176 | tf_op jit(solution)/shard_map/ppermute | solution.py:20
  59.5 0.0 collective-permute-done.13.refs_6_
  59.5 0.0 collective-permute-start.14
  59.6 0.1 collective-permute-start.18
  59.6 0.0 collective-permute-done.16.refs_1_
  59.7 0.0 copy-start
  59.7 1.6 %collective-permute-start.17 = (bf16[512,256]{1,0:T(8,128)(2,1)S(1)}, bf16[512,256]{1,0:T(8,128)(2,1)S(1)}, u32[]{:S(2)}, u32[]{:S(2)}) collective-permute-start(bf16[512,256]{1,0:T(8,128)(2,1)S(1)} %slice.6), channel_id=1, source_target_pairs={{0,16},{16,0},{1,17},{17,1},{2,18},{18,2},{3,19},{19,3},{4,20},{20... | collective-permute-start | bytes 786440 | tf_op jit(solution)/shard_map/ppermute | solution.py:24
  61.2 0.0 collective-permute-done.10.refs_2_
  61.2 0.0 collective-permute-done.11.refs_3_
  61.2 0.0 collective-permute-done.14.refs_7_
  61.3 0.7 gather.1.rows_ref
  62.0 1.8 %project0.1 = (bf16[128,512]{1,0:T(8,128)(2,1)S(1)}, bf16[128,512]{1,0:T(8,128)(2,1)S(1)}, bf16[128,512]{1,0:T(8,128)(2,1)S(1)}, bf16[128,512]{1,0:T(8,128)(2,1)S(1)}) custom-call(s32[3]{0:T(128)S(1)} %pad_add_fusion.place_ref, bf16[512,2048]{1,0:T(8,128)(2,1)S(1)} %gather.1.rows_ref, bf16[2048,256]{1,0:T(8,128)(2,1)S(1)} %copy-done, ...), custom_call_target="tpu_custom_call" | custom-call | tf_op jit(solution)/shard_map/project0/pallas_call | solution.py:275
  63.8 0.3 collective-permute-start.22
  64.1 0.9 %collective-permute-start.23 = (bf16[128,512]{1,0:T(8,128)(2,1)S(1)}, bf16[128,512]{1,0:T(8,128)(2,1)S(1)}, u32[]{:S(2)}, u32[]{:S(2)}) collective-permute-start(bf16[128,512]{1,0:T(8,128)(2,1)S(1)} %get-tuple-element.53), channel_id=1, source_target_pairs={{0,2},{1,3},{2,0},{3,1},{4,6},{5,7},{6,4},{7,5},{8,10},{9,11},{10,... | collective-permute-start | bytes 393224 | tf_op jit(solution)/shard_map/ppermute | solution.py:20
  65.0 0.7 collective-permute-start.24
  65.7 2.6 %collective-permute-done.18.refs_4_ = bf16[512,256]{1,0:T(8,128)(2,1)S(1)} collective-permute-done((bf16[512,256]{1,0:T(8,128)(2,1)S(1)}, bf16[512,256]{1,0:T(8,128)(2,1)S(1)}, u32[]{:S(2)}, u32[]{:S(2)}) %collective-permute-start.18) | collective-permute-done | bytes 262176 | tf_op jit(solution)/shard_map/ppermute | solution.py:20
  68.3 0.1 collective-permute-done.17.refs_3_
  68.5 1.8 %project1.1 = (bf16[128,512]{1,0:T(8,128)(2,1)S(1)}, bf16[128,512]{1,0:T(8,128)(2,1)S(1)}, bf16[128,512]{1,0:T(8,128)(2,1)S(1)}, bf16[128,512]{1,0:T(8,128)(2,1)S(1)}) custom-call(s32[3]{0:T(128)S(1)} %pad_add_fusion.place_ref, bf16[512,2048]{1,0:T(8,128)(2,1)S(1)} %gather.1.rows_ref, bf16[1024,256]{1,0:T(8,128)(2,1)S(1)} %collective-permute-done.4.refs_0_, ...), custom_call_target="tpu_custom_call" | custom-call | tf_op jit(solution)/shard_map/project1/pallas_call | solution.py:275
  70.3 0.1 collective-permute-start.19
  70.4 1.0 %collective-permute-start.20 = (bf16[128,512]{1,0:T(8,128)(2,1)S(1)}, bf16[128,512]{1,0:T(8,128)(2,1)S(1)}, u32[]{:S(2)}, u32[]{:S(2)}) collective-permute-start(bf16[128,512]{1,0:T(8,128)(2,1)S(1)} %get-tuple-element.49), channel_id=1, source_target_pairs={{0,2},{1,3},{2,0},{3,1},{4,6},{5,7},{6,4},{7,5},{8,10},{9,11},{10,... | collective-permute-start | bytes 393224 | tf_op jit(solution)/shard_map/ppermute | solution.py:20
  71.3 0.0 collective-permute-done.22.refs_1_
  71.3 0.9 %collective-permute-start.21 = (bf16[128,512]{1,0:T(8,128)(2,1)S(1)}, bf16[128,512]{1,0:T(8,128)(2,1)S(1)}, u32[]{:S(2)}, u32[]{:S(2)}) collective-permute-start(bf16[128,512]{1,0:T(8,128)(2,1)S(1)} %get-tuple-element.50), channel_id=1, source_target_pairs={{0,3},{1,2},{2,1},{3,0},{4,7},{5,6},{6,5},{7,4},{8,11},{9,10},{10,... | collective-permute-start | bytes 393224 | tf_op jit(solution)/shard_map/ppermute | solution.py:20
  72.2 0.0 collective-permute-done.23.refs_2_
  72.2 0.0 collective-permute-done.24.refs_3_
  72.2 1.4 %place0.1.refs_4_ = bf16[128,4096]{1,0:T(8,128)(2,1)} custom-call(s32[3]{0:T(128)S(1)} %pad_add_fusion.place_ref, bf16[128,512]{1,0:T(8,128)(2,1)S(1)} %get-tuple-element.51.refs_0_, bf16[128,512]{1,0:T(8,128)(2,1)S(1)} %collective-permute-done.22.refs_1_, bf16[128,512]{1,0:T(8,128)(2,1)S(1)} %collective-permute-done.23.refs_2_, ...), custom_call_target="tpu_custom_call" | custom-call | tf_op jit(solution)/shard_map/place0/pallas_call | solution.py:281
  73.6 0.0 collective-permute-done.19.refs_1_
  73.6 3.1 %collective-permute-done.20.refs_2_ = bf16[128,512]{1,0:T(8,128)(2,1)S(1)} collective-permute-done((bf16[128,512]{1,0:T(8,128)(2,1)S(1)}, bf16[128,512]{1,0:T(8,128)(2,1)S(1)}, u32[]{:S(2)}, u32[]{:S(2)}) %collective-permute-start.20) | collective-permute-done | bytes 131104 | tf_op jit(solution)/shard_map/ppermute | solution.py:20
  76.7 1.9 %collective-permute-done.21.refs_3_ = bf16[128,512]{1,0:T(8,128)(2,1)S(1)} collective-permute-done((bf16[128,512]{1,0:T(8,128)(2,1)S(1)}, bf16[128,512]{1,0:T(8,128)(2,1)S(1)}, u32[]{:S(2)}, u32[]{:S(2)}) %collective-permute-start.21) | collective-permute-done | bytes 131104 | tf_op jit(solution)/shard_map/ppermute | solution.py:20
  78.6 1.4 %place1.1 = bf16[128,4096]{1,0:T(8,128)(2,1)} custom-call(s32[3]{0:T(128)S(1)} %pad_add_fusion.place_ref, bf16[128,512]{1,0:T(8,128)(2,1)S(1)} %get-tuple-element.47.refs_0_, bf16[128,512]{1,0:T(8,128)(2,1)S(1)} %collective-permute-done.19.refs_1_, bf16[128,512]{1,0:T(8,128)(2,1)S(1)} %collective-permute-done.20.refs_2_, ...), custom_call_target="tpu_custom_call", output_to_operand_aliasing={{}: (5, {})} | custom-call | tf_op jit(solution)/shard_map/place1/pallas_call | solution.py:281
  (4 shorter events, 0.0 us)
Async XLA Ops:
  1.7 28.2 %collective-permute-start.4 = (bf16[1024,256]{1,0:T(8,128)(2,1)S(1)}, bf16[1024,256]{1,0:T(8,128)(2,1)S(1)}, u32[]{:S(2)}, u32[]{:S(2)}) collective-permute-start(bf16[1024,256]{1,0:T(8,128)(2,1)S(1)} %pack.1.other_ref), channel_id=1, source_target_pairs={{0,4},{1,5},{2,6},{3,7},{4,0},{5,1},{6,2},{7,3},{8,12},{9,13},{10,... | collective-permute-start | bytes 1572872 | tf_op jit(solution)/shard_map/ppermute | solution.py:20
  4.8 25.6 %collective-permute-start.3 = (bf16[1024,256]{1,0:T(8,128)(2,1)S(1)}, bf16[1024,256]{1,0:T(8,128)(2,1)S(1)}, u32[]{:S(2)}, u32[]{:S(2)}) collective-permute-start(bf16[1024,256]{1,0:T(8,128)(2,1)S(1)} %pack.1.other_ref), channel_id=1, source_target_pairs={{0,8},{1,9},{2,10},{3,11},{4,12},{5,13},{6,14},{7,15},{8,0},{9,1},... | collective-permute-start | bytes 1572872 | tf_op jit(solution)/shard_map/ppermute | solution.py:20
  9.2 11.4 %collective-permute-start.2 = (bf16[384,512]{1,0:T(8,128)(2,1)S(1)}, bf16[384,512]{1,0:T(8,128)(2,1)S(1)}, u32[]{:S(2)}, u32[]{:S(2)}) collective-permute-start(bf16[384,512]{1,0:T(8,128)(2,1)S(1)} %get-tuple-element.33), channel_id=1, source_target_pairs={{0,3},{1,2},{2,1},{3,0},{4,7},{5,6},{6,5},{7,4},{8,11},{9,10},{10,... | collective-permute-start | bytes 1179656 | tf_op jit(solution)/shard_map/ppermute | solution.py:20
  9.6 36.7 %copy-start.1 = (s32[16]{0:T(128)S(1)}, s32[16]{0:T(128)}, u32[]{:S(2)}) copy-start(s32[16]{0:T(128)} %doc_ref.3) | copy-start | bytes 196
  9.6 19.4 %collective-permute-start.1 = (bf16[384,512]{1,0:T(8,128)(2,1)S(1)}, bf16[384,512]{1,0:T(8,128)(2,1)S(1)}, u32[]{:S(2)}, u32[]{:S(2)}) collective-permute-start(bf16[384,512]{1,0:T(8,128)(2,1)S(1)} %get-tuple-element.30.other_ref), channel_id=1, source_target_pairs={{0,2},{1,3},{2,0},{3,1},{4,6},{5,7},{6,4},{7,5},{8,10},{9,11},{10,... | collective-permute-start | bytes 1179656 | tf_op jit(solution)/shard_map/ppermute | solution.py:20
  12.7 16.4 %collective-permute-start = (bf16[384,512]{1,0:T(8,128)(2,1)S(1)}, bf16[384,512]{1,0:T(8,128)(2,1)S(1)}, u32[]{:S(2)}, u32[]{:S(2)}) collective-permute-start(bf16[384,512]{1,0:T(8,128)(2,1)S(1)} %get-tuple-element.32), channel_id=1, source_target_pairs={{0,1},{1,0},{2,3},{3,2},{4,5},{5,4},{6,7},{7,6},{8,9},{9,8},{10,11... | collective-permute-start | bytes 1179656 | tf_op jit(solution)/shard_map/ppermute | solution.py:20
  30.3 19.5 %collective-permute-start.15 = (bf16[1024,256]{1,0:T(8,128)(2,1)S(1)}, bf16[1024,256]{1,0:T(8,128)(2,1)S(1)}, u32[]{:S(2)}, u32[]{:S(2)}) collective-permute-start(bf16[1024,256]{1,0:T(8,128)(2,1)S(1)} %collective-permute-done.3.refs_1_), channel_id=1, source_target_pairs={{0,16},{16,0},{1,17},{17,1},{2,18},{18,2},{3,19},{19,3},{4,20},{20... | collective-permute-start | bytes 1572872 | tf_op jit(solution)/shard_map/ppermute | solution.py:24
  31.8 14.5 %collective-permute-start.5 = (bf16[256,512]{1,0:T(8,128)(2,1)S(1)}, bf16[256,512]{1,0:T(8,128)(2,1)S(1)}, u32[]{:S(2)}, u32[]{:S(2)}) collective-permute-start(bf16[256,512]{1,0:T(8,128)(2,1)S(1)} %get-tuple-element.36), channel_id=1, source_target_pairs={{0,4},{1,5},{2,6},{3,7},{4,0},{5,1},{6,2},{7,3},{8,12},{9,13},{10,... | collective-permute-start | bytes 786440 | tf_op jit(solution)/shard_map/ppermute | solution.py:20
  32.3 9.6 %collective-permute-start.6 = (bf16[128,512]{1,0:T(8,128)(2,1)S(1)}, bf16[128,512]{1,0:T(8,128)(2,1)S(1)}, u32[]{:S(2)}, u32[]{:S(2)}) collective-permute-start(bf16[128,512]{1,0:T(8,128)(2,1)S(1)} %get-tuple-element.37), channel_id=1, source_target_pairs={{0,8},{1,9},{2,10},{3,11},{4,12},{5,13},{6,14},{7,15},{8,0},{9,1},... | collective-permute-start | bytes 393224 | tf_op jit(solution)/shard_map/ppermute | solution.py:20
  34.9 11.0 %collective-permute-start.7 = (bf16[128,512]{1,0:T(8,128)(2,1)S(1)}, bf16[128,512]{1,0:T(8,128)(2,1)S(1)}, u32[]{:S(2)}, u32[]{:S(2)}) collective-permute-start(bf16[128,512]{1,0:T(8,128)(2,1)S(1)} %get-tuple-element.37), channel_id=1, source_target_pairs={{0,12},{1,13},{2,14},{3,15},{4,8},{5,9},{6,10},{7,11},{8,4},{9,5},... | collective-permute-start | bytes 393224 | tf_op jit(solution)/shard_map/ppermute | solution.py:20
  41.9 14.8 %collective-permute-start.9 = (bf16[1024,256]{1,0:T(8,128)(2,1)S(1)}, bf16[1024,256]{1,0:T(8,128)(2,1)S(1)}, u32[]{:S(2)}, u32[]{:S(2)}) collective-permute-start(bf16[1024,256]{1,0:T(8,128)(2,1)S(1)} %collective-permute-done.3.refs_1_), channel_id=1, source_target_pairs={{0,4},{1,5},{2,6},{3,7},{4,0},{5,1},{6,2},{7,3},{8,12},{9,13},{10,... | collective-permute-start | bytes 1572872 | tf_op jit(solution)/shard_map/ppermute | solution.py:20
  48.7 8.0 %collective-permute-start.8 = (bf16[256,512]{1,0:T(8,128)(2,1)S(1)}, bf16[256,512]{1,0:T(8,128)(2,1)S(1)}, u32[]{:S(2)}, u32[]{:S(2)}) collective-permute-start(bf16[256,512]{1,0:T(8,128)(2,1)S(1)} %attend0.1.refs_7_.refs_0_), channel_id=1, source_target_pairs={{0,2},{1,3},{2,0},{3,1},{4,6},{5,7},{6,4},{7,5},{8,10},{9,11},{10,... | collective-permute-start | bytes 786440 | tf_op jit(solution)/shard_map/ppermute | solution.py:20
  49.9 9.8 %collective-permute-start.16 = (bf16[1024,256]{1,0:T(8,128)(2,1)S(1)}, bf16[1024,256]{1,0:T(8,128)(2,1)S(1)}, u32[]{:S(2)}, u32[]{:S(2)}) collective-permute-start(bf16[1024,256]{1,0:T(8,128)(2,1)S(1)} %collective-permute-done.4.refs_0_), channel_id=1, source_target_pairs={{0,16},{16,0},{1,17},{17,1},{2,18},{18,2},{3,19},{19,3},{4,20},{20... | collective-permute-start | bytes 1572872 | tf_op jit(solution)/shard_map/ppermute | solution.py:24
  52.8 6.8 %collective-permute-start.12 = (bf16[256,512]{1,0:T(8,128)(2,1)S(1)}, bf16[256,512]{1,0:T(8,128)(2,1)S(1)}, u32[]{:S(2)}, u32[]{:S(2)}) collective-permute-start(bf16[256,512]{1,0:T(8,128)(2,1)S(1)} %attend1.1.refs_1_), channel_id=1, source_target_pairs={{0,2},{1,3},{2,0},{3,1},{4,6},{5,7},{6,4},{7,5},{8,10},{9,11},{10,... | collective-permute-start | bytes 786440 | tf_op jit(solution)/shard_map/ppermute | solution.py:20
  56.7 2.8 %collective-permute-start.13 = (bf16[256,512]{1,0:T(8,128)(2,1)S(1)}, bf16[256,512]{1,0:T(8,128)(2,1)S(1)}, u32[]{:S(2)}, u32[]{:S(2)}) collective-permute-start(bf16[256,512]{1,0:T(8,128)(2,1)S(1)} %collective-permute-done.8.refs_4_), channel_id=1, source_target_pairs={{0,1},{1,0},{2,3},{3,2},{4,5},{5,4},{6,7},{7,6},{8,9},{9,8},{10,11... | collective-permute-start | bytes 786440 | tf_op jit(solution)/shard_map/ppermute | solution.py:20
  56.7 4.5 %collective-permute-start.10 = (bf16[256,512]{1,0:T(8,128)(2,1)S(1)}, bf16[256,512]{1,0:T(8,128)(2,1)S(1)}, u32[]{:S(2)}, u32[]{:S(2)}) collective-permute-start(bf16[256,512]{1,0:T(8,128)(2,1)S(1)} %attend0.1.refs_7_.refs_0_), channel_id=1, source_target_pairs={{0,1},{1,0},{2,3},{3,2},{4,5},{5,4},{6,7},{7,6},{8,9},{9,8},{10,11... | collective-permute-start | bytes 786440 | tf_op jit(solution)/shard_map/ppermute | solution.py:20
  57.2 4.0 %collective-permute-start.11 = (bf16[256,512]{1,0:T(8,128)(2,1)S(1)}, bf16[256,512]{1,0:T(8,128)(2,1)S(1)}, u32[]{:S(2)}, u32[]{:S(2)}) collective-permute-start(bf16[256,512]{1,0:T(8,128)(2,1)S(1)} %attend1.1.refs_1_), channel_id=1, source_target_pairs={{0,1},{1,0},{2,3},{3,2},{4,5},{5,4},{6,7},{7,6},{8,9},{9,8},{10,11... | collective-permute-start | bytes 786440 | tf_op jit(solution)/shard_map/ppermute | solution.py:20
  59.5 1.7 %collective-permute-start.14 = (bf16[256,512]{1,0:T(8,128)(2,1)S(1)}, bf16[256,512]{1,0:T(8,128)(2,1)S(1)}, u32[]{:S(2)}, u32[]{:S(2)}) collective-permute-start(bf16[256,512]{1,0:T(8,128)(2,1)S(1)} %collective-permute-done.12.refs_5_), channel_id=1, source_target_pairs={{0,1},{1,0},{2,3},{3,2},{4,5},{5,4},{6,7},{7,6},{8,9},{9,8},{10,11... | collective-permute-start | bytes 786440 | tf_op jit(solution)/shard_map/ppermute | solution.py:20
  59.6 8.8 %collective-permute-start.18 = (bf16[512,256]{1,0:T(8,128)(2,1)S(1)}, bf16[512,256]{1,0:T(8,128)(2,1)S(1)}, u32[]{:S(2)}, u32[]{:S(2)}) collective-permute-start(bf16[512,256]{1,0:T(8,128)(2,1)S(1)} %slice.7), channel_id=1, source_target_pairs={{0,4},{1,5},{2,6},{3,7},{4,0},{5,1},{6,2},{7,3},{8,12},{9,13},{10,... | collective-permute-start | bytes 786440 | tf_op jit(solution)/shard_map/ppermute | solution.py:20
  59.7 2.3 %copy-start = (bf16[2048,256]{1,0:T(8,128)(2,1)S(1)}, bf16[2048,256]{1,0:T(8,128)(2,1)}, u32[]{:S(2)}) copy-start(bf16[2048,256]{1,0:T(8,128)(2,1)} %refs_0_.1) | copy-start | bytes 3145732
  59.7 8.8 %collective-permute-start.17 = (bf16[512,256]{1,0:T(8,128)(2,1)S(1)}, bf16[512,256]{1,0:T(8,128)(2,1)S(1)}, u32[]{:S(2)}, u32[]{:S(2)}) collective-permute-start(bf16[512,256]{1,0:T(8,128)(2,1)S(1)} %slice.6), channel_id=1, source_target_pairs={{0,16},{16,0},{1,17},{17,1},{2,18},{18,2},{3,19},{19,3},{4,20},{20... | collective-permute-start | bytes 786440 | tf_op jit(solution)/shard_map/ppermute | solution.py:24
  63.8 7.6 %collective-permute-start.22 = (bf16[128,512]{1,0:T(8,128)(2,1)S(1)}, bf16[128,512]{1,0:T(8,128)(2,1)S(1)}, u32[]{:S(2)}, u32[]{:S(2)}) collective-permute-start(bf16[128,512]{1,0:T(8,128)(2,1)S(1)} %get-tuple-element.52), channel_id=1, source_target_pairs={{0,1},{1,0},{2,3},{3,2},{4,5},{5,4},{6,7},{7,6},{8,9},{9,8},{10,11... | collective-permute-start | bytes 393224 | tf_op jit(solution)/shard_map/ppermute | solution.py:20
  64.1 8.2 %collective-permute-start.23 = (bf16[128,512]{1,0:T(8,128)(2,1)S(1)}, bf16[128,512]{1,0:T(8,128)(2,1)S(1)}, u32[]{:S(2)}, u32[]{:S(2)}) collective-permute-start(bf16[128,512]{1,0:T(8,128)(2,1)S(1)} %get-tuple-element.53), channel_id=1, source_target_pairs={{0,2},{1,3},{2,0},{3,1},{4,6},{5,7},{6,4},{7,5},{8,10},{9,11},{10,... | collective-permute-start | bytes 393224 | tf_op jit(solution)/shard_map/ppermute | solution.py:20
  65.0 7.2 %collective-permute-start.24 = (bf16[128,512]{1,0:T(8,128)(2,1)S(1)}, bf16[128,512]{1,0:T(8,128)(2,1)S(1)}, u32[]{:S(2)}, u32[]{:S(2)}) collective-permute-start(bf16[128,512]{1,0:T(8,128)(2,1)S(1)} %get-tuple-element.54), channel_id=1, source_target_pairs={{0,3},{1,2},{2,1},{3,0},{4,7},{5,6},{6,5},{7,4},{8,11},{9,10},{10,... | collective-permute-start | bytes 393224 | tf_op jit(solution)/shard_map/ppermute | solution.py:20
  70.3 3.4 %collective-permute-start.19 = (bf16[128,512]{1,0:T(8,128)(2,1)S(1)}, bf16[128,512]{1,0:T(8,128)(2,1)S(1)}, u32[]{:S(2)}, u32[]{:S(2)}) collective-permute-start(bf16[128,512]{1,0:T(8,128)(2,1)S(1)} %get-tuple-element.48), channel_id=1, source_target_pairs={{0,1},{1,0},{2,3},{3,2},{4,5},{5,4},{6,7},{7,6},{8,9},{9,8},{10,11... | collective-permute-start | bytes 393224 | tf_op jit(solution)/shard_map/ppermute | solution.py:20
  70.4 6.4 %collective-permute-start.20 = (bf16[128,512]{1,0:T(8,128)(2,1)S(1)}, bf16[128,512]{1,0:T(8,128)(2,1)S(1)}, u32[]{:S(2)}, u32[]{:S(2)}) collective-permute-start(bf16[128,512]{1,0:T(8,128)(2,1)S(1)} %get-tuple-element.49), channel_id=1, source_target_pairs={{0,2},{1,3},{2,0},{3,1},{4,6},{5,7},{6,4},{7,5},{8,10},{9,11},{10,... | collective-permute-start | bytes 393224 | tf_op jit(solution)/shard_map/ppermute | solution.py:20
  71.3 7.3 %collective-permute-start.21 = (bf16[128,512]{1,0:T(8,128)(2,1)S(1)}, bf16[128,512]{1,0:T(8,128)(2,1)S(1)}, u32[]{:S(2)}, u32[]{:S(2)}) collective-permute-start(bf16[128,512]{1,0:T(8,128)(2,1)S(1)} %get-tuple-element.50), channel_id=1, source_target_pairs={{0,3},{1,2},{2,1},{3,0},{4,7},{5,6},{6,5},{7,4},{8,11},{9,10},{10,... | collective-permute-start | bytes 393224 | tf_op jit(solution)/shard_map/ppermute | solution.py:20

commit v8 on v7

--- a/solution.py
+++ b/solution.py
@@ -181,13 +181,13 @@
 
 def place_kernel(group, place_ref, *refs):
     sources, out_ref, sems = refs[:4], refs[-2], refs[-1]
-    wide = sources[0].shape[1] // 2
+    wide = out_ref.shape[1] // 16
     copies = []
     for j, source in enumerate(sources):
-        for q, mask in enumerate(((0, HIGH), (LOW, LOW | HIGH))[group]):
+        for q, mask in enumerate(((0, HIGH, LOW), (LOW | HIGH,))[group]):
             at = pl.multiple_of(jnp.bitwise_xor(place_ref[2], mask | j) * wide, wide)
             to = out_ref.at[:, pl.ds(at, wide)]
-            copies.append(pltpu.make_async_copy(source.at[:, q * wide : (q + 1) * wide], to, sems.at[2 * j + q]))
+            copies.append(pltpu.make_async_copy(source.at[:, q * wide : (q + 1) * wide], to, sems.at[len(copies)]))
     run_copies(copies)
 
 
@@ -271,8 +271,8 @@
 
     (rows,) = call(gather_kernel, [(4 * length, width)], vmem(8), name="gather")(places, *mixed)
     received = []
-    for n, blocks in enumerate(((own_block, half_h, other_h), (ours_l, other_l, half_d, *other_d))):
-        parts = call(project_kernel, [(length, 2 * wide)] * 4, vmem(1 + len(blocks)), name="project%d" % n)(
+    for count, blocks in ((3, (own_block, half_h, other_h, ours_l, other_l)), (1, (half_d, *other_d))):
+        parts = call(project_kernel, [(length, count * wide)] * 4, vmem(1 + len(blocks)), name="project%d" % count)(
             places, rows, *blocks
         )
         received += [parts[0]] + [swap(parts[j], j) for j in (1, 2, 3)]
@@ -283,7 +283,7 @@
             [(length, 16 * wide)],
             anywhere(4 + len(earlier)),
             anywhere(1),
-            scratch_shapes=[pltpu.SemaphoreType.DMA((8,))],
+            scratch_shapes=[pltpu.SemaphoreType.DMA((4 if earlier else 12,))],
             input_output_aliases={5: 0} if earlier else {},
             name="place%d" % n,
         )(places, *received[4 * n : 4 * n + 4], *earlier)

time: 80.2 us -> 79.5 us (level)
  transfers between devices with their start and end apart: 25 -> 25, of which waited for: 12 -> 14; matrix products, arithmetic and copies ran while one was open for 0% -> 0% of each run, Pallas kernels for 19% -> 19%
where the time goes in v8:
time: 79.5 us; the launch traced here: 79.3 us
  waiting for transfers between devices  36.7 us (46%)
  starting transfers between devices  24.5 us (31%)
  Pallas kernels  17.9 us (23%)
    ppermute x22, waiting for transfers between devices, swap(): return lax.ppermute(value, 'ctx', pairs)  36.6 us
    ppermute x22, starting transfers between devices, swap(): return lax.ppermute(value, 'ctx', pairs)  20.9 us
    pallas_call x2, Pallas kernels, per_device_fast(): call(functools.partial(attention_kernel, n), [(2 * length, share)], [pl.B...  4.77 us
    pallas_call x2, Pallas kernels, per_device_fast(): call(project_kernel, [(length, count * wide)] * 4, vmem(1 + len(blocks)),...  3.58 us
    ppermute x3, starting transfers between devices, swap_groups(): return lax.ppermute(value, 'groups', [(0, 1), (1, 0)])  3.57 us
    pallas_call x2, Pallas kernels, per_device_fast(): call(functools.partial(place_kernel, n), [(length, 16 * wide)], anywhere(...  2.78 us
    pallas_call x1, Pallas kernels, per_device_fast(): call(functools.partial(pack_kernel, (1, 0)), [(3 * length, share)] * 2, a...  1.8 us
    pallas_call x1, Pallas kernels, per_device_fast(): call(functools.partial(pack_kernel, (2, 3)), [(3 * length, share)] * 2, a...  1.8 us
  transfers between devices with their start and end apart: 25, of which 14 were waited for; matrix products, arithmetic and copies ran while one was open for 0% of the time, Pallas kernels for 19%

profile of v8, /device:TPU:0, one launch (start us, length us, event | category | flops | bytes accessed | tf_op | source)
XLA Modules:
  0.0 79.3 jit_solution(11823666043340042894)
XLA Ops:
  0.0 0.1 pad_add_fusion.place_ref
  0.1 1.6 %pack.1.other_ref = bf16[1024,256]{1,0:T(8,128)(2,1)S(1)} custom-call(s32[3]{0:T(128)S(1)} %pad_add_fusion.place_ref, bf16[128,2048]{1,0:T(8,128)(2,1)} %q_ref.5, bf16[128,2048]{1,0:T(8,128)(2,1)} %k_ref.5, bf16[128,2048]{1,0:T(8,128)(2,1)} %v_ref.5, bf16[2048,256]{1,0:T(8,128)(2,1)} %refs_0_.1), custom_call_target="tpu_custom_call" | custom-call | tf_op jit(solution)/shard_map/pack/pallas_call | solution.py:215
  1.7 3.1 %collective-permute-start.4 = (bf16[1024,256]{1,0:T(8,128)(2,1)S(1)}, bf16[1024,256]{1,0:T(8,128)(2,1)S(1)}, u32[]{:S(2)}, u32[]{:S(2)}) collective-permute-start(bf16[1024,256]{1,0:T(8,128)(2,1)S(1)} %pack.1.other_ref), channel_id=1, source_target_pairs={{0,4},{1,5},{2,6},{3,7},{4,0},{5,1},{6,2},{7,3},{8,12},{9,13},{10,... | collective-permute-start | bytes 1572872 | tf_op jit(solution)/shard_map/ppermute | solution.py:20
  4.8 2.6 %collective-permute-start.3 = (bf16[1024,256]{1,0:T(8,128)(2,1)S(1)}, bf16[1024,256]{1,0:T(8,128)(2,1)S(1)}, u32[]{:S(2)}, u32[]{:S(2)}) collective-permute-start(bf16[1024,256]{1,0:T(8,128)(2,1)S(1)} %pack.1.other_ref), channel_id=1, source_target_pairs={{0,8},{1,9},{2,10},{3,11},{4,12},{5,13},{6,14},{7,15},{8,0},{9,1},... | collective-permute-start | bytes 1572872 | tf_op jit(solution)/shard_map/ppermute | solution.py:20
  7.4 1.8 %pack0.1 = (bf16[384,512]{1,0:T(8,128)(2,1)S(1)}, bf16[384,512]{1,0:T(8,128)(2,1)S(1)}) custom-call(s32[3]{0:T(128)S(1)} %pad_add_fusion.place_ref, bf16[128,2048]{1,0:T(8,128)(2,1)} %q_ref.5, bf16[128,2048]{1,0:T(8,128)(2,1)} %k_ref.5, bf16[128,2048]{1,0:T(8,128)(2,1)} %v_ref.5, bf16[1024,256]{1,0:T(8,128)(2,1)S(1)} %pack.1.other_ref), custom_call_target="tpu_custom_call" | custom-call | tf_op jit(solution)/shard_map/pack0/pallas_call | solution.py:222
  9.2 0.5 collective-permute-start.2
  9.6 1.2 %collective-permute-start.1 = (bf16[384,512]{1,0:T(8,128)(2,1)S(1)}, bf16[384,512]{1,0:T(8,128)(2,1)S(1)}, u32[]{:S(2)}, u32[]{:S(2)}) collective-permute-start(bf16[384,512]{1,0:T(8,128)(2,1)S(1)} %get-tuple-element.30.other_ref), channel_id=1, source_target_pairs={{0,2},{1,3},{2,0},{3,1},{4,6},{5,7},{6,4},{7,5},{8,10},{9,11},{10,... | collective-permute-start | bytes 1179656 | tf_op jit(solution)/shard_map/ppermute | solution.py:20
  10.8 1.8 %pack1.1 = (bf16[384,512]{1,0:T(8,128)(2,1)S(1)}, bf16[384,512]{1,0:T(8,128)(2,1)S(1)}) custom-call(s32[3]{0:T(128)S(1)} %pad_add_fusion.place_ref, bf16[128,2048]{1,0:T(8,128)(2,1)} %q_ref.5, bf16[128,2048]{1,0:T(8,128)(2,1)} %k_ref.5, bf16[128,2048]{1,0:T(8,128)(2,1)} %v_ref.5, bf16[384,512]{1,0:T(8,128)(2,1)S(1)} %get-tuple-element.30.other_ref), custom_call_target="tpu_custom_call" | custom-call | flops 2000000000 | bytes 40000000 | tf_op jit(solution)/shard_map/pack1/pallas_call | solution.py:229
  12.7 0.3 collective-permute-start
  13.0 7.6 %collective-permute-done.2.a3.refs_3_ = bf16[384,512]{1,0:T(8,128)(2,1)S(1)} collective-permute-done((bf16[384,512]{1,0:T(8,128)(2,1)S(1)}, bf16[384,512]{1,0:T(8,128)(2,1)S(1)}, u32[]{:S(2)}, u32[]{:S(2)}) %collective-permute-start.2) | collective-permute-done | bytes 393248 | tf_op jit(solution)/shard_map/ppermute | solution.py:20
  20.6 8.5 %collective-permute-done.1.a2.refs_2_ = bf16[384,512]{1,0:T(8,128)(2,1)S(1)} collective-permute-done((bf16[384,512]{1,0:T(8,128)(2,1)S(1)}, bf16[384,512]{1,0:T(8,128)(2,1)S(1)}, u32[]{:S(2)}, u32[]{:S(2)}) %collective-permute-start.1) | collective-permute-done | bytes 393248 | tf_op jit(solution)/shard_map/ppermute | solution.py:20
  29.1 0.0 collective-permute-done.a1.refs_1_
  29.1 0.8 %coarse.1 = (bf16[256,512]{1,0:T(8,128)(2,1)S(1)}, bf16[128,512]{1,0:T(8,128)(2,1)S(1)}) custom-call(s32[3]{0:T(128)S(1)} %pad_add_fusion.place_ref, bf16[384,512]{1,0:T(8,128)(2,1)S(1)} %get-tuple-element.31.a0.refs_0_.refs_7_, bf16[384,512]{1,0:T(8,128)(2,1)S(1)} %collective-permute-done.a1.refs_1_, ...), custom_call_target="tpu_custom_call" | custom-call | tf_op jit(solution)/shard_map/coarse/pallas_call | solution.py:240
  29.9 0.0 collective-permute-done.4.refs_3_
  29.9 0.4 collective-permute-done.3.refs_1_
  30.3 1.5 %collective-permute-start.15 = (bf16[1024,256]{1,0:T(8,128)(2,1)S(1)}, bf16[1024,256]{1,0:T(8,128)(2,1)S(1)}, u32[]{:S(2)}, u32[]{:S(2)}) collective-permute-start(bf16[1024,256]{1,0:T(8,128)(2,1)S(1)} %collective-permute-done.3.refs_1_), channel_id=1, source_target_pairs={{0,16},{16,0},{1,17},{17,1},{2,18},{18,2},{3,19},{19,3},{4,20},{20... | collective-permute-start | bytes 1572872 | tf_op jit(solution)/shard_map/ppermute | solution.py:24
  31.8 0.4 collective-permute-start.5
  32.3 2.6 %collective-permute-start.6 = (bf16[128,512]{1,0:T(8,128)(2,1)S(1)}, bf16[128,512]{1,0:T(8,128)(2,1)S(1)}, u32[]{:S(2)}, u32[]{:S(2)}) collective-permute-start(bf16[128,512]{1,0:T(8,128)(2,1)S(1)} %get-tuple-element.37), channel_id=1, source_target_pairs={{0,8},{1,9},{2,10},{3,11},{4,12},{5,13},{6,14},{7,15},{8,0},{9,1},... | collective-permute-start | bytes 393224 | tf_op jit(solution)/shard_map/ppermute | solution.py:20
  34.9 1.4 %collective-permute-start.7 = (bf16[128,512]{1,0:T(8,128)(2,1)S(1)}, bf16[128,512]{1,0:T(8,128)(2,1)S(1)}, u32[]{:S(2)}, u32[]{:S(2)}) collective-permute-start(bf16[128,512]{1,0:T(8,128)(2,1)S(1)} %get-tuple-element.37), channel_id=1, source_target_pairs={{0,12},{1,13},{2,14},{3,15},{4,8},{5,9},{6,10},{7,11},{8,4},{9,5},... | collective-permute-start | bytes 393224 | tf_op jit(solution)/shard_map/ppermute | solution.py:20
  36.2 5.7 %collective-permute-done.6.refs_5_ = bf16[128,512]{1,0:T(8,128)(2,1)S(1)} collective-permute-done((bf16[128,512]{1,0:T(8,128)(2,1)S(1)}, bf16[128,512]{1,0:T(8,128)(2,1)S(1)}, u32[]{:S(2)}, u32[]{:S(2)}) %collective-permute-start.6) | collective-permute-done | bytes 131104 | tf_op jit(solution)/shard_map/ppermute | solution.py:20
  41.9 2.2 %collective-permute-start.9 = (bf16[1024,256]{1,0:T(8,128)(2,1)S(1)}, bf16[1024,256]{1,0:T(8,128)(2,1)S(1)}, u32[]{:S(2)}, u32[]{:S(2)}) collective-permute-start(bf16[1024,256]{1,0:T(8,128)(2,1)S(1)} %collective-permute-done.3.refs_1_), channel_id=1, source_target_pairs={{0,4},{1,5},{2,6},{3,7},{4,0},{5,1},{6,2},{7,3},{8,12},{9,13},{10,... | collective-permute-start | bytes 1572872 | tf_op jit(solution)/shard_map/ppermute | solution.py:20
  44.1 1.7 %collective-permute-done.7.refs_6_ = bf16[128,512]{1,0:T(8,128)(2,1)S(1)} collective-permute-done((bf16[128,512]{1,0:T(8,128)(2,1)S(1)}, bf16[128,512]{1,0:T(8,128)(2,1)S(1)}, u32[]{:S(2)}, u32[]{:S(2)}) %collective-permute-start.7) | collective-permute-done | bytes 131104 | tf_op jit(solution)/shard_map/ppermute | solution.py:20
  45.9 0.4 collective-permute-done.5.refs_4_
  46.3 0.0 copy-done.1
  46.3 2.4 %attend0.1.refs_7_.refs_0_ = bf16[256,512]{1,0:T(8,128)(2,1)S(1)} custom-call(s32[3]{0:T(128)S(1)} %pad_add_fusion.place_ref, s32[16]{0:T(128)S(1)} %copy-done.1, bf16[384,512]{1,0:T(8,128)(2,1)S(1)} %get-tuple-element.31.a0.refs_0_.refs_7_, bf16[384,512]{1,0:T(8,128)(2,1)S(1)} %collective-permute-done.a1.refs_1_, ...), custom_call_target="tpu_custom_call" | custom-call | flops 2000000000 | bytes 40000000 | tf_op jit(solution)/shard_map/attend0/pallas_call | solution.py:255
  48.7 1.1 %collective-permute-start.8 = (bf16[256,512]{1,0:T(8,128)(2,1)S(1)}, bf16[256,512]{1,0:T(8,128)(2,1)S(1)}, u32[]{:S(2)}, u32[]{:S(2)}) collective-permute-start(bf16[256,512]{1,0:T(8,128)(2,1)S(1)} %attend0.1.refs_7_.refs_0_), channel_id=1, source_target_pairs={{0,2},{1,3},{2,0},{3,1},{4,6},{5,7},{6,4},{7,5},{8,10},{9,11},{10,... | collective-permute-start | bytes 786440 | tf_op jit(solution)/shard_map/ppermute | solution.py:20
  49.9 0.0 collective-permute-done.15.refs_2_
  49.9 0.5 collective-permute-start.16
  50.4 2.4 %attend1.1.refs_1_ = bf16[256,512]{1,0:T(8,128)(2,1)S(1)} custom-call(s32[3]{0:T(128)S(1)} %pad_add_fusion.place_ref, s32[16]{0:T(128)S(1)} %copy-done.1, bf16[384,512]{1,0:T(8,128)(2,1)S(1)} %get-tuple-element.31.a0.refs_0_.refs_7_, bf16[384,512]{1,0:T(8,128)(2,1)S(1)} %collective-permute-done.a1.refs_1_, ...), custom_call_target="tpu_custom_call" | custom-call | flops 2000000000 | bytes 40000000 | tf_op jit(solution)/shard_map/attend1/pallas_call | solution.py:255
  52.8 1.0 %collective-permute-start.12 = (bf16[256,512]{1,0:T(8,128)(2,1)S(1)}, bf16[256,512]{1,0:T(8,128)(2,1)S(1)}, u32[]{:S(2)}, u32[]{:S(2)}) collective-permute-start(bf16[256,512]{1,0:T(8,128)(2,1)S(1)} %attend1.1.refs_1_), channel_id=1, source_target_pairs={{0,2},{1,3},{2,0},{3,1},{4,6},{5,7},{6,4},{7,5},{8,10},{9,11},{10,... | collective-permute-start | bytes 786440 | tf_op jit(solution)/shard_map/ppermute | solution.py:20
  53.8 2.9 %collective-permute-done.8.refs_4_ = bf16[256,512]{1,0:T(8,128)(2,1)S(1)} collective-permute-done((bf16[256,512]{1,0:T(8,128)(2,1)S(1)}, bf16[256,512]{1,0:T(8,128)(2,1)S(1)}, u32[]{:S(2)}, u32[]{:S(2)}) %collective-permute-start.8) | collective-permute-done | bytes 262176 | tf_op jit(solution)/shard_map/ppermute | solution.py:20
  56.7 0.0 collective-permute-done.9.refs_0_
  56.7 0.0 collective-permute-start.13
  56.7 0.5 collective-permute-start.10
  57.2 0.0 collective-permute-start.11
  57.2 2.3 %collective-permute-done.12.refs_5_ = bf16[256,512]{1,0:T(8,128)(2,1)S(1)} collective-permute-done((bf16[256,512]{1,0:T(8,128)(2,1)S(1)}, bf16[256,512]{1,0:T(8,128)(2,1)S(1)}, u32[]{:S(2)}, u32[]{:S(2)}) %collective-permute-start.12) | collective-permute-done | bytes 262176 | tf_op jit(solution)/shard_map/ppermute | solution.py:20
  59.5 0.0 collective-permute-done.13.refs_6_
  59.5 0.0 collective-permute-start.14
  59.6 0.1 collective-permute-start.18
  59.6 0.0 collective-permute-done.16.refs_4_
  59.7 0.0 copy-start
  59.7 1.6 %collective-permute-start.17 = (bf16[512,256]{1,0:T(8,128)(2,1)S(1)}, bf16[512,256]{1,0:T(8,128)(2,1)S(1)}, u32[]{:S(2)}, u32[]{:S(2)}) collective-permute-start(bf16[512,256]{1,0:T(8,128)(2,1)S(1)} %slice.6), channel_id=1, source_target_pairs={{0,16},{16,0},{1,17},{17,1},{2,18},{18,2},{3,19},{19,3},{4,20},{20... | collective-permute-start | bytes 786440 | tf_op jit(solution)/shard_map/ppermute | solution.py:24
  61.2 0.0 collective-permute-done.10.refs_2_
  61.2 0.0 collective-permute-done.11.refs_3_
  61.2 0.0 collective-permute-done.14.refs_7_
  61.3 0.7 gather.1.rows_ref
  62.0 2.3 %project3.1 = (bf16[128,768]{1,0:T(8,128)(2,1)S(1)}, bf16[128,768]{1,0:T(8,128)(2,1)S(1)}, bf16[128,768]{1,0:T(8,128)(2,1)S(1)}, bf16[128,768]{1,0:T(8,128)(2,1)S(1)}) custom-call(s32[3]{0:T(128)S(1)} %pad_add_fusion.place_ref, bf16[512,2048]{1,0:T(8,128)(2,1)S(1)} %gather.1.rows_ref, bf16[2048,256]{1,0:T(8,128)(2,1)S(1)} %copy-done, ...), custom_call_target="tpu_custom_call" | custom-call | tf_op jit(solution)/shard_map/project3/pallas_call | solution.py:275
  64.3 0.3 collective-permute-start.22
  64.6 0.9 %collective-permute-start.23 = (bf16[128,768]{1,0:T(8,128)(2,1)S(1)}, bf16[128,768]{1,0:T(8,128)(2,1)S(1)}, u32[]{:S(2)}, u32[]{:S(2)}) collective-permute-start(bf16[128,768]{1,0:T(8,128)(2,1)S(1)} %get-tuple-element.53), channel_id=1, source_target_pairs={{0,2},{1,3},{2,0},{3,1},{4,6},{5,7},{6,4},{7,5},{8,10},{9,11},{10,... | collective-permute-start | bytes 589832 | tf_op jit(solution)/shard_map/ppermute | solution.py:20
  65.5 0.7 collective-permute-start.24
  66.2 2.1 %collective-permute-done.18.refs_2_ = bf16[512,256]{1,0:T(8,128)(2,1)S(1)} collective-permute-done((bf16[512,256]{1,0:T(8,128)(2,1)S(1)}, bf16[512,256]{1,0:T(8,128)(2,1)S(1)}, u32[]{:S(2)}, u32[]{:S(2)}) %collective-permute-start.18) | collective-permute-done | bytes 262176 | tf_op jit(solution)/shard_map/ppermute | solution.py:20
  68.3 0.1 collective-permute-done.17.refs_1_
  68.5 1.2 %project1.1 = (bf16[128,256]{1,0:T(8,128)(2,1)S(1)}, bf16[128,256]{1,0:T(8,128)(2,1)S(1)}, bf16[128,256]{1,0:T(8,128)(2,1)S(1)}, bf16[128,256]{1,0:T(8,128)(2,1)S(1)}) custom-call(s32[3]{0:T(128)S(1)} %pad_add_fusion.place_ref, bf16[512,2048]{1,0:T(8,128)(2,1)S(1)} %gather.1.rows_ref, bf16[1024,256]{1,0:T(8,128)(2,1)S(1)} %collective-permute-done.9.refs_0_, ...), custom_call_target="tpu_custom_call" | custom-call | tf_op jit(solution)/shard_map/project1/pallas_call | solution.py:275
  69.7 0.1 collective-permute-start.19
  69.8 1.0 %collective-permute-start.20 = (bf16[128,256]{1,0:T(8,128)(2,1)S(1)}, bf16[128,256]{1,0:T(8,128)(2,1)S(1)}, u32[]{:S(2)}, u32[]{:S(2)}) collective-permute-start(bf16[128,256]{1,0:T(8,128)(2,1)S(1)} %get-tuple-element.49), channel_id=1, source_target_pairs={{0,2},{1,3},{2,0},{3,1},{4,6},{5,7},{6,4},{7,5},{8,10},{9,11},{10,... | collective-permute-start | bytes 196616 | tf_op jit(solution)/shard_map/ppermute | solution.py:20
  70.8 0.0 collective-permute-done.22.refs_1_
  70.8 0.9 %collective-permute-start.21 = (bf16[128,256]{1,0:T(8,128)(2,1)S(1)}, bf16[128,256]{1,0:T(8,128)(2,1)S(1)}, u32[]{:S(2)}, u32[]{:S(2)}) collective-permute-start(bf16[128,256]{1,0:T(8,128)(2,1)S(1)} %get-tuple-element.50), channel_id=1, source_target_pairs={{0,3},{1,2},{2,1},{3,0},{4,7},{5,6},{6,5},{7,4},{8,11},{9,10},{10,... | collective-permute-start | bytes 196616 | tf_op jit(solution)/shard_map/ppermute | solution.py:20
  71.7 0.7 collective-permute-done.23.refs_2_
  72.3 2.9 %collective-permute-done.24.refs_3_ = bf16[128,768]{1,0:T(8,128)(2,1)S(1)} collective-permute-done((bf16[128,768]{1,0:T(8,128)(2,1)S(1)}, bf16[128,768]{1,0:T(8,128)(2,1)S(1)}, u32[]{:S(2)}, u32[]{:S(2)}) %collective-permute-start.24) | collective-permute-done | bytes 196640 | tf_op jit(solution)/shard_map/ppermute | solution.py:20
  75.3 1.5 %place0.1.refs_4_ = bf16[128,4096]{1,0:T(8,128)(2,1)} custom-call(s32[3]{0:T(128)S(1)} %pad_add_fusion.place_ref, bf16[128,768]{1,0:T(8,128)(2,1)S(1)} %get-tuple-element.51.refs_0_, bf16[128,768]{1,0:T(8,128)(2,1)S(1)} %collective-permute-done.22.refs_1_, bf16[128,768]{1,0:T(8,128)(2,1)S(1)} %collective-permute-done.23.refs_2_, ...), custom_call_target="tpu_custom_call" | custom-call | tf_op jit(solution)/shard_map/place0/pallas_call | solution.py:281
  76.8 0.0 collective-permute-done.19.refs_1_
  76.8 1.2 %collective-permute-done.20.refs_2_ = bf16[128,256]{1,0:T(8,128)(2,1)S(1)} collective-permute-done((bf16[128,256]{1,0:T(8,128)(2,1)S(1)}, bf16[128,256]{1,0:T(8,128)(2,1)S(1)}, u32[]{:S(2)}, u32[]{:S(2)}) %collective-permute-start.20) | collective-permute-done | bytes 65568 | tf_op jit(solution)/shard_map/ppermute | solution.py:20
  78.0 0.1 collective-permute-done.21.refs_3_
  78.1 1.3 %place1.1 = bf16[128,4096]{1,0:T(8,128)(2,1)} custom-call(s32[3]{0:T(128)S(1)} %pad_add_fusion.place_ref, bf16[128,256]{1,0:T(8,128)(2,1)S(1)} %get-tuple-element.47.refs_0_, bf16[128,256]{1,0:T(8,128)(2,1)S(1)} %collective-permute-done.19.refs_1_, bf16[128,256]{1,0:T(8,128)(2,1)S(1)} %collective-permute-done.20.refs_2_, ...), custom_call_target="tpu_custom_call", output_to_operand_aliasing={{}: (5, {})} | custom-call | tf_op jit(solution)/shard_map/place1/pallas_call | solution.py:281
  (4 shorter events, 0.0 us)
Async XLA Ops:
  1.7 28.2 %collective-permute-start.4 = (bf16[1024,256]{1,0:T(8,128)(2,1)S(1)}, bf16[1024,256]{1,0:T(8,128)(2,1)S(1)}, u32[]{:S(2)}, u32[]{:S(2)}) collective-permute-start(bf16[1024,256]{1,0:T(8,128)(2,1)S(1)} %pack.1.other_ref), channel_id=1, source_target_pairs={{0,4},{1,5},{2,6},{3,7},{4,0},{5,1},{6,2},{7,3},{8,12},{9,13},{10,... | collective-permute-start | bytes 1572872 | tf_op jit(solution)/shard_map/ppermute | solution.py:20
  4.8 25.6 %collective-permute-start.3 = (bf16[1024,256]{1,0:T(8,128)(2,1)S(1)}, bf16[1024,256]{1,0:T(8,128)(2,1)S(1)}, u32[]{:S(2)}, u32[]{:S(2)}) collective-permute-start(bf16[1024,256]{1,0:T(8,128)(2,1)S(1)} %pack.1.other_ref), channel_id=1, source_target_pairs={{0,8},{1,9},{2,10},{3,11},{4,12},{5,13},{6,14},{7,15},{8,0},{9,1},... | collective-permute-start | bytes 1572872 | tf_op jit(solution)/shard_map/ppermute | solution.py:20
  9.2 11.4 %collective-permute-start.2 = (bf16[384,512]{1,0:T(8,128)(2,1)S(1)}, bf16[384,512]{1,0:T(8,128)(2,1)S(1)}, u32[]{:S(2)}, u32[]{:S(2)}) collective-permute-start(bf16[384,512]{1,0:T(8,128)(2,1)S(1)} %get-tuple-element.33), channel_id=1, source_target_pairs={{0,3},{1,2},{2,1},{3,0},{4,7},{5,6},{6,5},{7,4},{8,11},{9,10},{10,... | collective-permute-start | bytes 1179656 | tf_op jit(solution)/shard_map/ppermute | solution.py:20
  9.6 36.7 %copy-start.1 = (s32[16]{0:T(128)S(1)}, s32[16]{0:T(128)}, u32[]{:S(2)}) copy-start(s32[16]{0:T(128)} %doc_ref.3) | copy-start | bytes 196
  9.6 19.4 %collective-permute-start.1 = (bf16[384,512]{1,0:T(8,128)(2,1)S(1)}, bf16[384,512]{1,0:T(8,128)(2,1)S(1)}, u32[]{:S(2)}, u32[]{:S(2)}) collective-permute-start(bf16[384,512]{1,0:T(8,128)(2,1)S(1)} %get-tuple-element.30.other_ref), channel_id=1, source_target_pairs={{0,2},{1,3},{2,0},{3,1},{4,6},{5,7},{6,4},{7,5},{8,10},{9,11},{10,... | collective-permute-start | bytes 1179656 | tf_op jit(solution)/shard_map/ppermute | solution.py:20
  12.7 16.4 %collective-permute-start = (bf16[384,512]{1,0:T(8,128)(2,1)S(1)}, bf16[384,512]{1,0:T(8,128)(2,1)S(1)}, u32[]{:S(2)}, u32[]{:S(2)}) collective-permute-start(bf16[384,512]{1,0:T(8,128)(2,1)S(1)} %get-tuple-element.32), channel_id=1, source_target_pairs={{0,1},{1,0},{2,3},{3,2},{4,5},{5,4},{6,7},{7,6},{8,9},{9,8},{10,11... | collective-permute-start | bytes 1179656 | tf_op jit(solution)/shard_map/ppermute | solution.py:20
  30.3 19.5 %collective-permute-start.15 = (bf16[1024,256]{1,0:T(8,128)(2,1)S(1)}, bf16[1024,256]{1,0:T(8,128)(2,1)S(1)}, u32[]{:S(2)}, u32[]{:S(2)}) collective-permute-start(bf16[1024,256]{1,0:T(8,128)(2,1)S(1)} %collective-permute-done.3.refs_1_), channel_id=1, source_target_pairs={{0,16},{16,0},{1,17},{17,1},{2,18},{18,2},{3,19},{19,3},{4,20},{20... | collective-permute-start | bytes 1572872 | tf_op jit(solution)/shard_map/ppermute | solution.py:24
  31.8 14.5 %collective-permute-start.5 = (bf16[256,512]{1,0:T(8,128)(2,1)S(1)}, bf16[256,512]{1,0:T(8,128)(2,1)S(1)}, u32[]{:S(2)}, u32[]{:S(2)}) collective-permute-start(bf16[256,512]{1,0:T(8,128)(2,1)S(1)} %get-tuple-element.36), channel_id=1, source_target_pairs={{0,4},{1,5},{2,6},{3,7},{4,0},{5,1},{6,2},{7,3},{8,12},{9,13},{10,... | collective-permute-start | bytes 786440 | tf_op jit(solution)/shard_map/ppermute | solution.py:20
  32.3 9.6 %collective-permute-start.6 = (bf16[128,512]{1,0:T(8,128)(2,1)S(1)}, bf16[128,512]{1,0:T(8,128)(2,1)S(1)}, u32[]{:S(2)}, u32[]{:S(2)}) collective-permute-start(bf16[128,512]{1,0:T(8,128)(2,1)S(1)} %get-tuple-element.37), channel_id=1, source_target_pairs={{0,8},{1,9},{2,10},{3,11},{4,12},{5,13},{6,14},{7,15},{8,0},{9,1},... | collective-permute-start | bytes 393224 | tf_op jit(solution)/shard_map/ppermute | solution.py:20
  34.9 11.0 %collective-permute-start.7 = (bf16[128,512]{1,0:T(8,128)(2,1)S(1)}, bf16[128,512]{1,0:T(8,128)(2,1)S(1)}, u32[]{:S(2)}, u32[]{:S(2)}) collective-permute-start(bf16[128,512]{1,0:T(8,128)(2,1)S(1)} %get-tuple-element.37), channel_id=1, source_target_pairs={{0,12},{1,13},{2,14},{3,15},{4,8},{5,9},{6,10},{7,11},{8,4},{9,5},... | collective-permute-start | bytes 393224 | tf_op jit(solution)/shard_map/ppermute | solution.py:20
  41.9 14.8 %collective-permute-start.9 = (bf16[1024,256]{1,0:T(8,128)(2,1)S(1)}, bf16[1024,256]{1,0:T(8,128)(2,1)S(1)}, u32[]{:S(2)}, u32[]{:S(2)}) collective-permute-start(bf16[1024,256]{1,0:T(8,128)(2,1)S(1)} %collective-permute-done.3.refs_1_), channel_id=1, source_target_pairs={{0,4},{1,5},{2,6},{3,7},{4,0},{5,1},{6,2},{7,3},{8,12},{9,13},{10,... | collective-permute-start | bytes 1572872 | tf_op jit(solution)/shard_map/ppermute | solution.py:20
  48.7 8.0 %collective-permute-start.8 = (bf16[256,512]{1,0:T(8,128)(2,1)S(1)}, bf16[256,512]{1,0:T(8,128)(2,1)S(1)}, u32[]{:S(2)}, u32[]{:S(2)}) collective-permute-start(bf16[256,512]{1,0:T(8,128)(2,1)S(1)} %attend0.1.refs_7_.refs_0_), channel_id=1, source_target_pairs={{0,2},{1,3},{2,0},{3,1},{4,6},{5,7},{6,4},{7,5},{8,10},{9,11},{10,... | collective-permute-start | bytes 786440 | tf_op jit(solution)/shard_map/ppermute | solution.py:20
  49.9 9.8 %collective-permute-start.16 = (bf16[1024,256]{1,0:T(8,128)(2,1)S(1)}, bf16[1024,256]{1,0:T(8,128)(2,1)S(1)}, u32[]{:S(2)}, u32[]{:S(2)}) collective-permute-start(bf16[1024,256]{1,0:T(8,128)(2,1)S(1)} %collective-permute-done.4.refs_3_), channel_id=1, source_target_pairs={{0,16},{16,0},{1,17},{17,1},{2,18},{18,2},{3,19},{19,3},{4,20},{20... | collective-permute-start | bytes 1572872 | tf_op jit(solution)/shard_map/ppermute | solution.py:24
  52.8 6.8 %collective-permute-start.12 = (bf16[256,512]{1,0:T(8,128)(2,1)S(1)}, bf16[256,512]{1,0:T(8,128)(2,1)S(1)}, u32[]{:S(2)}, u32[]{:S(2)}) collective-permute-start(bf16[256,512]{1,0:T(8,128)(2,1)S(1)} %attend1.1.refs_1_), channel_id=1, source_target_pairs={{0,2},{1,3},{2,0},{3,1},{4,6},{5,7},{6,4},{7,5},{8,10},{9,11},{10,... | collective-permute-start | bytes 786440 | tf_op jit(solution)/shard_map/ppermute | solution.py:20
  56.7 2.8 %collective-permute-start.13 = (bf16[256,512]{1,0:T(8,128)(2,1)S(1)}, bf16[256,512]{1,0:T(8,128)(2,1)S(1)}, u32[]{:S(2)}, u32[]{:S(2)}) collective-permute-start(bf16[256,512]{1,0:T(8,128)(2,1)S(1)} %collective-permute-done.8.refs_4_), channel_id=1, source_target_pairs={{0,1},{1,0},{2,3},{3,2},{4,5},{5,4},{6,7},{7,6},{8,9},{9,8},{10,11... | collective-permute-start | bytes 786440 | tf_op jit(solution)/shard_map/ppermute | solution.py:20
  56.7 4.5 %collective-permute-start.10 = (bf16[256,512]{1,0:T(8,128)(2,1)S(1)}, bf16[256,512]{1,0:T(8,128)(2,1)S(1)}, u32[]{:S(2)}, u32[]{:S(2)}) collective-permute-start(bf16[256,512]{1,0:T(8,128)(2,1)S(1)} %attend0.1.refs_7_.refs_0_), channel_id=1, source_target_pairs={{0,1},{1,0},{2,3},{3,2},{4,5},{5,4},{6,7},{7,6},{8,9},{9,8},{10,11... | collective-permute-start | bytes 786440 | tf_op jit(solution)/shard_map/ppermute | solution.py:20
  57.2 4.0 %collective-permute-start.11 = (bf16[256,512]{1,0:T(8,128)(2,1)S(1)}, bf16[256,512]{1,0:T(8,128)(2,1)S(1)}, u32[]{:S(2)}, u32[]{:S(2)}) collective-permute-start(bf16[256,512]{1,0:T(8,128)(2,1)S(1)} %attend1.1.refs_1_), channel_id=1, source_target_pairs={{0,1},{1,0},{2,3},{3,2},{4,5},{5,4},{6,7},{7,6},{8,9},{9,8},{10,11... | collective-permute-start | bytes 786440 | tf_op jit(solution)/shard_map/ppermute | solution.py:20
  59.5 1.7 %collective-permute-start.14 = (bf16[256,512]{1,0:T(8,128)(2,1)S(1)}, bf16[256,512]{1,0:T(8,128)(2,1)S(1)}, u32[]{:S(2)}, u32[]{:S(2)}) collective-permute-start(bf16[256,512]{1,0:T(8,128)(2,1)S(1)} %collective-permute-done.12.refs_5_), channel_id=1, source_target_pairs={{0,1},{1,0},{2,3},{3,2},{4,5},{5,4},{6,7},{7,6},{8,9},{9,8},{10,11... | collective-permute-start | bytes 786440 | tf_op jit(solution)/shard_map/ppermute | solution.py:20
  59.6 8.8 %collective-permute-start.18 = (bf16[512,256]{1,0:T(8,128)(2,1)S(1)}, bf16[512,256]{1,0:T(8,128)(2,1)S(1)}, u32[]{:S(2)}, u32[]{:S(2)}) collective-permute-start(bf16[512,256]{1,0:T(8,128)(2,1)S(1)} %slice.7), channel_id=1, source_target_pairs={{0,4},{1,5},{2,6},{3,7},{4,0},{5,1},{6,2},{7,3},{8,12},{9,13},{10,... | collective-permute-start | bytes 786440 | tf_op jit(solution)/shard_map/ppermute | solution.py:20
  59.7 2.3 %copy-start = (bf16[2048,256]{1,0:T(8,128)(2,1)S(1)}, bf16[2048,256]{1,0:T(8,128)(2,1)}, u32[]{:S(2)}) copy-start(bf16[2048,256]{1,0:T(8,128)(2,1)} %refs_0_.1) | copy-start | bytes 3145732
  59.7 8.8 %collective-permute-start.17 = (bf16[512,256]{1,0:T(8,128)(2,1)S(1)}, bf16[512,256]{1,0:T(8,128)(2,1)S(1)}, u32[]{:S(2)}, u32[]{:S(2)}) collective-permute-start(bf16[512,256]{1,0:T(8,128)(2,1)S(1)} %slice.6), channel_id=1, source_target_pairs={{0,16},{16,0},{1,17},{17,1},{2,18},{18,2},{3,19},{19,3},{4,20},{20... | collective-permute-start | bytes 786440 | tf_op jit(solution)/shard_map/ppermute | solution.py:24
  64.3 6.5 %collective-permute-start.22 = (bf16[128,768]{1,0:T(8,128)(2,1)S(1)}, bf16[128,768]{1,0:T(8,128)(2,1)S(1)}, u32[]{:S(2)}, u32[]{:S(2)}) collective-permute-start(bf16[128,768]{1,0:T(8,128)(2,1)S(1)} %get-tuple-element.52), channel_id=1, source_target_pairs={{0,1},{1,0},{2,3},{3,2},{4,5},{5,4},{6,7},{7,6},{8,9},{9,8},{10,11... | collective-permute-start | bytes 589832 | tf_op jit(solution)/shard_map/ppermute | solution.py:20
  64.6 7.7 %collective-permute-start.23 = (bf16[128,768]{1,0:T(8,128)(2,1)S(1)}, bf16[128,768]{1,0:T(8,128)(2,1)S(1)}, u32[]{:S(2)}, u32[]{:S(2)}) collective-permute-start(bf16[128,768]{1,0:T(8,128)(2,1)S(1)} %get-tuple-element.53), channel_id=1, source_target_pairs={{0,2},{1,3},{2,0},{3,1},{4,6},{5,7},{6,4},{7,5},{8,10},{9,11},{10,... | collective-permute-start | bytes 589832 | tf_op jit(solution)/shard_map/ppermute | solution.py:20
  65.5 9.7 %collective-permute-start.24 = (bf16[128,768]{1,0:T(8,128)(2,1)S(1)}, bf16[128,768]{1,0:T(8,128)(2,1)S(1)}, u32[]{:S(2)}, u32[]{:S(2)}) collective-permute-start(bf16[128,768]{1,0:T(8,128)(2,1)S(1)} %get-tuple-element.54), channel_id=1, source_target_pairs={{0,3},{1,2},{2,1},{3,0},{4,7},{5,6},{6,5},{7,4},{8,11},{9,10},{10,... | collective-permute-start | bytes 589832 | tf_op jit(solution)/shard_map/ppermute | solution.py:20
  69.7 7.1 %collective-permute-start.19 = (bf16[128,256]{1,0:T(8,128)(2,1)S(1)}, bf16[128,256]{1,0:T(8,128)(2,1)S(1)}, u32[]{:S(2)}, u32[]{:S(2)}) collective-permute-start(bf16[128,256]{1,0:T(8,128)(2,1)S(1)} %get-tuple-element.48), channel_id=1, source_target_pairs={{0,1},{1,0},{2,3},{3,2},{4,5},{5,4},{6,7},{7,6},{8,9},{9,8},{10,11... | collective-permute-start | bytes 196616 | tf_op jit(solution)/shard_map/ppermute | solution.py:20
  69.8 8.2 %collective-permute-start.20 = (bf16[128,256]{1,0:T(8,128)(2,1)S(1)}, bf16[128,256]{1,0:T(8,128)(2,1)S(1)}, u32[]{:S(2)}, u32[]{:S(2)}) collective-permute-start(bf16[128,256]{1,0:T(8,128)(2,1)S(1)} %get-tuple-element.49), channel_id=1, source_target_pairs={{0,2},{1,3},{2,0},{3,1},{4,6},{5,7},{6,4},{7,5},{8,10},{9,11},{10,... | collective-permute-start | bytes 196616 | tf_op jit(solution)/shard_map/ppermute | solution.py:20
  70.8 7.3 %collective-permute-start.21 = (bf16[128,256]{1,0:T(8,128)(2,1)S(1)}, bf16[128,256]{1,0:T(8,128)(2,1)S(1)}, u32[]{:S(2)}, u32[]{:S(2)}) collective-permute-start(bf16[128,256]{1,0:T(8,128)(2,1)S(1)} %get-tuple-element.50), channel_id=1, source_target_pairs={{0,3},{1,2},{2,1},{3,0},{4,7},{5,6},{6,5},{7,4},{8,11},{9,10},{10,... | collective-permute-start | bytes 196616 | tf_op jit(solution)/shard_map/ppermute | solution.py:20

commit v9 on v8

--- a/solution.py
+++ b/solution.py
@@ -126,12 +126,19 @@
         jnp.where(document == doc_ref[jnp.bitwise_xor(place_ref[2], 2 * half + part)], 0.0, -jnp.inf)
         for part in range(2)
     ]
+    def score_of(head):
+        columns = slice(head * HD, (head + 1) * HD)
+        query = jnp.concatenate([own[2 * half + part][0:128, columns] for part in range(2)], 0)
+        return lax.dot_general(
+            query, key_ref[:, columns], (((1,), (1,)), ((), ())), preferred_element_type=jnp.float32
+        )
+
+    following = score_of(0)
     for head in range(heads):
         columns = slice(head * HD, (head + 1) * HD)
-        query = jnp.concatenate([own[2 * half + part][0:128, columns] for part in range(2)], 0)
-        score = lax.dot_general(
-            query, key_ref[:, columns], (((1,), (1,)), ((), ())), preferred_element_type=jnp.float32
-        )
+        score = following
+        if head + 1 < heads:
+            following = score_of(head + 1)
         raised, inverse = [], []
         for part in range(2):
             biased = score[128 * part : 128 * part + 128, :] + bias[part]

time: 79.5 us -> 78.7 us (0.990)
  Pallas kernels: 17.9 us -> 17 us
    pallas_call x2, Pallas kernels: 4.77 us -> 3.9 us  [per_device_fast(): call(functools.partial(attention_kernel, n), [(2 * length, share)], [pl.B...]
  transfers between devices with their start and end apart: 25 -> 25, of which waited for: 14 -> 16; matrix products, arithmetic and copies ran while one was open for 0% -> 0% of each run, Pallas kernels for 19% -> 18%
where the time goes in v9:
time: 78.7 us; the launch traced here: 78.5 us
  waiting for transfers between devices  37.1 us (47%)
  starting transfers between devices  24.1 us (31%)
  Pallas kernels  17 us (22%)
    ppermute x22, waiting for transfers between devices, swap(): return lax.ppermute(value, 'ctx', pairs)  36.6 us
    ppermute x22, starting transfers between devices, swap(): return lax.ppermute(value, 'ctx', pairs)  20.9 us
    pallas_call x2, Pallas kernels, per_device_fast(): call(functools.partial(attention_kernel, n), [(2 * length, share)], [pl.B...  3.9 us
    pallas_call x2, Pallas kernels, per_device_fast(): call(project_kernel, [(length, count * wide)] * 4, vmem(1 + len(blocks)),...  3.58 us
    ppermute x3, starting transfers between devices, swap_groups(): return lax.ppermute(value, 'groups', [(0, 1), (1, 0)])  3.16 us
    pallas_call x2, Pallas kernels, per_device_fast(): call(functools.partial(place_kernel, n), [(length, 16 * wide)], anywhere(...  2.78 us
    pallas_call x1, Pallas kernels, per_device_fast(): call(functools.partial(pack_kernel, (1, 0)), [(3 * length, share)] * 2, a...  1.8 us
    pallas_call x1, Pallas kernels, per_device_fast(): call(functools.partial(pack_kernel, (2, 3)), [(3 * length, share)] * 2, a...  1.8 us
  transfers between devices with their start and end apart: 25, of which 16 were waited for; matrix products, arithmetic and copies ran while one was open for 0% of the time, Pallas kernels for 18%

profile of v9, /device:TPU:0, one launch (start us, length us, event | category | flops | bytes accessed | tf_op | source)
XLA Modules:
  0.0 78.5 jit_solution(13457470320117121773)
XLA Ops:
  0.0 0.1 pad_add_fusion.place_ref
  0.1 1.6 %pack.1.other_ref = bf16[1024,256]{1,0:T(8,128)(2,1)S(1)} custom-call(s32[3]{0:T(128)S(1)} %pad_add_fusion.place_ref, bf16[128,2048]{1,0:T(8,128)(2,1)} %q_ref.5, bf16[128,2048]{1,0:T(8,128)(2,1)} %k_ref.5, bf16[128,2048]{1,0:T(8,128)(2,1)} %v_ref.5, bf16[2048,256]{1,0:T(8,128)(2,1)} %refs_0_.1), custom_call_target="tpu_custom_call" | custom-call | tf_op jit(solution)/shard_map/pack/pallas_call | solution.py:222
  1.7 3.1 %collective-permute-start.4 = (bf16[1024,256]{1,0:T(8,128)(2,1)S(1)}, bf16[1024,256]{1,0:T(8,128)(2,1)S(1)}, u32[]{:S(2)}, u32[]{:S(2)}) collective-permute-start(bf16[1024,256]{1,0:T(8,128)(2,1)S(1)} %pack.1.other_ref), channel_id=1, source_target_pairs={{0,4},{1,5},{2,6},{3,7},{4,0},{5,1},{6,2},{7,3},{8,12},{9,13},{10,... | collective-permute-start | bytes 1572872 | tf_op jit(solution)/shard_map/ppermute | solution.py:20
  4.8 2.6 %collective-permute-start.3 = (bf16[1024,256]{1,0:T(8,128)(2,1)S(1)}, bf16[1024,256]{1,0:T(8,128)(2,1)S(1)}, u32[]{:S(2)}, u32[]{:S(2)}) collective-permute-start(bf16[1024,256]{1,0:T(8,128)(2,1)S(1)} %pack.1.other_ref), channel_id=1, source_target_pairs={{0,8},{1,9},{2,10},{3,11},{4,12},{5,13},{6,14},{7,15},{8,0},{9,1},... | collective-permute-start | bytes 1572872 | tf_op jit(solution)/shard_map/ppermute | solution.py:20
  7.4 1.8 %pack0.1 = (bf16[384,512]{1,0:T(8,128)(2,1)S(1)}, bf16[384,512]{1,0:T(8,128)(2,1)S(1)}) custom-call(s32[3]{0:T(128)S(1)} %pad_add_fusion.place_ref, bf16[128,2048]{1,0:T(8,128)(2,1)} %q_ref.5, bf16[128,2048]{1,0:T(8,128)(2,1)} %k_ref.5, bf16[128,2048]{1,0:T(8,128)(2,1)} %v_ref.5, bf16[1024,256]{1,0:T(8,128)(2,1)S(1)} %pack.1.other_ref), custom_call_target="tpu_custom_call" | custom-call | tf_op jit(solution)/shard_map/pack0/pallas_call | solution.py:229
  9.2 0.5 collective-permute-start.2
  9.6 1.2 %collective-permute-start.1 = (bf16[384,512]{1,0:T(8,128)(2,1)S(1)}, bf16[384,512]{1,0:T(8,128)(2,1)S(1)}, u32[]{:S(2)}, u32[]{:S(2)}) collective-permute-start(bf16[384,512]{1,0:T(8,128)(2,1)S(1)} %get-tuple-element.30.other_ref), channel_id=1, source_target_pairs={{0,2},{1,3},{2,0},{3,1},{4,6},{5,7},{6,4},{7,5},{8,10},{9,11},{10,... | collective-permute-start | bytes 1179656 | tf_op jit(solution)/shard_map/ppermute | solution.py:20
  10.8 1.8 %pack1.1 = (bf16[384,512]{1,0:T(8,128)(2,1)S(1)}, bf16[384,512]{1,0:T(8,128)(2,1)S(1)}) custom-call(s32[3]{0:T(128)S(1)} %pad_add_fusion.place_ref, bf16[128,2048]{1,0:T(8,128)(2,1)} %q_ref.5, bf16[128,2048]{1,0:T(8,128)(2,1)} %k_ref.5, bf16[128,2048]{1,0:T(8,128)(2,1)} %v_ref.5, bf16[384,512]{1,0:T(8,128)(2,1)S(1)} %get-tuple-element.30.other_ref), custom_call_target="tpu_custom_call" | custom-call | flops 2000000000 | bytes 40000000 | tf_op jit(solution)/shard_map/pack1/pallas_call | solution.py:236
  12.7 0.3 collective-permute-start
  13.0 7.6 %collective-permute-done.2.a3.refs_3_ = bf16[384,512]{1,0:T(8,128)(2,1)S(1)} collective-permute-done((bf16[384,512]{1,0:T(8,128)(2,1)S(1)}, bf16[384,512]{1,0:T(8,128)(2,1)S(1)}, u32[]{:S(2)}, u32[]{:S(2)}) %collective-permute-start.2) | collective-permute-done | bytes 393248 | tf_op jit(solution)/shard_map/ppermute | solution.py:20
  20.6 8.5 %collective-permute-done.1.a2.refs_2_ = bf16[384,512]{1,0:T(8,128)(2,1)S(1)} collective-permute-done((bf16[384,512]{1,0:T(8,128)(2,1)S(1)}, bf16[384,512]{1,0:T(8,128)(2,1)S(1)}, u32[]{:S(2)}, u32[]{:S(2)}) %collective-permute-start.1) | collective-permute-done | bytes 393248 | tf_op jit(solution)/shard_map/ppermute | solution.py:20
  29.1 0.0 collective-permute-done.a1.refs_1_
  29.1 0.8 %coarse.1 = (bf16[256,512]{1,0:T(8,128)(2,1)S(1)}, bf16[128,512]{1,0:T(8,128)(2,1)S(1)}) custom-call(s32[3]{0:T(128)S(1)} %pad_add_fusion.place_ref, bf16[384,512]{1,0:T(8,128)(2,1)S(1)} %get-tuple-element.31.a0.refs_0_.refs_7_, bf16[384,512]{1,0:T(8,128)(2,1)S(1)} %collective-permute-done.a1.refs_1_, ...), custom_call_target="tpu_custom_call" | custom-call | tf_op jit(solution)/shard_map/coarse/pallas_call | solution.py:247
  29.9 0.0 collective-permute-done.4.refs_3_
  29.9 0.4 collective-permute-done.3.refs_1_
  30.3 1.5 %collective-permute-start.15 = (bf16[1024,256]{1,0:T(8,128)(2,1)S(1)}, bf16[1024,256]{1,0:T(8,128)(2,1)S(1)}, u32[]{:S(2)}, u32[]{:S(2)}) collective-permute-start(bf16[1024,256]{1,0:T(8,128)(2,1)S(1)} %collective-permute-done.3.refs_1_), channel_id=1, source_target_pairs={{0,16},{16,0},{1,17},{17,1},{2,18},{18,2},{3,19},{19,3},{4,20},{20... | collective-permute-start | bytes 1572872 | tf_op jit(solution)/shard_map/ppermute | solution.py:24
  31.8 0.4 collective-permute-start.5
  32.3 2.6 %collective-permute-start.6 = (bf16[128,512]{1,0:T(8,128)(2,1)S(1)}, bf16[128,512]{1,0:T(8,128)(2,1)S(1)}, u32[]{:S(2)}, u32[]{:S(2)}) collective-permute-start(bf16[128,512]{1,0:T(8,128)(2,1)S(1)} %get-tuple-element.37), channel_id=1, source_target_pairs={{0,8},{1,9},{2,10},{3,11},{4,12},{5,13},{6,14},{7,15},{8,0},{9,1},... | collective-permute-start | bytes 393224 | tf_op jit(solution)/shard_map/ppermute | solution.py:20
  34.9 1.4 %collective-permute-start.7 = (bf16[128,512]{1,0:T(8,128)(2,1)S(1)}, bf16[128,512]{1,0:T(8,128)(2,1)S(1)}, u32[]{:S(2)}, u32[]{:S(2)}) collective-permute-start(bf16[128,512]{1,0:T(8,128)(2,1)S(1)} %get-tuple-element.37), channel_id=1, source_target_pairs={{0,12},{1,13},{2,14},{3,15},{4,8},{5,9},{6,10},{7,11},{8,4},{9,5},... | collective-permute-start | bytes 393224 | tf_op jit(solution)/shard_map/ppermute | solution.py:20
  36.2 5.7 %collective-permute-done.6.refs_5_ = bf16[128,512]{1,0:T(8,128)(2,1)S(1)} collective-permute-done((bf16[128,512]{1,0:T(8,128)(2,1)S(1)}, bf16[128,512]{1,0:T(8,128)(2,1)S(1)}, u32[]{:S(2)}, u32[]{:S(2)}) %collective-permute-start.6) | collective-permute-done | bytes 131104 | tf_op jit(solution)/shard_map/ppermute | solution.py:20
  41.9 2.2 %collective-permute-start.9 = (bf16[1024,256]{1,0:T(8,128)(2,1)S(1)}, bf16[1024,256]{1,0:T(8,128)(2,1)S(1)}, u32[]{:S(2)}, u32[]{:S(2)}) collective-permute-start(bf16[1024,256]{1,0:T(8,128)(2,1)S(1)} %collective-permute-done.3.refs_1_), channel_id=1, source_target_pairs={{0,4},{1,5},{2,6},{3,7},{4,0},{5,1},{6,2},{7,3},{8,12},{9,13},{10,... | collective-permute-start | bytes 1572872 | tf_op jit(solution)/shard_map/ppermute | solution.py:20
  44.1 1.7 %collective-permute-done.7.refs_6_ = bf16[128,512]{1,0:T(8,128)(2,1)S(1)} collective-permute-done((bf16[128,512]{1,0:T(8,128)(2,1)S(1)}, bf16[128,512]{1,0:T(8,128)(2,1)S(1)}, u32[]{:S(2)}, u32[]{:S(2)}) %collective-permute-start.7) | collective-permute-done | bytes 131104 | tf_op jit(solution)/shard_map/ppermute | solution.py:20
  45.9 0.4 collective-permute-done.5.refs_4_
  46.3 0.0 copy-done.1
  46.3 1.9 %attend0.1.refs_7_.refs_0_ = bf16[256,512]{1,0:T(8,128)(2,1)S(1)} custom-call(s32[3]{0:T(128)S(1)} %pad_add_fusion.place_ref, s32[16]{0:T(128)S(1)} %copy-done.1, bf16[384,512]{1,0:T(8,128)(2,1)S(1)} %get-tuple-element.31.a0.refs_0_.refs_7_, bf16[384,512]{1,0:T(8,128)(2,1)S(1)} %collective-permute-done.a1.refs_1_, ...), custom_call_target="tpu_custom_call" | custom-call | flops 2000000000 | bytes 40000000 | tf_op jit(solution)/shard_map/attend0/pallas_call | solution.py:262
  48.3 1.1 %collective-permute-start.8 = (bf16[256,512]{1,0:T(8,128)(2,1)S(1)}, bf16[256,512]{1,0:T(8,128)(2,1)S(1)}, u32[]{:S(2)}, u32[]{:S(2)}) collective-permute-start(bf16[256,512]{1,0:T(8,128)(2,1)S(1)} %attend0.1.refs_7_.refs_0_), channel_id=1, source_target_pairs={{0,2},{1,3},{2,0},{3,1},{4,6},{5,7},{6,4},{7,5},{8,10},{9,11},{10,... | collective-permute-start | bytes 786440 | tf_op jit(solution)/shard_map/ppermute | solution.py:20
  49.4 0.0 collective-permute-done.15.refs_2_
  49.4 0.5 collective-permute-start.16
  49.9 1.9 %attend1.1.refs_1_ = bf16[256,512]{1,0:T(8,128)(2,1)S(1)} custom-call(s32[3]{0:T(128)S(1)} %pad_add_fusion.place_ref, s32[16]{0:T(128)S(1)} %copy-done.1, bf16[384,512]{1,0:T(8,128)(2,1)S(1)} %get-tuple-element.31.a0.refs_0_.refs_7_, bf16[384,512]{1,0:T(8,128)(2,1)S(1)} %collective-permute-done.a1.refs_1_, ...), custom_call_target="tpu_custom_call" | custom-call | flops 2000000000 | bytes 40000000 | tf_op jit(solution)/shard_map/attend1/pallas_call | solution.py:262
  51.9 1.0 %collective-permute-start.12 = (bf16[256,512]{1,0:T(8,128)(2,1)S(1)}, bf16[256,512]{1,0:T(8,128)(2,1)S(1)}, u32[]{:S(2)}, u32[]{:S(2)}) collective-permute-start(bf16[256,512]{1,0:T(8,128)(2,1)S(1)} %attend1.1.refs_1_), channel_id=1, source_target_pairs={{0,2},{1,3},{2,0},{3,1},{4,6},{5,7},{6,4},{7,5},{8,10},{9,11},{10,... | collective-permute-start | bytes 786440 | tf_op jit(solution)/shard_map/ppermute | solution.py:20
  52.9 2.9 %collective-permute-done.8.refs_4_ = bf16[256,512]{1,0:T(8,128)(2,1)S(1)} collective-permute-done((bf16[256,512]{1,0:T(8,128)(2,1)S(1)}, bf16[256,512]{1,0:T(8,128)(2,1)S(1)}, u32[]{:S(2)}, u32[]{:S(2)}) %collective-permute-start.8) | collective-permute-done | bytes 262176 | tf_op jit(solution)/shard_map/ppermute | solution.py:20
  55.8 0.5 collective-permute-done.9.refs_0_
  56.3 0.0 collective-permute-start.13
  56.3 0.5 collective-permute-start.10
  56.8 0.0 collective-permute-start.11
  56.8 1.8 %collective-permute-done.12.refs_5_ = bf16[256,512]{1,0:T(8,128)(2,1)S(1)} collective-permute-done((bf16[256,512]{1,0:T(8,128)(2,1)S(1)}, bf16[256,512]{1,0:T(8,128)(2,1)S(1)}, u32[]{:S(2)}, u32[]{:S(2)}) %collective-permute-start.12) | collective-permute-done | bytes 262176 | tf_op jit(solution)/shard_map/ppermute | solution.py:20
  58.7 0.0 collective-permute-done.13.refs_6_
  58.7 0.0 collective-permute-start.14
  58.7 0.1 collective-permute-start.18
  58.8 0.4 collective-permute-done.16.refs_4_
  59.2 0.0 copy-start
  59.2 1.1 %collective-permute-start.17 = (bf16[512,256]{1,0:T(8,128)(2,1)S(1)}, bf16[512,256]{1,0:T(8,128)(2,1)S(1)}, u32[]{:S(2)}, u32[]{:S(2)}) collective-permute-start(bf16[512,256]{1,0:T(8,128)(2,1)S(1)} %slice.6), channel_id=1, source_target_pairs={{0,16},{16,0},{1,17},{17,1},{2,18},{18,2},{3,19},{19,3},{4,20},{20... | collective-permute-start | bytes 786440 | tf_op jit(solution)/shard_map/ppermute | solution.py:24
  60.4 0.0 collective-permute-done.10.refs_2_
  60.4 0.0 collective-permute-done.11.refs_3_
  60.4 0.0 collective-permute-done.14.refs_7_
  60.4 0.7 gather.1.rows_ref
  61.1 2.3 %project3.1 = (bf16[128,768]{1,0:T(8,128)(2,1)S(1)}, bf16[128,768]{1,0:T(8,128)(2,1)S(1)}, bf16[128,768]{1,0:T(8,128)(2,1)S(1)}, bf16[128,768]{1,0:T(8,128)(2,1)S(1)}) custom-call(s32[3]{0:T(128)S(1)} %pad_add_fusion.place_ref, bf16[512,2048]{1,0:T(8,128)(2,1)S(1)} %gather.1.rows_ref, bf16[2048,256]{1,0:T(8,128)(2,1)S(1)} %copy-done, ...), custom_call_target="tpu_custom_call" | custom-call | tf_op jit(solution)/shard_map/project3/pallas_call | solution.py:282
  63.4 0.3 collective-permute-start.22
  63.7 0.9 %collective-permute-start.23 = (bf16[128,768]{1,0:T(8,128)(2,1)S(1)}, bf16[128,768]{1,0:T(8,128)(2,1)S(1)}, u32[]{:S(2)}, u32[]{:S(2)}) collective-permute-start(bf16[128,768]{1,0:T(8,128)(2,1)S(1)} %get-tuple-element.53), channel_id=1, source_target_pairs={{0,2},{1,3},{2,0},{3,1},{4,6},{5,7},{6,4},{7,5},{8,10},{9,11},{10,... | collective-permute-start | bytes 589832 | tf_op jit(solution)/shard_map/ppermute | solution.py:20
  64.7 0.7 collective-permute-start.24
  65.4 2.1 %collective-permute-done.18.refs_2_ = bf16[512,256]{1,0:T(8,128)(2,1)S(1)} collective-permute-done((bf16[512,256]{1,0:T(8,128)(2,1)S(1)}, bf16[512,256]{1,0:T(8,128)(2,1)S(1)}, u32[]{:S(2)}, u32[]{:S(2)}) %collective-permute-start.18) | collective-permute-done | bytes 262176 | tf_op jit(solution)/shard_map/ppermute | solution.py:20
  67.5 0.1 collective-permute-done.17.refs_1_
  67.6 1.2 %project1.1 = (bf16[128,256]{1,0:T(8,128)(2,1)S(1)}, bf16[128,256]{1,0:T(8,128)(2,1)S(1)}, bf16[128,256]{1,0:T(8,128)(2,1)S(1)}, bf16[128,256]{1,0:T(8,128)(2,1)S(1)}) custom-call(s32[3]{0:T(128)S(1)} %pad_add_fusion.place_ref, bf16[512,2048]{1,0:T(8,128)(2,1)S(1)} %gather.1.rows_ref, bf16[1024,256]{1,0:T(8,128)(2,1)S(1)} %collective-permute-done.9.refs_0_, ...), custom_call_target="tpu_custom_call" | custom-call | tf_op jit(solution)/shard_map/project1/pallas_call | solution.py:282
  68.8 0.1 collective-permute-start.19
  68.9 1.0 %collective-permute-start.20 = (bf16[128,256]{1,0:T(8,128)(2,1)S(1)}, bf16[128,256]{1,0:T(8,128)(2,1)S(1)}, u32[]{:S(2)}, u32[]{:S(2)}) collective-permute-start(bf16[128,256]{1,0:T(8,128)(2,1)S(1)} %get-tuple-element.49), channel_id=1, source_target_pairs={{0,2},{1,3},{2,0},{3,1},{4,6},{5,7},{6,4},{7,5},{8,10},{9,11},{10,... | collective-permute-start | bytes 196616 | tf_op jit(solution)/shard_map/ppermute | solution.py:20
  69.9 0.0 collective-permute-done.22.refs_1_
  69.9 0.9 %collective-permute-start.21 = (bf16[128,256]{1,0:T(8,128)(2,1)S(1)}, bf16[128,256]{1,0:T(8,128)(2,1)S(1)}, u32[]{:S(2)}, u32[]{:S(2)}) collective-permute-start(bf16[128,256]{1,0:T(8,128)(2,1)S(1)} %get-tuple-element.50), channel_id=1, source_target_pairs={{0,3},{1,2},{2,1},{3,0},{4,7},{5,6},{6,5},{7,4},{8,11},{9,10},{10,... | collective-permute-start | bytes 196616 | tf_op jit(solution)/shard_map/ppermute | solution.py:20
  70.8 0.7 collective-permute-done.23.refs_2_
  71.5 2.9 %collective-permute-done.24.refs_3_ = bf16[128,768]{1,0:T(8,128)(2,1)S(1)} collective-permute-done((bf16[128,768]{1,0:T(8,128)(2,1)S(1)}, bf16[128,768]{1,0:T(8,128)(2,1)S(1)}, u32[]{:S(2)}, u32[]{:S(2)}) %collective-permute-start.24) | collective-permute-done | bytes 196640 | tf_op jit(solution)/shard_map/ppermute | solution.py:20
  74.4 1.5 %place0.1.refs_4_ = bf16[128,4096]{1,0:T(8,128)(2,1)} custom-call(s32[3]{0:T(128)S(1)} %pad_add_fusion.place_ref, bf16[128,768]{1,0:T(8,128)(2,1)S(1)} %get-tuple-element.51.refs_0_, bf16[128,768]{1,0:T(8,128)(2,1)S(1)} %collective-permute-done.22.refs_1_, bf16[128,768]{1,0:T(8,128)(2,1)S(1)} %collective-permute-done.23.refs_2_, ...), custom_call_target="tpu_custom_call" | custom-call | tf_op jit(solution)/shard_map/place0/pallas_call | solution.py:288
  75.9 0.0 collective-permute-done.19.refs_1_
  75.9 1.2 %collective-permute-done.20.refs_2_ = bf16[128,256]{1,0:T(8,128)(2,1)S(1)} collective-permute-done((bf16[128,256]{1,0:T(8,128)(2,1)S(1)}, bf16[128,256]{1,0:T(8,128)(2,1)S(1)}, u32[]{:S(2)}, u32[]{:S(2)}) %collective-permute-start.20) | collective-permute-done | bytes 65568 | tf_op jit(solution)/shard_map/ppermute | solution.py:20
  77.1 0.1 collective-permute-done.21.refs_3_
  77.2 1.3 %place1.1 = bf16[128,4096]{1,0:T(8,128)(2,1)} custom-call(s32[3]{0:T(128)S(1)} %pad_add_fusion.place_ref, bf16[128,256]{1,0:T(8,128)(2,1)S(1)} %get-tuple-element.47.refs_0_, bf16[128,256]{1,0:T(8,128)(2,1)S(1)} %collective-permute-done.19.refs_1_, bf16[128,256]{1,0:T(8,128)(2,1)S(1)} %collective-permute-done.20.refs_2_, ...), custom_call_target="tpu_custom_call", output_to_operand_aliasing={{}: (5, {})} | custom-call | tf_op jit(solution)/shard_map/place1/pallas_call | solution.py:288
  (4 shorter events, 0.0 us)
Async XLA Ops:
  1.7 28.2 %collective-permute-start.4 = (bf16[1024,256]{1,0:T(8,128)(2,1)S(1)}, bf16[1024,256]{1,0:T(8,128)(2,1)S(1)}, u32[]{:S(2)}, u32[]{:S(2)}) collective-permute-start(bf16[1024,256]{1,0:T(8,128)(2,1)S(1)} %pack.1.other_ref), channel_id=1, source_target_pairs={{0,4},{1,5},{2,6},{3,7},{4,0},{5,1},{6,2},{7,3},{8,12},{9,13},{10,... | collective-permute-start | bytes 1572872 | tf_op jit(solution)/shard_map/ppermute | solution.py:20
  4.8 25.6 %collective-permute-start.3 = (bf16[1024,256]{1,0:T(8,128)(2,1)S(1)}, bf16[1024,256]{1,0:T(8,128)(2,1)S(1)}, u32[]{:S(2)}, u32[]{:S(2)}) collective-permute-start(bf16[1024,256]{1,0:T(8,128)(2,1)S(1)} %pack.1.other_ref), channel_id=1, source_target_pairs={{0,8},{1,9},{2,10},{3,11},{4,12},{5,13},{6,14},{7,15},{8,0},{9,1},... | collective-permute-start | bytes 1572872 | tf_op jit(solution)/shard_map/ppermute | solution.py:20
  9.2 11.4 %collective-permute-start.2 = (bf16[384,512]{1,0:T(8,128)(2,1)S(1)}, bf16[384,512]{1,0:T(8,128)(2,1)S(1)}, u32[]{:S(2)}, u32[]{:S(2)}) collective-permute-start(bf16[384,512]{1,0:T(8,128)(2,1)S(1)} %get-tuple-element.33), channel_id=1, source_target_pairs={{0,3},{1,2},{2,1},{3,0},{4,7},{5,6},{6,5},{7,4},{8,11},{9,10},{10,... | collective-permute-start | bytes 1179656 | tf_op jit(solution)/shard_map/ppermute | solution.py:20
  9.6 36.7 %copy-start.1 = (s32[16]{0:T(128)S(1)}, s32[16]{0:T(128)}, u32[]{:S(2)}) copy-start(s32[16]{0:T(128)} %doc_ref.3) | copy-start | bytes 196
  9.6 19.4 %collective-permute-start.1 = (bf16[384,512]{1,0:T(8,128)(2,1)S(1)}, bf16[384,512]{1,0:T(8,128)(2,1)S(1)}, u32[]{:S(2)}, u32[]{:S(2)}) collective-permute-start(bf16[384,512]{1,0:T(8,128)(2,1)S(1)} %get-tuple-element.30.other_ref), channel_id=1, source_target_pairs={{0,2},{1,3},{2,0},{3,1},{4,6},{5,7},{6,4},{7,5},{8,10},{9,11},{10,... | collective-permute-start | bytes 1179656 | tf_op jit(solution)/shard_map/ppermute | solution.py:20
  12.7 16.4 %collective-permute-start = (bf16[384,512]{1,0:T(8,128)(2,1)S(1)}, bf16[384,512]{1,0:T(8,128)(2,1)S(1)}, u32[]{:S(2)}, u32[]{:S(2)}) collective-permute-start(bf16[384,512]{1,0:T(8,128)(2,1)S(1)} %get-tuple-element.32), channel_id=1, source_target_pairs={{0,1},{1,0},{2,3},{3,2},{4,5},{5,4},{6,7},{7,6},{8,9},{9,8},{10,11... | collective-permute-start | bytes 1179656 | tf_op jit(solution)/shard_map/ppermute | solution.py:20
  30.3 19.1 %collective-permute-start.15 = (bf16[1024,256]{1,0:T(8,128)(2,1)S(1)}, bf16[1024,256]{1,0:T(8,128)(2,1)S(1)}, u32[]{:S(2)}, u32[]{:S(2)}) collective-permute-start(bf16[1024,256]{1,0:T(8,128)(2,1)S(1)} %collective-permute-done.3.refs_1_), channel_id=1, source_target_pairs={{0,16},{16,0},{1,17},{17,1},{2,18},{18,2},{3,19},{19,3},{4,20},{20... | collective-permute-start | bytes 1572872 | tf_op jit(solution)/shard_map/ppermute | solution.py:24
  31.8 14.5 %collective-permute-start.5 = (bf16[256,512]{1,0:T(8,128)(2,1)S(1)}, bf16[256,512]{1,0:T(8,128)(2,1)S(1)}, u32[]{:S(2)}, u32[]{:S(2)}) collective-permute-start(bf16[256,512]{1,0:T(8,128)(2,1)S(1)} %get-tuple-element.36), channel_id=1, source_target_pairs={{0,4},{1,5},{2,6},{3,7},{4,0},{5,1},{6,2},{7,3},{8,12},{9,13},{10,... | collective-permute-start | bytes 786440 | tf_op jit(solution)/shard_map/ppermute | solution.py:20
  32.3 9.6 %collective-permute-start.6 = (bf16[128,512]{1,0:T(8,128)(2,1)S(1)}, bf16[128,512]{1,0:T(8,128)(2,1)S(1)}, u32[]{:S(2)}, u32[]{:S(2)}) collective-permute-start(bf16[128,512]{1,0:T(8,128)(2,1)S(1)} %get-tuple-element.37), channel_id=1, source_target_pairs={{0,8},{1,9},{2,10},{3,11},{4,12},{5,13},{6,14},{7,15},{8,0},{9,1},... | collective-permute-start | bytes 393224 | tf_op jit(solution)/shard_map/ppermute | solution.py:20
  34.9 11.0 %collective-permute-start.7 = (bf16[128,512]{1,0:T(8,128)(2,1)S(1)}, bf16[128,512]{1,0:T(8,128)(2,1)S(1)}, u32[]{:S(2)}, u32[]{:S(2)}) collective-permute-start(bf16[128,512]{1,0:T(8,128)(2,1)S(1)} %get-tuple-element.37), channel_id=1, source_target_pairs={{0,12},{1,13},{2,14},{3,15},{4,8},{5,9},{6,10},{7,11},{8,4},{9,5},... | collective-permute-start | bytes 393224 | tf_op jit(solution)/shard_map/ppermute | solution.py:20
  41.9 14.4 %collective-permute-start.9 = (bf16[1024,256]{1,0:T(8,128)(2,1)S(1)}, bf16[1024,256]{1,0:T(8,128)(2,1)S(1)}, u32[]{:S(2)}, u32[]{:S(2)}) collective-permute-start(bf16[1024,256]{1,0:T(8,128)(2,1)S(1)} %collective-permute-done.3.refs_1_), channel_id=1, source_target_pairs={{0,4},{1,5},{2,6},{3,7},{4,0},{5,1},{6,2},{7,3},{8,12},{9,13},{10,... | collective-permute-start | bytes 1572872 | tf_op jit(solution)/shard_map/ppermute | solution.py:20
  48.3 7.6 %collective-permute-start.8 = (bf16[256,512]{1,0:T(8,128)(2,1)S(1)}, bf16[256,512]{1,0:T(8,128)(2,1)S(1)}, u32[]{:S(2)}, u32[]{:S(2)}) collective-permute-start(bf16[256,512]{1,0:T(8,128)(2,1)S(1)} %attend0.1.refs_7_.refs_0_), channel_id=1, source_target_pairs={{0,2},{1,3},{2,0},{3,1},{4,6},{5,7},{6,4},{7,5},{8,10},{9,11},{10,... | collective-permute-start | bytes 786440 | tf_op jit(solution)/shard_map/ppermute | solution.py:20
  49.4 9.8 %collective-permute-start.16 = (bf16[1024,256]{1,0:T(8,128)(2,1)S(1)}, bf16[1024,256]{1,0:T(8,128)(2,1)S(1)}, u32[]{:S(2)}, u32[]{:S(2)}) collective-permute-start(bf16[1024,256]{1,0:T(8,128)(2,1)S(1)} %collective-permute-done.4.refs_3_), channel_id=1, source_target_pairs={{0,16},{16,0},{1,17},{17,1},{2,18},{18,2},{3,19},{19,3},{4,20},{20... | collective-permute-start | bytes 1572872 | tf_op jit(solution)/shard_map/ppermute | solution.py:24
  51.9 6.7 %collective-permute-start.12 = (bf16[256,512]{1,0:T(8,128)(2,1)S(1)}, bf16[256,512]{1,0:T(8,128)(2,1)S(1)}, u32[]{:S(2)}, u32[]{:S(2)}) collective-permute-start(bf16[256,512]{1,0:T(8,128)(2,1)S(1)} %attend1.1.refs_1_), channel_id=1, source_target_pairs={{0,2},{1,3},{2,0},{3,1},{4,6},{5,7},{6,4},{7,5},{8,10},{9,11},{10,... | collective-permute-start | bytes 786440 | tf_op jit(solution)/shard_map/ppermute | solution.py:20
  56.3 2.3 %collective-permute-start.13 = (bf16[256,512]{1,0:T(8,128)(2,1)S(1)}, bf16[256,512]{1,0:T(8,128)(2,1)S(1)}, u32[]{:S(2)}, u32[]{:S(2)}) collective-permute-start(bf16[256,512]{1,0:T(8,128)(2,1)S(1)} %collective-permute-done.8.refs_4_), channel_id=1, source_target_pairs={{0,1},{1,0},{2,3},{3,2},{4,5},{5,4},{6,7},{7,6},{8,9},{9,8},{10,11... | collective-permute-start | bytes 786440 | tf_op jit(solution)/shard_map/ppermute | solution.py:20
  56.3 4.0 %collective-permute-start.10 = (bf16[256,512]{1,0:T(8,128)(2,1)S(1)}, bf16[256,512]{1,0:T(8,128)(2,1)S(1)}, u32[]{:S(2)}, u32[]{:S(2)}) collective-permute-start(bf16[256,512]{1,0:T(8,128)(2,1)S(1)} %attend0.1.refs_7_.refs_0_), channel_id=1, source_target_pairs={{0,1},{1,0},{2,3},{3,2},{4,5},{5,4},{6,7},{7,6},{8,9},{9,8},{10,11... | collective-permute-start | bytes 786440 | tf_op jit(solution)/shard_map/ppermute | solution.py:20
  56.8 3.5 %collective-permute-start.11 = (bf16[256,512]{1,0:T(8,128)(2,1)S(1)}, bf16[256,512]{1,0:T(8,128)(2,1)S(1)}, u32[]{:S(2)}, u32[]{:S(2)}) collective-permute-start(bf16[256,512]{1,0:T(8,128)(2,1)S(1)} %attend1.1.refs_1_), channel_id=1, source_target_pairs={{0,1},{1,0},{2,3},{3,2},{4,5},{5,4},{6,7},{7,6},{8,9},{9,8},{10,11... | collective-permute-start | bytes 786440 | tf_op jit(solution)/shard_map/ppermute | solution.py:20
  58.7 1.7 %collective-permute-start.14 = (bf16[256,512]{1,0:T(8,128)(2,1)S(1)}, bf16[256,512]{1,0:T(8,128)(2,1)S(1)}, u32[]{:S(2)}, u32[]{:S(2)}) collective-permute-start(bf16[256,512]{1,0:T(8,128)(2,1)S(1)} %collective-permute-done.12.refs_5_), channel_id=1, source_target_pairs={{0,1},{1,0},{2,3},{3,2},{4,5},{5,4},{6,7},{7,6},{8,9},{9,8},{10,11... | collective-permute-start | bytes 786440 | tf_op jit(solution)/shard_map/ppermute | solution.py:20
  58.7 8.8 %collective-permute-start.18 = (bf16[512,256]{1,0:T(8,128)(2,1)S(1)}, bf16[512,256]{1,0:T(8,128)(2,1)S(1)}, u32[]{:S(2)}, u32[]{:S(2)}) collective-permute-start(bf16[512,256]{1,0:T(8,128)(2,1)S(1)} %slice.7), channel_id=1, source_target_pairs={{0,4},{1,5},{2,6},{3,7},{4,0},{5,1},{6,2},{7,3},{8,12},{9,13},{10,... | collective-permute-start | bytes 786440 | tf_op jit(solution)/shard_map/ppermute | solution.py:20
  59.2 1.9 %copy-start = (bf16[2048,256]{1,0:T(8,128)(2,1)S(1)}, bf16[2048,256]{1,0:T(8,128)(2,1)}, u32[]{:S(2)}) copy-start(bf16[2048,256]{1,0:T(8,128)(2,1)} %refs_0_.1) | copy-start | bytes 3145732
  59.2 8.4 %collective-permute-start.17 = (bf16[512,256]{1,0:T(8,128)(2,1)S(1)}, bf16[512,256]{1,0:T(8,128)(2,1)S(1)}, u32[]{:S(2)}, u32[]{:S(2)}) collective-permute-start(bf16[512,256]{1,0:T(8,128)(2,1)S(1)} %slice.6), channel_id=1, source_target_pairs={{0,16},{16,0},{1,17},{17,1},{2,18},{18,2},{3,19},{19,3},{4,20},{20... | collective-permute-start | bytes 786440 | tf_op jit(solution)/shard_map/ppermute | solution.py:24
  63.4 6.5 %collective-permute-start.22 = (bf16[128,768]{1,0:T(8,128)(2,1)S(1)}, bf16[128,768]{1,0:T(8,128)(2,1)S(1)}, u32[]{:S(2)}, u32[]{:S(2)}) collective-permute-start(bf16[128,768]{1,0:T(8,128)(2,1)S(1)} %get-tuple-element.52), channel_id=1, source_target_pairs={{0,1},{1,0},{2,3},{3,2},{4,5},{5,4},{6,7},{7,6},{8,9},{9,8},{10,11... | collective-permute-start | bytes 589832 | tf_op jit(solution)/shard_map/ppermute | solution.py:20
  63.7 7.7 %collective-permute-start.23 = (bf16[128,768]{1,0:T(8,128)(2,1)S(1)}, bf16[128,768]{1,0:T(8,128)(2,1)S(1)}, u32[]{:S(2)}, u32[]{:S(2)}) collective-permute-start(bf16[128,768]{1,0:T(8,128)(2,1)S(1)} %get-tuple-element.53), channel_id=1, source_target_pairs={{0,2},{1,3},{2,0},{3,1},{4,6},{5,7},{6,4},{7,5},{8,10},{9,11},{10,... | collective-permute-start | bytes 589832 | tf_op jit(solution)/shard_map/ppermute | solution.py:20
  64.7 9.7 %collective-permute-start.24 = (bf16[128,768]{1,0:T(8,128)(2,1)S(1)}, bf16[128,768]{1,0:T(8,128)(2,1)S(1)}, u32[]{:S(2)}, u32[]{:S(2)}) collective-permute-start(bf16[128,768]{1,0:T(8,128)(2,1)S(1)} %get-tuple-element.54), channel_id=1, source_target_pairs={{0,3},{1,2},{2,1},{3,0},{4,7},{5,6},{6,5},{7,4},{8,11},{9,10},{10,... | collective-permute-start | bytes 589832 | tf_op jit(solution)/shard_map/ppermute | solution.py:20
  68.8 7.1 %collective-permute-start.19 = (bf16[128,256]{1,0:T(8,128)(2,1)S(1)}, bf16[128,256]{1,0:T(8,128)(2,1)S(1)}, u32[]{:S(2)}, u32[]{:S(2)}) collective-permute-start(bf16[128,256]{1,0:T(8,128)(2,1)S(1)} %get-tuple-element.48), channel_id=1, source_target_pairs={{0,1},{1,0},{2,3},{3,2},{4,5},{5,4},{6,7},{7,6},{8,9},{9,8},{10,11... | collective-permute-start | bytes 196616 | tf_op jit(solution)/shard_map/ppermute | solution.py:20
  68.9 8.2 %collective-permute-start.20 = (bf16[128,256]{1,0:T(8,128)(2,1)S(1)}, bf16[128,256]{1,0:T(8,128)(2,1)S(1)}, u32[]{:S(2)}, u32[]{:S(2)}) collective-permute-start(bf16[128,256]{1,0:T(8,128)(2,1)S(1)} %get-tuple-element.49), channel_id=1, source_target_pairs={{0,2},{1,3},{2,0},{3,1},{4,6},{5,7},{6,4},{7,5},{8,10},{9,11},{10,... | collective-permute-start | bytes 196616 | tf_op jit(solution)/shard_map/ppermute | solution.py:20
  69.9 7.3 %collective-permute-start.21 = (bf16[128,256]{1,0:T(8,128)(2,1)S(1)}, bf16[128,256]{1,0:T(8,128)(2,1)S(1)}, u32[]{:S(2)}, u32[]{:S(2)}) collective-permute-start(bf16[128,256]{1,0:T(8,128)(2,1)S(1)} %get-tuple-element.50), channel_id=1, source_target_pairs={{0,3},{1,2},{2,1},{3,0},{4,7},{5,6},{6,5},{7,4},{8,11},{9,10},{10,... | collective-permute-start | bytes 196616 | tf_op jit(solution)/shard_map/ppermute | solution.py:20

commit v10 on v9

--- a/solution.py
+++ b/solution.py
@@ -113,7 +113,8 @@
     for n, rows_ref in enumerate((key_ref, value_ref)):
         at = 128 + 128 * n
         for part in range(2):
-            rows_ref[128 * part : 128 * part + 128, :] = own[2 * half + part][at : at + 128, :]
+            if n == 1:
+                rows_ref[128 * part : 128 * part + 128, :] = own[2 * half + part][at : at + 128, :]
             rows_ref[256 + 64 * part : 320 + 64 * part, :] = halve(own[2 - 2 * half + part][at : at + 128, :])
         rows_ref[384:512, :] = l_ref[128 * n : 128 * n + 128, :]
         rows_ref[512:576, :] = h_ref[64 * n : 64 * n + 64, :]
@@ -129,8 +130,13 @@
     def score_of(head):
         columns = slice(head * HD, (head + 1) * HD)
         query = jnp.concatenate([own[2 * half + part][0:128, columns] for part in range(2)], 0)
-        return lax.dot_general(
-            query, key_ref[:, columns], (((1,), (1,)), ((), ())), preferred_element_type=jnp.float32
+        runs = [own[2 * half + part][128:256, columns] for part in range(2)] + [key_ref[256:640, columns]]
+        return jnp.concatenate(
+            [
+                lax.dot_general(query, run, (((1,), (1,)), ((), ())), preferred_element_type=jnp.float32)
+                for run in runs
+            ],
+            1,
         )
 
     following = score_of(0)
@@ -254,7 +260,7 @@
     half_d = swap(after(half_h, far[1]), LOW)
     other_l = swap_groups(after(ours_l, other_h))
     quarter = depth // 4
-    other_d = [swap_groups(after(half_d, other_l)[:quarter]), swap(after(other_h, half_d)[quarter:], LOW)]
+    other_d = [swap_groups(after(half_d, other_l)[:quarter]), swap(other_h[quarter:], LOW)]
 
     pieces = [[None] * 2 for _ in range(4)]
     before = near[1]

time: 78.7 us -> 78.7 us (level)
  no operation moved by 1% of the time
where the time goes in v10:
time: 78.7 us; the launch traced here: 78.5 us
  waiting for transfers between devices  37.1 us (47%)
  starting transfers between devices  24.1 us (31%)
  Pallas kernels  17 us (22%)
    ppermute x22, waiting for transfers between devices, swap(): return lax.ppermute(value, 'ctx', pairs)  36.6 us
    ppermute x22, starting transfers between devices, swap(): return lax.ppermute(value, 'ctx', pairs)  20.9 us
    pallas_call x2, Pallas kernels, per_device_fast(): call(functools.partial(attention_kernel, n), [(2 * length, share)], [pl.B...  3.9 us
    pallas_call x2, Pallas kernels, per_device_fast(): call(project_kernel, [(length, count * wide)] * 4, vmem(1 + len(blocks)),...  3.58 us
    ppermute x3, starting transfers between devices, swap_groups(): return lax.ppermute(value, 'groups', [(0, 1), (1, 0)])  3.17 us
    pallas_call x2, Pallas kernels, per_device_fast(): call(functools.partial(place_kernel, n), [(length, 16 * wide)], anywhere(...  2.78 us
    pallas_call x1, Pallas kernels, per_device_fast(): call(functools.partial(pack_kernel, (1, 0)), [(3 * length, share)] * 2, a...  1.8 us
    pallas_call x1, Pallas kernels, per_device_fast(): call(functools.partial(pack_kernel, (2, 3)), [(3 * length, share)] * 2, a...  1.8 us
  transfers between devices with their start and end apart: 25, of which 16 were waited for; matrix products, arithmetic and copies ran while one was open for 0% of the time, Pallas kernels for 18%

profile of v10, /device:TPU:0, one launch (start us, length us, event | category | flops | bytes accessed | tf_op | source)
XLA Modules:
  0.0 78.5 jit_solution(15122714800932357020)
XLA Ops:
  0.0 0.1 pad_add_fusion.place_ref
  0.1 1.6 %pack.1.other_ref = bf16[1024,256]{1,0:T(8,128)(2,1)S(1)} custom-call(s32[3]{0:T(128)S(1)} %pad_add_fusion.place_ref, bf16[128,2048]{1,0:T(8,128)(2,1)} %q_ref.5, bf16[128,2048]{1,0:T(8,128)(2,1)} %k_ref.5, bf16[128,2048]{1,0:T(8,128)(2,1)} %v_ref.5, bf16[2048,256]{1,0:T(8,128)(2,1)} %refs_0_.1), custom_call_target="tpu_custom_call" | custom-call | tf_op jit(solution)/shard_map/pack/pallas_call | solution.py:228
  1.7 3.1 %collective-permute-start.4 = (bf16[1024,256]{1,0:T(8,128)(2,1)S(1)}, bf16[1024,256]{1,0:T(8,128)(2,1)S(1)}, u32[]{:S(2)}, u32[]{:S(2)}) collective-permute-start(bf16[1024,256]{1,0:T(8,128)(2,1)S(1)} %pack.1.other_ref), channel_id=1, source_target_pairs={{0,4},{1,5},{2,6},{3,7},{4,0},{5,1},{6,2},{7,3},{8,12},{9,13},{10,... | collective-permute-start | bytes 1572872 | tf_op jit(solution)/shard_map/ppermute | solution.py:20
  4.8 2.6 %collective-permute-start.3 = (bf16[1024,256]{1,0:T(8,128)(2,1)S(1)}, bf16[1024,256]{1,0:T(8,128)(2,1)S(1)}, u32[]{:S(2)}, u32[]{:S(2)}) collective-permute-start(bf16[1024,256]{1,0:T(8,128)(2,1)S(1)} %pack.1.other_ref), channel_id=1, source_target_pairs={{0,8},{1,9},{2,10},{3,11},{4,12},{5,13},{6,14},{7,15},{8,0},{9,1},... | collective-permute-start | bytes 1572872 | tf_op jit(solution)/shard_map/ppermute | solution.py:20
  7.4 1.8 %pack0.1 = (bf16[384,512]{1,0:T(8,128)(2,1)S(1)}, bf16[384,512]{1,0:T(8,128)(2,1)S(1)}) custom-call(s32[3]{0:T(128)S(1)} %pad_add_fusion.place_ref, bf16[128,2048]{1,0:T(8,128)(2,1)} %q_ref.5, bf16[128,2048]{1,0:T(8,128)(2,1)} %k_ref.5, bf16[128,2048]{1,0:T(8,128)(2,1)} %v_ref.5, bf16[1024,256]{1,0:T(8,128)(2,1)S(1)} %pack.1.other_ref), custom_call_target="tpu_custom_call" | custom-call | tf_op jit(solution)/shard_map/pack0/pallas_call | solution.py:235
  9.2 0.5 collective-permute-start.2
  9.6 1.2 %collective-permute-start.1 = (bf16[384,512]{1,0:T(8,128)(2,1)S(1)}, bf16[384,512]{1,0:T(8,128)(2,1)S(1)}, u32[]{:S(2)}, u32[]{:S(2)}) collective-permute-start(bf16[384,512]{1,0:T(8,128)(2,1)S(1)} %get-tuple-element.29.other_ref), channel_id=1, source_target_pairs={{0,2},{1,3},{2,0},{3,1},{4,6},{5,7},{6,4},{7,5},{8,10},{9,11},{10,... | collective-permute-start | bytes 1179656 | tf_op jit(solution)/shard_map/ppermute | solution.py:20
  10.8 1.8 %pack1.1 = (bf16[384,512]{1,0:T(8,128)(2,1)S(1)}, bf16[384,512]{1,0:T(8,128)(2,1)S(1)}) custom-call(s32[3]{0:T(128)S(1)} %pad_add_fusion.place_ref, bf16[128,2048]{1,0:T(8,128)(2,1)} %q_ref.5, bf16[128,2048]{1,0:T(8,128)(2,1)} %k_ref.5, bf16[128,2048]{1,0:T(8,128)(2,1)} %v_ref.5, bf16[384,512]{1,0:T(8,128)(2,1)S(1)} %get-tuple-element.29.other_ref), custom_call_target="tpu_custom_call" | custom-call | flops 2000000000 | bytes 40000000 | tf_op jit(solution)/shard_map/pack1/pallas_call | solution.py:242
  12.7 0.3 collective-permute-start
  13.0 7.6 %collective-permute-done.2.a3.refs_3_ = bf16[384,512]{1,0:T(8,128)(2,1)S(1)} collective-permute-done((bf16[384,512]{1,0:T(8,128)(2,1)S(1)}, bf16[384,512]{1,0:T(8,128)(2,1)S(1)}, u32[]{:S(2)}, u32[]{:S(2)}) %collective-permute-start.2) | collective-permute-done | bytes 393248 | tf_op jit(solution)/shard_map/ppermute | solution.py:20
  20.6 8.5 %collective-permute-done.1.a2.refs_2_ = bf16[384,512]{1,0:T(8,128)(2,1)S(1)} collective-permute-done((bf16[384,512]{1,0:T(8,128)(2,1)S(1)}, bf16[384,512]{1,0:T(8,128)(2,1)S(1)}, u32[]{:S(2)}, u32[]{:S(2)}) %collective-permute-start.1) | collective-permute-done | bytes 393248 | tf_op jit(solution)/shard_map/ppermute | solution.py:20
  29.1 0.0 collective-permute-done.a1.refs_1_
  29.1 0.8 %coarse.1 = (bf16[256,512]{1,0:T(8,128)(2,1)S(1)}, bf16[128,512]{1,0:T(8,128)(2,1)S(1)}) custom-call(s32[3]{0:T(128)S(1)} %pad_add_fusion.place_ref, bf16[384,512]{1,0:T(8,128)(2,1)S(1)} %get-tuple-element.30.a0.refs_0_.refs_7_, bf16[384,512]{1,0:T(8,128)(2,1)S(1)} %collective-permute-done.a1.refs_1_, ...), custom_call_target="tpu_custom_call" | custom-call | tf_op jit(solution)/shard_map/coarse/pallas_call | solution.py:253
  29.9 0.0 collective-permute-done.4.refs_3_
  29.9 0.4 collective-permute-done.3.refs_1_
  30.3 1.5 %collective-permute-start.15 = (bf16[1024,256]{1,0:T(8,128)(2,1)S(1)}, bf16[1024,256]{1,0:T(8,128)(2,1)S(1)}, u32[]{:S(2)}, u32[]{:S(2)}) collective-permute-start(bf16[1024,256]{1,0:T(8,128)(2,1)S(1)} %collective-permute-done.3.refs_1_), channel_id=1, source_target_pairs={{0,16},{16,0},{1,17},{17,1},{2,18},{18,2},{3,19},{19,3},{4,20},{20... | collective-permute-start | bytes 1572872 | tf_op jit(solution)/shard_map/ppermute | solution.py:24
  31.8 0.4 collective-permute-start.5
  32.3 2.6 %collective-permute-start.6 = (bf16[128,512]{1,0:T(8,128)(2,1)S(1)}, bf16[128,512]{1,0:T(8,128)(2,1)S(1)}, u32[]{:S(2)}, u32[]{:S(2)}) collective-permute-start(bf16[128,512]{1,0:T(8,128)(2,1)S(1)} %get-tuple-element.36), channel_id=1, source_target_pairs={{0,8},{1,9},{2,10},{3,11},{4,12},{5,13},{6,14},{7,15},{8,0},{9,1},... | collective-permute-start | bytes 393224 | tf_op jit(solution)/shard_map/ppermute | solution.py:20
  34.9 1.4 %collective-permute-start.7 = (bf16[128,512]{1,0:T(8,128)(2,1)S(1)}, bf16[128,512]{1,0:T(8,128)(2,1)S(1)}, u32[]{:S(2)}, u32[]{:S(2)}) collective-permute-start(bf16[128,512]{1,0:T(8,128)(2,1)S(1)} %get-tuple-element.36), channel_id=1, source_target_pairs={{0,12},{1,13},{2,14},{3,15},{4,8},{5,9},{6,10},{7,11},{8,4},{9,5},... | collective-permute-start | bytes 393224 | tf_op jit(solution)/shard_map/ppermute | solution.py:20
  36.2 5.7 %collective-permute-done.6.refs_5_ = bf16[128,512]{1,0:T(8,128)(2,1)S(1)} collective-permute-done((bf16[128,512]{1,0:T(8,128)(2,1)S(1)}, bf16[128,512]{1,0:T(8,128)(2,1)S(1)}, u32[]{:S(2)}, u32[]{:S(2)}) %collective-permute-start.6) | collective-permute-done | bytes 131104 | tf_op jit(solution)/shard_map/ppermute | solution.py:20
  41.9 2.2 %collective-permute-start.9 = (bf16[1024,256]{1,0:T(8,128)(2,1)S(1)}, bf16[1024,256]{1,0:T(8,128)(2,1)S(1)}, u32[]{:S(2)}, u32[]{:S(2)}) collective-permute-start(bf16[1024,256]{1,0:T(8,128)(2,1)S(1)} %collective-permute-done.3.refs_1_), channel_id=1, source_target_pairs={{0,4},{1,5},{2,6},{3,7},{4,0},{5,1},{6,2},{7,3},{8,12},{9,13},{10,... | collective-permute-start | bytes 1572872 | tf_op jit(solution)/shard_map/ppermute | solution.py:20
  44.1 1.7 %collective-permute-done.7.refs_6_ = bf16[128,512]{1,0:T(8,128)(2,1)S(1)} collective-permute-done((bf16[128,512]{1,0:T(8,128)(2,1)S(1)}, bf16[128,512]{1,0:T(8,128)(2,1)S(1)}, u32[]{:S(2)}, u32[]{:S(2)}) %collective-permute-start.7) | collective-permute-done | bytes 131104 | tf_op jit(solution)/shard_map/ppermute | solution.py:20
  45.9 0.4 collective-permute-done.5.refs_4_
  46.3 0.0 copy-done.1
  46.3 1.9 %attend0.1.refs_7_.refs_0_ = bf16[256,512]{1,0:T(8,128)(2,1)S(1)} custom-call(s32[3]{0:T(128)S(1)} %pad_add_fusion.place_ref, s32[16]{0:T(128)S(1)} %copy-done.1, bf16[384,512]{1,0:T(8,128)(2,1)S(1)} %get-tuple-element.30.a0.refs_0_.refs_7_, bf16[384,512]{1,0:T(8,128)(2,1)S(1)} %collective-permute-done.a1.refs_1_, ...), custom_call_target="tpu_custom_call" | custom-call | flops 2000000000 | bytes 40000000 | tf_op jit(solution)/shard_map/attend0/pallas_call | solution.py:268
  48.3 1.2 %collective-permute-start.8 = (bf16[256,512]{1,0:T(8,128)(2,1)S(1)}, bf16[256,512]{1,0:T(8,128)(2,1)S(1)}, u32[]{:S(2)}, u32[]{:S(2)}) collective-permute-start(bf16[256,512]{1,0:T(8,128)(2,1)S(1)} %attend0.1.refs_7_.refs_0_), channel_id=1, source_target_pairs={{0,2},{1,3},{2,0},{3,1},{4,6},{5,7},{6,4},{7,5},{8,10},{9,11},{10,... | collective-permute-start | bytes 786440 | tf_op jit(solution)/shard_map/ppermute | solution.py:20
  49.4 0.0 collective-permute-done.15.refs_2_
  49.4 0.5 collective-permute-start.16
  50.0 1.9 %attend1.1.refs_1_ = bf16[256,512]{1,0:T(8,128)(2,1)S(1)} custom-call(s32[3]{0:T(128)S(1)} %pad_add_fusion.place_ref, s32[16]{0:T(128)S(1)} %copy-done.1, bf16[384,512]{1,0:T(8,128)(2,1)S(1)} %get-tuple-element.30.a0.refs_0_.refs_7_, bf16[384,512]{1,0:T(8,128)(2,1)S(1)} %collective-permute-done.a1.refs_1_, ...), custom_call_target="tpu_custom_call" | custom-call | flops 2000000000 | bytes 40000000 | tf_op jit(solution)/shard_map/attend1/pallas_call | solution.py:268
  51.9 1.0 %collective-permute-start.12 = (bf16[256,512]{1,0:T(8,128)(2,1)S(1)}, bf16[256,512]{1,0:T(8,128)(2,1)S(1)}, u32[]{:S(2)}, u32[]{:S(2)}) collective-permute-start(bf16[256,512]{1,0:T(8,128)(2,1)S(1)} %attend1.1.refs_1_), channel_id=1, source_target_pairs={{0,2},{1,3},{2,0},{3,1},{4,6},{5,7},{6,4},{7,5},{8,10},{9,11},{10,... | collective-permute-start | bytes 786440 | tf_op jit(solution)/shard_map/ppermute | solution.py:20
  52.9 2.9 %collective-permute-done.8.refs_4_ = bf16[256,512]{1,0:T(8,128)(2,1)S(1)} collective-permute-done((bf16[256,512]{1,0:T(8,128)(2,1)S(1)}, bf16[256,512]{1,0:T(8,128)(2,1)S(1)}, u32[]{:S(2)}, u32[]{:S(2)}) %collective-permute-start.8) | collective-permute-done | bytes 262176 | tf_op jit(solution)/shard_map/ppermute | solution.py:20
  55.9 0.5 collective-permute-done.9.refs_0_
  56.3 0.0 collective-permute-start.13
  56.3 0.5 collective-permute-start.10
  56.8 0.0 collective-permute-start.11
  56.8 1.8 %collective-permute-done.12.refs_5_ = bf16[256,512]{1,0:T(8,128)(2,1)S(1)} collective-permute-done((bf16[256,512]{1,0:T(8,128)(2,1)S(1)}, bf16[256,512]{1,0:T(8,128)(2,1)S(1)}, u32[]{:S(2)}, u32[]{:S(2)}) %collective-permute-start.12) | collective-permute-done | bytes 262176 | tf_op jit(solution)/shard_map/ppermute | solution.py:20
  58.7 0.0 collective-permute-done.13.refs_6_
  58.7 0.0 collective-permute-start.14
  58.7 0.1 collective-permute-start.18
  58.8 0.4 collective-permute-done.16.refs_4_
  59.2 0.0 copy-start
  59.2 1.2 %collective-permute-start.17 = (bf16[512,256]{1,0:T(8,128)(2,1)S(1)}, bf16[512,256]{1,0:T(8,128)(2,1)S(1)}, u32[]{:S(2)}, u32[]{:S(2)}) collective-permute-start(bf16[512,256]{1,0:T(8,128)(2,1)S(1)} %slice.6), channel_id=1, source_target_pairs={{0,16},{16,0},{1,17},{17,1},{2,18},{18,2},{3,19},{19,3},{4,20},{20... | collective-permute-start | bytes 786440 | tf_op jit(solution)/shard_map/ppermute | solution.py:24
  60.4 0.0 collective-permute-done.10.refs_2_
  60.4 0.0 collective-permute-done.11.refs_3_
  60.4 0.0 collective-permute-done.14.refs_7_
  60.4 0.7 gather.1.rows_ref
  61.1 2.3 %project3.1 = (bf16[128,768]{1,0:T(8,128)(2,1)S(1)}, bf16[128,768]{1,0:T(8,128)(2,1)S(1)}, bf16[128,768]{1,0:T(8,128)(2,1)S(1)}, bf16[128,768]{1,0:T(8,128)(2,1)S(1)}) custom-call(s32[3]{0:T(128)S(1)} %pad_add_fusion.place_ref, bf16[512,2048]{1,0:T(8,128)(2,1)S(1)} %gather.1.rows_ref, bf16[2048,256]{1,0:T(8,128)(2,1)S(1)} %copy-done, ...), custom_call_target="tpu_custom_call" | custom-call | tf_op jit(solution)/shard_map/project3/pallas_call | solution.py:288
  63.5 0.3 collective-permute-start.22
  63.7 0.9 %collective-permute-start.23 = (bf16[128,768]{1,0:T(8,128)(2,1)S(1)}, bf16[128,768]{1,0:T(8,128)(2,1)S(1)}, u32[]{:S(2)}, u32[]{:S(2)}) collective-permute-start(bf16[128,768]{1,0:T(8,128)(2,1)S(1)} %get-tuple-element.51), channel_id=1, source_target_pairs={{0,2},{1,3},{2,0},{3,1},{4,6},{5,7},{6,4},{7,5},{8,10},{9,11},{10,... | collective-permute-start | bytes 589832 | tf_op jit(solution)/shard_map/ppermute | solution.py:20
  64.7 0.7 collective-permute-start.24
  65.4 2.1 %collective-permute-done.18.refs_2_ = bf16[512,256]{1,0:T(8,128)(2,1)S(1)} collective-permute-done((bf16[512,256]{1,0:T(8,128)(2,1)S(1)}, bf16[512,256]{1,0:T(8,128)(2,1)S(1)}, u32[]{:S(2)}, u32[]{:S(2)}) %collective-permute-start.18) | collective-permute-done | bytes 262176 | tf_op jit(solution)/shard_map/ppermute | solution.py:20
  67.5 0.1 collective-permute-done.17.refs_1_
  67.6 1.2 %project1.1 = (bf16[128,256]{1,0:T(8,128)(2,1)S(1)}, bf16[128,256]{1,0:T(8,128)(2,1)S(1)}, bf16[128,256]{1,0:T(8,128)(2,1)S(1)}, bf16[128,256]{1,0:T(8,128)(2,1)S(1)}) custom-call(s32[3]{0:T(128)S(1)} %pad_add_fusion.place_ref, bf16[512,2048]{1,0:T(8,128)(2,1)S(1)} %gather.1.rows_ref, bf16[1024,256]{1,0:T(8,128)(2,1)S(1)} %collective-permute-done.9.refs_0_, ...), custom_call_target="tpu_custom_call" | custom-call | tf_op jit(solution)/shard_map/project1/pallas_call | solution.py:288
  68.9 0.1 collective-permute-start.19
  68.9 1.0 %collective-permute-start.20 = (bf16[128,256]{1,0:T(8,128)(2,1)S(1)}, bf16[128,256]{1,0:T(8,128)(2,1)S(1)}, u32[]{:S(2)}, u32[]{:S(2)}) collective-permute-start(bf16[128,256]{1,0:T(8,128)(2,1)S(1)} %get-tuple-element.47), channel_id=1, source_target_pairs={{0,2},{1,3},{2,0},{3,1},{4,6},{5,7},{6,4},{7,5},{8,10},{9,11},{10,... | collective-permute-start | bytes 196616 | tf_op jit(solution)/shard_map/ppermute | solution.py:20
  69.9 0.0 collective-permute-done.22.refs_1_
  69.9 0.9 %collective-permute-start.21 = (bf16[128,256]{1,0:T(8,128)(2,1)S(1)}, bf16[128,256]{1,0:T(8,128)(2,1)S(1)}, u32[]{:S(2)}, u32[]{:S(2)}) collective-permute-start(bf16[128,256]{1,0:T(8,128)(2,1)S(1)} %get-tuple-element.48), channel_id=1, source_target_pairs={{0,3},{1,2},{2,1},{3,0},{4,7},{5,6},{6,5},{7,4},{8,11},{9,10},{10,... | collective-permute-start | bytes 196616 | tf_op jit(solution)/shard_map/ppermute | solution.py:20
  70.8 0.7 collective-permute-done.23.refs_2_
  71.5 2.9 %collective-permute-done.24.refs_3_ = bf16[128,768]{1,0:T(8,128)(2,1)S(1)} collective-permute-done((bf16[128,768]{1,0:T(8,128)(2,1)S(1)}, bf16[128,768]{1,0:T(8,128)(2,1)S(1)}, u32[]{:S(2)}, u32[]{:S(2)}) %collective-permute-start.24) | collective-permute-done | bytes 196640 | tf_op jit(solution)/shard_map/ppermute | solution.py:20
  74.4 1.5 %place0.1.refs_4_ = bf16[128,4096]{1,0:T(8,128)(2,1)} custom-call(s32[3]{0:T(128)S(1)} %pad_add_fusion.place_ref, bf16[128,768]{1,0:T(8,128)(2,1)S(1)} %get-tuple-element.49.refs_0_, bf16[128,768]{1,0:T(8,128)(2,1)S(1)} %collective-permute-done.22.refs_1_, bf16[128,768]{1,0:T(8,128)(2,1)S(1)} %collective-permute-done.23.refs_2_, ...), custom_call_target="tpu_custom_call" | custom-call | tf_op jit(solution)/shard_map/place0/pallas_call | solution.py:294
  75.9 0.0 collective-permute-done.19.refs_1_
  75.9 1.2 %collective-permute-done.20.refs_2_ = bf16[128,256]{1,0:T(8,128)(2,1)S(1)} collective-permute-done((bf16[128,256]{1,0:T(8,128)(2,1)S(1)}, bf16[128,256]{1,0:T(8,128)(2,1)S(1)}, u32[]{:S(2)}, u32[]{:S(2)}) %collective-permute-start.20) | collective-permute-done | bytes 65568 | tf_op jit(solution)/shard_map/ppermute | solution.py:20
  77.1 0.1 collective-permute-done.21.refs_3_
  77.2 1.3 %place1.1 = bf16[128,4096]{1,0:T(8,128)(2,1)} custom-call(s32[3]{0:T(128)S(1)} %pad_add_fusion.place_ref, bf16[128,256]{1,0:T(8,128)(2,1)S(1)} %get-tuple-element.45.refs_0_, bf16[128,256]{1,0:T(8,128)(2,1)S(1)} %collective-permute-done.19.refs_1_, bf16[128,256]{1,0:T(8,128)(2,1)S(1)} %collective-permute-done.20.refs_2_, ...), custom_call_target="tpu_custom_call", output_to_operand_aliasing={{}: (5, {})} | custom-call | tf_op jit(solution)/shard_map/place1/pallas_call | solution.py:294
  (4 shorter events, 0.0 us)
Async XLA Ops:
  1.7 28.2 %collective-permute-start.4 = (bf16[1024,256]{1,0:T(8,128)(2,1)S(1)}, bf16[1024,256]{1,0:T(8,128)(2,1)S(1)}, u32[]{:S(2)}, u32[]{:S(2)}) collective-permute-start(bf16[1024,256]{1,0:T(8,128)(2,1)S(1)} %pack.1.other_ref), channel_id=1, source_target_pairs={{0,4},{1,5},{2,6},{3,7},{4,0},{5,1},{6,2},{7,3},{8,12},{9,13},{10,... | collective-permute-start | bytes 1572872 | tf_op jit(solution)/shard_map/ppermute | solution.py:20
  4.8 25.6 %collective-permute-start.3 = (bf16[1024,256]{1,0:T(8,128)(2,1)S(1)}, bf16[1024,256]{1,0:T(8,128)(2,1)S(1)}, u32[]{:S(2)}, u32[]{:S(2)}) collective-permute-start(bf16[1024,256]{1,0:T(8,128)(2,1)S(1)} %pack.1.other_ref), channel_id=1, source_target_pairs={{0,8},{1,9},{2,10},{3,11},{4,12},{5,13},{6,14},{7,15},{8,0},{9,1},... | collective-permute-start | bytes 1572872 | tf_op jit(solution)/shard_map/ppermute | solution.py:20
  9.2 11.4 %collective-permute-start.2 = (bf16[384,512]{1,0:T(8,128)(2,1)S(1)}, bf16[384,512]{1,0:T(8,128)(2,1)S(1)}, u32[]{:S(2)}, u32[]{:S(2)}) collective-permute-start(bf16[384,512]{1,0:T(8,128)(2,1)S(1)} %get-tuple-element.32), channel_id=1, source_target_pairs={{0,3},{1,2},{2,1},{3,0},{4,7},{5,6},{6,5},{7,4},{8,11},{9,10},{10,... | collective-permute-start | bytes 1179656 | tf_op jit(solution)/shard_map/ppermute | solution.py:20
  9.6 36.7 %copy-start.1 = (s32[16]{0:T(128)S(1)}, s32[16]{0:T(128)}, u32[]{:S(2)}) copy-start(s32[16]{0:T(128)} %doc_ref.3) | copy-start | bytes 196
  9.6 19.4 %collective-permute-start.1 = (bf16[384,512]{1,0:T(8,128)(2,1)S(1)}, bf16[384,512]{1,0:T(8,128)(2,1)S(1)}, u32[]{:S(2)}, u32[]{:S(2)}) collective-permute-start(bf16[384,512]{1,0:T(8,128)(2,1)S(1)} %get-tuple-element.29.other_ref), channel_id=1, source_target_pairs={{0,2},{1,3},{2,0},{3,1},{4,6},{5,7},{6,4},{7,5},{8,10},{9,11},{10,... | collective-permute-start | bytes 1179656 | tf_op jit(solution)/shard_map/ppermute | solution.py:20
  12.7 16.4 %collective-permute-start = (bf16[384,512]{1,0:T(8,128)(2,1)S(1)}, bf16[384,512]{1,0:T(8,128)(2,1)S(1)}, u32[]{:S(2)}, u32[]{:S(2)}) collective-permute-start(bf16[384,512]{1,0:T(8,128)(2,1)S(1)} %get-tuple-element.31), channel_id=1, source_target_pairs={{0,1},{1,0},{2,3},{3,2},{4,5},{5,4},{6,7},{7,6},{8,9},{9,8},{10,11... | collective-permute-start | bytes 1179656 | tf_op jit(solution)/shard_map/ppermute | solution.py:20
  30.3 19.1 %collective-permute-start.15 = (bf16[1024,256]{1,0:T(8,128)(2,1)S(1)}, bf16[1024,256]{1,0:T(8,128)(2,1)S(1)}, u32[]{:S(2)}, u32[]{:S(2)}) collective-permute-start(bf16[1024,256]{1,0:T(8,128)(2,1)S(1)} %collective-permute-done.3.refs_1_), channel_id=1, source_target_pairs={{0,16},{16,0},{1,17},{17,1},{2,18},{18,2},{3,19},{19,3},{4,20},{20... | collective-permute-start | bytes 1572872 | tf_op jit(solution)/shard_map/ppermute | solution.py:24
  31.8 14.5 %collective-permute-start.5 = (bf16[256,512]{1,0:T(8,128)(2,1)S(1)}, bf16[256,512]{1,0:T(8,128)(2,1)S(1)}, u32[]{:S(2)}, u32[]{:S(2)}) collective-permute-start(bf16[256,512]{1,0:T(8,128)(2,1)S(1)} %get-tuple-element.35), channel_id=1, source_target_pairs={{0,4},{1,5},{2,6},{3,7},{4,0},{5,1},{6,2},{7,3},{8,12},{9,13},{10,... | collective-permute-start | bytes 786440 | tf_op jit(solution)/shard_map/ppermute | solution.py:20
  32.3 9.6 %collective-permute-start.6 = (bf16[128,512]{1,0:T(8,128)(2,1)S(1)}, bf16[128,512]{1,0:T(8,128)(2,1)S(1)}, u32[]{:S(2)}, u32[]{:S(2)}) collective-permute-start(bf16[128,512]{1,0:T(8,128)(2,1)S(1)} %get-tuple-element.36), channel_id=1, source_target_pairs={{0,8},{1,9},{2,10},{3,11},{4,12},{5,13},{6,14},{7,15},{8,0},{9,1},... | collective-permute-start | bytes 393224 | tf_op jit(solution)/shard_map/ppermute | solution.py:20
  34.9 11.0 %collective-permute-start.7 = (bf16[128,512]{1,0:T(8,128)(2,1)S(1)}, bf16[128,512]{1,0:T(8,128)(2,1)S(1)}, u32[]{:S(2)}, u32[]{:S(2)}) collective-permute-start(bf16[128,512]{1,0:T(8,128)(2,1)S(1)} %get-tuple-element.36), channel_id=1, source_target_pairs={{0,12},{1,13},{2,14},{3,15},{4,8},{5,9},{6,10},{7,11},{8,4},{9,5},... | collective-permute-start | bytes 393224 | tf_op jit(solution)/shard_map/ppermute | solution.py:20
  41.9 14.4 %collective-permute-start.9 = (bf16[1024,256]{1,0:T(8,128)(2,1)S(1)}, bf16[1024,256]{1,0:T(8,128)(2,1)S(1)}, u32[]{:S(2)}, u32[]{:S(2)}) collective-permute-start(bf16[1024,256]{1,0:T(8,128)(2,1)S(1)} %collective-permute-done.3.refs_1_), channel_id=1, source_target_pairs={{0,4},{1,5},{2,6},{3,7},{4,0},{5,1},{6,2},{7,3},{8,12},{9,13},{10,... | collective-permute-start | bytes 1572872 | tf_op jit(solution)/shard_map/ppermute | solution.py:20
  48.3 7.6 %collective-permute-start.8 = (bf16[256,512]{1,0:T(8,128)(2,1)S(1)}, bf16[256,512]{1,0:T(8,128)(2,1)S(1)}, u32[]{:S(2)}, u32[]{:S(2)}) collective-permute-start(bf16[256,512]{1,0:T(8,128)(2,1)S(1)} %attend0.1.refs_7_.refs_0_), channel_id=1, source_target_pairs={{0,2},{1,3},{2,0},{3,1},{4,6},{5,7},{6,4},{7,5},{8,10},{9,11},{10,... | collective-permute-start | bytes 786440 | tf_op jit(solution)/shard_map/ppermute | solution.py:20
  49.4 9.8 %collective-permute-start.16 = (bf16[1024,256]{1,0:T(8,128)(2,1)S(1)}, bf16[1024,256]{1,0:T(8,128)(2,1)S(1)}, u32[]{:S(2)}, u32[]{:S(2)}) collective-permute-start(bf16[1024,256]{1,0:T(8,128)(2,1)S(1)} %collective-permute-done.4.refs_3_), channel_id=1, source_target_pairs={{0,16},{16,0},{1,17},{17,1},{2,18},{18,2},{3,19},{19,3},{4,20},{20... | collective-permute-start | bytes 1572872 | tf_op jit(solution)/shard_map/ppermute | solution.py:24
  51.9 6.8 %collective-permute-start.12 = (bf16[256,512]{1,0:T(8,128)(2,1)S(1)}, bf16[256,512]{1,0:T(8,128)(2,1)S(1)}, u32[]{:S(2)}, u32[]{:S(2)}) collective-permute-start(bf16[256,512]{1,0:T(8,128)(2,1)S(1)} %attend1.1.refs_1_), channel_id=1, source_target_pairs={{0,2},{1,3},{2,0},{3,1},{4,6},{5,7},{6,4},{7,5},{8,10},{9,11},{10,... | collective-permute-start | bytes 786440 | tf_op jit(solution)/shard_map/ppermute | solution.py:20
  56.3 2.4 %collective-permute-start.13 = (bf16[256,512]{1,0:T(8,128)(2,1)S(1)}, bf16[256,512]{1,0:T(8,128)(2,1)S(1)}, u32[]{:S(2)}, u32[]{:S(2)}) collective-permute-start(bf16[256,512]{1,0:T(8,128)(2,1)S(1)} %collective-permute-done.8.refs_4_), channel_id=1, source_target_pairs={{0,1},{1,0},{2,3},{3,2},{4,5},{5,4},{6,7},{7,6},{8,9},{9,8},{10,11... | collective-permute-start | bytes 786440 | tf_op jit(solution)/shard_map/ppermute | solution.py:20
  56.3 4.1 %collective-permute-start.10 = (bf16[256,512]{1,0:T(8,128)(2,1)S(1)}, bf16[256,512]{1,0:T(8,128)(2,1)S(1)}, u32[]{:S(2)}, u32[]{:S(2)}) collective-permute-start(bf16[256,512]{1,0:T(8,128)(2,1)S(1)} %attend0.1.refs_7_.refs_0_), channel_id=1, source_target_pairs={{0,1},{1,0},{2,3},{3,2},{4,5},{5,4},{6,7},{7,6},{8,9},{9,8},{10,11... | collective-permute-start | bytes 786440 | tf_op jit(solution)/shard_map/ppermute | solution.py:20
  56.8 3.6 %collective-permute-start.11 = (bf16[256,512]{1,0:T(8,128)(2,1)S(1)}, bf16[256,512]{1,0:T(8,128)(2,1)S(1)}, u32[]{:S(2)}, u32[]{:S(2)}) collective-permute-start(bf16[256,512]{1,0:T(8,128)(2,1)S(1)} %attend1.1.refs_1_), channel_id=1, source_target_pairs={{0,1},{1,0},{2,3},{3,2},{4,5},{5,4},{6,7},{7,6},{8,9},{9,8},{10,11... | collective-permute-start | bytes 786440 | tf_op jit(solution)/shard_map/ppermute | solution.py:20
  58.7 1.7 %collective-permute-start.14 = (bf16[256,512]{1,0:T(8,128)(2,1)S(1)}, bf16[256,512]{1,0:T(8,128)(2,1)S(1)}, u32[]{:S(2)}, u32[]{:S(2)}) collective-permute-start(bf16[256,512]{1,0:T(8,128)(2,1)S(1)} %collective-permute-done.12.refs_5_), channel_id=1, source_target_pairs={{0,1},{1,0},{2,3},{3,2},{4,5},{5,4},{6,7},{7,6},{8,9},{9,8},{10,11... | collective-permute-start | bytes 786440 | tf_op jit(solution)/shard_map/ppermute | solution.py:20
  58.7 8.8 %collective-permute-start.18 = (bf16[512,256]{1,0:T(8,128)(2,1)S(1)}, bf16[512,256]{1,0:T(8,128)(2,1)S(1)}, u32[]{:S(2)}, u32[]{:S(2)}) collective-permute-start(bf16[512,256]{1,0:T(8,128)(2,1)S(1)} %slice.8), channel_id=1, source_target_pairs={{0,4},{1,5},{2,6},{3,7},{4,0},{5,1},{6,2},{7,3},{8,12},{9,13},{10,... | collective-permute-start | bytes 786440 | tf_op jit(solution)/shard_map/ppermute | solution.py:20
  59.2 1.9 %copy-start = (bf16[2048,256]{1,0:T(8,128)(2,1)S(1)}, bf16[2048,256]{1,0:T(8,128)(2,1)}, u32[]{:S(2)}) copy-start(bf16[2048,256]{1,0:T(8,128)(2,1)} %refs_0_.1) | copy-start | bytes 3145732
  59.2 8.4 %collective-permute-start.17 = (bf16[512,256]{1,0:T(8,128)(2,1)S(1)}, bf16[512,256]{1,0:T(8,128)(2,1)S(1)}, u32[]{:S(2)}, u32[]{:S(2)}) collective-permute-start(bf16[512,256]{1,0:T(8,128)(2,1)S(1)} %slice.6), channel_id=1, source_target_pairs={{0,16},{16,0},{1,17},{17,1},{2,18},{18,2},{3,19},{19,3},{4,20},{20... | collective-permute-start | bytes 786440 | tf_op jit(solution)/shard_map/ppermute | solution.py:24
  63.5 6.5 %collective-permute-start.22 = (bf16[128,768]{1,0:T(8,128)(2,1)S(1)}, bf16[128,768]{1,0:T(8,128)(2,1)S(1)}, u32[]{:S(2)}, u32[]{:S(2)}) collective-permute-start(bf16[128,768]{1,0:T(8,128)(2,1)S(1)} %get-tuple-element.50), channel_id=1, source_target_pairs={{0,1},{1,0},{2,3},{3,2},{4,5},{5,4},{6,7},{7,6},{8,9},{9,8},{10,11... | collective-permute-start | bytes 589832 | tf_op jit(solution)/shard_map/ppermute | solution.py:20
  63.7 7.7 %collective-permute-start.23 = (bf16[128,768]{1,0:T(8,128)(2,1)S(1)}, bf16[128,768]{1,0:T(8,128)(2,1)S(1)}, u32[]{:S(2)}, u32[]{:S(2)}) collective-permute-start(bf16[128,768]{1,0:T(8,128)(2,1)S(1)} %get-tuple-element.51), channel_id=1, source_target_pairs={{0,2},{1,3},{2,0},{3,1},{4,6},{5,7},{6,4},{7,5},{8,10},{9,11},{10,... | collective-permute-start | bytes 589832 | tf_op jit(solution)/shard_map/ppermute | solution.py:20
  64.7 9.7 %collective-permute-start.24 = (bf16[128,768]{1,0:T(8,128)(2,1)S(1)}, bf16[128,768]{1,0:T(8,128)(2,1)S(1)}, u32[]{:S(2)}, u32[]{:S(2)}) collective-permute-start(bf16[128,768]{1,0:T(8,128)(2,1)S(1)} %get-tuple-element.52), channel_id=1, source_target_pairs={{0,3},{1,2},{2,1},{3,0},{4,7},{5,6},{6,5},{7,4},{8,11},{9,10},{10,... | collective-permute-start | bytes 589832 | tf_op jit(solution)/shard_map/ppermute | solution.py:20
  68.9 7.1 %collective-permute-start.19 = (bf16[128,256]{1,0:T(8,128)(2,1)S(1)}, bf16[128,256]{1,0:T(8,128)(2,1)S(1)}, u32[]{:S(2)}, u32[]{:S(2)}) collective-permute-start(bf16[128,256]{1,0:T(8,128)(2,1)S(1)} %get-tuple-element.46), channel_id=1, source_target_pairs={{0,1},{1,0},{2,3},{3,2},{4,5},{5,4},{6,7},{7,6},{8,9},{9,8},{10,11... | collective-permute-start | bytes 196616 | tf_op jit(solution)/shard_map/ppermute | solution.py:20
  68.9 8.2 %collective-permute-start.20 = (bf16[128,256]{1,0:T(8,128)(2,1)S(1)}, bf16[128,256]{1,0:T(8,128)(2,1)S(1)}, u32[]{:S(2)}, u32[]{:S(2)}) collective-permute-start(bf16[128,256]{1,0:T(8,128)(2,1)S(1)} %get-tuple-element.47), channel_id=1, source_target_pairs={{0,2},{1,3},{2,0},{3,1},{4,6},{5,7},{6,4},{7,5},{8,10},{9,11},{10,... | collective-permute-start | bytes 196616 | tf_op jit(solution)/shard_map/ppermute | solution.py:20
  69.9 7.3 %collective-permute-start.21 = (bf16[128,256]{1,0:T(8,128)(2,1)S(1)}, bf16[128,256]{1,0:T(8,128)(2,1)S(1)}, u32[]{:S(2)}, u32[]{:S(2)}) collective-permute-start(bf16[128,256]{1,0:T(8,128)(2,1)S(1)} %get-tuple-element.48), channel_id=1, source_target_pairs={{0,3},{1,2},{2,1},{3,0},{4,7},{5,6},{6,5},{7,4},{8,11},{9,10},{10,... | collective-permute-start | bytes 196616 | tf_op jit(solution)/shard_map/ppermute | solution.py:20

commit v11 on v10

--- a/solution.py
+++ b/solution.py
@@ -113,8 +113,6 @@
     for n, rows_ref in enumerate((key_ref, value_ref)):
         at = 128 + 128 * n
         for part in range(2):
-            if n == 1:
-                rows_ref[128 * part : 128 * part + 128, :] = own[2 * half + part][at : at + 128, :]
             rows_ref[256 + 64 * part : 320 + 64 * part, :] = halve(own[2 - 2 * half + part][at : at + 128, :])
         rows_ref[384:512, :] = l_ref[128 * n : 128 * n + 128, :]
         rows_ref[512:576, :] = h_ref[64 * n : 64 * n + 64, :]
@@ -151,7 +149,12 @@
             power = jnp.exp2((biased - jnp.max(biased, axis=-1, keepdims=True)) * (HD ** (-0.5) * LOG2_E))
             raised.append(power.astype(jnp.bfloat16))
             inverse.append(1.0 / jnp.sum(power, axis=-1, keepdims=True))
-        mixed = jnp.dot(jnp.concatenate(raised, 0), value_ref[:, columns], preferred_element_type=jnp.float32)
+        raised = jnp.concatenate(raised, 0)
+        mixed = jnp.dot(raised[:, 256:640], value_ref[256:640, columns], preferred_element_type=jnp.float32)
+        for part in range(2):
+            run = slice(128 * part, 128 * part + 128)
+            values = own[2 * half + part][256:384, columns]
+            mixed += jnp.dot(raised[:, run], values, preferred_element_type=jnp.float32)
         for part in range(2):
             run = slice(128 * part, 128 * part + 128)
             out_ref[run, columns] = (mixed[run, :] * inverse[part]).astype(jnp.bfloat16)

time: 78.7 us -> 78.6 us (level)
  no operation moved by 1% of the time
where the time goes in v11:
time: 78.6 us; the launch traced here: 78.5 us
  waiting for transfers between devices  37.2 us (47%)
  starting transfers between devices  24 us (31%)
  Pallas kernels  17 us (22%)
    ppermute x22, waiting for transfers between devices, swap(): return lax.ppermute(value, 'ctx', pairs)  36.6 us
    ppermute x22, starting transfers between devices, swap(): return lax.ppermute(value, 'ctx', pairs)  20.9 us
    pallas_call x2, Pallas kernels, per_device_fast(): call(functools.partial(attention_kernel, n), [(2 * length, share)], [pl.B...  3.87 us
    pallas_call x2, Pallas kernels, per_device_fast(): call(project_kernel, [(length, count * wide)] * 4, vmem(1 + len(blocks)),...  3.58 us
    ppermute x3, starting transfers between devices, swap_groups(): return lax.ppermute(value, 'groups', [(0, 1), (1, 0)])  3.14 us
    pallas_call x2, Pallas kernels, per_device_fast(): call(functools.partial(place_kernel, n), [(length, 16 * wide)], anywhere(...  2.78 us
    pallas_call x1, Pallas kernels, per_device_fast(): call(functools.partial(pack_kernel, (1, 0)), [(3 * length, share)] * 2, a...  1.8 us
    pallas_call x1, Pallas kernels, per_device_fast(): call(functools.partial(pack_kernel, (2, 3)), [(3 * length, share)] * 2, a...  1.8 us
  transfers between devices with their start and end apart: 25, of which 16 were waited for; matrix products, arithmetic and copies ran while one was open for 0% of the time, Pallas kernels for 18%

profile of v11, /device:TPU:0, one launch (start us, length us, event | category | flops | bytes accessed | tf_op | source)
XLA Modules:
  0.0 78.5 jit_solution(6502195520198012379)
XLA Ops:
  0.0 0.1 pad_add_fusion.place_ref
  0.1 1.6 %pack.1.other_ref = bf16[1024,256]{1,0:T(8,128)(2,1)S(1)} custom-call(s32[3]{0:T(128)S(1)} %pad_add_fusion.place_ref, bf16[128,2048]{1,0:T(8,128)(2,1)} %q_ref.5, bf16[128,2048]{1,0:T(8,128)(2,1)} %k_ref.5, bf16[128,2048]{1,0:T(8,128)(2,1)} %v_ref.5, bf16[2048,256]{1,0:T(8,128)(2,1)} %refs_0_.1), custom_call_target="tpu_custom_call" | custom-call | tf_op jit(solution)/shard_map/pack/pallas_call | solution.py:231
  1.7 3.1 %collective-permute-start.4 = (bf16[1024,256]{1,0:T(8,128)(2,1)S(1)}, bf16[1024,256]{1,0:T(8,128)(2,1)S(1)}, u32[]{:S(2)}, u32[]{:S(2)}) collective-permute-start(bf16[1024,256]{1,0:T(8,128)(2,1)S(1)} %pack.1.other_ref), channel_id=1, source_target_pairs={{0,4},{1,5},{2,6},{3,7},{4,0},{5,1},{6,2},{7,3},{8,12},{9,13},{10,... | collective-permute-start | bytes 1572872 | tf_op jit(solution)/shard_map/ppermute | solution.py:20
  4.8 2.6 %collective-permute-start.3 = (bf16[1024,256]{1,0:T(8,128)(2,1)S(1)}, bf16[1024,256]{1,0:T(8,128)(2,1)S(1)}, u32[]{:S(2)}, u32[]{:S(2)}) collective-permute-start(bf16[1024,256]{1,0:T(8,128)(2,1)S(1)} %pack.1.other_ref), channel_id=1, source_target_pairs={{0,8},{1,9},{2,10},{3,11},{4,12},{5,13},{6,14},{7,15},{8,0},{9,1},... | collective-permute-start | bytes 1572872 | tf_op jit(solution)/shard_map/ppermute | solution.py:20
  7.4 1.8 %pack0.1 = (bf16[384,512]{1,0:T(8,128)(2,1)S(1)}, bf16[384,512]{1,0:T(8,128)(2,1)S(1)}) custom-call(s32[3]{0:T(128)S(1)} %pad_add_fusion.place_ref, bf16[128,2048]{1,0:T(8,128)(2,1)} %q_ref.5, bf16[128,2048]{1,0:T(8,128)(2,1)} %k_ref.5, bf16[128,2048]{1,0:T(8,128)(2,1)} %v_ref.5, bf16[1024,256]{1,0:T(8,128)(2,1)S(1)} %pack.1.other_ref), custom_call_target="tpu_custom_call" | custom-call | tf_op jit(solution)/shard_map/pack0/pallas_call | solution.py:238
  9.2 0.5 collective-permute-start.2
  9.6 1.2 %collective-permute-start.1 = (bf16[384,512]{1,0:T(8,128)(2,1)S(1)}, bf16[384,512]{1,0:T(8,128)(2,1)S(1)}, u32[]{:S(2)}, u32[]{:S(2)}) collective-permute-start(bf16[384,512]{1,0:T(8,128)(2,1)S(1)} %get-tuple-element.29.other_ref), channel_id=1, source_target_pairs={{0,2},{1,3},{2,0},{3,1},{4,6},{5,7},{6,4},{7,5},{8,10},{9,11},{10,... | collective-permute-start | bytes 1179656 | tf_op jit(solution)/shard_map/ppermute | solution.py:20
  10.8 1.8 %pack1.1 = (bf16[384,512]{1,0:T(8,128)(2,1)S(1)}, bf16[384,512]{1,0:T(8,128)(2,1)S(1)}) custom-call(s32[3]{0:T(128)S(1)} %pad_add_fusion.place_ref, bf16[128,2048]{1,0:T(8,128)(2,1)} %q_ref.5, bf16[128,2048]{1,0:T(8,128)(2,1)} %k_ref.5, bf16[128,2048]{1,0:T(8,128)(2,1)} %v_ref.5, bf16[384,512]{1,0:T(8,128)(2,1)S(1)} %get-tuple-element.29.other_ref), custom_call_target="tpu_custom_call" | custom-call | flops 2000000000 | bytes 40000000 | tf_op jit(solution)/shard_map/pack1/pallas_call | solution.py:245
  12.7 0.3 collective-permute-start
  13.0 7.6 %collective-permute-done.2.a3.refs_3_ = bf16[384,512]{1,0:T(8,128)(2,1)S(1)} collective-permute-done((bf16[384,512]{1,0:T(8,128)(2,1)S(1)}, bf16[384,512]{1,0:T(8,128)(2,1)S(1)}, u32[]{:S(2)}, u32[]{:S(2)}) %collective-permute-start.2) | collective-permute-done | bytes 393248 | tf_op jit(solution)/shard_map/ppermute | solution.py:20
  20.6 8.5 %collective-permute-done.1.a2.refs_2_ = bf16[384,512]{1,0:T(8,128)(2,1)S(1)} collective-permute-done((bf16[384,512]{1,0:T(8,128)(2,1)S(1)}, bf16[384,512]{1,0:T(8,128)(2,1)S(1)}, u32[]{:S(2)}, u32[]{:S(2)}) %collective-permute-start.1) | collective-permute-done | bytes 393248 | tf_op jit(solution)/shard_map/ppermute | solution.py:20
  29.1 0.0 collective-permute-done.a1.refs_1_
  29.1 0.8 %coarse.1 = (bf16[256,512]{1,0:T(8,128)(2,1)S(1)}, bf16[128,512]{1,0:T(8,128)(2,1)S(1)}) custom-call(s32[3]{0:T(128)S(1)} %pad_add_fusion.place_ref, bf16[384,512]{1,0:T(8,128)(2,1)S(1)} %get-tuple-element.30.a0.refs_0_.refs_7_, bf16[384,512]{1,0:T(8,128)(2,1)S(1)} %collective-permute-done.a1.refs_1_, ...), custom_call_target="tpu_custom_call" | custom-call | tf_op jit(solution)/shard_map/coarse/pallas_call | solution.py:256
  29.9 0.0 collective-permute-done.4.refs_3_
  29.9 0.4 collective-permute-done.3.refs_1_
  30.3 1.5 %collective-permute-start.15 = (bf16[1024,256]{1,0:T(8,128)(2,1)S(1)}, bf16[1024,256]{1,0:T(8,128)(2,1)S(1)}, u32[]{:S(2)}, u32[]{:S(2)}) collective-permute-start(bf16[1024,256]{1,0:T(8,128)(2,1)S(1)} %collective-permute-done.3.refs_1_), channel_id=1, source_target_pairs={{0,16},{16,0},{1,17},{17,1},{2,18},{18,2},{3,19},{19,3},{4,20},{20... | collective-permute-start | bytes 1572872 | tf_op jit(solution)/shard_map/ppermute | solution.py:24
  31.8 0.4 collective-permute-start.5
  32.3 2.6 %collective-permute-start.6 = (bf16[128,512]{1,0:T(8,128)(2,1)S(1)}, bf16[128,512]{1,0:T(8,128)(2,1)S(1)}, u32[]{:S(2)}, u32[]{:S(2)}) collective-permute-start(bf16[128,512]{1,0:T(8,128)(2,1)S(1)} %get-tuple-element.36), channel_id=1, source_target_pairs={{0,8},{1,9},{2,10},{3,11},{4,12},{5,13},{6,14},{7,15},{8,0},{9,1},... | collective-permute-start | bytes 393224 | tf_op jit(solution)/shard_map/ppermute | solution.py:20
  34.9 1.4 %collective-permute-start.7 = (bf16[128,512]{1,0:T(8,128)(2,1)S(1)}, bf16[128,512]{1,0:T(8,128)(2,1)S(1)}, u32[]{:S(2)}, u32[]{:S(2)}) collective-permute-start(bf16[128,512]{1,0:T(8,128)(2,1)S(1)} %get-tuple-element.36), channel_id=1, source_target_pairs={{0,12},{1,13},{2,14},{3,15},{4,8},{5,9},{6,10},{7,11},{8,4},{9,5},... | collective-permute-start | bytes 393224 | tf_op jit(solution)/shard_map/ppermute | solution.py:20
  36.2 5.7 %collective-permute-done.6.refs_5_ = bf16[128,512]{1,0:T(8,128)(2,1)S(1)} collective-permute-done((bf16[128,512]{1,0:T(8,128)(2,1)S(1)}, bf16[128,512]{1,0:T(8,128)(2,1)S(1)}, u32[]{:S(2)}, u32[]{:S(2)}) %collective-permute-start.6) | collective-permute-done | bytes 131104 | tf_op jit(solution)/shard_map/ppermute | solution.py:20
  41.9 2.2 %collective-permute-start.9 = (bf16[1024,256]{1,0:T(8,128)(2,1)S(1)}, bf16[1024,256]{1,0:T(8,128)(2,1)S(1)}, u32[]{:S(2)}, u32[]{:S(2)}) collective-permute-start(bf16[1024,256]{1,0:T(8,128)(2,1)S(1)} %collective-permute-done.3.refs_1_), channel_id=1, source_target_pairs={{0,4},{1,5},{2,6},{3,7},{4,0},{5,1},{6,2},{7,3},{8,12},{9,13},{10,... | collective-permute-start | bytes 1572872 | tf_op jit(solution)/shard_map/ppermute | solution.py:20
  44.1 1.7 %collective-permute-done.7.refs_6_ = bf16[128,512]{1,0:T(8,128)(2,1)S(1)} collective-permute-done((bf16[128,512]{1,0:T(8,128)(2,1)S(1)}, bf16[128,512]{1,0:T(8,128)(2,1)S(1)}, u32[]{:S(2)}, u32[]{:S(2)}) %collective-permute-start.7) | collective-permute-done | bytes 131104 | tf_op jit(solution)/shard_map/ppermute | solution.py:20
  45.9 0.4 collective-permute-done.5.refs_4_
  46.3 0.0 copy-done.1
  46.3 1.9 %attend0.1.refs_7_.refs_0_ = bf16[256,512]{1,0:T(8,128)(2,1)S(1)} custom-call(s32[3]{0:T(128)S(1)} %pad_add_fusion.place_ref, s32[16]{0:T(128)S(1)} %copy-done.1, bf16[384,512]{1,0:T(8,128)(2,1)S(1)} %get-tuple-element.30.a0.refs_0_.refs_7_, bf16[384,512]{1,0:T(8,128)(2,1)S(1)} %collective-permute-done.a1.refs_1_, ...), custom_call_target="tpu_custom_call" | custom-call | flops 2000000000 | bytes 40000000 | tf_op jit(solution)/shard_map/attend0/pallas_call | solution.py:271
  48.3 1.2 %collective-permute-start.8 = (bf16[256,512]{1,0:T(8,128)(2,1)S(1)}, bf16[256,512]{1,0:T(8,128)(2,1)S(1)}, u32[]{:S(2)}, u32[]{:S(2)}) collective-permute-start(bf16[256,512]{1,0:T(8,128)(2,1)S(1)} %attend0.1.refs_7_.refs_0_), channel_id=1, source_target_pairs={{0,2},{1,3},{2,0},{3,1},{4,6},{5,7},{6,4},{7,5},{8,10},{9,11},{10,... | collective-permute-start | bytes 786440 | tf_op jit(solution)/shard_map/ppermute | solution.py:20
  49.4 0.0 collective-permute-done.15.refs_2_
  49.4 0.5 collective-permute-start.16
  49.9 1.9 %attend1.1.refs_1_ = bf16[256,512]{1,0:T(8,128)(2,1)S(1)} custom-call(s32[3]{0:T(128)S(1)} %pad_add_fusion.place_ref, s32[16]{0:T(128)S(1)} %copy-done.1, bf16[384,512]{1,0:T(8,128)(2,1)S(1)} %get-tuple-element.30.a0.refs_0_.refs_7_, bf16[384,512]{1,0:T(8,128)(2,1)S(1)} %collective-permute-done.a1.refs_1_, ...), custom_call_target="tpu_custom_call" | custom-call | flops 2000000000 | bytes 40000000 | tf_op jit(solution)/shard_map/attend1/pallas_call | solution.py:271
  51.9 1.0 %collective-permute-start.12 = (bf16[256,512]{1,0:T(8,128)(2,1)S(1)}, bf16[256,512]{1,0:T(8,128)(2,1)S(1)}, u32[]{:S(2)}, u32[]{:S(2)}) collective-permute-start(bf16[256,512]{1,0:T(8,128)(2,1)S(1)} %attend1.1.refs_1_), channel_id=1, source_target_pairs={{0,2},{1,3},{2,0},{3,1},{4,6},{5,7},{6,4},{7,5},{8,10},{9,11},{10,... | collective-permute-start | bytes 786440 | tf_op jit(solution)/shard_map/ppermute | solution.py:20
  52.9 2.9 %collective-permute-done.8.refs_4_ = bf16[256,512]{1,0:T(8,128)(2,1)S(1)} collective-permute-done((bf16[256,512]{1,0:T(8,128)(2,1)S(1)}, bf16[256,512]{1,0:T(8,128)(2,1)S(1)}, u32[]{:S(2)}, u32[]{:S(2)}) %collective-permute-start.8) | collective-permute-done | bytes 262176 | tf_op jit(solution)/shard_map/ppermute | solution.py:20
  55.8 0.5 collective-permute-done.9.refs_0_
  56.3 0.0 collective-permute-start.13
  56.3 0.5 collective-permute-start.10
  56.8 0.0 collective-permute-start.11
  56.8 1.8 %collective-permute-done.12.refs_5_ = bf16[256,512]{1,0:T(8,128)(2,1)S(1)} collective-permute-done((bf16[256,512]{1,0:T(8,128)(2,1)S(1)}, bf16[256,512]{1,0:T(8,128)(2,1)S(1)}, u32[]{:S(2)}, u32[]{:S(2)}) %collective-permute-start.12) | collective-permute-done | bytes 262176 | tf_op jit(solution)/shard_map/ppermute | solution.py:20
  58.6 0.0 collective-permute-done.13.refs_6_
  58.6 0.0 collective-permute-start.14
  58.7 0.1 collective-permute-start.18
  58.7 0.4 collective-permute-done.16.refs_4_
  59.2 0.0 copy-start
  59.2 1.1 %collective-permute-start.17 = (bf16[512,256]{1,0:T(8,128)(2,1)S(1)}, bf16[512,256]{1,0:T(8,128)(2,1)S(1)}, u32[]{:S(2)}, u32[]{:S(2)}) collective-permute-start(bf16[512,256]{1,0:T(8,128)(2,1)S(1)} %slice.6), channel_id=1, source_target_pairs={{0,16},{16,0},{1,17},{17,1},{2,18},{18,2},{3,19},{19,3},{4,20},{20... | collective-permute-start | bytes 786440 | tf_op jit(solution)/shard_map/ppermute | solution.py:24
  60.4 0.0 collective-permute-done.10.refs_2_
  60.4 0.0 collective-permute-done.11.refs_3_
  60.4 0.0 collective-permute-done.14.refs_7_
  60.4 0.7 gather.1.rows_ref
  61.1 2.3 %project3.1 = (bf16[128,768]{1,0:T(8,128)(2,1)S(1)}, bf16[128,768]{1,0:T(8,128)(2,1)S(1)}, bf16[128,768]{1,0:T(8,128)(2,1)S(1)}, bf16[128,768]{1,0:T(8,128)(2,1)S(1)}) custom-call(s32[3]{0:T(128)S(1)} %pad_add_fusion.place_ref, bf16[512,2048]{1,0:T(8,128)(2,1)S(1)} %gather.1.rows_ref, bf16[2048,256]{1,0:T(8,128)(2,1)S(1)} %copy-done, ...), custom_call_target="tpu_custom_call" | custom-call | tf_op jit(solution)/shard_map/project3/pallas_call | solution.py:291
  63.4 0.3 collective-permute-start.22
  63.7 0.9 %collective-permute-start.23 = (bf16[128,768]{1,0:T(8,128)(2,1)S(1)}, bf16[128,768]{1,0:T(8,128)(2,1)S(1)}, u32[]{:S(2)}, u32[]{:S(2)}) collective-permute-start(bf16[128,768]{1,0:T(8,128)(2,1)S(1)} %get-tuple-element.51), channel_id=1, source_target_pairs={{0,2},{1,3},{2,0},{3,1},{4,6},{5,7},{6,4},{7,5},{8,10},{9,11},{10,... | collective-permute-start | bytes 589832 | tf_op jit(solution)/shard_map/ppermute | solution.py:20
  64.6 0.7 collective-permute-start.24
  65.3 2.1 %collective-permute-done.18.refs_2_ = bf16[512,256]{1,0:T(8,128)(2,1)S(1)} collective-permute-done((bf16[512,256]{1,0:T(8,128)(2,1)S(1)}, bf16[512,256]{1,0:T(8,128)(2,1)S(1)}, u32[]{:S(2)}, u32[]{:S(2)}) %collective-permute-start.18) | collective-permute-done | bytes 262176 | tf_op jit(solution)/shard_map/ppermute | solution.py:20
  67.5 0.1 collective-permute-done.17.refs_1_
  67.6 1.2 %project1.1 = (bf16[128,256]{1,0:T(8,128)(2,1)S(1)}, bf16[128,256]{1,0:T(8,128)(2,1)S(1)}, bf16[128,256]{1,0:T(8,128)(2,1)S(1)}, bf16[128,256]{1,0:T(8,128)(2,1)S(1)}) custom-call(s32[3]{0:T(128)S(1)} %pad_add_fusion.place_ref, bf16[512,2048]{1,0:T(8,128)(2,1)S(1)} %gather.1.rows_ref, bf16[1024,256]{1,0:T(8,128)(2,1)S(1)} %collective-permute-done.9.refs_0_, ...), custom_call_target="tpu_custom_call" | custom-call | tf_op jit(solution)/shard_map/project1/pallas_call | solution.py:291
  68.8 0.1 collective-permute-start.19
  68.9 1.0 %collective-permute-start.20 = (bf16[128,256]{1,0:T(8,128)(2,1)S(1)}, bf16[128,256]{1,0:T(8,128)(2,1)S(1)}, u32[]{:S(2)}, u32[]{:S(2)}) collective-permute-start(bf16[128,256]{1,0:T(8,128)(2,1)S(1)} %get-tuple-element.47), channel_id=1, source_target_pairs={{0,2},{1,3},{2,0},{3,1},{4,6},{5,7},{6,4},{7,5},{8,10},{9,11},{10,... | collective-permute-start | bytes 196616 | tf_op jit(solution)/shard_map/ppermute | solution.py:20
  69.9 0.0 collective-permute-done.22.refs_1_
  69.9 0.9 %collective-permute-start.21 = (bf16[128,256]{1,0:T(8,128)(2,1)S(1)}, bf16[128,256]{1,0:T(8,128)(2,1)S(1)}, u32[]{:S(2)}, u32[]{:S(2)}) collective-permute-start(bf16[128,256]{1,0:T(8,128)(2,1)S(1)} %get-tuple-element.48), channel_id=1, source_target_pairs={{0,3},{1,2},{2,1},{3,0},{4,7},{5,6},{6,5},{7,4},{8,11},{9,10},{10,... | collective-permute-start | bytes 196616 | tf_op jit(solution)/shard_map/ppermute | solution.py:20
  70.8 0.7 collective-permute-done.23.refs_2_
  71.4 2.9 %collective-permute-done.24.refs_3_ = bf16[128,768]{1,0:T(8,128)(2,1)S(1)} collective-permute-done((bf16[128,768]{1,0:T(8,128)(2,1)S(1)}, bf16[128,768]{1,0:T(8,128)(2,1)S(1)}, u32[]{:S(2)}, u32[]{:S(2)}) %collective-permute-start.24) | collective-permute-done | bytes 196640 | tf_op jit(solution)/shard_map/ppermute | solution.py:20
  74.4 1.5 %place0.1.refs_4_ = bf16[128,4096]{1,0:T(8,128)(2,1)} custom-call(s32[3]{0:T(128)S(1)} %pad_add_fusion.place_ref, bf16[128,768]{1,0:T(8,128)(2,1)S(1)} %get-tuple-element.49.refs_0_, bf16[128,768]{1,0:T(8,128)(2,1)S(1)} %collective-permute-done.22.refs_1_, bf16[128,768]{1,0:T(8,128)(2,1)S(1)} %collective-permute-done.23.refs_2_, ...), custom_call_target="tpu_custom_call" | custom-call | tf_op jit(solution)/shard_map/place0/pallas_call | solution.py:297
  75.9 0.0 collective-permute-done.19.refs_1_
  75.9 1.2 %collective-permute-done.20.refs_2_ = bf16[128,256]{1,0:T(8,128)(2,1)S(1)} collective-permute-done((bf16[128,256]{1,0:T(8,128)(2,1)S(1)}, bf16[128,256]{1,0:T(8,128)(2,1)S(1)}, u32[]{:S(2)}, u32[]{:S(2)}) %collective-permute-start.20) | collective-permute-done | bytes 65568 | tf_op jit(solution)/shard_map/ppermute | solution.py:20
  77.1 0.1 collective-permute-done.21.refs_3_
  77.2 1.3 %place1.1 = bf16[128,4096]{1,0:T(8,128)(2,1)} custom-call(s32[3]{0:T(128)S(1)} %pad_add_fusion.place_ref, bf16[128,256]{1,0:T(8,128)(2,1)S(1)} %get-tuple-element.45.refs_0_, bf16[128,256]{1,0:T(8,128)(2,1)S(1)} %collective-permute-done.19.refs_1_, bf16[128,256]{1,0:T(8,128)(2,1)S(1)} %collective-permute-done.20.refs_2_, ...), custom_call_target="tpu_custom_call", output_to_operand_aliasing={{}: (5, {})} | custom-call | tf_op jit(solution)/shard_map/place1/pallas_call | solution.py:297
  (4 shorter events, 0.0 us)
Async XLA Ops:
  1.7 28.2 %collective-permute-start.4 = (bf16[1024,256]{1,0:T(8,128)(2,1)S(1)}, bf16[1024,256]{1,0:T(8,128)(2,1)S(1)}, u32[]{:S(2)}, u32[]{:S(2)}) collective-permute-start(bf16[1024,256]{1,0:T(8,128)(2,1)S(1)} %pack.1.other_ref), channel_id=1, source_target_pairs={{0,4},{1,5},{2,6},{3,7},{4,0},{5,1},{6,2},{7,3},{8,12},{9,13},{10,... | collective-permute-start | bytes 1572872 | tf_op jit(solution)/shard_map/ppermute | solution.py:20
  4.8 25.6 %collective-permute-start.3 = (bf16[1024,256]{1,0:T(8,128)(2,1)S(1)}, bf16[1024,256]{1,0:T(8,128)(2,1)S(1)}, u32[]{:S(2)}, u32[]{:S(2)}) collective-permute-start(bf16[1024,256]{1,0:T(8,128)(2,1)S(1)} %pack.1.other_ref), channel_id=1, source_target_pairs={{0,8},{1,9},{2,10},{3,11},{4,12},{5,13},{6,14},{7,15},{8,0},{9,1},... | collective-permute-start | bytes 1572872 | tf_op jit(solution)/shard_map/ppermute | solution.py:20
  9.2 11.4 %collective-permute-start.2 = (bf16[384,512]{1,0:T(8,128)(2,1)S(1)}, bf16[384,512]{1,0:T(8,128)(2,1)S(1)}, u32[]{:S(2)}, u32[]{:S(2)}) collective-permute-start(bf16[384,512]{1,0:T(8,128)(2,1)S(1)} %get-tuple-element.32), channel_id=1, source_target_pairs={{0,3},{1,2},{2,1},{3,0},{4,7},{5,6},{6,5},{7,4},{8,11},{9,10},{10,... | collective-permute-start | bytes 1179656 | tf_op jit(solution)/shard_map/ppermute | solution.py:20
  9.6 36.7 %copy-start.1 = (s32[16]{0:T(128)S(1)}, s32[16]{0:T(128)}, u32[]{:S(2)}) copy-start(s32[16]{0:T(128)} %doc_ref.3) | copy-start | bytes 196
  9.6 19.4 %collective-permute-start.1 = (bf16[384,512]{1,0:T(8,128)(2,1)S(1)}, bf16[384,512]{1,0:T(8,128)(2,1)S(1)}, u32[]{:S(2)}, u32[]{:S(2)}) collective-permute-start(bf16[384,512]{1,0:T(8,128)(2,1)S(1)} %get-tuple-element.29.other_ref), channel_id=1, source_target_pairs={{0,2},{1,3},{2,0},{3,1},{4,6},{5,7},{6,4},{7,5},{8,10},{9,11},{10,... | collective-permute-start | bytes 1179656 | tf_op jit(solution)/shard_map/ppermute | solution.py:20
  12.7 16.4 %collective-permute-start = (bf16[384,512]{1,0:T(8,128)(2,1)S(1)}, bf16[384,512]{1,0:T(8,128)(2,1)S(1)}, u32[]{:S(2)}, u32[]{:S(2)}) collective-permute-start(bf16[384,512]{1,0:T(8,128)(2,1)S(1)} %get-tuple-element.31), channel_id=1, source_target_pairs={{0,1},{1,0},{2,3},{3,2},{4,5},{5,4},{6,7},{7,6},{8,9},{9,8},{10,11... | collective-permute-start | bytes 1179656 | tf_op jit(solution)/shard_map/ppermute | solution.py:20
  30.3 19.1 %collective-permute-start.15 = (bf16[1024,256]{1,0:T(8,128)(2,1)S(1)}, bf16[1024,256]{1,0:T(8,128)(2,1)S(1)}, u32[]{:S(2)}, u32[]{:S(2)}) collective-permute-start(bf16[1024,256]{1,0:T(8,128)(2,1)S(1)} %collective-permute-done.3.refs_1_), channel_id=1, source_target_pairs={{0,16},{16,0},{1,17},{17,1},{2,18},{18,2},{3,19},{19,3},{4,20},{20... | collective-permute-start | bytes 1572872 | tf_op jit(solution)/shard_map/ppermute | solution.py:24
  31.8 14.5 %collective-permute-start.5 = (bf16[256,512]{1,0:T(8,128)(2,1)S(1)}, bf16[256,512]{1,0:T(8,128)(2,1)S(1)}, u32[]{:S(2)}, u32[]{:S(2)}) collective-permute-start(bf16[256,512]{1,0:T(8,128)(2,1)S(1)} %get-tuple-element.35), channel_id=1, source_target_pairs={{0,4},{1,5},{2,6},{3,7},{4,0},{5,1},{6,2},{7,3},{8,12},{9,13},{10,... | collective-permute-start | bytes 786440 | tf_op jit(solution)/shard_map/ppermute | solution.py:20
  32.3 9.6 %collective-permute-start.6 = (bf16[128,512]{1,0:T(8,128)(2,1)S(1)}, bf16[128,512]{1,0:T(8,128)(2,1)S(1)}, u32[]{:S(2)}, u32[]{:S(2)}) collective-permute-start(bf16[128,512]{1,0:T(8,128)(2,1)S(1)} %get-tuple-element.36), channel_id=1, source_target_pairs={{0,8},{1,9},{2,10},{3,11},{4,12},{5,13},{6,14},{7,15},{8,0},{9,1},... | collective-permute-start | bytes 393224 | tf_op jit(solution)/shard_map/ppermute | solution.py:20
  34.9 11.0 %collective-permute-start.7 = (bf16[128,512]{1,0:T(8,128)(2,1)S(1)}, bf16[128,512]{1,0:T(8,128)(2,1)S(1)}, u32[]{:S(2)}, u32[]{:S(2)}) collective-permute-start(bf16[128,512]{1,0:T(8,128)(2,1)S(1)} %get-tuple-element.36), channel_id=1, source_target_pairs={{0,12},{1,13},{2,14},{3,15},{4,8},{5,9},{6,10},{7,11},{8,4},{9,5},... | collective-permute-start | bytes 393224 | tf_op jit(solution)/shard_map/ppermute | solution.py:20
  41.9 14.4 %collective-permute-start.9 = (bf16[1024,256]{1,0:T(8,128)(2,1)S(1)}, bf16[1024,256]{1,0:T(8,128)(2,1)S(1)}, u32[]{:S(2)}, u32[]{:S(2)}) collective-permute-start(bf16[1024,256]{1,0:T(8,128)(2,1)S(1)} %collective-permute-done.3.refs_1_), channel_id=1, source_target_pairs={{0,4},{1,5},{2,6},{3,7},{4,0},{5,1},{6,2},{7,3},{8,12},{9,13},{10,... | collective-permute-start | bytes 1572872 | tf_op jit(solution)/shard_map/ppermute | solution.py:20
  48.3 7.6 %collective-permute-start.8 = (bf16[256,512]{1,0:T(8,128)(2,1)S(1)}, bf16[256,512]{1,0:T(8,128)(2,1)S(1)}, u32[]{:S(2)}, u32[]{:S(2)}) collective-permute-start(bf16[256,512]{1,0:T(8,128)(2,1)S(1)} %attend0.1.refs_7_.refs_0_), channel_id=1, source_target_pairs={{0,2},{1,3},{2,0},{3,1},{4,6},{5,7},{6,4},{7,5},{8,10},{9,11},{10,... | collective-permute-start | bytes 786440 | tf_op jit(solution)/shard_map/ppermute | solution.py:20
  49.4 9.8 %collective-permute-start.16 = (bf16[1024,256]{1,0:T(8,128)(2,1)S(1)}, bf16[1024,256]{1,0:T(8,128)(2,1)S(1)}, u32[]{:S(2)}, u32[]{:S(2)}) collective-permute-start(bf16[1024,256]{1,0:T(8,128)(2,1)S(1)} %collective-permute-done.4.refs_3_), channel_id=1, source_target_pairs={{0,16},{16,0},{1,17},{17,1},{2,18},{18,2},{3,19},{19,3},{4,20},{20... | collective-permute-start | bytes 1572872 | tf_op jit(solution)/shard_map/ppermute | solution.py:24
  51.9 6.8 %collective-permute-start.12 = (bf16[256,512]{1,0:T(8,128)(2,1)S(1)}, bf16[256,512]{1,0:T(8,128)(2,1)S(1)}, u32[]{:S(2)}, u32[]{:S(2)}) collective-permute-start(bf16[256,512]{1,0:T(8,128)(2,1)S(1)} %attend1.1.refs_1_), channel_id=1, source_target_pairs={{0,2},{1,3},{2,0},{3,1},{4,6},{5,7},{6,4},{7,5},{8,10},{9,11},{10,... | collective-permute-start | bytes 786440 | tf_op jit(solution)/shard_map/ppermute | solution.py:20
  56.3 2.3 %collective-permute-start.13 = (bf16[256,512]{1,0:T(8,128)(2,1)S(1)}, bf16[256,512]{1,0:T(8,128)(2,1)S(1)}, u32[]{:S(2)}, u32[]{:S(2)}) collective-permute-start(bf16[256,512]{1,0:T(8,128)(2,1)S(1)} %collective-permute-done.8.refs_4_), channel_id=1, source_target_pairs={{0,1},{1,0},{2,3},{3,2},{4,5},{5,4},{6,7},{7,6},{8,9},{9,8},{10,11... | collective-permute-start | bytes 786440 | tf_op jit(solution)/shard_map/ppermute | solution.py:20
  56.3 4.0 %collective-permute-start.10 = (bf16[256,512]{1,0:T(8,128)(2,1)S(1)}, bf16[256,512]{1,0:T(8,128)(2,1)S(1)}, u32[]{:S(2)}, u32[]{:S(2)}) collective-permute-start(bf16[256,512]{1,0:T(8,128)(2,1)S(1)} %attend0.1.refs_7_.refs_0_), channel_id=1, source_target_pairs={{0,1},{1,0},{2,3},{3,2},{4,5},{5,4},{6,7},{7,6},{8,9},{9,8},{10,11... | collective-permute-start | bytes 786440 | tf_op jit(solution)/shard_map/ppermute | solution.py:20
  56.8 3.5 %collective-permute-start.11 = (bf16[256,512]{1,0:T(8,128)(2,1)S(1)}, bf16[256,512]{1,0:T(8,128)(2,1)S(1)}, u32[]{:S(2)}, u32[]{:S(2)}) collective-permute-start(bf16[256,512]{1,0:T(8,128)(2,1)S(1)} %attend1.1.refs_1_), channel_id=1, source_target_pairs={{0,1},{1,0},{2,3},{3,2},{4,5},{5,4},{6,7},{7,6},{8,9},{9,8},{10,11... | collective-permute-start | bytes 786440 | tf_op jit(solution)/shard_map/ppermute | solution.py:20
  58.6 1.7 %collective-permute-start.14 = (bf16[256,512]{1,0:T(8,128)(2,1)S(1)}, bf16[256,512]{1,0:T(8,128)(2,1)S(1)}, u32[]{:S(2)}, u32[]{:S(2)}) collective-permute-start(bf16[256,512]{1,0:T(8,128)(2,1)S(1)} %collective-permute-done.12.refs_5_), channel_id=1, source_target_pairs={{0,1},{1,0},{2,3},{3,2},{4,5},{5,4},{6,7},{7,6},{8,9},{9,8},{10,11... | collective-permute-start | bytes 786440 | tf_op jit(solution)/shard_map/ppermute | solution.py:20
  58.7 8.8 %collective-permute-start.18 = (bf16[512,256]{1,0:T(8,128)(2,1)S(1)}, bf16[512,256]{1,0:T(8,128)(2,1)S(1)}, u32[]{:S(2)}, u32[]{:S(2)}) collective-permute-start(bf16[512,256]{1,0:T(8,128)(2,1)S(1)} %slice.8), channel_id=1, source_target_pairs={{0,4},{1,5},{2,6},{3,7},{4,0},{5,1},{6,2},{7,3},{8,12},{9,13},{10,... | collective-permute-start | bytes 786440 | tf_op jit(solution)/shard_map/ppermute | solution.py:20
  59.2 1.9 %copy-start = (bf16[2048,256]{1,0:T(8,128)(2,1)S(1)}, bf16[2048,256]{1,0:T(8,128)(2,1)}, u32[]{:S(2)}) copy-start(bf16[2048,256]{1,0:T(8,128)(2,1)} %refs_0_.1) | copy-start | bytes 3145732
  59.2 8.4 %collective-permute-start.17 = (bf16[512,256]{1,0:T(8,128)(2,1)S(1)}, bf16[512,256]{1,0:T(8,128)(2,1)S(1)}, u32[]{:S(2)}, u32[]{:S(2)}) collective-permute-start(bf16[512,256]{1,0:T(8,128)(2,1)S(1)} %slice.6), channel_id=1, source_target_pairs={{0,16},{16,0},{1,17},{17,1},{2,18},{18,2},{3,19},{19,3},{4,20},{20... | collective-permute-start | bytes 786440 | tf_op jit(solution)/shard_map/ppermute | solution.py:24
  63.4 6.5 %collective-permute-start.22 = (bf16[128,768]{1,0:T(8,128)(2,1)S(1)}, bf16[128,768]{1,0:T(8,128)(2,1)S(1)}, u32[]{:S(2)}, u32[]{:S(2)}) collective-permute-start(bf16[128,768]{1,0:T(8,128)(2,1)S(1)} %get-tuple-element.50), channel_id=1, source_target_pairs={{0,1},{1,0},{2,3},{3,2},{4,5},{5,4},{6,7},{7,6},{8,9},{9,8},{10,11... | collective-permute-start | bytes 589832 | tf_op jit(solution)/shard_map/ppermute | solution.py:20
  63.7 7.7 %collective-permute-start.23 = (bf16[128,768]{1,0:T(8,128)(2,1)S(1)}, bf16[128,768]{1,0:T(8,128)(2,1)S(1)}, u32[]{:S(2)}, u32[]{:S(2)}) collective-permute-start(bf16[128,768]{1,0:T(8,128)(2,1)S(1)} %get-tuple-element.51), channel_id=1, source_target_pairs={{0,2},{1,3},{2,0},{3,1},{4,6},{5,7},{6,4},{7,5},{8,10},{9,11},{10,... | collective-permute-start | bytes 589832 | tf_op jit(solution)/shard_map/ppermute | solution.py:20
  64.6 9.7 %collective-permute-start.24 = (bf16[128,768]{1,0:T(8,128)(2,1)S(1)}, bf16[128,768]{1,0:T(8,128)(2,1)S(1)}, u32[]{:S(2)}, u32[]{:S(2)}) collective-permute-start(bf16[128,768]{1,0:T(8,128)(2,1)S(1)} %get-tuple-element.52), channel_id=1, source_target_pairs={{0,3},{1,2},{2,1},{3,0},{4,7},{5,6},{6,5},{7,4},{8,11},{9,10},{10,... | collective-permute-start | bytes 589832 | tf_op jit(solution)/shard_map/ppermute | solution.py:20
  68.8 7.1 %collective-permute-start.19 = (bf16[128,256]{1,0:T(8,128)(2,1)S(1)}, bf16[128,256]{1,0:T(8,128)(2,1)S(1)}, u32[]{:S(2)}, u32[]{:S(2)}) collective-permute-start(bf16[128,256]{1,0:T(8,128)(2,1)S(1)} %get-tuple-element.46), channel_id=1, source_target_pairs={{0,1},{1,0},{2,3},{3,2},{4,5},{5,4},{6,7},{7,6},{8,9},{9,8},{10,11... | collective-permute-start | bytes 196616 | tf_op jit(solution)/shard_map/ppermute | solution.py:20
  68.9 8.2 %collective-permute-start.20 = (bf16[128,256]{1,0:T(8,128)(2,1)S(1)}, bf16[128,256]{1,0:T(8,128)(2,1)S(1)}, u32[]{:S(2)}, u32[]{:S(2)}) collective-permute-start(bf16[128,256]{1,0:T(8,128)(2,1)S(1)} %get-tuple-element.47), channel_id=1, source_target_pairs={{0,2},{1,3},{2,0},{3,1},{4,6},{5,7},{6,4},{7,5},{8,10},{9,11},{10,... | collective-permute-start | bytes 196616 | tf_op jit(solution)/shard_map/ppermute | solution.py:20
  69.9 7.3 %collective-permute-start.21 = (bf16[128,256]{1,0:T(8,128)(2,1)S(1)}, bf16[128,256]{1,0:T(8,128)(2,1)S(1)}, u32[]{:S(2)}, u32[]{:S(2)}) collective-permute-start(bf16[128,256]{1,0:T(8,128)(2,1)S(1)} %get-tuple-element.48), channel_id=1, source_target_pairs={{0,3},{1,2},{2,1},{3,0},{4,7},{5,6},{6,5},{7,4},{8,11},{9,10},{10,... | collective-permute-start | bytes 196616 | tf_op jit(solution)/shard_map/ppermute | solution.py:20
